TPU v7x, 32 devices: a whole 2x2x4 slice. The times are simulated.
32 devices in a mesh: energy: 8 (over z, x), slab: 2 (over core), rep: 2 (over y).
Axes of the slice: x: 2, y: 2, z: 4, core: 2. Of those that a mesh axis runs over, the one named last changes fastest.
Arguments:
- green_blocks: bfloat16 [8, 2, 512, 512], P('energy', 'slab', 'rep'), may hold values from -1 to 1
- occupation: float32 [8], P('energy'), may hold values from 0.1 to 1
- offsets: int32 [2], replicated, may hold values from 1 to 4, as said below
- coulomb: float32 [2, 512, 512], P('slab', 'rep'), may hold values from -0.9 to 0.9
- hamiltonian: float32 [2, 512, 512], P('slab', 'rep'), may hold values from -0.25 to 0.25
- onsite_level: float32 [8], P('energy'), may hold values from 2 to 3
- green_steps: int32 [8], P('energy'), may hold values from 1 to 2, as said below
- screen_steps: int32 [2], replicated, may hold values from 0 to 2, as said below
Outputs:
- green_next: float32 [8, 2, 512, 512], P('energy', 'slab', 'rep')
- screened: bfloat16 [2, 2, 512, 512], P(None, 'slab', 'rep')
Inputs may be any that keep to these rules, and one draw needn't show every extreme that they name: `offsets`: some frequency has offset 4; every other frequency has a smaller one. `green_steps`: some energy takes 2 turns. `screen_steps`: some frequency takes 2 turns; every other frequency takes fewer.
All inputs are finite; a program needn't handle non-finite values.
Results may differ from a plain program's by a relative error of at most 0.0004.
Values may be sent and summed in bfloat16 or wider, within the bound.
No kernel may reach another device: no remote copies, remote signals or barrier semaphores. Data moves between devices by JAX's collectives and lax.ppermute only.
A program may use at most 64 MiB of HBM per device.

v0:
```python
import jax
import jax.numpy as jnp
from jax import lax
from jax.sharding import PartitionSpec as P

SHIFTS = 4
FREQS = 2
NG = 2
NW = 2


precise = lax.Precision.HIGHEST


def from_behind(block, axis, distance):
    devices = range(lax.axis_size(axis))
    route = [(i - distance, i) for i in devices if i - distance in devices]
    return lax.ppermute(block, axis, route)


def broadcast(block, axis, owner):
    block = jnp.where(lax.axis_index(axis) == owner, block, jnp.zeros_like(block))
    return lax.psum(block, axis)


def with_halo(value, sides, width):
    for axis, dim in sides:
        peers, length = (lax.axis_size(axis), value.shape[dim])
        up = [(i, (i + 1) % peers) for i in range(peers - 1)]
        down = [(j, i) for i, j in up]
        last = lax.slice_in_dim(value, length - width, length, axis=dim)
        first = lax.slice_in_dim(value, 0, width, axis=dim)
        before = lax.ppermute(last, axis, up)
        after = lax.ppermute(first, axis, down)
        value = jnp.concatenate([before, value, after], axis=dim)
    return value


def row_product(first_factor, second_factor):
    return jnp.einsum("esij,esjk->esik", first_factor, second_factor, precision=precise)


def full_rows(block_rows):
    return lax.all_gather(block_rows, "rep", axis=2, tiled=True)


def newton_rows(operator, initial, known_full, counts, turn_total):
    operator_full = lax.all_gather(operator, "rep", axis=2, tiled=True)
    iterate = initial
    for turn_index in range(turn_total):
        if turn_index == 0 and known_full is not None:
            iterate_full = known_full
        else:
            iterate_full = full_rows(iterate)
        composed = row_product(row_product(iterate, operator_full), iterate_full)
        iterate = jnp.where(
            (turn_index < counts)[:, None, None, None], 2.0 * iterate - composed, iterate
        )
    return iterate


def body(
    green_blocks, occupation, offsets, coulomb, hamiltonian, onsite_level, green_steps, screen_steps
):
    local_count, _, half_rows, full_width = green_blocks.shape
    energies = local_count * lax.axis_size("energy")
    entry_scale = full_width ** (-0.5)
    shift_count = -(-SHIFTS // local_count)
    pieces = []
    received = green_blocks
    for distance in range(1, shift_count + 1):
        received = from_behind(received, "energy", 1)
        pieces.insert(0, received)
    extended = jnp.concatenate(pieces + [green_blocks], axis=0)
    anchor = shift_count * local_count
    lowered = jnp.stack(
        [
            lax.dynamic_slice_in_dim(extended, anchor - offsets[index], local_count, 0)
            for index in range(FREQS)
        ]
    )
    lowered_wide = lowered.astype(jnp.float32)
    weighted = occupation[:, None, None, None] * green_blocks.astype(jnp.float32)
    partial_value = jnp.sum(weighted[None] * lowered_wide, axis=1) * energies ** (-0.5)
    polarization = lax.psum(partial_value, "energy")
    rep_start = lax.axis_index("rep") * half_rows
    col_index = lax.broadcasted_iota(jnp.int32, (half_rows, full_width), 1)
    row_index = lax.broadcasted_iota(jnp.int32, (half_rows, full_width), 0) + rep_start
    identity_rows = (col_index == row_index).astype(jnp.float32)
    identity_full = jnp.eye(full_width, dtype=jnp.float32)[None, None]
    owner_index = lax.axis_index("energy") % FREQS
    polar_own = lax.dynamic_index_in_dim(polarization, owner_index, 0, keepdims=True)
    screen_operator = identity_rows + entry_scale * coulomb[None] * polar_own
    count_own = lax.dynamic_index_in_dim(screen_steps, owner_index, 0, keepdims=True)
    screen_start = jnp.broadcast_to(identity_rows, screen_operator.shape)
    inverse = newton_rows(screen_operator, screen_start, identity_full, count_own, NW)
    inverse_full = full_rows(inverse)
    screened_own = row_product(coulomb[None], inverse_full).astype(jnp.bfloat16)
    screened = jnp.stack([broadcast(screened_own, "energy", index)[0] for index in range(FREQS)])
    self_energy = (
        jnp.sum(lowered_wide * screened.astype(jnp.float32)[:, None], axis=0) * entry_scale
    )
    neighbours = with_halo(green_blocks, (("slab", 1),), 1)
    contact = (neighbours[:, 0:1].astype(jnp.float32) + neighbours[:, 2:3].astype(jnp.float32)) * (
        0.5 * entry_scale
    )
    dyson_rows = (
        onsite_level[:, None, None, None] * identity_rows
        + hamiltonian[None]
        - self_energy
        - contact
    )
    diagonal = jnp.sum(dyson_rows * identity_rows, axis=-1)
    initial = identity_rows * (1.0 / diagonal)[..., None]
    green_next = newton_rows(dyson_rows, initial, None, green_steps, NG)
    return (green_next, screened)


def solution(mesh):
    return jax.shard_map(
        body,
        mesh=mesh,
        in_specs=(
            P("energy", "slab", "rep", None),
            P("energy"),
            P(),
            P("slab", "rep", None),
            P("slab", "rep", None),
            P("energy"),
            P("energy"),
            P(),
        ),
        out_specs=(P("energy", "slab", "rep", None), P(None, "slab", "rep", None)),
        check_vma=False,
    )
```

profile of v0, /device:TPU:26, one launch (start us, length us, event | category | flops | bytes accessed | tf_op | source)
XLA Modules:
  0.0 357.3 jit_solution(1811731379270840315)
XLA Ops:
  7.2 0.0 all-reduce.4.cloned.1.call-start
  7.2 1.1 copy.17
  8.3 1.3 collective-permute-start
  9.6 8.6 %collective-permute-done = bf16[1,1,256,512]{2,3,1,0:T(8,128)(2,1)S(1)} collective-permute-done((bf16[1,1,256,512]{2,3,1,0:T(8,128)(2,1)S(1)}, bf16[1,1,256,512]{2,3,1,0:T(8,128)(2,1)S(1)}, u32[]{:S(2)}, u32[]{:S(2)}) %collective-permute-start) | collective-permute-done | bytes 262176 | tf_op jit(solution)/shard_map/ppermute | solution.py:18
  18.2 1.3 collective-permute-start.1
  19.5 7.8 %collective-permute-done.1 = bf16[1,1,256,512]{2,3,1,0:T(8,128)(2,1)S(1)} collective-permute-done((bf16[1,1,256,512]{2,3,1,0:T(8,128)(2,1)S(1)}, bf16[1,1,256,512]{2,3,1,0:T(8,128)(2,1)S(1)}, u32[]{:S(2)}, u32[]{:S(2)}) %collective-permute-start.1) | collective-permute-done | bytes 262176 | tf_op jit(solution)/shard_map/ppermute | solution.py:18
  27.3 1.3 collective-permute-start.2
  28.6 7.5 %collective-permute-done.2 = bf16[1,1,256,512]{2,3,1,0:T(8,128)(2,1)S(1)} collective-permute-done((bf16[1,1,256,512]{2,3,1,0:T(8,128)(2,1)S(1)}, bf16[1,1,256,512]{2,3,1,0:T(8,128)(2,1)S(1)}, u32[]{:S(2)}, u32[]{:S(2)}) %collective-permute-start.2) | collective-permute-done | bytes 262176 | tf_op jit(solution)/shard_map/ppermute | solution.py:18
  36.1 1.3 collective-permute-start.3
  37.4 1.3 fusion.24
  42.0 1.0 multiply_bitcast_fusion
  43.0 0.2 copy.20
  43.2 1.8 collective-permute-done.3
  45.2 0.0 copy-start.4
  45.2 1.1 multiply_multiply_fusion
  46.3 0.0 all-reduce.4.cloned.1.call-update
  46.3 0.0 all-gather.10.cloned.1.call-start
  46.4 0.2 copy.19
  46.6 0.0 copy-start.8
  46.6 79.3 %all-reduce.4.cloned.1.call-done = f32[2,1,256,512]{2,3,1,0:T(8,128)} async-done(((f32[2,1,256,512]{2,3,1,0:T(8,128)}), f32[2,1,256,512]{2,3,1,0:T(8,128)}) %all-reduce.4.cloned.1.call-update) | async-done | bytes 1048592 | tf_op jit(solution)/shard_map/psum | solution.py:85
  125.9 1.9 fusion.18
  127.8 0.0 all-gather.10.cloned.1.call-update
  127.9 0.0 all-gather.16.cloned.1.call-start
  127.9 0.6 dynamic_slice.16
  129.2 21.1 %all-gather.10.cloned.1.call-done = f32[1,1,512,512]{2,3,1,0:T(8,128)} async-done(((f32[1,1,256,512]{2,3,1,0:T(8,128)}), f32[1,1,512,512]{2,3,1,0:T(8,128)}) %all-gather.10.cloned.1.call-update) | async-done | bytes 1048592 | tf_op jit(solution)/shard_map/all_gather | solution.py:48
  150.2 2.0 fusion.12
  152.2 1.4 fusion.4
  153.6 0.0 all-gather.16.cloned.1.call-update
  153.6 0.0 all-gather.18.cloned.1.call-start
  154.4 2.1 fusion.10
  156.5 18.6 %all-gather.16.cloned.1.call-done = f32[512,512]{1,0:T(8,128)} async-done(((f32[256,512]{1,0:T(8,128)}), f32[512,512]{1,0:T(8,128)}) %all-gather.16.cloned.1.call-update) | async-done | bytes 1048592 | tf_op jit(solution)/shard_map/all_gather | solution.py:44
  175.1 3.1 fusion
  178.1 0.0 all-gather.18.cloned.1.call-update
  178.2 0.0 all-reduce.6.cloned.1.call-start
  178.2 0.0 copy-start.7
  178.2 21.4 %all-gather.18.cloned.1.call-done = f32[512,512]{1,0:T(8,128)} async-done(((f32[256,512]{1,0:T(8,128)}), f32[512,512]{1,0:T(8,128)}) %all-gather.18.cloned.1.call-update) | async-done | bytes 1048592 | tf_op jit(solution)/shard_map/all_gather | solution.py:44
  199.6 3.8 %select_bitcast_fusion.1 = (bf16[1,1,256,512]{2,3,1,0:T(8,128)(2,1)}, bf16[1,1,256,512]{2,3,1,0:T(8,128)(2,1)}) fusion(pred[]{:T(512)S(6)} %eq.72, pred[]{:T(512)S(6)} %eq.76, f32[512,512]{1,0:T(8,128)} %all-gather.18.cloned.1.call-done, f32[1,256,512]{2,1,0:T(8,128)S(1)} %copy-done.4), kind=kOutput, calls=%fused_computation.41 | convolution fusion | flops 805699584 | bytes 2097154 | tf_op jit(solution)/shard_map/esij,esjk->esik/dot_general | solution.py:40
  203.4 0.0 all-reduce.6.cloned.1.call-update
  203.5 0.0 all-gather.12.cloned.1.call-start
  203.5 1.6 collective-permute-start.4
  205.1 1.3 collective-permute-start.5
  206.4 0.2 copy.16
  207.3 67.5 %all-reduce.6.cloned.1.call-done = (bf16[1,1,256,512]{2,3,1,0:T(8,128)(2,1)}, bf16[1,1,256,512]{2,3,1,0:T(8,128)(2,1)}) async-done(((bf16[1,1,256,512]{2,3,1,0:T(8,128)(2,1)}, bf16[1,1,256,512]{2,3,1,0:T(8,128)(2,1)}), (bf16[1,1,256,512]{2,3,1,0:T(8,128)(2,1)}, bf16[1,1,256,512]{2,3,1,0:T(8,128)(2,1)})) %all-reduce.6.cloned.1.call-update) | async-done | bytes 524304 | tf_op jit(solution)/shard_map/psum | solution.py:23
  274.7 1.2 multiply_reduce_fusion
  276.0 0.0 collective-permute-done.4
  276.0 0.0 collective-permute-done.5
  276.0 1.0 select_reduce_fusion
  277.0 0.0 all-gather.12.cloned.1.call-update
  277.0 0.0 all-gather.14.cloned.1.call-start
  277.1 0.8 fusion.19
  277.9 0.0 all-gather.14.cloned.1.call-update
  277.9 0.2 all-gather.20.cloned.1.call-start
  278.8 1.1 compare_select_fusion
  279.9 19.4 %all-gather.12.cloned.1.call-done = f32[1,1,512,512]{2,3,1,0:T(8,128)} async-done(((f32[1,1,256,512]{2,3,1,0:T(8,128)}), f32[1,1,512,512]{2,3,1,0:T(8,128)}) %all-gather.12.cloned.1.call-update) | async-done | bytes 1048592 | tf_op jit(solution)/shard_map/all_gather | solution.py:48
  299.4 2.3 fusion.8
  301.6 21.1 %all-gather.14.cloned.1.call-done = f32[1,1,512,512]{2,3,1,0:T(8,128)} async-done(((f32[1,1,256,512]{2,3,1,0:T(8,128)}), f32[1,1,512,512]{2,3,1,0:T(8,128)}) %all-gather.14.cloned.1.call-update) | async-done | bytes 1048592 | tf_op jit(solution)/shard_map/all_gather | solution.py:44
  322.8 3.2 fusion.1
  326.0 0.0 all-gather.20.cloned.1.call-update
  326.0 0.1 pad_maximum_fusion
  326.1 1.0 copy.23
  327.1 0.5 copy-done.2
  327.5 1.0 fusion.6
  328.6 18.8 %all-gather.20.cloned.1.call-done = f32[512,512]{1,0:T(8,128)} async-done(((f32[256,512]{1,0:T(8,128)}), f32[512,512]{1,0:T(8,128)}) %all-gather.20.cloned.1.call-update) | async-done | bytes 1048592 | tf_op jit(solution)/shard_map/all_gather | solution.py:44
  347.4 3.1 fusion.3
  (22 shorter events, 0.2 us)
Async XLA Ops:
  7.2 118.7 %all-reduce.4.cloned.1.call-start = ((), (), s32[]{:S(2)}) async-start(), calls=%async_computation | async-start | bytes 2097152 | tf_op jit(solution)/shard_map/psum | solution.py:85
  8.3 9.9 %collective-permute-start = (bf16[1,1,256,512]{2,3,1,0:T(8,128)(2,1)S(1)}, bf16[1,1,256,512]{2,3,1,0:T(8,128)(2,1)S(1)}, u32[]{:S(2)}, u32[]{:S(2)}) collective-permute-start(bf16[1,1,256,512]{2,3,1,0:T(8,128)(2,1)S(1)} %copy.17), channel_id=1, source_target_pairs={{0,4},{4,8},{8,12},{12,16},{16,20},{20,24},{24,28},{1,5},{5,9},{9,... | collective-permute-start | bytes 786440 | tf_op jit(solution)/shard_map/ppermute | solution.py:18
  18.2 9.1 %collective-permute-start.1 = (bf16[1,1,256,512]{2,3,1,0:T(8,128)(2,1)S(1)}, bf16[1,1,256,512]{2,3,1,0:T(8,128)(2,1)S(1)}, u32[]{:S(2)}, u32[]{:S(2)}) collective-permute-start(bf16[1,1,256,512]{2,3,1,0:T(8,128)(2,1)S(1)} %collective-permute-done), channel_id=1, source_target_pairs={{0,4},{4,8},{8,12},{12,16},{16,20},{20,24},{24,28},{1,5},{5,9},{9,... | collective-permute-start | bytes 786440 | tf_op jit(solution)/shard_map/ppermute | solution.py:18
  27.3 8.8 %collective-permute-start.2 = (bf16[1,1,256,512]{2,3,1,0:T(8,128)(2,1)S(1)}, bf16[1,1,256,512]{2,3,1,0:T(8,128)(2,1)S(1)}, u32[]{:S(2)}, u32[]{:S(2)}) collective-permute-start(bf16[1,1,256,512]{2,3,1,0:T(8,128)(2,1)S(1)} %collective-permute-done.1), channel_id=1, source_target_pairs={{0,4},{4,8},{8,12},{12,16},{16,20},{20,24},{24,28},{1,5},{5,9},{9,... | collective-permute-start | bytes 786440 | tf_op jit(solution)/shard_map/ppermute | solution.py:18
  36.1 8.9 %collective-permute-start.3 = (bf16[1,1,256,512]{2,3,1,0:T(8,128)(2,1)S(1)}, bf16[1,1,256,512]{2,3,1,0:T(8,128)(2,1)S(1)}, u32[]{:S(2)}, u32[]{:S(2)}) collective-permute-start(bf16[1,1,256,512]{2,3,1,0:T(8,128)(2,1)S(1)} %collective-permute-done.2), channel_id=1, source_target_pairs={{0,4},{4,8},{8,12},{12,16},{16,20},{20,24},{24,28},{1,5},{5,9},{9,... | collective-permute-start | bytes 786440 | tf_op jit(solution)/shard_map/ppermute | solution.py:18
  45.2 1.2 copy-start.4
  46.3 103.9 %all-gather.10.cloned.1.call-start = ((), (), s32[]{:S(2)}) async-start(), calls=%async_computation.1 | async-start | bytes 1572864 | tf_op jit(solution)/shard_map/all_gather | solution.py:48
  46.6 81.3 %copy-start.8 = (s32[2]{0:T(128)S(1)}, s32[2]{0:T(128)}, u32[]{:S(2)}) copy-start(s32[2]{0:T(128)} %param.15) | copy-start | bytes 28
  127.9 47.2 %all-gather.16.cloned.1.call-start = ((), (), s32[]{:S(2)}) async-start(), calls=%async_computation.4 | async-start | bytes 1572864 | tf_op jit(solution)/shard_map/all_gather | solution.py:44
  152.2 2.2 copy-start.3
  153.6 21.5 %copy-start.1 = (f32[256,512]{1,0:T(8,128)S(1)}, f32[256,512]{1,0:T(8,128)}, u32[]{:S(2)}) copy-start(f32[256,512]{1,0:T(8,128)} %fusion.4) | copy-start | bytes 1572868
  153.6 46.0 %all-gather.18.cloned.1.call-start = ((), (), s32[]{:S(2)}) async-start(), calls=%async_computation.5 | async-start | bytes 1572864 | tf_op jit(solution)/shard_map/all_gather | solution.py:44
  178.2 96.6 %all-reduce.6.cloned.1.call-start = ((), (), s32[]{:S(2)}) async-start(), calls=%async_computation.7 | async-start | bytes 1048576 | tf_op jit(solution)/shard_map/psum | solution.py:23
  178.2 28.2 %copy-start.7 = (f32[1,256,512]{2,1,0:T(8,128)S(1)}, f32[1,256,512]{2,1,0:T(8,128)}, u32[]{:S(2)}) copy-start(f32[1,256,512]{2,1,0:T(8,128)} %param.12) | copy-start | bytes 1572868
  203.5 95.9 %all-gather.12.cloned.1.call-start = ((), (), s32[]{:S(2)}) async-start(), calls=%async_computation.2 | async-start | bytes 1572864 | tf_op jit(solution)/shard_map/all_gather | solution.py:48
  203.5 72.5 %collective-permute-start.4 = (bf16[1,1,256,512]{2,3,1,0:T(8,128)(2,1)S(1)}, bf16[1,1,256,512]{2,3,1,0:T(8,128)(2,1)S(1)}, u32[]{:S(2)}, u32[]{:S(2)}) collective-permute-start(bf16[1,1,256,512]{2,3,1,0:T(8,128)(2,1)S(1)} %copy.17), channel_id=1, source_target_pairs={{0,2},{1,3},{4,6},{5,7},{8,10},{9,11},{12,14},{13,15},{16,18},{17,... | collective-permute-start | bytes 786440 | tf_op jit(solution)/shard_map/ppermute | solution.py:33
  205.1 70.9 %collective-permute-start.5 = (bf16[1,1,256,512]{2,3,1,0:T(8,128)(2,1)S(1)}, bf16[1,1,256,512]{2,3,1,0:T(8,128)(2,1)S(1)}, u32[]{:S(2)}, u32[]{:S(2)}) collective-permute-start(bf16[1,1,256,512]{2,3,1,0:T(8,128)(2,1)S(1)} %copy.17), channel_id=1, source_target_pairs={{2,0},{3,1},{6,4},{7,5},{10,8},{11,9},{14,12},{15,13},{18,16},{19,... | collective-permute-start | bytes 786440 | tf_op jit(solution)/shard_map/ppermute | solution.py:34
  277.0 45.8 %all-gather.14.cloned.1.call-start = ((), (), s32[]{:S(2)}) async-start(), calls=%async_computation.3 | async-start | bytes 1572864 | tf_op jit(solution)/shard_map/all_gather | solution.py:44
  277.9 69.5 %all-gather.20.cloned.1.call-start = ((), (), s32[]{:S(2)}) async-start(), calls=%async_computation.6 | async-start | bytes 1572864 | tf_op jit(solution)/shard_map/all_gather | solution.py:44
  322.8 3.2 copy-start.5
  322.8 3.2 copy-start.6
  326.0 1.1 copy-start
  326.0 1.6 copy-start.2
Sparse Core Ops, SparseCore 0:
  46.5 79.3 all-reduce.3
  128.0 22.1 all-gather.9
  153.8 21.2 all-gather.15
  178.3 21.2 all-gather.17
  203.6 71.1 all-reduce.5
  277.1 22.1 all-gather.11
  301.5 21.2 all-gather.13
  326.1 21.2 all-gather.19
where the time goes:
time: 360 us; the launch traced here: 357 us
  waiting for transfers between devices  293 us (81%)
  matrix products  21.9 us (6%)
  between operations  20.4 us (6%)
  starting transfers between devices  8.52 us (2%)
  other arithmetic  8.24 us (2%)
  local copies, waits for them, and re-layouts  5.22 us (1%)
    all_gather x4, waiting for transfers between devices, full_rows(): return lax.all_gather(block_rows, 'rep', axis=2, tiled=True)  79.9 us
    psum x1, waiting for transfers between devices, body(): polarization = lax.psum(partial_value, 'energy')  79.3 us
    psum x1, waiting for transfers between devices, broadcast(): return lax.psum(block, axis)  67.5 us
    all_gather x2, waiting for transfers between devices, newton_rows(): operator_full = lax.all_gather(operator, 'rep', axis=2, tiled=True)  40.5 us
    ppermute x4, waiting for transfers between devices, from_behind(): return lax.ppermute(block, axis, route)  25.8 us
    dot_general x9, matrix products, row_product(): jnp.einsum('esij,esjk->esik', first_factor, second_factor, precision=prec...  21.9 us
  transfers between devices with their start and end apart: 14, of which 12 were waited for; matrix products, arithmetic and copies ran while one was open for 4% of the time, Pallas kernels for 0%

commit v1 on v0

v1 whole, which is shorter than its diff:
```python
import jax
import jax.numpy as jnp
from jax import lax
from jax.sharding import PartitionSpec as P

SHIFTS = 4
FREQS = 2

coded = jnp.float16
near = lax.Precision.HIGH


def shifted(block, axis, distance):
    count = lax.axis_size(axis)
    route = [(i, i + distance) for i in range(count - distance)]
    return lax.ppermute(block, axis, route)


def product(first, second):
    return lax.dot_general(
        first, second, (((1,), (0,)), ((), ())), precision=near,
        preferred_element_type=jnp.float32,
    )


def lowered_blocks(block, offsets):
    two = shifted(block, "energy", 2)
    four = shifted(two, "energy", 2)
    other = jnp.min(offsets)
    odd = shifted(jnp.where(other == 3, two, block), "energy", 1)
    less = jnp.where(other == 2, two, odd)
    return [jnp.where(offsets[f] == SHIFTS, four, less) for f in range(FREQS)]


def split3(value):
    high = lax.reduce_precision(value, 8, 7)
    middle = lax.reduce_precision(value - high, 8, 7)
    return high, middle, value - high - middle


def every_energy(block, weight):
    energies = lax.axis_size("energy")
    rows, width = block.shape
    share = rows // energies
    parts = jnp.stack([w.astype(block.dtype) for w in split3(weight)])
    extra = jnp.zeros((energies, 8, width), block.dtype).at[:, :3, :].set(
        jnp.broadcast_to(parts[None, :, None], (energies, 3, width))
    )
    sent = jnp.concatenate([block.reshape(energies, share, width), extra], axis=1)
    got = lax.all_to_all(sent, "energy", 0, 0, tiled=True)
    tail = got[:, share:share + 3, :].astype(jnp.float32)
    return got[:, :share, :], tail[:, 0:1] + tail[:, 1:2] + tail[:, 2:3]


def gather_energy(chunk):
    energies = lax.axis_size("energy")
    if energies % 2 or energies > 16:
        return lax.all_gather(chunk, "energy", axis=0)
    outer = energies // 2
    here = lax.axis_index("energy") // 2
    whole = jnp.zeros((outer,) + chunk.shape, chunk.dtype)
    whole = lax.dynamic_update_index_in_dim(whole, chunk, here, 0)
    for k in range(1, outer):
        route = [(z * 2 + x, (z + k) % outer * 2 + x) for z in range(outer) for x in range(2)]
        got = lax.ppermute(chunk, "energy", route)
        whole = lax.dynamic_update_index_in_dim(whole, got, (here - k) % outer, 0)
    return whole


def gather_square(part):
    energies = lax.axis_size("energy")
    swap = [(e, e ^ 1) for e in range(energies)]
    turn = [(0, 1), (1, 0)]
    cross = [(e * 2 + r, (e ^ 1) * 2 + 1 - r) for e in range(energies) for r in range(2)]
    beside = lax.ppermute(part, "energy", swap)
    above = lax.ppermute(part, "rep", turn)
    apart = lax.ppermute(part, ("energy", "rep"), cross)
    first_x = lax.axis_index("energy") % 2 == 0
    first_y = lax.axis_index("rep") == 0

    def paired(own, other):
        return jnp.stack([jnp.where(first_x, own, other), jnp.where(first_x, other, own)], axis=1)

    mine = paired(part, beside)
    theirs = paired(above, apart)
    return jnp.stack([jnp.where(first_y, mine, theirs), jnp.where(first_y, theirs, mine)])


def gather_rows(chunk):
    energies = lax.axis_size("energy")
    freqs, share, width = chunk.shape
    if energies % 2 or energies > 16 or lax.axis_size("rep") != 2:
        whole = lax.all_gather(chunk, ("rep", "energy"), axis=1, tiled=True)
        return whole
    whole = gather_square(gather_energy(chunk))
    whole = jnp.moveaxis(whole, 3, 0)
    return whole.reshape(freqs, -1, width)


def body(
    green_blocks, occupation, offsets, coulomb, hamiltonian, onsite_level, green_steps, screen_steps
):
    green = green_blocks[0, 0]
    bare = coulomb[0]
    rows, width = green.shape
    energies = lax.axis_size("energy")
    share = rows // energies
    entry_scale = width ** (-0.5)
    place = lax.axis_index("energy")
    rep_start = lax.axis_index("rep") * rows

    everything, weights = every_energy(green, occupation[0])
    wide = everything.astype(jnp.float32)
    weighted = wide * weights
    padded = jnp.concatenate([jnp.zeros((SHIFTS,) + wide.shape[1:], wide.dtype), wide], axis=0)
    bare_share = lax.dynamic_slice_in_dim(bare, place * share, share, 0)
    chunks = []
    for f in range(FREQS):
        low = lax.dynamic_slice_in_dim(padded, SHIFTS - offsets[f], energies, 0)
        polar = jnp.sum(weighted * low, axis=0) * energies ** (-0.5)
        chunks.append(-entry_scale * bare_share * polar)
    ratio = gather_rows(jnp.stack(chunks).astype(coded)).astype(jnp.float32)

    lowered = lowered_blocks(green, offsets)
    slabs = lax.axis_size("slab")
    if slabs == 2:
        beside = lax.ppermute(green, "slab", [(0, 1), (1, 0)]).astype(jnp.float32)
    else:
        up = [(i, i + 1) for i in range(slabs - 1)]
        down = [(j, i) for i, j in up]
        beside = lax.ppermute(green, "slab", up).astype(jnp.float32) + lax.ppermute(
            green, "slab", down
        ).astype(jnp.float32)

    once = [bare + product(bare, ratio[f]) for f in range(FREQS)]
    twice_at = jnp.argmax(screen_steps)
    ratio_twice = lax.dynamic_index_in_dim(ratio, twice_at, 0, keepdims=False)
    once_twice = jnp.where(twice_at == 0, once[0], once[1])
    twice = once_twice + product(product(once_twice, ratio_twice), ratio_twice)
    screened = jnp.stack(
        [
            jnp.where(
                screen_steps[f] == 0, bare, jnp.where(screen_steps[f] == 1, once[f], twice)
            )
            for f in range(FREQS)
        ]
    ).astype(jnp.bfloat16)

    energy_terms = sum(
        lowered[f].astype(jnp.float32) * screened[f].astype(jnp.float32) for f in range(FREQS)
    )
    rest = hamiltonian[0] - entry_scale * energy_terms - (0.5 * entry_scale) * beside
    col_index = lax.broadcasted_iota(jnp.int32, (rows, width), 1)
    row_index = lax.broadcasted_iota(jnp.int32, (rows, width), 0) + rep_start
    on_diagonal = col_index == row_index
    level = onsite_level[0]
    diagonal = level + jnp.sum(jnp.where(on_diagonal, rest, 0.0), axis=1, keepdims=True)
    off = jnp.where(on_diagonal, 0.0, rest)
    largest = jnp.max(jnp.abs(off), axis=1, keepdims=True)
    largest = jnp.where(largest > 0.0, largest, 1.0)
    unit = off / largest
    factor = -largest / diagonal
    inverse = 1.0 / diagonal
    factor_row = jnp.sum(jnp.where(on_diagonal, factor, 0.0), axis=0)
    inverse_row = jnp.sum(jnp.where(on_diagonal, inverse, 0.0), axis=0)
    turn = [(0, 1), (1, 0)]
    vectors = jnp.stack([factor_row, inverse_row])
    if lax.axis_size("rep") == 2:
        vectors = vectors + lax.ppermute(vectors, "rep", turn)
        mine = unit.astype(coded)
        theirs = lax.ppermute(mine, "rep", turn)
        first = lax.axis_index("rep") == 0
        full = jnp.concatenate(
            [jnp.where(first, mine, theirs), jnp.where(first, theirs, mine)], axis=0
        ).astype(jnp.float32)
    else:
        vectors = lax.psum(vectors, "rep")
        full = lax.all_gather(unit.astype(coded), "rep", axis=0, tiled=True).astype(jnp.float32)
    factors, inverses = vectors[0:1], vectors[1:2]
    step = unit * factor
    square = product(step * factors, full)
    cube = product(square * factors, full)
    near_one = jnp.where(on_diagonal, 1.0, step)
    total = near_one + jnp.where(green_steps[0] >= 2, square + cube, 0.0)
    return (total * inverses)[None, None], screened[:, None]


def solution(mesh):
    return jax.shard_map(
        body,
        mesh=mesh,
        in_specs=(
            P("energy", "slab", "rep", None),
            P("energy"),
            P(),
            P("slab", "rep", None),
            P("slab", "rep", None),
            P("energy"),
            P("energy"),
            P(),
        ),
        out_specs=(P("energy", "slab", "rep", None), P(None, "slab", "rep", None)),
        check_vma=False,
    )
```

time: 360 us -> 78 us (0.22)
  the two profiles are of different devices: /device:TPU:26 before, /device:TPU:0 now
where the time goes in v1:
time: 78 us; the launch traced here: 77.4 us
  starting transfers between devices  29.3 us (38%)
  between operations  16.7 us (21%)
  waiting for transfers between devices  14.5 us (19%)
  local copies, waits for them, and re-layouts  6.28 us (8%)
  other arithmetic  5.52 us (7%)
  matrix products  5.13 us (7%)
    ppermute x3, starting transfers between devices, shifted(): return lax.ppermute(block, axis, route)  11 us
    all_to_all x1, starting transfers between devices, every_energy(): got = lax.all_to_all(sent, 'energy', 0, 0, tiled=True)  7.41 us
    ppermute x1, waiting for transfers between devices, body(): theirs = lax.ppermute(mine, 'rep', turn)  5.76 us
    dot_general x6, matrix products, product(): lax.dot_general(first, second, (((1,), (0,)), ((), ())), precision=near,...  5.13 us
    ppermute x3, starting transfers between devices, gather_energy(): got = lax.ppermute(chunk, 'energy', route)  5.05 us
    unnamed x16, local copies, waits for them, and re-layouts  4.69 us
    ppermute x1, waiting for transfers between devices, gather_square(): above = lax.ppermute(part, 'rep', turn)  4.12 us
    ppermute x3, waiting for transfers between devices, gather_energy(): got = lax.ppermute(chunk, 'energy', route)  3.79 us
  transfers between devices with their start and end apart: 13, of which 6 were waited for; matrix products, arithmetic and copies ran while one was open for 12% of the time, Pallas kernels for 0%

profile of v1, /device:TPU:0, one launch (start us, length us, event | category | flops | bytes accessed | tf_op | source)
XLA Modules:
  0.0 77.4 jit_solution(14606405041144275618)
XLA Ops:
  4.9 0.1 select_maximum_fusion
  5.0 0.1 pad.21.clone
  5.1 1.8 %pad_maximum_fusion.7 = bf16[8,40,512]{2,1,0:T(8,128)(2,1)} fusion(bf16[8,32,512]{2,1,0:T(8,128)(2,1)} %bitcast.121, bf16[40]{0:T(256)(128)(2,1)S(1)} %pad.21.clone), kind=kLoop, calls=%fused_computation.47 | loop fusion | flops 655360 | bytes 589904 | tf_op jit(solution)/shard_map/concatenate | solution.py:49
  6.8 0.0 copy-start.1
  6.8 7.4 %all-to-all-start = ((bf16[8,40,512]{2,1,0:T(8,128)(2,1)}), bf16[8,40,512]{2,1,0:T(8,128)(2,1)S(1)}, u32[]{:S(2)}, u32[]{:S(2)}) async-start(bf16[8,40,512]{2,1,0:T(8,128)(2,1)} %pad_maximum_fusion.7), calls=%async_computation | async-start | bytes 655360 | tf_op jit(solution)/shard_map/all_to_all | solution.py:50
  14.3 0.0 copy-done.1
  14.3 0.1 copy.20
  14.4 3.9 %collective-permute-start = (bf16[256,512]{0,1:T(8,128)(2,1)S(1)}, bf16[256,512]{0,1:T(8,128)(2,1)S(1)}, u32[]{:S(2)}, u32[]{:S(2)}) collective-permute-start(bf16[256,512]{0,1:T(8,128)(2,1)S(1)} %bitcast.122), channel_id=1, source_target_pairs={{0,8},{4,12},{8,16},{12,20},{16,24},{20,28},{1,9},{5,13},{9,17},{1... | collective-permute-start | bytes 786440 | tf_op jit(solution)/shard_map/ppermute | solution.py:16
  18.3 0.1 collective-permute-start.9
  18.5 0.0 copy-start.4
  18.5 0.6 copy-done.4
  19.2 0.6 fusion.46
  22.4 0.0 copy-start.3
  22.4 0.6 copy-done.3
  23.0 0.6 fusion.45
  23.6 0.7 iota_reduce_fusion
  24.3 0.3 all-to-all-done
  24.6 0.1 slice_convert_fusion
  24.7 0.0 copy-start
  24.7 0.2 fusion.7
  24.9 0.9 %copy-done = f32[1,256,512]{2,1,0:T(8,128)S(1)} copy-done((f32[1,256,512]{2,1,0:T(8,128)S(1)}, f32[1,256,512]{2,1,0:T(8,128)}, u32[]{:S(2)}) %copy-start) | copy-done | bytes 524312
  25.8 1.2 %collective-permute-start.3 = (f16[2,32,512]{2,1,0:T(8,128)(2,1)S(1)}, f16[2,32,512]{2,1,0:T(8,128)(2,1)S(1)}, u32[]{:S(2)}, u32[]{:S(2)}) collective-permute-start(f16[2,32,512]{2,1,0:T(8,128)(2,1)S(1)} %pad_maximum_fusion.8), channel_id=1, source_target_pairs={{0,8},{4,12},{8,16},{12,20},{16,24},{20,28},{24,0},{28,4},{1,9},{5... | collective-permute-start | bytes 196616 | tf_op jit(solution)/shard_map/ppermute | solution.py:65
  27.0 1.1 %collective-permute-start.4 = (f16[2,32,512]{2,1,0:T(8,128)(2,1)S(1)}, f16[2,32,512]{2,1,0:T(8,128)(2,1)S(1)}, u32[]{:S(2)}, u32[]{:S(2)}) collective-permute-start(f16[2,32,512]{2,1,0:T(8,128)(2,1)S(1)} %pad_maximum_fusion.8), channel_id=1, source_target_pairs={{0,16},{4,20},{8,24},{12,28},{16,0},{20,4},{24,8},{28,12},{1,17},{... | collective-permute-start | bytes 196616 | tf_op jit(solution)/shard_map/ppermute | solution.py:65
  28.1 2.7 %collective-permute-start.5 = (f16[2,32,512]{2,1,0:T(8,128)(2,1)S(1)}, f16[2,32,512]{2,1,0:T(8,128)(2,1)S(1)}, u32[]{:S(2)}, u32[]{:S(2)}) collective-permute-start(f16[2,32,512]{2,1,0:T(8,128)(2,1)S(1)} %pad_maximum_fusion.8), channel_id=1, source_target_pairs={{0,24},{4,28},{8,0},{12,4},{16,8},{20,12},{24,16},{28,20},{1,25},{... | collective-permute-start | bytes 196616 | tf_op jit(solution)/shard_map/ppermute | solution.py:65
  30.9 1.4 %collective-permute-done.3 = f16[2,32,512]{2,1,0:T(8,128)(2,1)S(1)} collective-permute-done((f16[2,32,512]{2,1,0:T(8,128)(2,1)S(1)}, f16[2,32,512]{2,1,0:T(8,128)(2,1)S(1)}, u32[]{:S(2)}, u32[]{:S(2)}) %collective-permute-start.3) | collective-permute-done | bytes 65568 | tf_op jit(solution)/shard_map/ppermute | solution.py:65
  32.3 2.4 %collective-permute-done.4 = f16[2,32,512]{2,1,0:T(8,128)(2,1)S(1)} collective-permute-done((f16[2,32,512]{2,1,0:T(8,128)(2,1)S(1)}, f16[2,32,512]{2,1,0:T(8,128)(2,1)S(1)}, u32[]{:S(2)}, u32[]{:S(2)}) %collective-permute-start.4) | collective-permute-done | bytes 65568 | tf_op jit(solution)/shard_map/ppermute | solution.py:65
  34.7 0.0 collective-permute-done.5
  34.8 1.5 %collective-permute-start.6 = (f16[4,2,32,512]{3,2,0,1:T(8,128)(2,1)S(1)}, f16[4,2,32,512]{3,2,0,1:T(8,128)(2,1)S(1)}, u32[]{:S(2)}, u32[]{:S(2)}) collective-permute-start(f16[4,2,32,512]{3,2,0,1:T(8,128)(2,1)S(1)} %bitcast_dynamic-update-slice_fusion.2), channel_id=1, source_target_pairs={{0,4},{4,0},{8,12},{12,8},{16,20},{20,16},{24,28},{28,24},{1,5},{5... | collective-permute-start | bytes 786440 | tf_op jit(solution)/shard_map/ppermute | solution.py:75
  36.3 0.2 copy.21
  42.0 0.6 reduce_min.9
  43.9 0.0 copy-done.2
  44.0 0.2 copy.19
  46.1 1.6 %collective-permute-start.7 = (f16[4,2,32,512]{3,2,0,1:T(8,128)(2,1)S(1)}, f16[4,2,32,512]{3,2,0,1:T(8,128)(2,1)S(1)}, u32[]{:S(2)}, u32[]{:S(2)}) collective-permute-start(f16[4,2,32,512]{3,2,0,1:T(8,128)(2,1)S(1)} %bitcast_dynamic-update-slice_fusion.2), channel_id=1, source_target_pairs={{0,1},{1,0},{2,3},{3,2},{4,5},{5,4},{6,7},{7,6},{8,9},{9,8},{10,11... | collective-permute-start | bytes 786440 | tf_op jit(solution)/shard_map/ppermute | solution.py:76
  47.7 0.5 collective-permute-start.8
  48.2 0.0 collective-permute-done
  48.2 3.4 %collective-permute-start.2 = (bf16[256,512]{0,1:T(8,128)(2,1)S(1)}, bf16[256,512]{0,1:T(8,128)(2,1)S(1)}, u32[]{:S(2)}, u32[]{:S(2)}) collective-permute-start(bf16[256,512]{0,1:T(8,128)(2,1)S(1)} %broadcast_select_fusion.5), channel_id=1, source_target_pairs={{0,4},{4,8},{8,12},{12,16},{16,20},{20,24},{24,28},{1,5},{5,9},{9,... | collective-permute-start | bytes 786440 | tf_op jit(solution)/shard_map/ppermute | solution.py:16
  51.6 0.0 collective-permute-done.6
  51.6 3.7 %collective-permute-start.1 = (bf16[256,512]{0,1:T(8,128)(2,1)S(1)}, bf16[256,512]{0,1:T(8,128)(2,1)S(1)}, u32[]{:S(2)}, u32[]{:S(2)}) collective-permute-start(bf16[256,512]{0,1:T(8,128)(2,1)S(1)} %collective-permute-done), channel_id=1, source_target_pairs={{0,8},{4,12},{8,16},{12,20},{16,24},{20,28},{1,9},{5,13},{9,17},{1... | collective-permute-start | bytes 786440 | tf_op jit(solution)/shard_map/ppermute | solution.py:16
  55.4 0.1 select_bitcast_fusion.3
  55.5 4.1 %collective-permute-done.7 = f16[4,2,32,512]{3,2,0,1:T(8,128)(2,1)S(1)} collective-permute-done((f16[4,2,32,512]{3,2,0,1:T(8,128)(2,1)S(1)}, f16[4,2,32,512]{3,2,0,1:T(8,128)(2,1)S(1)}, u32[]{:S(2)}, u32[]{:S(2)}) %collective-permute-start.7) | collective-permute-done | bytes 262176 | tf_op jit(solution)/shard_map/ppermute | solution.py:76
  59.6 0.0 collective-permute-done.8
  59.6 0.1 select_bitcast_fusion.1
  59.7 0.3 broadcast_select_fusion.1
  60.1 0.4 pad_maximum_fusion
  60.5 0.3 fusion.43
  60.8 1.0 %fusion.2 = f32[256,512]{0,1:T(8,128)S(1)} fusion(f16[512,512]{1,0:T(8,128)(2,1)S(1)} %bitcast.118, f32[1,256,512]{2,1,0:T(8,128)S(1)} %copy-done, f32[1,256,512]{1,2,0:T(8,128)S(1)} %copy.21), kind=kOutput, calls=%fused_computation.5 | convolution fusion | flops 402784256 | bytes 2097152 | tf_op jit(solution)/shard_map/dot_general | solution.py:20
  61.8 1.0 %fusion.3 = f32[256,512]{0,1:T(8,128)S(1)} fusion(f16[512,512]{1,0:T(8,128)(2,1)S(1)} %bitcast.117, f32[1,256,512]{2,1,0:T(8,128)S(1)} %copy-done, f32[1,256,512]{1,2,0:T(8,128)S(1)} %copy.21), kind=kOutput, calls=%fused_computation.7 | convolution fusion | flops 402784256 | bytes 2097152 | tf_op jit(solution)/shard_map/dot_general | solution.py:20
  62.8 0.7 fusion.13
  63.4 1.0 %convolution_add_fusion.1 = bf16[256,512]{0,1:T(8,128)(2,1)S(1)} fusion(f32[256,512]{1,0:T(8,128)S(1)} %fusion.13, f16[2,512,512]{2,1,0:T(8,128)(2,1)S(1)} %bitcast.116, s32[]{:T(128)S(6)} %select_n.237, f32[256,512]{0,1:T(8,128)S(1)} %fusion.3, f32[256,512]{0,1:T(8,128)S(1)} %fusion.2, pred[]{:T(512)S(6)} %eq.73), kind=kOutput, calls=%fused_computation.3 | convolution fusion | flops 403046400 | bytes 2359301 | tf_op jit(solution)/shard_map/dot_general | solution.py:20
  64.5 0.0 collective-permute-done.9
  64.5 0.0 collective-permute-done.2
  64.5 0.0 collective-permute-done.1
  64.5 0.5 select_reduce_fusion.2
  65.0 0.3 select_reduce_fusion.1
  65.3 1.6 %collective-permute-start.10 = (f32[2,512]{1,0:T(2,128)S(1)}, f32[2,512]{1,0:T(2,128)S(1)}, u32[]{:S(2)}, u32[]{:S(2)}) collective-permute-start(f32[2,512]{1,0:T(2,128)S(1)} %pad_maximum_fusion.9), channel_id=1, source_target_pairs={{0,1},{1,0},{2,3},{3,2},{4,5},{5,4},{6,7},{7,6},{8,9},{9,8},{10,11... | collective-permute-start | bytes 12296 | tf_op jit(solution)/shard_map/ppermute | solution.py:169
  66.9 0.1 pad_maximum_fusion.4
  66.9 1.0 %copy.33 = bf16[2,1,256,512]{3,2,1,0:T(8,128)(2,1)} copy(bf16[2,1,256,512]{2,3,1,0:T(8,128)(2,1)S(1)} %pad_maximum_fusion.4) | data formatting | bytes 1048576
  67.9 0.5 collective-permute-start.11
  68.4 0.5 collective-permute-done.10
  69.0 5.8 %collective-permute-done.11 = f16[256,512]{0,1:T(8,128)(2,1)S(1)} collective-permute-done((f16[256,512]{0,1:T(8,128)(2,1)S(1)}, f16[256,512]{0,1:T(8,128)(2,1)S(1)}, u32[]{:S(2)}, u32[]{:S(2)}) %collective-permute-start.11) | collective-permute-done | bytes 262176 | tf_op jit(solution)/shard_map/ppermute | solution.py:171
  74.8 0.1 broadcast_select_fusion.3
  74.9 0.7 fusion.19
  75.6 0.8 fusion.5
  76.4 1.0 %copy.32 = f32[1,1,256,512]{3,2,1,0:T(8,128)} copy(f32[1,1,256,512]{2,3,1,0:T(8,128)S(1)} %fusion.5) | data formatting | bytes 1048576
  (17 shorter events, 0.3 us)
Async XLA Ops:
  6.8 7.4 %copy-start.1 = (bf16[1,1,256,512]{3,2,1,0:T(8,128)(2,1)S(1)}, bf16[1,1,256,512]{3,2,1,0:T(8,128)(2,1)}, u32[]{:S(2)}) copy-start(bf16[1,1,256,512]{3,2,1,0:T(8,128)(2,1)} %param.10) | copy-start | bytes 786436
  6.8 17.7 %all-to-all-start = ((bf16[8,40,512]{2,1,0:T(8,128)(2,1)}), bf16[8,40,512]{2,1,0:T(8,128)(2,1)S(1)}, u32[]{:S(2)}, u32[]{:S(2)}) async-start(bf16[8,40,512]{2,1,0:T(8,128)(2,1)} %pad_maximum_fusion.7), calls=%async_computation | async-start | bytes 655360 | tf_op jit(solution)/shard_map/all_to_all | solution.py:50
  14.4 33.8 %collective-permute-start = (bf16[256,512]{0,1:T(8,128)(2,1)S(1)}, bf16[256,512]{0,1:T(8,128)(2,1)S(1)}, u32[]{:S(2)}, u32[]{:S(2)}) collective-permute-start(bf16[256,512]{0,1:T(8,128)(2,1)S(1)} %bitcast.122), channel_id=1, source_target_pairs={{0,8},{4,12},{8,16},{12,20},{16,24},{20,28},{1,9},{5,13},{9,17},{1... | collective-permute-start | bytes 786440 | tf_op jit(solution)/shard_map/ppermute | solution.py:16
  18.3 46.1 %collective-permute-start.9 = (bf16[256,512]{0,1:T(8,128)(2,1)S(1)}, bf16[256,512]{0,1:T(8,128)(2,1)S(1)}, u32[]{:S(2)}, u32[]{:S(2)}) collective-permute-start(bf16[256,512]{0,1:T(8,128)(2,1)S(1)} %bitcast.123), channel_id=1, source_target_pairs={{0,2},{2,0},{1,3},{3,1},{4,6},{6,4},{5,7},{7,5},{8,10},{10,8},{9,1... | collective-permute-start | bytes 786440 | tf_op jit(solution)/shard_map/ppermute | solution.py:127
  18.5 0.7 copy-start.4
  22.4 0.7 copy-start.3
  24.7 1.0 %copy-start = (f32[1,256,512]{2,1,0:T(8,128)S(1)}, f32[1,256,512]{2,1,0:T(8,128)}, u32[]{:S(2)}) copy-start(f32[1,256,512]{2,1,0:T(8,128)} %param.13) | copy-start | bytes 1572868
  25.8 6.5 %collective-permute-start.3 = (f16[2,32,512]{2,1,0:T(8,128)(2,1)S(1)}, f16[2,32,512]{2,1,0:T(8,128)(2,1)S(1)}, u32[]{:S(2)}, u32[]{:S(2)}) collective-permute-start(f16[2,32,512]{2,1,0:T(8,128)(2,1)S(1)} %pad_maximum_fusion.8), channel_id=1, source_target_pairs={{0,8},{4,12},{8,16},{12,20},{16,24},{20,28},{24,0},{28,4},{1,9},{5... | collective-permute-start | bytes 196616 | tf_op jit(solution)/shard_map/ppermute | solution.py:65
  27.0 7.7 %collective-permute-start.4 = (f16[2,32,512]{2,1,0:T(8,128)(2,1)S(1)}, f16[2,32,512]{2,1,0:T(8,128)(2,1)S(1)}, u32[]{:S(2)}, u32[]{:S(2)}) collective-permute-start(f16[2,32,512]{2,1,0:T(8,128)(2,1)S(1)} %pad_maximum_fusion.8), channel_id=1, source_target_pairs={{0,16},{4,20},{8,24},{12,28},{16,0},{20,4},{24,8},{28,12},{1,17},{... | collective-permute-start | bytes 196616 | tf_op jit(solution)/shard_map/ppermute | solution.py:65
  28.1 6.6 %collective-permute-start.5 = (f16[2,32,512]{2,1,0:T(8,128)(2,1)S(1)}, f16[2,32,512]{2,1,0:T(8,128)(2,1)S(1)}, u32[]{:S(2)}, u32[]{:S(2)}) collective-permute-start(f16[2,32,512]{2,1,0:T(8,128)(2,1)S(1)} %pad_maximum_fusion.8), channel_id=1, source_target_pairs={{0,24},{4,28},{8,0},{12,4},{16,8},{20,12},{24,16},{28,20},{1,25},{... | collective-permute-start | bytes 196616 | tf_op jit(solution)/shard_map/ppermute | solution.py:65
  34.8 16.8 %collective-permute-start.6 = (f16[4,2,32,512]{3,2,0,1:T(8,128)(2,1)S(1)}, f16[4,2,32,512]{3,2,0,1:T(8,128)(2,1)S(1)}, u32[]{:S(2)}, u32[]{:S(2)}) collective-permute-start(f16[4,2,32,512]{3,2,0,1:T(8,128)(2,1)S(1)} %bitcast_dynamic-update-slice_fusion.2), channel_id=1, source_target_pairs={{0,4},{4,0},{8,12},{12,8},{16,20},{20,16},{24,28},{28,24},{1,5},{5... | collective-permute-start | bytes 786440 | tf_op jit(solution)/shard_map/ppermute | solution.py:75
  36.3 7.7 %copy-start.2 = (f32[1,256,512]{2,1,0:T(8,128)S(1)}, f32[1,256,512]{2,1,0:T(8,128)}, u32[]{:S(2)}) copy-start(f32[1,256,512]{2,1,0:T(8,128)} %param.14) | copy-start | bytes 1572868
  46.1 13.5 %collective-permute-start.7 = (f16[4,2,32,512]{3,2,0,1:T(8,128)(2,1)S(1)}, f16[4,2,32,512]{3,2,0,1:T(8,128)(2,1)S(1)}, u32[]{:S(2)}, u32[]{:S(2)}) collective-permute-start(f16[4,2,32,512]{3,2,0,1:T(8,128)(2,1)S(1)} %bitcast_dynamic-update-slice_fusion.2), channel_id=1, source_target_pairs={{0,1},{1,0},{2,3},{3,2},{4,5},{5,4},{6,7},{7,6},{8,9},{9,8},{10,11... | collective-permute-start | bytes 786440 | tf_op jit(solution)/shard_map/ppermute | solution.py:76
  47.7 11.9 %collective-permute-start.8 = (f16[4,2,32,512]{3,2,0,1:T(8,128)(2,1)S(1)}, f16[4,2,32,512]{3,2,0,1:T(8,128)(2,1)S(1)}, u32[]{:S(2)}, u32[]{:S(2)}) collective-permute-start(f16[4,2,32,512]{3,2,0,1:T(8,128)(2,1)S(1)} %bitcast_dynamic-update-slice_fusion.2), channel_id=1, source_target_pairs={{0,5},{1,4},{4,1},{5,0},{8,13},{9,12},{12,9},{13,8},{16,21},{17,20... | collective-permute-start | bytes 786440 | tf_op jit(solution)/shard_map/ppermute | solution.py:77
  48.2 16.3 %collective-permute-start.2 = (bf16[256,512]{0,1:T(8,128)(2,1)S(1)}, bf16[256,512]{0,1:T(8,128)(2,1)S(1)}, u32[]{:S(2)}, u32[]{:S(2)}) collective-permute-start(bf16[256,512]{0,1:T(8,128)(2,1)S(1)} %broadcast_select_fusion.5), channel_id=1, source_target_pairs={{0,4},{4,8},{8,12},{12,16},{16,20},{20,24},{24,28},{1,5},{5,9},{9,... | collective-permute-start | bytes 786440 | tf_op jit(solution)/shard_map/ppermute | solution.py:16
  51.6 12.9 %collective-permute-start.1 = (bf16[256,512]{0,1:T(8,128)(2,1)S(1)}, bf16[256,512]{0,1:T(8,128)(2,1)S(1)}, u32[]{:S(2)}, u32[]{:S(2)}) collective-permute-start(bf16[256,512]{0,1:T(8,128)(2,1)S(1)} %collective-permute-done), channel_id=1, source_target_pairs={{0,8},{4,12},{8,16},{12,20},{16,24},{20,28},{1,9},{5,13},{9,17},{1... | collective-permute-start | bytes 786440 | tf_op jit(solution)/shard_map/ppermute | solution.py:16
  65.3 3.7 %collective-permute-start.10 = (f32[2,512]{1,0:T(2,128)S(1)}, f32[2,512]{1,0:T(2,128)S(1)}, u32[]{:S(2)}, u32[]{:S(2)}) collective-permute-start(f32[2,512]{1,0:T(2,128)S(1)} %pad_maximum_fusion.9), channel_id=1, source_target_pairs={{0,1},{1,0},{2,3},{3,2},{4,5},{5,4},{6,7},{7,6},{8,9},{9,8},{10,11... | collective-permute-start | bytes 12296 | tf_op jit(solution)/shard_map/ppermute | solution.py:169
  67.9 6.8 %collective-permute-start.11 = (f16[256,512]{0,1:T(8,128)(2,1)S(1)}, f16[256,512]{0,1:T(8,128)(2,1)S(1)}, u32[]{:S(2)}, u32[]{:S(2)}) collective-permute-start(f16[256,512]{0,1:T(8,128)(2,1)S(1)} %get-tuple-element.45), channel_id=1, source_target_pairs={{0,1},{1,0},{2,3},{3,2},{4,5},{5,4},{6,7},{7,6},{8,9},{9,8},{10,11... | collective-permute-start | bytes 786440 | tf_op jit(solution)/shard_map/ppermute | solution.py:171

commit v2 on v0

v2 whole, which is shorter than its diff:
```python
import jax
import jax.numpy as jnp
from jax import lax
from jax.experimental import pallas as pl
from jax.experimental.pallas import tpu as pltpu
from jax.sharding import PartitionSpec as P

SHIFTS = 4
FREQS = 2
EXTRA = 8

coded = jnp.float16
VMEM = pltpu.VMEM
in_vmem = pl.BlockSpec(memory_space=pltpu.VMEM)
in_smem = pl.BlockSpec(memory_space=pltpu.SMEM)
in_place = pl.BlockSpec(memory_space=pl.ANY)


def halves(value):
    high = value.astype(jnp.bfloat16)
    return high, (value - high.astype(jnp.float32)).astype(jnp.bfloat16)


def dot(first, second):
    return jnp.dot(first, second, preferred_element_type=jnp.float32)


def product(first, high, low):
    top, rest = halves(first)
    return dot(top, high) + dot(top, low) + dot(rest, high)


def shifted(block, axis, distance):
    count = lax.axis_size(axis)
    route = [(i, i + distance) for i in range(count - distance)]
    return lax.ppermute(block, axis, route)


def prepare_kernel(weight_ref, block_ref, out_ref):
    energies, padded, width = out_ref.shape
    share = padded - EXTRA
    weight = jnp.full((EXTRA, width), weight_ref[0], jnp.float32)
    first = weight.astype(jnp.bfloat16).astype(jnp.float32)
    second = (weight - first).astype(jnp.bfloat16).astype(jnp.float32)
    third = weight - first - second
    row = lax.broadcasted_iota(jnp.int32, (EXTRA, width), 0)
    tail = jnp.where(row == 0, first, jnp.where(row == 1, second, third)).astype(jnp.bfloat16)
    for k in range(energies):
        out_ref[k, :share, :] = block_ref[k * share:(k + 1) * share, :]
        out_ref[k, share:, :] = tail


def polar_kernel(offsets_ref, got_ref, bare_ref, out_ref, padded, bare_rows, arrived):
    energies, tall, width = got_ref.shape
    share = tall - EXTRA
    place = lax.axis_index("energy")
    start = pl.multiple_of(place * share, share)
    copy = pltpu.make_async_copy(bare_ref.at[pl.ds(start, share), :], bare_rows, arrived)
    copy.start()
    padded[:SHIFTS] = jnp.zeros((SHIFTS, share, width), jnp.float32)
    for e in range(energies):
        padded[SHIFTS + e] = got_ref[e, :share, :].astype(jnp.float32)
    totals = [jnp.zeros((share, width), jnp.float32) for _ in range(FREQS)]
    for e in range(energies):
        tail = got_ref[e, share:, :].astype(jnp.float32)
        weighted = padded[SHIFTS + e] * (tail[0:1] + tail[1:2] + tail[2:3])
        for f in range(FREQS):
            totals[f] += weighted * padded[SHIFTS + e - offsets_ref[f]]
    copy.wait()
    factor = -(width ** -0.5) * energies ** -0.5
    for f in range(FREQS):
        out_ref[f] = totals[f] * (factor * bare_rows[...])


def polar_share(green, weight, offsets, bare):
    energies = lax.axis_size("energy")
    rows, width = green.shape
    share = rows // energies
    sent = pl.pallas_call(
        prepare_kernel,
        out_shape=jax.ShapeDtypeStruct((energies, share + EXTRA, width), green.dtype),
        in_specs=[in_smem, in_vmem],
        out_specs=in_vmem,
        name="prepare",
    )(weight, green)
    got = lax.all_to_all(sent, "energy", 0, 0, tiled=True)
    return pl.pallas_call(
        polar_kernel,
        out_shape=jax.ShapeDtypeStruct((FREQS, share, width), jnp.float32),
        in_specs=[in_smem, in_vmem, in_place],
        out_specs=in_vmem,
        scratch_shapes=[
            VMEM((SHIFTS + energies, share, width), jnp.float32),
            VMEM((share, width), jnp.float32),
            pltpu.SemaphoreType.DMA,
        ],
        name="polar",
    )(offsets, got, bare)


def polar_share_plain(green, weight, offsets, bare):
    energies = lax.axis_size("energy")
    rows, width = green.shape
    share = rows // energies
    weights = lax.all_gather(weight, "energy", axis=0, tiled=True)
    got = lax.all_to_all(green.reshape(energies, share, width), "energy", 0, 0, tiled=True)
    wide = got.astype(jnp.float32)
    weighted = wide * weights[:, None, None]
    padded = jnp.concatenate([jnp.zeros((SHIFTS,) + wide.shape[1:], wide.dtype), wide], axis=0)
    own = lax.dynamic_slice_in_dim(bare, lax.axis_index("energy") * share, share, 0)
    factor = -(width ** -0.5) * energies ** -0.5
    chunks = []
    for f in range(FREQS):
        low = lax.dynamic_slice_in_dim(padded, SHIFTS - offsets[f], energies, 0)
        chunks.append(factor * own * jnp.sum(weighted * low, axis=0))
    return jnp.stack(chunks)


def gather_energy(chunk):
    outer = lax.axis_size("energy") // 2
    here = lax.axis_index("energy") // 2
    whole = jnp.zeros((outer,) + chunk.shape, chunk.dtype)
    whole = lax.dynamic_update_index_in_dim(whole, chunk, here, 0)
    for k in range(1, outer):
        route = [(z * 2 + x, (z + k) % outer * 2 + x) for z in range(outer) for x in range(2)]
        got = lax.ppermute(chunk, "energy", route)
        whole = lax.dynamic_update_index_in_dim(whole, got, (here - k) % outer, 0)
    return whole


def gather_square(part):
    energies = lax.axis_size("energy")
    swap = [(e, e ^ 1) for e in range(energies)]
    turn = [(0, 1), (1, 0)]
    cross = [(e * 2 + r, (e ^ 1) * 2 + 1 - r) for e in range(energies) for r in range(2)]
    return [
        part,
        lax.ppermute(part, "energy", swap),
        lax.ppermute(part, "rep", turn),
        lax.ppermute(part, ("energy", "rep"), cross),
    ]


def gathered(chunk):
    energies = lax.axis_size("energy")
    chunk = chunk.astype(coded)
    if energies % 2 or energies > 16 or lax.axis_size("rep") != 2:
        pieces = [lax.all_gather(chunk, ("rep", "energy"), axis=1, tiled=True)]
    else:
        pieces = gather_square(gather_energy(chunk))
    return [piece.astype(jnp.float32) for piece in pieces]


def parts_of(value):
    size = jnp.abs(value)
    exponent = jnp.where(size > 0.0, jnp.floor(jnp.log2(jnp.where(size > 0.0, size, 1.0))), 0.0)
    exponent = jnp.clip(exponent, -120.0, 120.0)
    mantissa = value * jnp.exp2(-exponent)
    first = mantissa.astype(jnp.bfloat16).astype(jnp.float32)
    second = (mantissa - first).astype(jnp.bfloat16).astype(jnp.float32)
    return exponent, first, second


def whole_of(exponent, first, second):
    return (first + second) * jnp.exp2(exponent)


def dyson_kernel(pieces, offsets_ref, steps_ref, level_ref, bare_ref, hamiltonian_ref, two_ref,
                 four_ref, odd_ref, beside_refs, screened_ref, packed_ref, step_ref, own_ref,
                 high, low):
    rows, width = bare_ref.shape
    entry_scale = width ** -0.5
    energy, rep = lax.axis_index("energy"), lax.axis_index("rep")
    if len(pieces) == 1:
        for f in range(FREQS):
            high[f], low[f] = halves(pieces[0][f])
    else:
        outer, _, share, _ = pieces[0].shape
        x = energy % 2
        corners = [(x, rep), (1 - x, rep), (x, 1 - rep), (1 - x, 1 - rep)]
        for piece, (at_x, at_rep) in zip(pieces, corners):
            for z in range(outer):
                start = pl.multiple_of(at_rep * rows + z * 2 * share + at_x * share, share)
                for f in range(FREQS):
                    upper, lower = halves(piece[z, f])
                    high[f, pl.ds(start, share), :] = upper
                    low[f, pl.ds(start, share), :] = lower
    bare = bare_ref[...]
    once = [bare + product(bare, high[f], low[f]) for f in range(FREQS)]
    at = jnp.where(steps_ref[1] > steps_ref[0], 1, 0)
    last = jnp.where(at == 0, once[0], once[1])
    upper, lower = high[at], low[at]
    twice = last + product(product(last, upper, lower), upper, lower)
    other = jnp.minimum(offsets_ref[0], offsets_ref[1])
    less = jnp.where(other == 2, two_ref[...].astype(jnp.float32), odd_ref[...].astype(jnp.float32))
    four = four_ref[...].astype(jnp.float32)
    energy_terms = jnp.zeros((rows, width), jnp.float32)
    for f in range(FREQS):
        count = steps_ref[f]
        value = jnp.where(count == 0, bare, jnp.where(count == 1, once[f], twice))
        value = value.astype(jnp.bfloat16)
        screened_ref[f] = value
        lowered = jnp.where(offsets_ref[f] == SHIFTS, four, less)
        energy_terms += lowered * value.astype(jnp.float32)
    beside = sum(ref[...].astype(jnp.float32) for ref in beside_refs)
    rest = hamiltonian_ref[...] - entry_scale * energy_terms - (0.5 * entry_scale) * beside
    col = lax.broadcasted_iota(jnp.int32, (rows, width), 1)
    row = lax.broadcasted_iota(jnp.int32, (rows, width), 0) + rep * rows
    on = col == row
    diagonal = level_ref[0] + jnp.sum(jnp.where(on, rest, 0.0), axis=1, keepdims=True)
    off = jnp.where(on, 0.0, rest)
    largest = jnp.max(jnp.abs(off), axis=1, keepdims=True)
    largest = jnp.where(largest > 0.0, largest, 1.0)
    unit = off * (1.0 / largest)
    inverse = 1.0 / diagonal
    factor = -largest * inverse
    step_ref[...] = unit * factor
    factor_row = jnp.sum(jnp.where(on, factor, 0.0), axis=0, keepdims=True)
    inverse_row = jnp.sum(jnp.where(on, inverse, 0.0), axis=0, keepdims=True)
    blank = jnp.zeros((1, width), jnp.float32)
    packed_ref[:rows, :] = unit
    packed_ref[rows:, :] = jnp.concatenate(
        [*parts_of(factor_row), *parts_of(inverse_row), blank, blank], axis=0
    )
    own_ref[...] = jnp.concatenate([factor_row, inverse_row] + [blank] * 6, axis=0)


def dyson_rows(pieces, offsets, steps, level, bare, hamiltonian, two, four, odd, beside):
    rows, width = bare.shape
    count, sides = len(pieces), len(beside)

    def kernel(*refs):
        own, rest = refs[:count], refs[count:]
        named, rest = rest[:8], rest[8:]
        dyson_kernel(own, *named, rest[:sides], *rest[sides:])

    return pl.pallas_call(
        kernel,
        out_shape=(
            jax.ShapeDtypeStruct((FREQS, rows, width), jnp.bfloat16),
            jax.ShapeDtypeStruct((rows + EXTRA, width), jnp.float32),
            jax.ShapeDtypeStruct((rows, width), jnp.float32),
            jax.ShapeDtypeStruct((EXTRA, width), jnp.float32),
        ),
        in_specs=[in_vmem] * count + [in_smem] * 3 + [in_vmem] * (5 + sides),
        out_specs=(in_vmem,) * 4,
        scratch_shapes=[VMEM((FREQS, width, width), jnp.bfloat16)] * 2,
        name="dyson",
    )(*pieces, offsets, steps, level, bare, hamiltonian, two, four, odd, *beside)


def finish_kernel(steps_ref, step_ref, packed_ref, theirs_ref, own_ref, out_ref):
    rows, width = step_ref.shape
    rep = lax.axis_index("rep")
    first = rep == 0
    tail = theirs_ref[rows:, :]
    factors = own_ref[0:1] + whole_of(tail[0:1], tail[1:2], tail[2:3])
    inverses = own_ref[1:2] + whole_of(tail[3:4], tail[4:5], tail[5:6])
    mine = halves(packed_ref[:rows, :])
    theirs = halves(theirs_ref[:rows, :])

    def times_all(value):
        left, right = value[:, :rows], value[:, rows:]
        return product(jnp.where(first, left, right), *mine) + product(
            jnp.where(first, right, left), *theirs
        )

    step = step_ref[...]
    square = times_all(step * factors)
    cube = times_all(square * factors)
    col = lax.broadcasted_iota(jnp.int32, (rows, width), 1)
    row = lax.broadcasted_iota(jnp.int32, (rows, width), 0) + rep * rows
    total = jnp.where(col == row, 1.0, step)
    total = total + jnp.where(steps_ref[0] >= 2, square + cube, 0.0)
    out_ref[...] = total * inverses


def body(
    green_blocks, occupation, offsets, coulomb, hamiltonian, onsite_level, green_steps, screen_steps
):
    green = green_blocks[0, 0]
    bare = coulomb[0]
    rows, width = green.shape
    share = rows // lax.axis_size("energy")
    make = polar_share if share % 16 == 0 else polar_share_plain
    pieces = gathered(make(green, occupation, offsets, bare))

    two = shifted(green, "energy", 2)
    four = shifted(two, "energy", 2)
    odd = shifted(chosen(offsets, two, green), "energy", 1)

    slabs = lax.axis_size("slab")
    if slabs == 2:
        beside = [lax.ppermute(green, "slab", [(0, 1), (1, 0)])]
    else:
        up = [(i, i + 1) for i in range(slabs - 1)]
        down = [(j, i) for i, j in up]
        beside = [lax.ppermute(green, "slab", up), lax.ppermute(green, "slab", down)]

    screened, packed, step, own = dyson_rows(
        pieces, offsets, screen_steps, onsite_level, bare, hamiltonian[0], two, four, odd, beside
    )
    theirs = lax.ppermute(packed.astype(coded), "rep", [(0, 1), (1, 0)]).astype(jnp.float32)
    green_next = pl.pallas_call(
        finish_kernel,
        out_shape=jax.ShapeDtypeStruct((rows, width), jnp.float32),
        in_specs=[in_smem] + [in_vmem] * 4,
        out_specs=in_vmem,
        name="finish",
    )(green_steps, step, packed, theirs, own)
    return green_next[None, None], screened[:, None]


def chosen_kernel(offsets_ref, two_ref, green_ref, out_ref):
    three = jnp.minimum(offsets_ref[0], offsets_ref[1]) == 3

    @pl.when(three)
    def _():
        out_ref[...] = two_ref[...]

    @pl.when(jnp.logical_not(three))
    def _():
        out_ref[...] = green_ref[...]


def chosen(offsets, two, green):
    return pl.pallas_call(
        chosen_kernel,
        out_shape=jax.ShapeDtypeStruct(green.shape, green.dtype),
        in_specs=[in_smem, in_vmem, in_vmem],
        out_specs=in_vmem,
        name="chosen",
    )(offsets, two, green)


def solution(mesh):
    return jax.shard_map(
        body,
        mesh=mesh,
        in_specs=(
            P("energy", "slab", "rep", None),
            P("energy"),
            P(),
            P("slab", "rep", None),
            P("slab", "rep", None),
            P("energy"),
            P("energy"),
            P(),
        ),
        out_specs=(P("energy", "slab", "rep", None), P(None, "slab", "rep", None)),
        check_vma=False,
    )
```

time: 360 us -> 78 us (0.22)
  waiting for transfers between devices: 293 us -> 30.8 us
  matrix products: 21.9 us -> 0 us
  between operations: 20.4 us -> 2.73 us
  Pallas kernels: 0 us -> 15.3 us
  starting transfers between devices: 8.52 us -> 20.1 us
    psum x2 -> x0, waiting for transfers between devices: 147 us -> none  [the longest x1 79.3 us: body(): polarization = lax.psum(partial_value, 'energy')]
    all_gather x6 -> x0, waiting for transfers between devices: 120 us -> none  [the longest x4 79.9 us: full_rows(): return lax.all_gather(block_rows, 'rep', axis=2, tiled=True)]
    dot_general x9 -> x0, matrix products: 21.9 us -> none  [row_product(): jnp.einsum('esij,esjk->esik', first_factor, second_factor, precision=prec...]
    pallas_call x0 -> x5, Pallas kernels: none -> 15.3 us  [the longest x1 5.99 us: dyson_rows(): pl.pallas_call(kernel, out_shape=(jax.ShapeDtypeStruct((FREQS, rows, widt...]
    all_to_all x0 -> x1, waiting for transfers between devices: none -> 7.92 us  [polar_share(): got = lax.all_to_all(sent, 'energy', 0, 0, tiled=True)]
    ppermute x6 -> x11, starting transfers between devices: 8.01 us -> 14.1 us  [the longest x3 5.18 us: gather_energy(): got = lax.ppermute(chunk, 'energy', route)]
    all_to_all x0 -> x1, starting transfers between devices: none -> 6 us  [polar_share(): got = lax.all_to_all(sent, 'energy', 0, 0, tiled=True)]
    convert_element_type x0 -> x6, other arithmetic: none -> 5.41 us  [the longest x4 3.45 us: gathered(): return [piece.astype(jnp.float32) for piece in pieces]]
  transfers between devices with their start and end apart: 14 -> 12, of which waited for: 12 -> 7; matrix products, arithmetic and copies ran while one was open for 4% -> 5% of each run, Pallas kernels for 0% -> 2%
where the time goes in v2:
time: 78 us; the launch traced here: 77.5 us
  waiting for transfers between devices  30.8 us (39%)
  starting transfers between devices  20.1 us (26%)
  Pallas kernels  15.3 us (20%)
  other arithmetic  6.36 us (8%)
  between operations  2.73 us (4%)
  local copies, waits for them, and re-layouts  2.22 us (3%)
    ppermute x3, waiting for transfers between devices, gather_energy(): got = lax.ppermute(chunk, 'energy', route)  8.38 us
    all_to_all x1, waiting for transfers between devices, polar_share(): got = lax.all_to_all(sent, 'energy', 0, 0, tiled=True)  7.92 us
    all_to_all x1, starting transfers between devices, polar_share(): got = lax.all_to_all(sent, 'energy', 0, 0, tiled=True)  6 us
    pallas_call x1, Pallas kernels, dyson_rows(): pl.pallas_call(kernel, out_shape=(jax.ShapeDtypeStruct((FREQS, rows, widt...  5.99 us
    ppermute x1, waiting for transfers between devices, body(): lax.ppermute(packed.astype(coded), 'rep', [(0, 1), (1, 0)])  5.53 us
    ppermute x3, waiting for transfers between devices, shifted(): return lax.ppermute(block, axis, route)  5.36 us
    ppermute x3, starting transfers between devices, gather_energy(): got = lax.ppermute(chunk, 'energy', route)  5.18 us
    ppermute x3, starting transfers between devices, shifted(): return lax.ppermute(block, axis, route)  3.84 us
  transfers between devices with their start and end apart: 12, of which 7 were waited for; matrix products, arithmetic and copies ran while one was open for 5% of the time, Pallas kernels for 2%

profile of v2, /device:TPU:26, one launch (start us, length us, event | category | flops | bytes accessed | tf_op | source)
XLA Modules:
  0.0 77.5 jit_solution(15264335583967526597)
XLA Ops:
  1.3 1.7 %prepare.1 = bf16[8,40,512]{2,1,0:T(8,128)(2,1)} custom-call(f32[1]{0:T(128)S(6)} %copy.15.weight_ref, bf16[256,512]{1,0:T(8,128)(2,1)} %bitcast.17), custom_call_target="tpu_custom_call" | custom-call | tf_op jit(solution)/shard_map/prepare/pallas_call | solution.py:79
  3.0 6.0 %all-to-all-start = ((bf16[8,40,512]{2,1,0:T(8,128)(2,1)}), bf16[8,40,512]{2,1,0:T(8,128)(2,1)S(1)}, u32[]{:S(2)}, u32[]{:S(2)}) async-start(bf16[8,40,512]{2,1,0:T(8,128)(2,1)} %prepare.1), calls=%async_computation | async-start | bytes 655360 | tf_op jit(solution)/shard_map/all_to_all | solution.py:86
  9.0 7.9 %all-to-all-done.got_ref = bf16[8,40,512]{2,1,0:T(8,128)(2,1)S(1)} async-done(((bf16[8,40,512]{2,1,0:T(8,128)(2,1)}), bf16[8,40,512]{2,1,0:T(8,128)(2,1)S(1)}, u32[]{:S(2)}, u32[]{:S(2)}) %all-to-all-start) | async-done | bytes 327712 | tf_op jit(solution)/shard_map/all_to_all | solution.py:86
  16.9 0.0 copy-start
  16.9 0.7 copy-done
  17.6 2.5 %polar.1 = f32[2,32,512]{2,1,0:T(8,128)} custom-call(s32[2]{0:T(128)} %refs_4_.1, bf16[8,40,512]{2,1,0:T(8,128)(2,1)} %copy-done, f32[256,512]{1,0:T(8,128)} %bitcast.15), custom_call_target="tpu_custom_call" | custom-call | tf_op jit(solution)/shard_map/polar/pallas_call | solution.py:87
  20.1 0.0 copy-start.2
  20.2 1.0 %bitcast_dynamic-update-slice_fusion.3 = (f16[4,2,32,512]{3,2,1,0:T(8,128)(2,1)S(1)}, f16[2,32,512]{2,1,0:T(8,128)(2,1)S(1)}) fusion(f16[4,2,32,512]{3,2,1,0:T(8,128)(2,1)S(1)} %broadcast_in_dim.22, s32[]{:T(128)S(6)} %select_n.33, f32[2,32,512]{2,1,0:T(8,128)} %polar.1), kind=kLoop, calls=%fused_computation.3 | loop fusion | flops 32768 | bytes 262148 | tf_op jit(solution)/shard_map/jit(dynamic_update_index_in_dim)/dynamic_update_slice | solution.py:123
  21.1 2.4 %collective-permute-start = (f16[2,32,512]{2,1,0:T(8,128)(2,1)S(1)}, f16[2,32,512]{2,1,0:T(8,128)(2,1)S(1)}, u32[]{:S(2)}, u32[]{:S(2)}) collective-permute-start(f16[2,32,512]{2,1,0:T(8,128)(2,1)S(1)} %get-tuple-element.13), channel_id=1, source_target_pairs={{0,8},{4,12},{8,16},{12,20},{16,24},{20,28},{24,0},{28,4},{1,9},{5... | collective-permute-start | bytes 196616 | tf_op jit(solution)/shard_map/ppermute | solution.py:126
  23.5 0.0 copy-done.2
  23.5 1.3 %collective-permute-start.6 = (bf16[256,512]{1,0:T(8,128)(2,1)S(1)}, bf16[256,512]{1,0:T(8,128)(2,1)S(1)}, u32[]{:S(2)}, u32[]{:S(2)}) collective-permute-start(bf16[256,512]{1,0:T(8,128)(2,1)S(1)} %bitcast.19), channel_id=1, source_target_pairs={{0,8},{4,12},{8,16},{12,20},{16,24},{20,28},{1,9},{5,13},{9,17},{1... | collective-permute-start | bytes 786440 | tf_op jit(solution)/shard_map/ppermute | solution.py:36
  24.9 1.8 %collective-permute-start.1 = (f16[2,32,512]{2,1,0:T(8,128)(2,1)S(1)}, f16[2,32,512]{2,1,0:T(8,128)(2,1)S(1)}, u32[]{:S(2)}, u32[]{:S(2)}) collective-permute-start(f16[2,32,512]{2,1,0:T(8,128)(2,1)S(1)} %get-tuple-element.13), channel_id=1, source_target_pairs={{0,16},{4,20},{8,24},{12,28},{16,0},{20,4},{24,8},{28,12},{1,17},{... | collective-permute-start | bytes 196616 | tf_op jit(solution)/shard_map/ppermute | solution.py:126
  26.7 1.0 %collective-permute-start.2 = (f16[2,32,512]{2,1,0:T(8,128)(2,1)S(1)}, f16[2,32,512]{2,1,0:T(8,128)(2,1)S(1)}, u32[]{:S(2)}, u32[]{:S(2)}) collective-permute-start(f16[2,32,512]{2,1,0:T(8,128)(2,1)S(1)} %get-tuple-element.13), channel_id=1, source_target_pairs={{0,24},{4,28},{8,0},{12,4},{16,8},{20,12},{24,16},{28,20},{1,25},{... | collective-permute-start | bytes 196616 | tf_op jit(solution)/shard_map/ppermute | solution.py:126
  27.7 0.0 collective-permute-done
  27.7 8.4 %collective-permute-done.1 = f16[2,32,512]{2,1,0:T(8,128)(2,1)S(1)} collective-permute-done((f16[2,32,512]{2,1,0:T(8,128)(2,1)S(1)}, f16[2,32,512]{2,1,0:T(8,128)(2,1)S(1)}, u32[]{:S(2)}, u32[]{:S(2)}) %collective-permute-start.1) | collective-permute-done | bytes 65568 | tf_op jit(solution)/shard_map/ppermute | solution.py:126
  36.1 0.0 collective-permute-done.2
  36.1 0.3 collective-permute-start.3
  36.4 0.0 collective-permute-start.9
  36.4 1.5 %collective-permute-start.4 = (f16[4,2,32,512]{3,2,1,0:T(8,128)(2,1)S(1)}, f16[4,2,32,512]{3,2,1,0:T(8,128)(2,1)S(1)}, u32[]{:S(2)}, u32[]{:S(2)}) collective-permute-start(f16[4,2,32,512]{3,2,1,0:T(8,128)(2,1)S(1)} %bitcast_dynamic-update-slice_fusion), channel_id=1, source_target_pairs={{0,1},{1,0},{2,3},{3,2},{4,5},{5,4},{6,7},{7,6},{8,9},{9,8},{10,11... | collective-permute-start | bytes 786440 | tf_op jit(solution)/shard_map/ppermute | solution.py:139
  37.9 1.7 %collective-permute-start.5 = (f16[4,2,32,512]{3,2,1,0:T(8,128)(2,1)S(1)}, f16[4,2,32,512]{3,2,1,0:T(8,128)(2,1)S(1)}, u32[]{:S(2)}, u32[]{:S(2)}) collective-permute-start(f16[4,2,32,512]{3,2,1,0:T(8,128)(2,1)S(1)} %bitcast_dynamic-update-slice_fusion), channel_id=1, source_target_pairs={{0,5},{1,4},{4,1},{5,0},{8,13},{9,12},{12,9},{13,8},{16,21},{17,20... | collective-permute-start | bytes 786440 | tf_op jit(solution)/shard_map/ppermute | solution.py:140
  39.7 0.0 collective-permute-done.6.two_ref.refs_9_
  39.7 0.0 copy-start.1
  39.7 0.7 copy-done.1
  40.4 1.8 %chosen.1 = bf16[256,512]{1,0:T(8,128)(2,1)} custom-call(s32[2]{0:T(128)} %refs_4_.1, bf16[256,512]{1,0:T(8,128)(2,1)} %copy-done.1, bf16[256,512]{1,0:T(8,128)(2,1)} %bitcast.18), custom_call_target="tpu_custom_call" | custom-call | tf_op jit(solution)/shard_map/chosen/pallas_call | solution.py:327
  42.2 1.3 %collective-permute-start.8 = (bf16[256,512]{1,0:T(8,128)(2,1)}, bf16[256,512]{1,0:T(8,128)(2,1)S(1)}, u32[]{:S(2)}, u32[]{:S(2)}) collective-permute-start(bf16[256,512]{1,0:T(8,128)(2,1)} %chosen.1), channel_id=1, source_target_pairs={{0,4},{4,8},{8,12},{12,16},{16,20},{20,24},{24,28},{1,5},{5,9},{9,... | collective-permute-start | bytes 786440 | tf_op jit(solution)/shard_map/ppermute | solution.py:36
  43.5 0.8 %collective-permute-done.3 = f16[4,2,32,512]{3,2,1,0:T(8,128)(2,1)S(1)} collective-permute-done((f16[4,2,32,512]{3,2,1,0:T(8,128)(2,1)S(1)}, f16[4,2,32,512]{3,2,1,0:T(8,128)(2,1)S(1)}, u32[]{:S(2)}, u32[]{:S(2)}) %collective-permute-start.3) | collective-permute-done | bytes 262176 | tf_op jit(solution)/shard_map/ppermute | solution.py:138
  44.3 1.3 %collective-permute-start.7 = (bf16[256,512]{1,0:T(8,128)(2,1)}, bf16[256,512]{1,0:T(8,128)(2,1)S(1)}, u32[]{:S(2)}, u32[]{:S(2)}) collective-permute-start(bf16[256,512]{1,0:T(8,128)(2,1)} %copy-done.1), channel_id=1, source_target_pairs={{0,8},{4,12},{8,16},{12,20},{16,24},{20,28},{1,9},{5,13},{9,17},{1... | collective-permute-start | bytes 786440 | tf_op jit(solution)/shard_map/ppermute | solution.py:36
  46.2 0.9 %convert_element_type.22.refs_0_ = f32[4,2,32,512]{3,2,1,0:T(8,128)} convert(f16[4,2,32,512]{3,2,1,0:T(8,128)(2,1)S(1)} %bitcast_dynamic-update-slice_fusion) | non-fusion elementwise | flops 131072 | bytes 786432 | tf_op jit(solution)/shard_map/convert_element_type | solution.py:151
  47.1 0.9 %convert_element_type.23.refs_1_ = f32[4,2,32,512]{3,2,1,0:T(8,128)} convert(f16[4,2,32,512]{3,2,1,0:T(8,128)(2,1)S(1)} %collective-permute-done.3) | non-fusion elementwise | flops 131072 | bytes 786432 | tf_op jit(solution)/shard_map/convert_element_type | solution.py:151
  48.0 2.8 %collective-permute-done.4 = f16[4,2,32,512]{3,2,1,0:T(8,128)(2,1)S(1)} collective-permute-done((f16[4,2,32,512]{3,2,1,0:T(8,128)(2,1)S(1)}, f16[4,2,32,512]{3,2,1,0:T(8,128)(2,1)S(1)}, u32[]{:S(2)}, u32[]{:S(2)}) %collective-permute-start.4) | collective-permute-done | bytes 262176 | tf_op jit(solution)/shard_map/ppermute | solution.py:139
  50.8 0.9 %convert_element_type.24.refs_2_ = f32[4,2,32,512]{3,2,1,0:T(8,128)} convert(f16[4,2,32,512]{3,2,1,0:T(8,128)(2,1)S(1)} %collective-permute-done.4) | non-fusion elementwise | flops 131072 | bytes 786432 | tf_op jit(solution)/shard_map/convert_element_type | solution.py:151
  51.6 0.0 collective-permute-done.5
  51.6 0.9 %convert_element_type.25.refs_3_ = f32[4,2,32,512]{3,2,1,0:T(8,128)} convert(f16[4,2,32,512]{3,2,1,0:T(8,128)(2,1)S(1)} %collective-permute-done.5) | non-fusion elementwise | flops 131072 | bytes 786432 | tf_op jit(solution)/shard_map/convert_element_type | solution.py:151
  52.5 0.0 collective-permute-done.9.refs_12_
  52.5 0.0 copy-start.3
  52.5 1.3 %collective-permute-done.8.refs_11_ = bf16[256,512]{1,0:T(8,128)(2,1)S(1)} collective-permute-done((bf16[256,512]{1,0:T(8,128)(2,1)}, bf16[256,512]{1,0:T(8,128)(2,1)S(1)}, u32[]{:S(2)}, u32[]{:S(2)}) %collective-permute-start.8) | collective-permute-done | bytes 262176 | tf_op jit(solution)/shard_map/ppermute | solution.py:36
  53.8 0.0 copy-start.4
  53.8 4.0 %collective-permute-done.7.refs_10_ = bf16[256,512]{1,0:T(8,128)(2,1)S(1)} collective-permute-done((bf16[256,512]{1,0:T(8,128)(2,1)}, bf16[256,512]{1,0:T(8,128)(2,1)S(1)}, u32[]{:S(2)}, u32[]{:S(2)}) %collective-permute-start.7) | collective-permute-done | bytes 262176 | tf_op jit(solution)/shard_map/ppermute | solution.py:36
  57.9 0.0 copy-start.5
  57.9 0.0 copy-done.3
  57.9 0.0 copy-done.4
  57.9 0.7 copy-done.5
  58.6 6.0 %dyson.1 = (bf16[2,256,512]{2,1,0:T(8,128)(2,1)}, f32[264,512]{1,0:T(8,128)}, f32[256,512]{1,0:T(8,128)}, f32[8,512]{1,0:T(8,128)}) custom-call(f32[4,2,32,512]{3,2,1,0:T(8,128)} %convert_element_type.22.refs_0_, f32[4,2,32,512]{3,2,1,0:T(8,128)} %convert_element_type.23.refs_1_, f32[4,2,32,512]{3,2,1,0:T(8,128)} %convert_element_type.24.refs_2_, ...), custom_call_target="tpu_custom_call" | custom-call | tf_op jit(solution)/shard_map/dyson/pallas_call | solution.py:237
  64.6 1.1 %convert_element_type.26 = f16[264,512]{1,0:T(8,128)(2,1)S(1)} convert(f32[264,512]{1,0:T(8,128)} %get-tuple-element.7.packed_ref) | non-fusion elementwise | flops 135168 | bytes 811008 | tf_op jit(solution)/shard_map/convert_element_type | solution.py:303
  65.6 1.5 %collective-permute-start.10 = (f16[264,512]{1,0:T(8,128)(2,1)S(1)}, f16[264,512]{1,0:T(8,128)(2,1)S(1)}, u32[]{:S(2)}, u32[]{:S(2)}) collective-permute-start(f16[264,512]{1,0:T(8,128)(2,1)S(1)} %convert_element_type.26), channel_id=1, source_target_pairs={{0,1},{1,0},{2,3},{3,2},{4,5},{5,4},{6,7},{7,6},{8,9},{9,8},{10,11... | collective-permute-start | bytes 811016 | tf_op jit(solution)/shard_map/ppermute | solution.py:303
  67.8 5.5 %collective-permute-done.10 = f16[264,512]{1,0:T(8,128)(2,1)S(1)} collective-permute-done((f16[264,512]{1,0:T(8,128)(2,1)S(1)}, f16[264,512]{1,0:T(8,128)(2,1)S(1)}, u32[]{:S(2)}, u32[]{:S(2)}) %collective-permute-start.10) | collective-permute-done | bytes 270368 | tf_op jit(solution)/shard_map/ppermute | solution.py:303
  73.3 0.9 %convert_element_type.27.theirs_ref = f32[264,512]{1,0:T(8,128)} convert(f16[264,512]{1,0:T(8,128)(2,1)S(1)} %collective-permute-done.10) | non-fusion elementwise | flops 135168 | bytes 811008 | tf_op jit(solution)/shard_map/convert_element_type | solution.py:303
  74.2 3.3 %finish.1 = f32[256,512]{1,0:T(8,128)} custom-call(s32[1]{0:T(128)S(6)} %copy.17.steps_ref, f32[256,512]{1,0:T(8,128)} %get-tuple-element.6.step_ref, f32[264,512]{1,0:T(8,128)} %get-tuple-element.7.packed_ref, f32[264,512]{1,0:T(8,128)} %convert_element_type.27.theirs_ref, f32[8,512]{1,0:T(8,128)} %get-tuple-element.8.own_ref), custom_call_target="tpu_custom_call" | custom-call | tf_op jit(solution)/shard_map/finish/pallas_call | solution.py:304
  (4 shorter events, 0.1 us)
Async XLA Ops:
  3.0 13.9 %all-to-all-start = ((bf16[8,40,512]{2,1,0:T(8,128)(2,1)}), bf16[8,40,512]{2,1,0:T(8,128)(2,1)S(1)}, u32[]{:S(2)}, u32[]{:S(2)}) async-start(bf16[8,40,512]{2,1,0:T(8,128)(2,1)} %prepare.1), calls=%async_computation | async-start | bytes 655360 | tf_op jit(solution)/shard_map/all_to_all | solution.py:86
  16.9 0.7 copy-start
  20.1 3.4 %copy-start.2 = (bf16[1,1,256,512]{3,2,1,0:T(8,128)(2,1)S(1)}, bf16[1,1,256,512]{3,2,1,0:T(8,128)(2,1)}, u32[]{:S(2)}) copy-start(bf16[1,1,256,512]{3,2,1,0:T(8,128)(2,1)} %param.8) | copy-start | bytes 786436
  21.1 6.5 %collective-permute-start = (f16[2,32,512]{2,1,0:T(8,128)(2,1)S(1)}, f16[2,32,512]{2,1,0:T(8,128)(2,1)S(1)}, u32[]{:S(2)}, u32[]{:S(2)}) collective-permute-start(f16[2,32,512]{2,1,0:T(8,128)(2,1)S(1)} %get-tuple-element.13), channel_id=1, source_target_pairs={{0,8},{4,12},{8,16},{12,20},{16,24},{20,28},{24,0},{28,4},{1,9},{5... | collective-permute-start | bytes 196616 | tf_op jit(solution)/shard_map/ppermute | solution.py:126
  23.5 16.1 %collective-permute-start.6 = (bf16[256,512]{1,0:T(8,128)(2,1)S(1)}, bf16[256,512]{1,0:T(8,128)(2,1)S(1)}, u32[]{:S(2)}, u32[]{:S(2)}) collective-permute-start(bf16[256,512]{1,0:T(8,128)(2,1)S(1)} %bitcast.19), channel_id=1, source_target_pairs={{0,8},{4,12},{8,16},{12,20},{16,24},{20,28},{1,9},{5,13},{9,17},{1... | collective-permute-start | bytes 786440 | tf_op jit(solution)/shard_map/ppermute | solution.py:36
  24.9 11.2 %collective-permute-start.1 = (f16[2,32,512]{2,1,0:T(8,128)(2,1)S(1)}, f16[2,32,512]{2,1,0:T(8,128)(2,1)S(1)}, u32[]{:S(2)}, u32[]{:S(2)}) collective-permute-start(f16[2,32,512]{2,1,0:T(8,128)(2,1)S(1)} %get-tuple-element.13), channel_id=1, source_target_pairs={{0,16},{4,20},{8,24},{12,28},{16,0},{20,4},{24,8},{28,12},{1,17},{... | collective-permute-start | bytes 196616 | tf_op jit(solution)/shard_map/ppermute | solution.py:126
  26.7 9.4 %collective-permute-start.2 = (f16[2,32,512]{2,1,0:T(8,128)(2,1)S(1)}, f16[2,32,512]{2,1,0:T(8,128)(2,1)S(1)}, u32[]{:S(2)}, u32[]{:S(2)}) collective-permute-start(f16[2,32,512]{2,1,0:T(8,128)(2,1)S(1)} %get-tuple-element.13), channel_id=1, source_target_pairs={{0,24},{4,28},{8,0},{12,4},{16,8},{20,12},{24,16},{28,20},{1,25},{... | collective-permute-start | bytes 196616 | tf_op jit(solution)/shard_map/ppermute | solution.py:126
  36.1 8.2 %collective-permute-start.3 = (f16[4,2,32,512]{3,2,1,0:T(8,128)(2,1)S(1)}, f16[4,2,32,512]{3,2,1,0:T(8,128)(2,1)S(1)}, u32[]{:S(2)}, u32[]{:S(2)}) collective-permute-start(f16[4,2,32,512]{3,2,1,0:T(8,128)(2,1)S(1)} %bitcast_dynamic-update-slice_fusion), channel_id=1, source_target_pairs={{0,4},{4,0},{8,12},{12,8},{16,20},{20,16},{24,28},{28,24},{1,5},{5... | collective-permute-start | bytes 786440 | tf_op jit(solution)/shard_map/ppermute | solution.py:138
  36.4 16.1 %collective-permute-start.9 = (bf16[256,512]{1,0:T(8,128)(2,1)S(1)}, bf16[256,512]{1,0:T(8,128)(2,1)S(1)}, u32[]{:S(2)}, u32[]{:S(2)}) collective-permute-start(bf16[256,512]{1,0:T(8,128)(2,1)S(1)} %bitcast.20), channel_id=1, source_target_pairs={{0,2},{2,0},{1,3},{3,1},{4,6},{6,4},{5,7},{7,5},{8,10},{10,8},{9,1... | collective-permute-start | bytes 786440 | tf_op jit(solution)/shard_map/ppermute | solution.py:294
  36.4 14.3 %collective-permute-start.4 = (f16[4,2,32,512]{3,2,1,0:T(8,128)(2,1)S(1)}, f16[4,2,32,512]{3,2,1,0:T(8,128)(2,1)S(1)}, u32[]{:S(2)}, u32[]{:S(2)}) collective-permute-start(f16[4,2,32,512]{3,2,1,0:T(8,128)(2,1)S(1)} %bitcast_dynamic-update-slice_fusion), channel_id=1, source_target_pairs={{0,1},{1,0},{2,3},{3,2},{4,5},{5,4},{6,7},{7,6},{8,9},{9,8},{10,11... | collective-permute-start | bytes 786440 | tf_op jit(solution)/shard_map/ppermute | solution.py:139
  37.9 13.7 %collective-permute-start.5 = (f16[4,2,32,512]{3,2,1,0:T(8,128)(2,1)S(1)}, f16[4,2,32,512]{3,2,1,0:T(8,128)(2,1)S(1)}, u32[]{:S(2)}, u32[]{:S(2)}) collective-permute-start(f16[4,2,32,512]{3,2,1,0:T(8,128)(2,1)S(1)} %bitcast_dynamic-update-slice_fusion), channel_id=1, source_target_pairs={{0,5},{1,4},{4,1},{5,0},{8,13},{9,12},{12,9},{13,8},{16,21},{17,20... | collective-permute-start | bytes 786440 | tf_op jit(solution)/shard_map/ppermute | solution.py:140
  39.7 0.7 copy-start.1
  42.2 11.7 %collective-permute-start.8 = (bf16[256,512]{1,0:T(8,128)(2,1)}, bf16[256,512]{1,0:T(8,128)(2,1)S(1)}, u32[]{:S(2)}, u32[]{:S(2)}) collective-permute-start(bf16[256,512]{1,0:T(8,128)(2,1)} %chosen.1), channel_id=1, source_target_pairs={{0,4},{4,8},{8,12},{12,16},{16,20},{20,24},{24,28},{1,5},{5,9},{9,... | collective-permute-start | bytes 786440 | tf_op jit(solution)/shard_map/ppermute | solution.py:36
  44.3 13.6 %collective-permute-start.7 = (bf16[256,512]{1,0:T(8,128)(2,1)}, bf16[256,512]{1,0:T(8,128)(2,1)S(1)}, u32[]{:S(2)}, u32[]{:S(2)}) collective-permute-start(bf16[256,512]{1,0:T(8,128)(2,1)} %copy-done.1), channel_id=1, source_target_pairs={{0,8},{4,12},{8,16},{12,20},{16,24},{20,28},{1,9},{5,13},{9,17},{1... | collective-permute-start | bytes 786440 | tf_op jit(solution)/shard_map/ppermute | solution.py:36
  52.5 5.4 %copy-start.3 = (bf16[256,512]{1,0:T(8,128)(2,1)}, bf16[256,512]{1,0:T(8,128)(2,1)S(1)}, u32[]{:S(2)}) copy-start(bf16[256,512]{1,0:T(8,128)(2,1)S(1)} %collective-permute-done.9.refs_12_) | copy-start | bytes 786436
  53.8 4.0 %copy-start.4 = (bf16[256,512]{1,0:T(8,128)(2,1)}, bf16[256,512]{1,0:T(8,128)(2,1)S(1)}, u32[]{:S(2)}) copy-start(bf16[256,512]{1,0:T(8,128)(2,1)S(1)} %collective-permute-done.8.refs_11_) | copy-start | bytes 786436
  57.9 0.7 copy-start.5
  65.6 7.7 %collective-permute-start.10 = (f16[264,512]{1,0:T(8,128)(2,1)S(1)}, f16[264,512]{1,0:T(8,128)(2,1)S(1)}, u32[]{:S(2)}, u32[]{:S(2)}) collective-permute-start(f16[264,512]{1,0:T(8,128)(2,1)S(1)} %convert_element_type.26), channel_id=1, source_target_pairs={{0,1},{1,0},{2,3},{3,2},{4,5},{5,4},{6,7},{7,6},{8,9},{9,8},{10,11... | collective-permute-start | bytes 811016 | tf_op jit(solution)/shard_map/ppermute | solution.py:303

commit v3 on v2

--- a/solution.py
+++ b/solution.py
@@ -14,6 +14,8 @@
 in_vmem = pl.BlockSpec(memory_space=pltpu.VMEM)
 in_smem = pl.BlockSpec(memory_space=pltpu.SMEM)
 in_place = pl.BlockSpec(memory_space=pl.ANY)
+small = pltpu.CompilerParams(vmem_limit_bytes=6 << 20)
+large = pltpu.CompilerParams(vmem_limit_bytes=16 << 20)
 
 
 def halves(value):
@@ -81,6 +83,7 @@
         out_shape=jax.ShapeDtypeStruct((energies, share + EXTRA, width), green.dtype),
         in_specs=[in_smem, in_vmem],
         out_specs=in_vmem,
+        compiler_params=small,
         name="prepare",
     )(weight, green)
     got = lax.all_to_all(sent, "energy", 0, 0, tiled=True)
@@ -94,6 +97,7 @@
             VMEM((share, width), jnp.float32),
             pltpu.SemaphoreType.DMA,
         ],
+        compiler_params=small,
         name="polar",
     )(offsets, got, bare)
 
@@ -245,6 +249,7 @@
         in_specs=[in_vmem] * count + [in_smem] * 3 + [in_vmem] * (5 + sides),
         out_specs=(in_vmem,) * 4,
         scratch_shapes=[VMEM((FREQS, width, width), jnp.bfloat16)] * 2,
+        compiler_params=large,
         name="dyson",
     )(*pieces, offsets, steps, level, bare, hamiltonian, two, four, odd, *beside)
 
@@ -306,6 +311,7 @@
         out_shape=jax.ShapeDtypeStruct((rows, width), jnp.float32),
         in_specs=[in_smem] + [in_vmem] * 4,
         out_specs=in_vmem,
+        compiler_params=large,
         name="finish",
     )(green_steps, step, packed, theirs, own)
     return green_next[None, None], screened[:, None]
@@ -329,6 +335,7 @@
         out_shape=jax.ShapeDtypeStruct(green.shape, green.dtype),
         in_specs=[in_smem, in_vmem, in_vmem],
         out_specs=in_vmem,
+        compiler_params=small,
         name="chosen",
     )(offsets, two, green)
 

time: 78 us -> 66.5 us (0.85)
  Pallas kernels: 15.3 us -> 8.07 us
  other arithmetic: 6.36 us -> 0.33 us
  waiting for transfers between devices: 30.8 us -> 33.8 us
  local copies, waits for them, and re-layouts: 2.22 us -> 1.04 us
    convert_element_type x4, other arithmetic: 3.45 us -> 0.22 us  [gathered(): return [piece.astype(jnp.float32) for piece in pieces]]
    pallas_call x1, Pallas kernels: 5.99 us -> 3.99 us  [dyson_rows(): pl.pallas_call(kernel, out_shape=(jax.ShapeDtypeStruct((FREQS, rows, widt...]
    ppermute x1, waiting for transfers between devices: 0.84 us -> 2.74 us  [gather_square(): lax.ppermute(part, 'energy', swap)]
    pallas_call x1, Pallas kernels: 2.5 us -> 0.82 us  [polar_share(): pl.pallas_call(polar_kernel, out_shape=jax.ShapeDtypeStruct((FREQS, share...]
    pallas_call x1, Pallas kernels: 3.3 us -> 1.95 us  [body(): pl.pallas_call(finish_kernel, out_shape=jax.ShapeDtypeStruct((rows, width...]
    ppermute x1, waiting for transfers between devices: 2.8 us -> 4.12 us  [gather_square(): lax.ppermute(part, 'rep', turn)]
    ppermute x3, waiting for transfers between devices: 5.36 us -> 4.08 us  [shifted(): return lax.ppermute(block, axis, route)]
    pallas_call x1, Pallas kernels: 1.77 us -> 0.57 us  [chosen(): pl.pallas_call(chosen_kernel, out_shape=jax.ShapeDtypeStruct(green.shape,...]
  transfers between devices with their start and end apart: 12 -> 12, of which waited for: 7 -> 8; matrix products, arithmetic and copies ran while one was open for 5% -> 0% of each run, Pallas kernels for 2% -> 1%
where the time goes in v3:
time: 66.5 us; the launch traced here: 66.1 us
  waiting for transfers between devices  33.8 us (51%)
  starting transfers between devices  20.1 us (30%)
  Pallas kernels  8.07 us (12%)
  between operations  2.81 us (4%)
  local copies, waits for them, and re-layouts  1.04 us (2%)
    ppermute x3, waiting for transfers between devices, gather_energy(): got = lax.ppermute(chunk, 'energy', route)  8.38 us
    all_to_all x1, waiting for transfers between devices, polar_share(): got = lax.all_to_all(sent, 'energy', 0, 0, tiled=True)  7.92 us
    all_to_all x1, starting transfers between devices, polar_share(): got = lax.all_to_all(sent, 'energy', 0, 0, tiled=True)  6 us
    ppermute x1, waiting for transfers between devices, body(): lax.ppermute(packed.astype(coded), 'rep', [(0, 1), (1, 0)])  5.52 us
    ppermute x3, starting transfers between devices, gather_energy(): got = lax.ppermute(chunk, 'energy', route)  5.18 us
    ppermute x1, waiting for transfers between devices, gather_square(): lax.ppermute(part, 'rep', turn)  4.12 us
    ppermute x3, waiting for transfers between devices, shifted(): return lax.ppermute(block, axis, route)  4.08 us
    pallas_call x1, Pallas kernels, dyson_rows(): pl.pallas_call(kernel, out_shape=(jax.ShapeDtypeStruct((FREQS, rows, widt...  3.99 us
  transfers between devices with their start and end apart: 12, of which 8 were waited for; matrix products, arithmetic and copies ran while one was open for 0% of the time, Pallas kernels for 1%

profile of v3, /device:TPU:26, one launch (start us, length us, event | category | flops | bytes accessed | tf_op | source)
XLA Modules:
  0.0 66.1 jit_solution(15479540197683095498)
XLA Ops:
  1.3 0.0 copy-start.1
  1.3 0.9 %copy-done.1 = bf16[1,1,256,512]{3,2,1,0:T(8,128)(2,1)S(1)} copy-done((bf16[1,1,256,512]{3,2,1,0:T(8,128)(2,1)S(1)}, bf16[1,1,256,512]{3,2,1,0:T(8,128)(2,1)}, u32[]{:S(2)}) %copy-start.1) | copy-done | bytes 262168
  2.2 0.0 copy-start
  2.2 0.7 %prepare.1 = bf16[8,40,512]{2,1,0:T(8,128)(2,1)} custom-call(f32[1]{0:T(128)S(6)} %copy.15.weight_ref, bf16[256,512]{1,0:T(8,128)(2,1)S(1)} %bitcast.17), custom_call_target="tpu_custom_call" | custom-call | tf_op jit(solution)/shard_map/prepare/pallas_call | solution.py:81
  3.0 6.0 %all-to-all-start = ((bf16[8,40,512]{2,1,0:T(8,128)(2,1)}), bf16[8,40,512]{2,1,0:T(8,128)(2,1)S(1)}, u32[]{:S(2)}, u32[]{:S(2)}) async-start(bf16[8,40,512]{2,1,0:T(8,128)(2,1)} %prepare.1), calls=%async_computation | async-start | bytes 655360 | tf_op jit(solution)/shard_map/all_to_all | solution.py:89
  9.0 0.0 copy-start.4
  9.0 7.9 %all-to-all-done.got_ref = bf16[8,40,512]{2,1,0:T(8,128)(2,1)S(1)} async-done(((bf16[8,40,512]{2,1,0:T(8,128)(2,1)}), bf16[8,40,512]{2,1,0:T(8,128)(2,1)S(1)}, u32[]{:S(2)}, u32[]{:S(2)}) %all-to-all-start) | async-done | bytes 327712 | tf_op jit(solution)/shard_map/all_to_all | solution.py:89
  16.9 0.0 copy-done
  16.9 0.0 copy-done.4
  16.9 0.8 %polar.1 = f32[2,32,512]{2,1,0:T(8,128)S(1)} custom-call(s32[2]{0:T(128)S(1)} %copy-done.4, bf16[8,40,512]{2,1,0:T(8,128)(2,1)S(1)} %all-to-all-done.got_ref, f32[256,512]{1,0:T(8,128)S(1)} %bitcast.15), custom_call_target="tpu_custom_call" | custom-call | tf_op jit(solution)/shard_map/polar/pallas_call | solution.py:90
  17.7 0.0 copy-start.2
  17.8 2.4 %collective-permute-start = (f16[2,32,512]{2,1,0:T(8,128)(2,1)S(1)}, f16[2,32,512]{2,1,0:T(8,128)(2,1)S(1)}, u32[]{:S(2)}, u32[]{:S(2)}) collective-permute-start(f16[2,32,512]{2,1,0:T(8,128)(2,1)S(1)} %get-tuple-element.13), channel_id=1, source_target_pairs={{0,8},{4,12},{8,16},{12,20},{16,24},{20,28},{24,0},{28,4},{1,9},{5... | collective-permute-start | bytes 196616 | tf_op jit(solution)/shard_map/ppermute | solution.py:130
  20.2 0.0 copy-done.2
  20.2 1.3 %collective-permute-start.6 = (bf16[256,512]{1,0:T(8,128)(2,1)S(1)}, bf16[256,512]{1,0:T(8,128)(2,1)S(1)}, u32[]{:S(2)}, u32[]{:S(2)}) collective-permute-start(bf16[256,512]{1,0:T(8,128)(2,1)S(1)} %bitcast.18), channel_id=1, source_target_pairs={{0,8},{4,12},{8,16},{12,20},{16,24},{20,28},{1,9},{5,13},{9,17},{1... | collective-permute-start | bytes 786440 | tf_op jit(solution)/shard_map/ppermute | solution.py:38
  21.6 1.8 %collective-permute-start.1 = (f16[2,32,512]{2,1,0:T(8,128)(2,1)S(1)}, f16[2,32,512]{2,1,0:T(8,128)(2,1)S(1)}, u32[]{:S(2)}, u32[]{:S(2)}) collective-permute-start(f16[2,32,512]{2,1,0:T(8,128)(2,1)S(1)} %get-tuple-element.13), channel_id=1, source_target_pairs={{0,16},{4,20},{8,24},{12,28},{16,0},{20,4},{24,8},{28,12},{1,17},{... | collective-permute-start | bytes 196616 | tf_op jit(solution)/shard_map/ppermute | solution.py:130
  23.4 1.0 %collective-permute-start.2 = (f16[2,32,512]{2,1,0:T(8,128)(2,1)S(1)}, f16[2,32,512]{2,1,0:T(8,128)(2,1)S(1)}, u32[]{:S(2)}, u32[]{:S(2)}) collective-permute-start(f16[2,32,512]{2,1,0:T(8,128)(2,1)S(1)} %get-tuple-element.13), channel_id=1, source_target_pairs={{0,24},{4,28},{8,0},{12,4},{16,8},{20,12},{24,16},{28,20},{1,25},{... | collective-permute-start | bytes 196616 | tf_op jit(solution)/shard_map/ppermute | solution.py:130
  24.3 0.0 collective-permute-done
  24.4 8.4 %collective-permute-done.1 = f16[2,32,512]{2,1,0:T(8,128)(2,1)S(1)} collective-permute-done((f16[2,32,512]{2,1,0:T(8,128)(2,1)S(1)}, f16[2,32,512]{2,1,0:T(8,128)(2,1)S(1)}, u32[]{:S(2)}, u32[]{:S(2)}) %collective-permute-start.1) | collective-permute-done | bytes 65568 | tf_op jit(solution)/shard_map/ppermute | solution.py:130
  32.7 0.0 collective-permute-done.2
  32.8 0.3 collective-permute-start.3
  33.1 0.0 collective-permute-start.9
  33.1 1.5 %collective-permute-start.4 = (f16[4,2,32,512]{3,2,1,0:T(8,128)(2,1)S(1)}, f16[4,2,32,512]{3,2,1,0:T(8,128)(2,1)S(1)}, u32[]{:S(2)}, u32[]{:S(2)}) collective-permute-start(f16[4,2,32,512]{3,2,1,0:T(8,128)(2,1)S(1)} %bitcast_dynamic-update-slice_fusion), channel_id=1, source_target_pairs={{0,1},{1,0},{2,3},{3,2},{4,5},{5,4},{6,7},{7,6},{8,9},{9,8},{10,11... | collective-permute-start | bytes 786440 | tf_op jit(solution)/shard_map/ppermute | solution.py:143
  34.6 1.7 %collective-permute-start.5 = (f16[4,2,32,512]{3,2,1,0:T(8,128)(2,1)S(1)}, f16[4,2,32,512]{3,2,1,0:T(8,128)(2,1)S(1)}, u32[]{:S(2)}, u32[]{:S(2)}) collective-permute-start(f16[4,2,32,512]{3,2,1,0:T(8,128)(2,1)S(1)} %bitcast_dynamic-update-slice_fusion), channel_id=1, source_target_pairs={{0,5},{1,4},{4,1},{5,0},{8,13},{9,12},{12,9},{13,8},{16,21},{17,20... | collective-permute-start | bytes 786440 | tf_op jit(solution)/shard_map/ppermute | solution.py:144
  36.3 0.0 collective-permute-done.6.two_ref.refs_9_
  36.3 0.6 chosen.1
  36.9 1.3 %collective-permute-start.8 = (bf16[256,512]{1,0:T(8,128)(2,1)S(1)}, bf16[256,512]{1,0:T(8,128)(2,1)S(1)}, u32[]{:S(2)}, u32[]{:S(2)}) collective-permute-start(bf16[256,512]{1,0:T(8,128)(2,1)S(1)} %chosen.1), channel_id=1, source_target_pairs={{0,4},{4,8},{8,12},{12,16},{16,20},{20,24},{24,28},{1,5},{5,9},{9,... | collective-permute-start | bytes 786440 | tf_op jit(solution)/shard_map/ppermute | solution.py:38
  38.2 2.7 %collective-permute-done.3 = f16[4,2,32,512]{3,2,1,0:T(8,128)(2,1)S(1)} collective-permute-done((f16[4,2,32,512]{3,2,1,0:T(8,128)(2,1)S(1)}, f16[4,2,32,512]{3,2,1,0:T(8,128)(2,1)S(1)}, u32[]{:S(2)}, u32[]{:S(2)}) %collective-permute-start.3) | collective-permute-done | bytes 262176 | tf_op jit(solution)/shard_map/ppermute | solution.py:142
  41.0 1.3 %collective-permute-start.7 = (bf16[256,512]{1,0:T(8,128)(2,1)S(1)}, bf16[256,512]{1,0:T(8,128)(2,1)S(1)}, u32[]{:S(2)}, u32[]{:S(2)}) collective-permute-start(bf16[256,512]{1,0:T(8,128)(2,1)S(1)} %collective-permute-done.6.two_ref.refs_9_), channel_id=1, source_target_pairs={{0,8},{4,12},{8,16},{12,20},{16,24},{20,28},{1,9},{5,13},{9,17},{1... | collective-permute-start | bytes 786440 | tf_op jit(solution)/shard_map/ppermute | solution.py:38
  42.9 0.1 convert_element_type.22.refs_0_
  43.0 0.1 convert_element_type.23.refs_1_
  43.0 4.1 %collective-permute-done.4 = f16[4,2,32,512]{3,2,1,0:T(8,128)(2,1)S(1)} collective-permute-done((f16[4,2,32,512]{3,2,1,0:T(8,128)(2,1)S(1)}, f16[4,2,32,512]{3,2,1,0:T(8,128)(2,1)S(1)}, u32[]{:S(2)}, u32[]{:S(2)}) %collective-permute-start.4) | collective-permute-done | bytes 262176 | tf_op jit(solution)/shard_map/ppermute | solution.py:143
  47.1 0.1 convert_element_type.24.refs_2_
  47.2 0.0 copy-start.3
  47.2 1.0 %collective-permute-done.5 = f16[4,2,32,512]{3,2,1,0:T(8,128)(2,1)S(1)} collective-permute-done((f16[4,2,32,512]{3,2,1,0:T(8,128)(2,1)S(1)}, f16[4,2,32,512]{3,2,1,0:T(8,128)(2,1)S(1)}, u32[]{:S(2)}, u32[]{:S(2)}) %collective-permute-start.5) | collective-permute-done | bytes 262176 | tf_op jit(solution)/shard_map/ppermute | solution.py:144
  48.3 0.1 convert_element_type.25.refs_3_
  48.3 0.0 copy-start.5
  48.3 0.0 collective-permute-done.9.refs_12_
  48.3 2.2 %collective-permute-done.8.refs_11_ = bf16[256,512]{1,0:T(8,128)(2,1)S(1)} collective-permute-done((bf16[256,512]{1,0:T(8,128)(2,1)S(1)}, bf16[256,512]{1,0:T(8,128)(2,1)S(1)}, u32[]{:S(2)}, u32[]{:S(2)}) %collective-permute-start.8) | collective-permute-done | bytes 262176 | tf_op jit(solution)/shard_map/ppermute | solution.py:38
  50.5 1.9 %collective-permute-done.7.refs_10_ = bf16[256,512]{1,0:T(8,128)(2,1)S(1)} collective-permute-done((bf16[256,512]{1,0:T(8,128)(2,1)S(1)}, bf16[256,512]{1,0:T(8,128)(2,1)S(1)}, u32[]{:S(2)}, u32[]{:S(2)}) %collective-permute-start.7) | collective-permute-done | bytes 262176 | tf_op jit(solution)/shard_map/ppermute | solution.py:38
  52.4 0.0 copy-done.3
  52.4 0.0 copy-done.5
  52.4 4.0 %dyson.1 = (bf16[2,256,512]{2,1,0:T(8,128)(2,1)}, f32[264,512]{1,0:T(8,128)S(1)}, f32[256,512]{1,0:T(8,128)S(1)}, f32[8,512]{1,0:T(8,128)S(1)}) custom-call(f32[4,2,32,512]{3,2,1,0:T(8,128)S(1)} %convert_element_type.22.refs_0_, f32[4,2,32,512]{3,2,1,0:T(8,128)S(1)} %convert_element_type.23.refs_1_, f32[4,2,32,512]{3,2,1,0:T(8,128)S(1)} %convert_element_type.24.refs_2_, ...), custom_call_target="tpu_custom_call" | custom-call | tf_op jit(solution)/shard_map/dyson/pallas_call | solution.py:241
  56.5 1.5 %collective-permute-start.10 = (f16[264,512]{1,0:T(8,128)(2,1)S(1)}, f16[264,512]{1,0:T(8,128)(2,1)S(1)}, u32[]{:S(2)}, u32[]{:S(2)}) collective-permute-start(f16[264,512]{1,0:T(8,128)(2,1)S(1)} %convert_element_type.26), channel_id=1, source_target_pairs={{0,1},{1,0},{2,3},{3,2},{4,5},{5,4},{6,7},{7,6},{8,9},{9,8},{10,11... | collective-permute-start | bytes 811016 | tf_op jit(solution)/shard_map/ppermute | solution.py:308
  58.6 5.5 %collective-permute-done.10 = f16[264,512]{1,0:T(8,128)(2,1)S(1)} collective-permute-done((f16[264,512]{1,0:T(8,128)(2,1)S(1)}, f16[264,512]{1,0:T(8,128)(2,1)S(1)}, u32[]{:S(2)}, u32[]{:S(2)}) %collective-permute-start.10) | collective-permute-done | bytes 270368 | tf_op jit(solution)/shard_map/ppermute | solution.py:308
  64.1 0.1 convert_element_type.27.theirs_ref
  64.2 2.0 %finish.1 = f32[256,512]{1,0:T(8,128)} custom-call(s32[1]{0:T(128)S(6)} %copy.17.steps_ref, f32[256,512]{1,0:T(8,128)S(1)} %get-tuple-element.6.step_ref, f32[264,512]{1,0:T(8,128)S(1)} %get-tuple-element.7.packed_ref, f32[264,512]{1,0:T(8,128)S(1)} %convert_element_type.27.theirs_ref, f32[8,512]{1,0:T(8,128)S(1)} %get-tuple-element.8.own_ref), custom_call_target="tpu_custom_call" | custom-call | tf_op jit(solution)/shard_map/finish/pallas_call | solution.py:309
  (6 shorter events, 0.1 us)
Async XLA Ops:
  1.3 1.0 %copy-start.1 = (bf16[1,1,256,512]{3,2,1,0:T(8,128)(2,1)S(1)}, bf16[1,1,256,512]{3,2,1,0:T(8,128)(2,1)}, u32[]{:S(2)}) copy-start(bf16[1,1,256,512]{3,2,1,0:T(8,128)(2,1)} %param.8) | copy-start | bytes 786436
  2.2 14.7 %copy-start = (f32[1,256,512]{2,1,0:T(8,128)S(1)}, f32[1,256,512]{2,1,0:T(8,128)}, u32[]{:S(2)}) copy-start(f32[1,256,512]{2,1,0:T(8,128)} %param.11) | copy-start | bytes 1572868
  3.0 13.9 %all-to-all-start = ((bf16[8,40,512]{2,1,0:T(8,128)(2,1)}), bf16[8,40,512]{2,1,0:T(8,128)(2,1)S(1)}, u32[]{:S(2)}, u32[]{:S(2)}) async-start(bf16[8,40,512]{2,1,0:T(8,128)(2,1)} %prepare.1), calls=%async_computation | async-start | bytes 655360 | tf_op jit(solution)/shard_map/all_to_all | solution.py:89
  9.0 7.9 %copy-start.4 = (s32[2]{0:T(128)S(1)}, s32[2]{0:T(128)}, u32[]{:S(2)}) copy-start(s32[2]{0:T(128)} %refs_4_.1) | copy-start | bytes 28
  17.7 2.5 %copy-start.2 = (bf16[1,1,256,512]{3,2,1,0:T(8,128)(2,1)S(1)}, bf16[1,1,256,512]{3,2,1,0:T(8,128)(2,1)}, u32[]{:S(2)}) copy-start(bf16[1,1,256,512]{3,2,1,0:T(8,128)(2,1)} %param.8) | copy-start | bytes 786436
  17.8 6.5 %collective-permute-start = (f16[2,32,512]{2,1,0:T(8,128)(2,1)S(1)}, f16[2,32,512]{2,1,0:T(8,128)(2,1)S(1)}, u32[]{:S(2)}, u32[]{:S(2)}) collective-permute-start(f16[2,32,512]{2,1,0:T(8,128)(2,1)S(1)} %get-tuple-element.13), channel_id=1, source_target_pairs={{0,8},{4,12},{8,16},{12,20},{16,24},{20,28},{24,0},{28,4},{1,9},{5... | collective-permute-start | bytes 196616 | tf_op jit(solution)/shard_map/ppermute | solution.py:130
  20.2 16.1 %collective-permute-start.6 = (bf16[256,512]{1,0:T(8,128)(2,1)S(1)}, bf16[256,512]{1,0:T(8,128)(2,1)S(1)}, u32[]{:S(2)}, u32[]{:S(2)}) collective-permute-start(bf16[256,512]{1,0:T(8,128)(2,1)S(1)} %bitcast.18), channel_id=1, source_target_pairs={{0,8},{4,12},{8,16},{12,20},{16,24},{20,28},{1,9},{5,13},{9,17},{1... | collective-permute-start | bytes 786440 | tf_op jit(solution)/shard_map/ppermute | solution.py:38
  21.6 11.2 %collective-permute-start.1 = (f16[2,32,512]{2,1,0:T(8,128)(2,1)S(1)}, f16[2,32,512]{2,1,0:T(8,128)(2,1)S(1)}, u32[]{:S(2)}, u32[]{:S(2)}) collective-permute-start(f16[2,32,512]{2,1,0:T(8,128)(2,1)S(1)} %get-tuple-element.13), channel_id=1, source_target_pairs={{0,16},{4,20},{8,24},{12,28},{16,0},{20,4},{24,8},{28,12},{1,17},{... | collective-permute-start | bytes 196616 | tf_op jit(solution)/shard_map/ppermute | solution.py:130
  23.4 9.4 %collective-permute-start.2 = (f16[2,32,512]{2,1,0:T(8,128)(2,1)S(1)}, f16[2,32,512]{2,1,0:T(8,128)(2,1)S(1)}, u32[]{:S(2)}, u32[]{:S(2)}) collective-permute-start(f16[2,32,512]{2,1,0:T(8,128)(2,1)S(1)} %get-tuple-element.13), channel_id=1, source_target_pairs={{0,24},{4,28},{8,0},{12,4},{16,8},{20,12},{24,16},{28,20},{1,25},{... | collective-permute-start | bytes 196616 | tf_op jit(solution)/shard_map/ppermute | solution.py:130
  32.8 8.2 %collective-permute-start.3 = (f16[4,2,32,512]{3,2,1,0:T(8,128)(2,1)S(1)}, f16[4,2,32,512]{3,2,1,0:T(8,128)(2,1)S(1)}, u32[]{:S(2)}, u32[]{:S(2)}) collective-permute-start(f16[4,2,32,512]{3,2,1,0:T(8,128)(2,1)S(1)} %bitcast_dynamic-update-slice_fusion), channel_id=1, source_target_pairs={{0,4},{4,0},{8,12},{12,8},{16,20},{20,16},{24,28},{28,24},{1,5},{5... | collective-permute-start | bytes 786440 | tf_op jit(solution)/shard_map/ppermute | solution.py:142
  33.1 15.2 %collective-permute-start.9 = (bf16[256,512]{1,0:T(8,128)(2,1)S(1)}, bf16[256,512]{1,0:T(8,128)(2,1)S(1)}, u32[]{:S(2)}, u32[]{:S(2)}) collective-permute-start(bf16[256,512]{1,0:T(8,128)(2,1)S(1)} %bitcast.19), channel_id=1, source_target_pairs={{0,2},{2,0},{1,3},{3,1},{4,6},{6,4},{5,7},{7,5},{8,10},{10,8},{9,1... | collective-permute-start | bytes 786440 | tf_op jit(solution)/shard_map/ppermute | solution.py:299
  33.1 14.1 %collective-permute-start.4 = (f16[4,2,32,512]{3,2,1,0:T(8,128)(2,1)S(1)}, f16[4,2,32,512]{3,2,1,0:T(8,128)(2,1)S(1)}, u32[]{:S(2)}, u32[]{:S(2)}) collective-permute-start(f16[4,2,32,512]{3,2,1,0:T(8,128)(2,1)S(1)} %bitcast_dynamic-update-slice_fusion), channel_id=1, source_target_pairs={{0,1},{1,0},{2,3},{3,2},{4,5},{5,4},{6,7},{7,6},{8,9},{9,8},{10,11... | collective-permute-start | bytes 786440 | tf_op jit(solution)/shard_map/ppermute | solution.py:143
  34.6 13.6 %collective-permute-start.5 = (f16[4,2,32,512]{3,2,1,0:T(8,128)(2,1)S(1)}, f16[4,2,32,512]{3,2,1,0:T(8,128)(2,1)S(1)}, u32[]{:S(2)}, u32[]{:S(2)}) collective-permute-start(f16[4,2,32,512]{3,2,1,0:T(8,128)(2,1)S(1)} %bitcast_dynamic-update-slice_fusion), channel_id=1, source_target_pairs={{0,5},{1,4},{4,1},{5,0},{8,13},{9,12},{12,9},{13,8},{16,21},{17,20... | collective-permute-start | bytes 786440 | tf_op jit(solution)/shard_map/ppermute | solution.py:144
  36.9 13.6 %collective-permute-start.8 = (bf16[256,512]{1,0:T(8,128)(2,1)S(1)}, bf16[256,512]{1,0:T(8,128)(2,1)S(1)}, u32[]{:S(2)}, u32[]{:S(2)}) collective-permute-start(bf16[256,512]{1,0:T(8,128)(2,1)S(1)} %chosen.1), channel_id=1, source_target_pairs={{0,4},{4,8},{8,12},{12,16},{16,20},{20,24},{24,28},{1,5},{5,9},{9,... | collective-permute-start | bytes 786440 | tf_op jit(solution)/shard_map/ppermute | solution.py:38
  41.0 11.4 %collective-permute-start.7 = (bf16[256,512]{1,0:T(8,128)(2,1)S(1)}, bf16[256,512]{1,0:T(8,128)(2,1)S(1)}, u32[]{:S(2)}, u32[]{:S(2)}) collective-permute-start(bf16[256,512]{1,0:T(8,128)(2,1)S(1)} %collective-permute-done.6.two_ref.refs_9_), channel_id=1, source_target_pairs={{0,8},{4,12},{8,16},{12,20},{16,24},{20,28},{1,9},{5,13},{9,17},{1... | collective-permute-start | bytes 786440 | tf_op jit(solution)/shard_map/ppermute | solution.py:38
  47.2 5.2 %copy-start.3 = (f32[1,256,512]{2,1,0:T(8,128)S(1)}, f32[1,256,512]{2,1,0:T(8,128)}, u32[]{:S(2)}) copy-start(f32[1,256,512]{2,1,0:T(8,128)} %param.12) | copy-start | bytes 1572868
  48.3 4.1 %copy-start.5 = (s32[2]{0:T(128)S(1)}, s32[2]{0:T(128)}, u32[]{:S(2)}) copy-start(s32[2]{0:T(128)} %refs_5_.1) | copy-start | bytes 28
  56.5 7.7 %collective-permute-start.10 = (f16[264,512]{1,0:T(8,128)(2,1)S(1)}, f16[264,512]{1,0:T(8,128)(2,1)S(1)}, u32[]{:S(2)}, u32[]{:S(2)}) collective-permute-start(f16[264,512]{1,0:T(8,128)(2,1)S(1)} %convert_element_type.26), channel_id=1, source_target_pairs={{0,1},{1,0},{2,3},{3,2},{4,5},{5,4},{6,7},{7,6},{8,9},{9,8},{10,11... | collective-permute-start | bytes 811016 | tf_op jit(solution)/shard_map/ppermute | solution.py:308

commit v4 on v3

--- a/solution.py
+++ b/solution.py
@@ -5,6 +5,7 @@
 from jax.experimental.pallas import tpu as pltpu
 from jax.sharding import PartitionSpec as P
 
+
 SHIFTS = 4
 FREQS = 2
 EXTRA = 8
@@ -14,8 +15,13 @@
 in_vmem = pl.BlockSpec(memory_space=pltpu.VMEM)
 in_smem = pl.BlockSpec(memory_space=pltpu.SMEM)
 in_place = pl.BlockSpec(memory_space=pl.ANY)
+in_hbm = pl.BlockSpec(memory_space=pltpu.HBM)
 small = pltpu.CompilerParams(vmem_limit_bytes=6 << 20)
 large = pltpu.CompilerParams(vmem_limit_bytes=16 << 20)
+
+
+def held(value):
+    return pltpu.with_memory_space_constraint(value, pltpu.HBM)
 
 
 def halves(value):
@@ -38,18 +44,33 @@
     return lax.ppermute(block, axis, route)
 
 
-def prepare_kernel(weight_ref, block_ref, out_ref):
+def prepare_kernel(weight_ref, block_ref, out_ref, tail, block_sem, tail_sem):
     energies, padded, width = out_ref.shape
     share = padded - EXTRA
+    copies = [
+        pltpu.make_async_copy(
+            block_ref.at[pl.ds(k * share, share), :], out_ref.at[k, pl.ds(0, share), :],
+            block_sem.at[k],
+        )
+        for k in range(energies)
+    ]
+    for copy in copies:
+        copy.start()
     weight = jnp.full((EXTRA, width), weight_ref[0], jnp.float32)
     first = weight.astype(jnp.bfloat16).astype(jnp.float32)
     second = (weight - first).astype(jnp.bfloat16).astype(jnp.float32)
     third = weight - first - second
     row = lax.broadcasted_iota(jnp.int32, (EXTRA, width), 0)
-    tail = jnp.where(row == 0, first, jnp.where(row == 1, second, third)).astype(jnp.bfloat16)
-    for k in range(energies):
-        out_ref[k, :share, :] = block_ref[k * share:(k + 1) * share, :]
-        out_ref[k, share:, :] = tail
+    parts = jnp.where(row == 0, first, jnp.where(row == 1, second, third))
+    tail[...] = parts.astype(jnp.bfloat16)
+    tails = [
+        pltpu.make_async_copy(tail, out_ref.at[k, pl.ds(share, EXTRA), :], tail_sem.at[k])
+        for k in range(energies)
+    ]
+    for copy in tails:
+        copy.start()
+    for copy in copies + tails:
+        copy.wait()
 
 
 def polar_kernel(offsets_ref, got_ref, bare_ref, out_ref, padded, bare_rows, arrived):
@@ -81,11 +102,16 @@
     sent = pl.pallas_call(
         prepare_kernel,
         out_shape=jax.ShapeDtypeStruct((energies, share + EXTRA, width), green.dtype),
-        in_specs=[in_smem, in_vmem],
-        out_specs=in_vmem,
+        in_specs=[in_smem, in_hbm],
+        out_specs=in_hbm,
+        scratch_shapes=[
+            VMEM((EXTRA, width), green.dtype),
+            pltpu.SemaphoreType.DMA((energies,)),
+            pltpu.SemaphoreType.DMA((energies,)),
+        ],
         compiler_params=small,
         name="prepare",
-    )(weight, green)
+    )(weight, held(green))
     got = lax.all_to_all(sent, "energy", 0, 0, tiled=True)
     return pl.pallas_call(
         polar_kernel,
@@ -125,7 +151,7 @@
     here = lax.axis_index("energy") // 2
     whole = jnp.zeros((outer,) + chunk.shape, chunk.dtype)
     whole = lax.dynamic_update_index_in_dim(whole, chunk, here, 0)
-    for k in range(1, outer):
+    for k in range(outer - 1, 0, -1):
         route = [(z * 2 + x, (z + k) % outer * 2 + x) for z in range(outer) for x in range(2)]
         got = lax.ppermute(chunk, "energy", route)
         whole = lax.dynamic_update_index_in_dim(whole, got, (here - k) % outer, 0)
@@ -137,12 +163,10 @@
     swap = [(e, e ^ 1) for e in range(energies)]
     turn = [(0, 1), (1, 0)]
     cross = [(e * 2 + r, (e ^ 1) * 2 + 1 - r) for e in range(energies) for r in range(2)]
-    return [
-        part,
-        lax.ppermute(part, "energy", swap),
-        lax.ppermute(part, "rep", turn),
-        lax.ppermute(part, ("energy", "rep"), cross),
-    ]
+    apart = lax.ppermute(part, ("energy", "rep"), cross)
+    beside = lax.ppermute(part, "energy", swap)
+    above = lax.ppermute(part, "rep", turn)
+    return [part, beside, above, apart]
 
 
 def gathered(chunk):
@@ -292,7 +316,7 @@
 
     two = shifted(green, "energy", 2)
     four = shifted(two, "energy", 2)
-    odd = shifted(chosen(offsets, two, green), "energy", 1)
+    odd = shifted(chosen(offsets, (screen_steps, green_steps, onsite_level), two, green), "energy", 1)
 
     slabs = lax.axis_size("slab")
     if slabs == 2:
@@ -317,7 +341,7 @@
     return green_next[None, None], screened[:, None]
 
 
-def chosen_kernel(offsets_ref, two_ref, green_ref, out_ref):
+def chosen_kernel(offsets_ref, screen_ref, green_steps_ref, level_ref, two_ref, green_ref, out_ref):
     three = jnp.minimum(offsets_ref[0], offsets_ref[1]) == 3
 
     @pl.when(three)
@@ -329,15 +353,15 @@
         out_ref[...] = green_ref[...]
 
 
-def chosen(offsets, two, green):
+def chosen(offsets, scalars, two, green):
     return pl.pallas_call(
         chosen_kernel,
         out_shape=jax.ShapeDtypeStruct(green.shape, green.dtype),
-        in_specs=[in_smem, in_vmem, in_vmem],
+        in_specs=[in_smem] * 4 + [in_vmem] * 2,
         out_specs=in_vmem,
         compiler_params=small,
         name="chosen",
-    )(offsets, two, green)
+    )(offsets, *scalars, two, green)
 
 
 def solution(mesh):

time: 66.5 us -> 76 us (1.14)
  Pallas kernels: 8.07 us -> 16.5 us
    pallas_call x1, Pallas kernels: 0.75 us -> 9.2 us  [polar_share(): pl.pallas_call(prepare_kernel, out_shape=jax.ShapeDtypeStruct((energies,...]
    ppermute x3, waiting for transfers between devices: 8.38 us -> 6.78 us  [gather_energy(): got = lax.ppermute(chunk, 'energy', route)]
    ppermute x3, waiting for transfers between devices: 7.9 us -> 8.88 us  [the longest x1 4.17 us: gather_square(): beside = lax.ppermute(part, 'energy', swap)]
where the time goes in v4:
time: 76 us; the launch traced here: 74.9 us
  waiting for transfers between devices  34 us (45%)
  starting transfers between devices  20.2 us (27%)
  Pallas kernels  16.5 us (22%)
  between operations  2.84 us (4%)
  local copies, waits for them, and re-layouts  0.92 us (1%)
    pallas_call x1, Pallas kernels, polar_share(): pl.pallas_call(prepare_kernel, out_shape=jax.ShapeDtypeStruct((energies,...  9.2 us
    all_to_all x1, waiting for transfers between devices, polar_share(): got = lax.all_to_all(sent, 'energy', 0, 0, tiled=True)  7.92 us
    ppermute x3, waiting for transfers between devices, gather_energy(): got = lax.ppermute(chunk, 'energy', route)  6.78 us
    all_to_all x1, starting transfers between devices, polar_share(): got = lax.all_to_all(sent, 'energy', 0, 0, tiled=True)  6.01 us
    ppermute x1, waiting for transfers between devices, body(): lax.ppermute(packed.astype(coded), 'rep', [(0, 1), (1, 0)])  6 us
    ppermute x3, starting transfers between devices, gather_energy(): got = lax.ppermute(chunk, 'energy', route)  5.13 us
    ppermute x3, waiting for transfers between devices, shifted(): return lax.ppermute(block, axis, route)  4.46 us
    ppermute x1, waiting for transfers between devices, gather_square(): beside = lax.ppermute(part, 'energy', swap)  4.17 us
  transfers between devices with their start and end apart: 12, of which 8 were waited for; matrix products, arithmetic and copies ran while one was open for 0% of the time, Pallas kernels for 1%

profile of v4, /device:TPU:26, one launch (start us, length us, event | category | flops | bytes accessed | tf_op | source)
XLA Modules:
  0.0 74.9 jit_solution(5745157903158464407)
XLA Ops:
  1.3 0.0 copy-start
  1.3 9.2 %prepare.1 = bf16[8,40,512]{2,1,0:T(8,128)(2,1)} custom-call(f32[1]{0:T(128)S(6)} %copy.15.weight_ref, bf16[256,512]{1,0:T(8,128)(2,1)} %bitcast.17), custom_call_target="tpu_custom_call" | custom-call | tf_op jit(solution)/shard_map/prepare/pallas_call | solution.py:102
  10.5 6.0 %all-to-all-start = ((bf16[8,40,512]{2,1,0:T(8,128)(2,1)}), bf16[8,40,512]{2,1,0:T(8,128)(2,1)S(1)}, u32[]{:S(2)}, u32[]{:S(2)}) async-start(bf16[8,40,512]{2,1,0:T(8,128)(2,1)} %prepare.1), calls=%async_computation | async-start | bytes 655360 | tf_op jit(solution)/shard_map/all_to_all | solution.py:115
  16.5 0.0 copy-start.3
  16.5 7.9 %all-to-all-done.got_ref = bf16[8,40,512]{2,1,0:T(8,128)(2,1)S(1)} async-done(((bf16[8,40,512]{2,1,0:T(8,128)(2,1)}), bf16[8,40,512]{2,1,0:T(8,128)(2,1)S(1)}, u32[]{:S(2)}, u32[]{:S(2)}) %all-to-all-start) | async-done | bytes 327712 | tf_op jit(solution)/shard_map/all_to_all | solution.py:115
  24.4 0.0 copy-done
  24.4 0.0 copy-done.3
  24.4 0.8 %polar.1 = f32[2,32,512]{2,1,0:T(8,128)S(1)} custom-call(s32[2]{0:T(128)S(1)} %copy-done.3, bf16[8,40,512]{2,1,0:T(8,128)(2,1)S(1)} %all-to-all-done.got_ref, f32[256,512]{1,0:T(8,128)S(1)} %bitcast.15), custom_call_target="tpu_custom_call" | custom-call | tf_op jit(solution)/shard_map/polar/pallas_call | solution.py:116
  25.3 0.0 copy-start.1
  25.3 0.1 collective-permute-start
  25.4 0.8 %copy-done.1 = bf16[1,1,256,512]{3,2,1,0:T(8,128)(2,1)S(1)} copy-done((bf16[1,1,256,512]{3,2,1,0:T(8,128)(2,1)S(1)}, bf16[1,1,256,512]{3,2,1,0:T(8,128)(2,1)}, u32[]{:S(2)}) %copy-start.1) | copy-done | bytes 262168
  26.2 1.3 %collective-permute-start.6 = (bf16[256,512]{1,0:T(8,128)(2,1)S(1)}, bf16[256,512]{1,0:T(8,128)(2,1)S(1)}, u32[]{:S(2)}, u32[]{:S(2)}) collective-permute-start(bf16[256,512]{1,0:T(8,128)(2,1)S(1)} %bitcast.18), channel_id=1, source_target_pairs={{0,8},{4,12},{8,16},{12,20},{16,24},{20,28},{1,9},{5,13},{9,17},{1... | collective-permute-start | bytes 786440 | tf_op jit(solution)/shard_map/ppermute | solution.py:44
  27.6 2.8 %collective-permute-start.1 = (f16[2,32,512]{2,1,0:T(8,128)(2,1)S(1)}, f16[2,32,512]{2,1,0:T(8,128)(2,1)S(1)}, u32[]{:S(2)}, u32[]{:S(2)}) collective-permute-start(f16[2,32,512]{2,1,0:T(8,128)(2,1)S(1)} %get-tuple-element.13), channel_id=1, source_target_pairs={{0,16},{4,20},{8,24},{12,28},{16,0},{20,4},{24,8},{28,12},{1,17},{... | collective-permute-start | bytes 196616 | tf_op jit(solution)/shard_map/ppermute | solution.py:156
  30.3 2.3 %collective-permute-start.2 = (f16[2,32,512]{2,1,0:T(8,128)(2,1)S(1)}, f16[2,32,512]{2,1,0:T(8,128)(2,1)S(1)}, u32[]{:S(2)}, u32[]{:S(2)}) collective-permute-start(f16[2,32,512]{2,1,0:T(8,128)(2,1)S(1)} %get-tuple-element.13), channel_id=1, source_target_pairs={{0,8},{4,12},{8,16},{12,20},{16,24},{20,28},{24,0},{28,4},{1,9},{5... | collective-permute-start | bytes 196616 | tf_op jit(solution)/shard_map/ppermute | solution.py:156
  32.6 0.0 collective-permute-done
  32.7 6.8 %collective-permute-done.1 = f16[2,32,512]{2,1,0:T(8,128)(2,1)S(1)} collective-permute-done((f16[2,32,512]{2,1,0:T(8,128)(2,1)S(1)}, f16[2,32,512]{2,1,0:T(8,128)(2,1)S(1)}, u32[]{:S(2)}, u32[]{:S(2)}) %collective-permute-start.1) | collective-permute-done | bytes 65568 | tf_op jit(solution)/shard_map/ppermute | solution.py:156
  39.5 0.0 collective-permute-done.2
  39.5 2.1 %collective-permute-start.5 = (f16[4,2,32,512]{3,2,1,0:T(8,128)(2,1)S(1)}, f16[4,2,32,512]{3,2,1,0:T(8,128)(2,1)S(1)}, u32[]{:S(2)}, u32[]{:S(2)}) collective-permute-start(f16[4,2,32,512]{3,2,1,0:T(8,128)(2,1)S(1)} %bitcast_dynamic-update-slice_fusion), channel_id=1, source_target_pairs={{0,5},{1,4},{4,1},{5,0},{8,13},{9,12},{12,9},{13,8},{16,21},{17,20... | collective-permute-start | bytes 786440 | tf_op jit(solution)/shard_map/ppermute | solution.py:166
  41.6 0.0 collective-permute-start.9
  42.2 0.0 copy-start.4
  42.9 0.6 collective-permute-start.4
  43.5 1.0 %collective-permute-start.3 = (f16[4,2,32,512]{3,2,1,0:T(8,128)(2,1)S(1)}, f16[4,2,32,512]{3,2,1,0:T(8,128)(2,1)S(1)}, u32[]{:S(2)}, u32[]{:S(2)}) collective-permute-start(f16[4,2,32,512]{3,2,1,0:T(8,128)(2,1)S(1)} %bitcast_dynamic-update-slice_fusion), channel_id=1, source_target_pairs={{0,4},{4,0},{8,12},{12,8},{16,20},{20,16},{24,28},{28,24},{1,5},{5... | collective-permute-start | bytes 786440 | tf_op jit(solution)/shard_map/ppermute | solution.py:167
  44.4 0.0 collective-permute-done.6.two_ref.refs_9_
  44.4 0.0 copy-done.4
  44.4 0.6 chosen.1
  45.0 1.3 %collective-permute-start.8 = (bf16[256,512]{1,0:T(8,128)(2,1)S(1)}, bf16[256,512]{1,0:T(8,128)(2,1)S(1)}, u32[]{:S(2)}, u32[]{:S(2)}) collective-permute-start(bf16[256,512]{1,0:T(8,128)(2,1)S(1)} %chosen.1), channel_id=1, source_target_pairs={{0,4},{4,8},{8,12},{12,16},{16,20},{20,24},{24,28},{1,5},{5,9},{9,... | collective-permute-start | bytes 786440 | tf_op jit(solution)/shard_map/ppermute | solution.py:44
  46.3 0.6 collective-permute-done.5
  46.9 1.3 %collective-permute-start.7 = (bf16[256,512]{1,0:T(8,128)(2,1)S(1)}, bf16[256,512]{1,0:T(8,128)(2,1)S(1)}, u32[]{:S(2)}, u32[]{:S(2)}) collective-permute-start(bf16[256,512]{1,0:T(8,128)(2,1)S(1)} %collective-permute-done.6.two_ref.refs_9_), channel_id=1, source_target_pairs={{0,8},{4,12},{8,16},{12,20},{16,24},{20,28},{1,9},{5,13},{9,17},{1... | collective-permute-start | bytes 786440 | tf_op jit(solution)/shard_map/ppermute | solution.py:44
  48.2 0.1 convert_element_type.22.refs_0_
  48.3 0.1 convert_element_type.25.refs_3_
  48.3 4.1 %collective-permute-done.4 = f16[4,2,32,512]{3,2,1,0:T(8,128)(2,1)S(1)} collective-permute-done((f16[4,2,32,512]{3,2,1,0:T(8,128)(2,1)S(1)}, f16[4,2,32,512]{3,2,1,0:T(8,128)(2,1)S(1)}, u32[]{:S(2)}, u32[]{:S(2)}) %collective-permute-start.4) | collective-permute-done | bytes 262176 | tf_op jit(solution)/shard_map/ppermute | solution.py:168
  52.4 0.1 convert_element_type.24.refs_2_
  52.5 0.0 copy-start.2
  52.5 4.2 %collective-permute-done.3 = f16[4,2,32,512]{3,2,1,0:T(8,128)(2,1)S(1)} collective-permute-done((f16[4,2,32,512]{3,2,1,0:T(8,128)(2,1)S(1)}, f16[4,2,32,512]{3,2,1,0:T(8,128)(2,1)S(1)}, u32[]{:S(2)}, u32[]{:S(2)}) %collective-permute-start.3) | collective-permute-done | bytes 262176 | tf_op jit(solution)/shard_map/ppermute | solution.py:167
  56.7 0.1 convert_element_type.23.refs_1_
  56.7 0.0 collective-permute-done.9.refs_12_
  56.8 1.4 %collective-permute-done.8.refs_11_ = bf16[256,512]{1,0:T(8,128)(2,1)S(1)} collective-permute-done((bf16[256,512]{1,0:T(8,128)(2,1)S(1)}, bf16[256,512]{1,0:T(8,128)(2,1)S(1)}, u32[]{:S(2)}, u32[]{:S(2)}) %collective-permute-start.8) | collective-permute-done | bytes 262176 | tf_op jit(solution)/shard_map/ppermute | solution.py:44
  58.1 3.1 %collective-permute-done.7.refs_10_ = bf16[256,512]{1,0:T(8,128)(2,1)S(1)} collective-permute-done((bf16[256,512]{1,0:T(8,128)(2,1)S(1)}, bf16[256,512]{1,0:T(8,128)(2,1)S(1)}, u32[]{:S(2)}, u32[]{:S(2)}) %collective-permute-start.7) | collective-permute-done | bytes 262176 | tf_op jit(solution)/shard_map/ppermute | solution.py:44
  61.2 0.0 copy-done.2
  61.2 4.0 %dyson.1 = (bf16[2,256,512]{2,1,0:T(8,128)(2,1)}, f32[264,512]{1,0:T(8,128)S(1)}, f32[256,512]{1,0:T(8,128)S(1)}, f32[8,512]{1,0:T(8,128)S(1)}) custom-call(f32[4,2,32,512]{3,2,1,0:T(8,128)S(1)} %convert_element_type.22.refs_0_, f32[4,2,32,512]{3,2,1,0:T(8,128)S(1)} %convert_element_type.23.refs_1_, f32[4,2,32,512]{3,2,1,0:T(8,128)S(1)} %convert_element_type.24.refs_2_, ...), custom_call_target="tpu_custom_call" | custom-call | tf_op jit(solution)/shard_map/dyson/pallas_call | solution.py:265
  65.3 1.6 %collective-permute-start.10 = (f16[264,512]{1,0:T(8,128)(2,1)S(1)}, f16[264,512]{1,0:T(8,128)(2,1)S(1)}, u32[]{:S(2)}, u32[]{:S(2)}) collective-permute-start(f16[264,512]{1,0:T(8,128)(2,1)S(1)} %convert_element_type.26), channel_id=1, source_target_pairs={{0,1},{1,0},{2,3},{3,2},{4,5},{5,4},{6,7},{7,6},{8,9},{9,8},{10,11... | collective-permute-start | bytes 811016 | tf_op jit(solution)/shard_map/ppermute | solution.py:332
  66.9 6.0 %collective-permute-done.10 = f16[264,512]{1,0:T(8,128)(2,1)S(1)} collective-permute-done((f16[264,512]{1,0:T(8,128)(2,1)S(1)}, f16[264,512]{1,0:T(8,128)(2,1)S(1)}, u32[]{:S(2)}, u32[]{:S(2)}) %collective-permute-start.10) | collective-permute-done | bytes 270368 | tf_op jit(solution)/shard_map/ppermute | solution.py:332
  72.8 0.1 convert_element_type.27.theirs_ref
  72.9 2.0 %finish.1 = f32[256,512]{1,0:T(8,128)} custom-call(s32[1]{0:T(128)S(6)} %copy.17.green_steps_ref.steps_ref, f32[256,512]{1,0:T(8,128)S(1)} %get-tuple-element.6.step_ref, f32[264,512]{1,0:T(8,128)S(1)} %get-tuple-element.7.packed_ref, f32[264,512]{1,0:T(8,128)S(1)} %convert_element_type.27.theirs_ref, f32[8,512]{1,0:T(8,128)S(1)} %get-tuple-element.8.own_ref), custom_call_target="tpu_custom_call" | custom-call | tf_op jit(solution)/shard_map/finish/pallas_call | solution.py:333
  (6 shorter events, 0.1 us)
Async XLA Ops:
  1.3 23.1 %copy-start = (f32[1,256,512]{2,1,0:T(8,128)S(1)}, f32[1,256,512]{2,1,0:T(8,128)}, u32[]{:S(2)}) copy-start(f32[1,256,512]{2,1,0:T(8,128)} %param.11) | copy-start | bytes 1572868
  10.5 13.9 %all-to-all-start = ((bf16[8,40,512]{2,1,0:T(8,128)(2,1)}), bf16[8,40,512]{2,1,0:T(8,128)(2,1)S(1)}, u32[]{:S(2)}, u32[]{:S(2)}) async-start(bf16[8,40,512]{2,1,0:T(8,128)(2,1)} %prepare.1), calls=%async_computation | async-start | bytes 655360 | tf_op jit(solution)/shard_map/all_to_all | solution.py:115
  16.5 7.9 %copy-start.3 = (s32[2]{0:T(128)S(1)}, s32[2]{0:T(128)}, u32[]{:S(2)}) copy-start(s32[2]{0:T(128)} %refs_4_.1) | copy-start | bytes 28
  25.3 1.0 %copy-start.1 = (bf16[1,1,256,512]{3,2,1,0:T(8,128)(2,1)S(1)}, bf16[1,1,256,512]{3,2,1,0:T(8,128)(2,1)}, u32[]{:S(2)}) copy-start(bf16[1,1,256,512]{3,2,1,0:T(8,128)(2,1)} %param.8) | copy-start | bytes 786436
  25.3 7.3 %collective-permute-start = (f16[2,32,512]{2,1,0:T(8,128)(2,1)S(1)}, f16[2,32,512]{2,1,0:T(8,128)(2,1)S(1)}, u32[]{:S(2)}, u32[]{:S(2)}) collective-permute-start(f16[2,32,512]{2,1,0:T(8,128)(2,1)S(1)} %get-tuple-element.13), channel_id=1, source_target_pairs={{0,24},{4,28},{8,0},{12,4},{16,8},{20,12},{24,16},{28,20},{1,25},{... | collective-permute-start | bytes 196616 | tf_op jit(solution)/shard_map/ppermute | solution.py:156
  26.2 18.2 %collective-permute-start.6 = (bf16[256,512]{1,0:T(8,128)(2,1)S(1)}, bf16[256,512]{1,0:T(8,128)(2,1)S(1)}, u32[]{:S(2)}, u32[]{:S(2)}) collective-permute-start(bf16[256,512]{1,0:T(8,128)(2,1)S(1)} %bitcast.18), channel_id=1, source_target_pairs={{0,8},{4,12},{8,16},{12,20},{16,24},{20,28},{1,9},{5,13},{9,17},{1... | collective-permute-start | bytes 786440 | tf_op jit(solution)/shard_map/ppermute | solution.py:44
  27.6 11.9 %collective-permute-start.1 = (f16[2,32,512]{2,1,0:T(8,128)(2,1)S(1)}, f16[2,32,512]{2,1,0:T(8,128)(2,1)S(1)}, u32[]{:S(2)}, u32[]{:S(2)}) collective-permute-start(f16[2,32,512]{2,1,0:T(8,128)(2,1)S(1)} %get-tuple-element.13), channel_id=1, source_target_pairs={{0,16},{4,20},{8,24},{12,28},{16,0},{20,4},{24,8},{28,12},{1,17},{... | collective-permute-start | bytes 196616 | tf_op jit(solution)/shard_map/ppermute | solution.py:156
  30.3 9.1 %collective-permute-start.2 = (f16[2,32,512]{2,1,0:T(8,128)(2,1)S(1)}, f16[2,32,512]{2,1,0:T(8,128)(2,1)S(1)}, u32[]{:S(2)}, u32[]{:S(2)}) collective-permute-start(f16[2,32,512]{2,1,0:T(8,128)(2,1)S(1)} %get-tuple-element.13), channel_id=1, source_target_pairs={{0,8},{4,12},{8,16},{12,20},{16,24},{20,28},{24,0},{28,4},{1,9},{5... | collective-permute-start | bytes 196616 | tf_op jit(solution)/shard_map/ppermute | solution.py:156
  39.5 7.4 %collective-permute-start.5 = (f16[4,2,32,512]{3,2,1,0:T(8,128)(2,1)S(1)}, f16[4,2,32,512]{3,2,1,0:T(8,128)(2,1)S(1)}, u32[]{:S(2)}, u32[]{:S(2)}) collective-permute-start(f16[4,2,32,512]{3,2,1,0:T(8,128)(2,1)S(1)} %bitcast_dynamic-update-slice_fusion), channel_id=1, source_target_pairs={{0,5},{1,4},{4,1},{5,0},{8,13},{9,12},{12,9},{13,8},{16,21},{17,20... | collective-permute-start | bytes 786440 | tf_op jit(solution)/shard_map/ppermute | solution.py:166
  41.6 15.2 %collective-permute-start.9 = (bf16[256,512]{1,0:T(8,128)(2,1)S(1)}, bf16[256,512]{1,0:T(8,128)(2,1)S(1)}, u32[]{:S(2)}, u32[]{:S(2)}) collective-permute-start(bf16[256,512]{1,0:T(8,128)(2,1)S(1)} %bitcast.19), channel_id=1, source_target_pairs={{0,2},{2,0},{1,3},{3,1},{4,6},{6,4},{5,7},{7,5},{8,10},{10,8},{9,1... | collective-permute-start | bytes 786440 | tf_op jit(solution)/shard_map/ppermute | solution.py:323
  42.2 2.2 %copy-start.4 = (s32[2]{0:T(128)S(1)}, s32[2]{0:T(128)}, u32[]{:S(2)}) copy-start(s32[2]{0:T(128)} %refs_5_.1) | copy-start | bytes 28
  42.9 9.6 %collective-permute-start.4 = (f16[4,2,32,512]{3,2,1,0:T(8,128)(2,1)S(1)}, f16[4,2,32,512]{3,2,1,0:T(8,128)(2,1)S(1)}, u32[]{:S(2)}, u32[]{:S(2)}) collective-permute-start(f16[4,2,32,512]{3,2,1,0:T(8,128)(2,1)S(1)} %bitcast_dynamic-update-slice_fusion), channel_id=1, source_target_pairs={{0,1},{1,0},{2,3},{3,2},{4,5},{5,4},{6,7},{7,6},{8,9},{9,8},{10,11... | collective-permute-start | bytes 786440 | tf_op jit(solution)/shard_map/ppermute | solution.py:168
  43.5 13.2 %collective-permute-start.3 = (f16[4,2,32,512]{3,2,1,0:T(8,128)(2,1)S(1)}, f16[4,2,32,512]{3,2,1,0:T(8,128)(2,1)S(1)}, u32[]{:S(2)}, u32[]{:S(2)}) collective-permute-start(f16[4,2,32,512]{3,2,1,0:T(8,128)(2,1)S(1)} %bitcast_dynamic-update-slice_fusion), channel_id=1, source_target_pairs={{0,4},{4,0},{8,12},{12,8},{16,20},{20,16},{24,28},{28,24},{1,5},{5... | collective-permute-start | bytes 786440 | tf_op jit(solution)/shard_map/ppermute | solution.py:167
  45.0 13.1 %collective-permute-start.8 = (bf16[256,512]{1,0:T(8,128)(2,1)S(1)}, bf16[256,512]{1,0:T(8,128)(2,1)S(1)}, u32[]{:S(2)}, u32[]{:S(2)}) collective-permute-start(bf16[256,512]{1,0:T(8,128)(2,1)S(1)} %chosen.1), channel_id=1, source_target_pairs={{0,4},{4,8},{8,12},{12,16},{16,20},{20,24},{24,28},{1,5},{5,9},{9,... | collective-permute-start | bytes 786440 | tf_op jit(solution)/shard_map/ppermute | solution.py:44
  46.9 14.3 %collective-permute-start.7 = (bf16[256,512]{1,0:T(8,128)(2,1)S(1)}, bf16[256,512]{1,0:T(8,128)(2,1)S(1)}, u32[]{:S(2)}, u32[]{:S(2)}) collective-permute-start(bf16[256,512]{1,0:T(8,128)(2,1)S(1)} %collective-permute-done.6.two_ref.refs_9_), channel_id=1, source_target_pairs={{0,8},{4,12},{8,16},{12,20},{16,24},{20,28},{1,9},{5,13},{9,17},{1... | collective-permute-start | bytes 786440 | tf_op jit(solution)/shard_map/ppermute | solution.py:44
  52.5 8.7 %copy-start.2 = (f32[1,256,512]{2,1,0:T(8,128)S(1)}, f32[1,256,512]{2,1,0:T(8,128)}, u32[]{:S(2)}) copy-start(f32[1,256,512]{2,1,0:T(8,128)} %param.12) | copy-start | bytes 1572868
  65.3 7.6 %collective-permute-start.10 = (f16[264,512]{1,0:T(8,128)(2,1)S(1)}, f16[264,512]{1,0:T(8,128)(2,1)S(1)}, u32[]{:S(2)}, u32[]{:S(2)}) collective-permute-start(f16[264,512]{1,0:T(8,128)(2,1)S(1)} %convert_element_type.26), channel_id=1, source_target_pairs={{0,1},{1,0},{2,3},{3,2},{4,5},{5,4},{6,7},{7,6},{8,9},{9,8},{10,11... | collective-permute-start | bytes 811016 | tf_op jit(solution)/shard_map/ppermute | solution.py:332

commit v5 on v3

--- a/solution.py
+++ b/solution.py
@@ -4,6 +4,7 @@
 from jax.experimental import pallas as pl
 from jax.experimental.pallas import tpu as pltpu
 from jax.sharding import PartitionSpec as P
+
 
 SHIFTS = 4
 FREQS = 2
@@ -125,7 +126,7 @@
     here = lax.axis_index("energy") // 2
     whole = jnp.zeros((outer,) + chunk.shape, chunk.dtype)
     whole = lax.dynamic_update_index_in_dim(whole, chunk, here, 0)
-    for k in range(1, outer):
+    for k in range(outer - 1, 0, -1):
         route = [(z * 2 + x, (z + k) % outer * 2 + x) for z in range(outer) for x in range(2)]
         got = lax.ppermute(chunk, "energy", route)
         whole = lax.dynamic_update_index_in_dim(whole, got, (here - k) % outer, 0)
@@ -137,12 +138,10 @@
     swap = [(e, e ^ 1) for e in range(energies)]
     turn = [(0, 1), (1, 0)]
     cross = [(e * 2 + r, (e ^ 1) * 2 + 1 - r) for e in range(energies) for r in range(2)]
-    return [
-        part,
-        lax.ppermute(part, "energy", swap),
-        lax.ppermute(part, "rep", turn),
-        lax.ppermute(part, ("energy", "rep"), cross),
-    ]
+    apart = lax.ppermute(part, ("energy", "rep"), cross)
+    beside = lax.ppermute(part, "energy", swap)
+    above = lax.ppermute(part, "rep", turn)
+    return [part, beside, above, apart]
 
 
 def gathered(chunk):
@@ -292,7 +291,7 @@
 
     two = shifted(green, "energy", 2)
     four = shifted(two, "energy", 2)
-    odd = shifted(chosen(offsets, two, green), "energy", 1)
+    odd = shifted(chosen(offsets, (screen_steps, green_steps, onsite_level), two, green), "energy", 1)
 
     slabs = lax.axis_size("slab")
     if slabs == 2:
@@ -317,7 +316,7 @@
     return green_next[None, None], screened[:, None]
 
 
-def chosen_kernel(offsets_ref, two_ref, green_ref, out_ref):
+def chosen_kernel(offsets_ref, screen_ref, green_steps_ref, level_ref, two_ref, green_ref, out_ref):
     three = jnp.minimum(offsets_ref[0], offsets_ref[1]) == 3
 
     @pl.when(three)
@@ -329,15 +328,15 @@
         out_ref[...] = green_ref[...]
 
 
-def chosen(offsets, two, green):
+def chosen(offsets, scalars, two, green):
     return pl.pallas_call(
         chosen_kernel,
         out_shape=jax.ShapeDtypeStruct(green.shape, green.dtype),
-        in_specs=[in_smem, in_vmem, in_vmem],
+        in_specs=[in_smem] * 4 + [in_vmem] * 2,
         out_specs=in_vmem,
         compiler_params=small,
         name="chosen",
-    )(offsets, two, green)
+    )(offsets, *scalars, two, green)
 
 
 def solution(mesh):

time: 66.5 us -> 68.5 us (1.030); the launches traced: 66.1 us -> 67.3 us
  local copies, waits for them, and re-layouts: 1.04 us -> 1.86 us
    ppermute x3, waiting for transfers between devices: 8.38 us -> 6.78 us  [gather_energy(): got = lax.ppermute(chunk, 'energy', route)]
    ppermute x3, waiting for transfers between devices: 7.9 us -> 8.88 us  [the longest x1 4.17 us: gather_square(): beside = lax.ppermute(part, 'energy', swap)]
    unnamed x12, local copies, waits for them, and re-layouts: 0.97 us -> 1.79 us
where the time goes in v5:
time: 68.5 us; the launch traced here: 67.3 us
  waiting for transfers between devices  34 us (50%)
  starting transfers between devices  20.2 us (29%)
  Pallas kernels  8.09 us (12%)
  between operations  2.83 us (4%)
  local copies, waits for them, and re-layouts  1.86 us (3%)
    all_to_all x1, waiting for transfers between devices, polar_share(): got = lax.all_to_all(sent, 'energy', 0, 0, tiled=True)  7.92 us
    ppermute x3, waiting for transfers between devices, gather_energy(): got = lax.ppermute(chunk, 'energy', route)  6.78 us
    all_to_all x1, starting transfers between devices, polar_share(): got = lax.all_to_all(sent, 'energy', 0, 0, tiled=True)  6 us
    ppermute x1, waiting for transfers between devices, body(): lax.ppermute(packed.astype(coded), 'rep', [(0, 1), (1, 0)])  6 us
    ppermute x3, starting transfers between devices, gather_energy(): got = lax.ppermute(chunk, 'energy', route)  5.13 us
    ppermute x3, waiting for transfers between devices, shifted(): return lax.ppermute(block, axis, route)  4.46 us
    ppermute x1, waiting for transfers between devices, gather_square(): beside = lax.ppermute(part, 'energy', swap)  4.17 us
    ppermute x1, waiting for transfers between devices, gather_square(): above = lax.ppermute(part, 'rep', turn)  4.12 us
  transfers between devices with their start and end apart: 12, of which 8 were waited for; matrix products, arithmetic and copies ran while one was open for 0% of the time, Pallas kernels for 1%

profile of v5, /device:TPU:26, one launch (start us, length us, event | category | flops | bytes accessed | tf_op | source)
XLA Modules:
  0.0 67.3 jit_solution(17743380380575612519)
XLA Ops:
  1.3 0.0 copy-start.1
  1.3 0.9 %copy-done.1 = bf16[1,1,256,512]{3,2,1,0:T(8,128)(2,1)S(1)} copy-done((bf16[1,1,256,512]{3,2,1,0:T(8,128)(2,1)S(1)}, bf16[1,1,256,512]{3,2,1,0:T(8,128)(2,1)}, u32[]{:S(2)}) %copy-start.1) | copy-done | bytes 262168
  2.2 0.0 copy-start
  2.2 0.7 %prepare.1 = bf16[8,40,512]{2,1,0:T(8,128)(2,1)} custom-call(f32[1]{0:T(128)S(6)} %copy.15.weight_ref, bf16[256,512]{1,0:T(8,128)(2,1)S(1)} %bitcast.17), custom_call_target="tpu_custom_call" | custom-call | tf_op jit(solution)/shard_map/prepare/pallas_call | solution.py:82
  3.0 6.0 %all-to-all-start = ((bf16[8,40,512]{2,1,0:T(8,128)(2,1)}), bf16[8,40,512]{2,1,0:T(8,128)(2,1)S(1)}, u32[]{:S(2)}, u32[]{:S(2)}) async-start(bf16[8,40,512]{2,1,0:T(8,128)(2,1)} %prepare.1), calls=%async_computation | async-start | bytes 655360 | tf_op jit(solution)/shard_map/all_to_all | solution.py:90
  9.0 0.0 copy-start.4
  9.0 7.9 %all-to-all-done.got_ref = bf16[8,40,512]{2,1,0:T(8,128)(2,1)S(1)} async-done(((bf16[8,40,512]{2,1,0:T(8,128)(2,1)}), bf16[8,40,512]{2,1,0:T(8,128)(2,1)S(1)}, u32[]{:S(2)}, u32[]{:S(2)}) %all-to-all-start) | async-done | bytes 327712 | tf_op jit(solution)/shard_map/all_to_all | solution.py:90
  16.9 0.0 copy-done
  16.9 0.0 copy-done.4
  16.9 0.8 %polar.1 = f32[2,32,512]{2,1,0:T(8,128)S(1)} custom-call(s32[2]{0:T(128)S(1)} %copy-done.4, bf16[8,40,512]{2,1,0:T(8,128)(2,1)S(1)} %all-to-all-done.got_ref, f32[256,512]{1,0:T(8,128)S(1)} %bitcast.15), custom_call_target="tpu_custom_call" | custom-call | tf_op jit(solution)/shard_map/polar/pallas_call | solution.py:91
  17.7 0.0 copy-start.2
  17.8 0.1 collective-permute-start
  17.9 0.8 %copy-done.2 = bf16[1,1,256,512]{3,2,1,0:T(8,128)(2,1)S(1)} copy-done((bf16[1,1,256,512]{3,2,1,0:T(8,128)(2,1)S(1)}, bf16[1,1,256,512]{3,2,1,0:T(8,128)(2,1)}, u32[]{:S(2)}) %copy-start.2) | copy-done | bytes 262168
  18.7 1.3 %collective-permute-start.6 = (bf16[256,512]{1,0:T(8,128)(2,1)S(1)}, bf16[256,512]{1,0:T(8,128)(2,1)S(1)}, u32[]{:S(2)}, u32[]{:S(2)}) collective-permute-start(bf16[256,512]{1,0:T(8,128)(2,1)S(1)} %bitcast.18), channel_id=1, source_target_pairs={{0,8},{4,12},{8,16},{12,20},{16,24},{20,28},{1,9},{5,13},{9,17},{1... | collective-permute-start | bytes 786440 | tf_op jit(solution)/shard_map/ppermute | solution.py:39
  20.0 2.8 %collective-permute-start.1 = (f16[2,32,512]{2,1,0:T(8,128)(2,1)S(1)}, f16[2,32,512]{2,1,0:T(8,128)(2,1)S(1)}, u32[]{:S(2)}, u32[]{:S(2)}) collective-permute-start(f16[2,32,512]{2,1,0:T(8,128)(2,1)S(1)} %get-tuple-element.13), channel_id=1, source_target_pairs={{0,16},{4,20},{8,24},{12,28},{16,0},{20,4},{24,8},{28,12},{1,17},{... | collective-permute-start | bytes 196616 | tf_op jit(solution)/shard_map/ppermute | solution.py:131
  22.8 2.3 %collective-permute-start.2 = (f16[2,32,512]{2,1,0:T(8,128)(2,1)S(1)}, f16[2,32,512]{2,1,0:T(8,128)(2,1)S(1)}, u32[]{:S(2)}, u32[]{:S(2)}) collective-permute-start(f16[2,32,512]{2,1,0:T(8,128)(2,1)S(1)} %get-tuple-element.13), channel_id=1, source_target_pairs={{0,8},{4,12},{8,16},{12,20},{16,24},{20,28},{24,0},{28,4},{1,9},{5... | collective-permute-start | bytes 196616 | tf_op jit(solution)/shard_map/ppermute | solution.py:131
  25.1 0.0 collective-permute-done
  25.1 6.8 %collective-permute-done.1 = f16[2,32,512]{2,1,0:T(8,128)(2,1)S(1)} collective-permute-done((f16[2,32,512]{2,1,0:T(8,128)(2,1)S(1)}, f16[2,32,512]{2,1,0:T(8,128)(2,1)S(1)}, u32[]{:S(2)}, u32[]{:S(2)}) %collective-permute-start.1) | collective-permute-done | bytes 65568 | tf_op jit(solution)/shard_map/ppermute | solution.py:131
  31.9 0.0 collective-permute-done.2
  32.0 2.1 %collective-permute-start.5 = (f16[4,2,32,512]{3,2,1,0:T(8,128)(2,1)S(1)}, f16[4,2,32,512]{3,2,1,0:T(8,128)(2,1)S(1)}, u32[]{:S(2)}, u32[]{:S(2)}) collective-permute-start(f16[4,2,32,512]{3,2,1,0:T(8,128)(2,1)S(1)} %bitcast_dynamic-update-slice_fusion), channel_id=1, source_target_pairs={{0,5},{1,4},{4,1},{5,0},{8,13},{9,12},{12,9},{13,8},{16,21},{17,20... | collective-permute-start | bytes 786440 | tf_op jit(solution)/shard_map/ppermute | solution.py:141
  34.0 0.0 collective-permute-start.9
  34.7 0.0 copy-start.5
  35.4 0.6 collective-permute-start.4
  35.9 1.0 %collective-permute-start.3 = (f16[4,2,32,512]{3,2,1,0:T(8,128)(2,1)S(1)}, f16[4,2,32,512]{3,2,1,0:T(8,128)(2,1)S(1)}, u32[]{:S(2)}, u32[]{:S(2)}) collective-permute-start(f16[4,2,32,512]{3,2,1,0:T(8,128)(2,1)S(1)} %bitcast_dynamic-update-slice_fusion), channel_id=1, source_target_pairs={{0,4},{4,0},{8,12},{12,8},{16,20},{20,16},{24,28},{28,24},{1,5},{5... | collective-permute-start | bytes 786440 | tf_op jit(solution)/shard_map/ppermute | solution.py:142
  36.9 0.0 collective-permute-done.6.two_ref.refs_9_
  36.9 0.0 copy-done.5
  36.9 0.6 chosen.1
  37.5 1.3 %collective-permute-start.8 = (bf16[256,512]{1,0:T(8,128)(2,1)S(1)}, bf16[256,512]{1,0:T(8,128)(2,1)S(1)}, u32[]{:S(2)}, u32[]{:S(2)}) collective-permute-start(bf16[256,512]{1,0:T(8,128)(2,1)S(1)} %chosen.1), channel_id=1, source_target_pairs={{0,4},{4,8},{8,12},{12,16},{16,20},{20,24},{24,28},{1,5},{5,9},{9,... | collective-permute-start | bytes 786440 | tf_op jit(solution)/shard_map/ppermute | solution.py:39
  38.8 0.6 collective-permute-done.5
  39.4 1.3 %collective-permute-start.7 = (bf16[256,512]{1,0:T(8,128)(2,1)S(1)}, bf16[256,512]{1,0:T(8,128)(2,1)S(1)}, u32[]{:S(2)}, u32[]{:S(2)}) collective-permute-start(bf16[256,512]{1,0:T(8,128)(2,1)S(1)} %collective-permute-done.6.two_ref.refs_9_), channel_id=1, source_target_pairs={{0,8},{4,12},{8,16},{12,20},{16,24},{20,28},{1,9},{5,13},{9,17},{1... | collective-permute-start | bytes 786440 | tf_op jit(solution)/shard_map/ppermute | solution.py:39
  40.7 0.1 convert_element_type.22.refs_0_
  40.7 0.1 convert_element_type.25.refs_3_
  40.8 4.1 %collective-permute-done.4 = f16[4,2,32,512]{3,2,1,0:T(8,128)(2,1)S(1)} collective-permute-done((f16[4,2,32,512]{3,2,1,0:T(8,128)(2,1)S(1)}, f16[4,2,32,512]{3,2,1,0:T(8,128)(2,1)S(1)}, u32[]{:S(2)}, u32[]{:S(2)}) %collective-permute-start.4) | collective-permute-done | bytes 262176 | tf_op jit(solution)/shard_map/ppermute | solution.py:143
  44.9 0.1 convert_element_type.24.refs_2_
  45.0 0.0 copy-start.3
  45.0 4.2 %collective-permute-done.3 = f16[4,2,32,512]{3,2,1,0:T(8,128)(2,1)S(1)} collective-permute-done((f16[4,2,32,512]{3,2,1,0:T(8,128)(2,1)S(1)}, f16[4,2,32,512]{3,2,1,0:T(8,128)(2,1)S(1)}, u32[]{:S(2)}, u32[]{:S(2)}) %collective-permute-start.3) | collective-permute-done | bytes 262176 | tf_op jit(solution)/shard_map/ppermute | solution.py:142
  49.2 0.1 convert_element_type.23.refs_1_
  49.2 0.0 collective-permute-done.9.refs_12_
  49.2 1.4 %collective-permute-done.8.refs_11_ = bf16[256,512]{1,0:T(8,128)(2,1)S(1)} collective-permute-done((bf16[256,512]{1,0:T(8,128)(2,1)S(1)}, bf16[256,512]{1,0:T(8,128)(2,1)S(1)}, u32[]{:S(2)}, u32[]{:S(2)}) %collective-permute-start.8) | collective-permute-done | bytes 262176 | tf_op jit(solution)/shard_map/ppermute | solution.py:39
  50.6 3.1 %collective-permute-done.7.refs_10_ = bf16[256,512]{1,0:T(8,128)(2,1)S(1)} collective-permute-done((bf16[256,512]{1,0:T(8,128)(2,1)S(1)}, bf16[256,512]{1,0:T(8,128)(2,1)S(1)}, u32[]{:S(2)}, u32[]{:S(2)}) %collective-permute-start.7) | collective-permute-done | bytes 262176 | tf_op jit(solution)/shard_map/ppermute | solution.py:39
  53.7 0.0 copy-done.3
  53.7 4.0 %dyson.1 = (bf16[2,256,512]{2,1,0:T(8,128)(2,1)}, f32[264,512]{1,0:T(8,128)S(1)}, f32[256,512]{1,0:T(8,128)S(1)}, f32[8,512]{1,0:T(8,128)S(1)}) custom-call(f32[4,2,32,512]{3,2,1,0:T(8,128)S(1)} %convert_element_type.22.refs_0_, f32[4,2,32,512]{3,2,1,0:T(8,128)S(1)} %convert_element_type.23.refs_1_, f32[4,2,32,512]{3,2,1,0:T(8,128)S(1)} %convert_element_type.24.refs_2_, ...), custom_call_target="tpu_custom_call" | custom-call | tf_op jit(solution)/shard_map/dyson/pallas_call | solution.py:240
  57.7 1.6 %collective-permute-start.10 = (f16[264,512]{1,0:T(8,128)(2,1)S(1)}, f16[264,512]{1,0:T(8,128)(2,1)S(1)}, u32[]{:S(2)}, u32[]{:S(2)}) collective-permute-start(f16[264,512]{1,0:T(8,128)(2,1)S(1)} %convert_element_type.26), channel_id=1, source_target_pairs={{0,1},{1,0},{2,3},{3,2},{4,5},{5,4},{6,7},{7,6},{8,9},{9,8},{10,11... | collective-permute-start | bytes 811016 | tf_op jit(solution)/shard_map/ppermute | solution.py:307
  59.3 6.0 %collective-permute-done.10 = f16[264,512]{1,0:T(8,128)(2,1)S(1)} collective-permute-done((f16[264,512]{1,0:T(8,128)(2,1)S(1)}, f16[264,512]{1,0:T(8,128)(2,1)S(1)}, u32[]{:S(2)}, u32[]{:S(2)}) %collective-permute-start.10) | collective-permute-done | bytes 270368 | tf_op jit(solution)/shard_map/ppermute | solution.py:307
  65.3 0.1 convert_element_type.27.theirs_ref
  65.4 2.0 %finish.1 = f32[256,512]{1,0:T(8,128)} custom-call(s32[1]{0:T(128)S(6)} %copy.17.green_steps_ref.steps_ref, f32[256,512]{1,0:T(8,128)S(1)} %get-tuple-element.6.step_ref, f32[264,512]{1,0:T(8,128)S(1)} %get-tuple-element.7.packed_ref, f32[264,512]{1,0:T(8,128)S(1)} %convert_element_type.27.theirs_ref, f32[8,512]{1,0:T(8,128)S(1)} %get-tuple-element.8.own_ref), custom_call_target="tpu_custom_call" | custom-call | tf_op jit(solution)/shard_map/finish/pallas_call | solution.py:308
  (6 shorter events, 0.1 us)
Async XLA Ops:
  1.3 1.0 %copy-start.1 = (bf16[1,1,256,512]{3,2,1,0:T(8,128)(2,1)S(1)}, bf16[1,1,256,512]{3,2,1,0:T(8,128)(2,1)}, u32[]{:S(2)}) copy-start(bf16[1,1,256,512]{3,2,1,0:T(8,128)(2,1)} %param.8) | copy-start | bytes 786436
  2.2 14.7 %copy-start = (f32[1,256,512]{2,1,0:T(8,128)S(1)}, f32[1,256,512]{2,1,0:T(8,128)}, u32[]{:S(2)}) copy-start(f32[1,256,512]{2,1,0:T(8,128)} %param.11) | copy-start | bytes 1572868
  3.0 13.9 %all-to-all-start = ((bf16[8,40,512]{2,1,0:T(8,128)(2,1)}), bf16[8,40,512]{2,1,0:T(8,128)(2,1)S(1)}, u32[]{:S(2)}, u32[]{:S(2)}) async-start(bf16[8,40,512]{2,1,0:T(8,128)(2,1)} %prepare.1), calls=%async_computation | async-start | bytes 655360 | tf_op jit(solution)/shard_map/all_to_all | solution.py:90
  9.0 7.9 %copy-start.4 = (s32[2]{0:T(128)S(1)}, s32[2]{0:T(128)}, u32[]{:S(2)}) copy-start(s32[2]{0:T(128)} %refs_4_.1) | copy-start | bytes 28
  17.7 1.0 %copy-start.2 = (bf16[1,1,256,512]{3,2,1,0:T(8,128)(2,1)S(1)}, bf16[1,1,256,512]{3,2,1,0:T(8,128)(2,1)}, u32[]{:S(2)}) copy-start(bf16[1,1,256,512]{3,2,1,0:T(8,128)(2,1)} %param.8) | copy-start | bytes 786436
  17.8 7.3 %collective-permute-start = (f16[2,32,512]{2,1,0:T(8,128)(2,1)S(1)}, f16[2,32,512]{2,1,0:T(8,128)(2,1)S(1)}, u32[]{:S(2)}, u32[]{:S(2)}) collective-permute-start(f16[2,32,512]{2,1,0:T(8,128)(2,1)S(1)} %get-tuple-element.13), channel_id=1, source_target_pairs={{0,24},{4,28},{8,0},{12,4},{16,8},{20,12},{24,16},{28,20},{1,25},{... | collective-permute-start | bytes 196616 | tf_op jit(solution)/shard_map/ppermute | solution.py:131
  18.7 18.2 %collective-permute-start.6 = (bf16[256,512]{1,0:T(8,128)(2,1)S(1)}, bf16[256,512]{1,0:T(8,128)(2,1)S(1)}, u32[]{:S(2)}, u32[]{:S(2)}) collective-permute-start(bf16[256,512]{1,0:T(8,128)(2,1)S(1)} %bitcast.18), channel_id=1, source_target_pairs={{0,8},{4,12},{8,16},{12,20},{16,24},{20,28},{1,9},{5,13},{9,17},{1... | collective-permute-start | bytes 786440 | tf_op jit(solution)/shard_map/ppermute | solution.py:39
  20.0 11.9 %collective-permute-start.1 = (f16[2,32,512]{2,1,0:T(8,128)(2,1)S(1)}, f16[2,32,512]{2,1,0:T(8,128)(2,1)S(1)}, u32[]{:S(2)}, u32[]{:S(2)}) collective-permute-start(f16[2,32,512]{2,1,0:T(8,128)(2,1)S(1)} %get-tuple-element.13), channel_id=1, source_target_pairs={{0,16},{4,20},{8,24},{12,28},{16,0},{20,4},{24,8},{28,12},{1,17},{... | collective-permute-start | bytes 196616 | tf_op jit(solution)/shard_map/ppermute | solution.py:131
  22.8 9.1 %collective-permute-start.2 = (f16[2,32,512]{2,1,0:T(8,128)(2,1)S(1)}, f16[2,32,512]{2,1,0:T(8,128)(2,1)S(1)}, u32[]{:S(2)}, u32[]{:S(2)}) collective-permute-start(f16[2,32,512]{2,1,0:T(8,128)(2,1)S(1)} %get-tuple-element.13), channel_id=1, source_target_pairs={{0,8},{4,12},{8,16},{12,20},{16,24},{20,28},{24,0},{28,4},{1,9},{5... | collective-permute-start | bytes 196616 | tf_op jit(solution)/shard_map/ppermute | solution.py:131
  32.0 7.4 %collective-permute-start.5 = (f16[4,2,32,512]{3,2,1,0:T(8,128)(2,1)S(1)}, f16[4,2,32,512]{3,2,1,0:T(8,128)(2,1)S(1)}, u32[]{:S(2)}, u32[]{:S(2)}) collective-permute-start(f16[4,2,32,512]{3,2,1,0:T(8,128)(2,1)S(1)} %bitcast_dynamic-update-slice_fusion), channel_id=1, source_target_pairs={{0,5},{1,4},{4,1},{5,0},{8,13},{9,12},{12,9},{13,8},{16,21},{17,20... | collective-permute-start | bytes 786440 | tf_op jit(solution)/shard_map/ppermute | solution.py:141
  34.0 15.2 %collective-permute-start.9 = (bf16[256,512]{1,0:T(8,128)(2,1)S(1)}, bf16[256,512]{1,0:T(8,128)(2,1)S(1)}, u32[]{:S(2)}, u32[]{:S(2)}) collective-permute-start(bf16[256,512]{1,0:T(8,128)(2,1)S(1)} %bitcast.19), channel_id=1, source_target_pairs={{0,2},{2,0},{1,3},{3,1},{4,6},{6,4},{5,7},{7,5},{8,10},{10,8},{9,1... | collective-permute-start | bytes 786440 | tf_op jit(solution)/shard_map/ppermute | solution.py:298
  34.7 2.2 %copy-start.5 = (s32[2]{0:T(128)S(1)}, s32[2]{0:T(128)}, u32[]{:S(2)}) copy-start(s32[2]{0:T(128)} %refs_5_.1) | copy-start | bytes 28
  35.4 9.6 %collective-permute-start.4 = (f16[4,2,32,512]{3,2,1,0:T(8,128)(2,1)S(1)}, f16[4,2,32,512]{3,2,1,0:T(8,128)(2,1)S(1)}, u32[]{:S(2)}, u32[]{:S(2)}) collective-permute-start(f16[4,2,32,512]{3,2,1,0:T(8,128)(2,1)S(1)} %bitcast_dynamic-update-slice_fusion), channel_id=1, source_target_pairs={{0,1},{1,0},{2,3},{3,2},{4,5},{5,4},{6,7},{7,6},{8,9},{9,8},{10,11... | collective-permute-start | bytes 786440 | tf_op jit(solution)/shard_map/ppermute | solution.py:143
  35.9 13.2 %collective-permute-start.3 = (f16[4,2,32,512]{3,2,1,0:T(8,128)(2,1)S(1)}, f16[4,2,32,512]{3,2,1,0:T(8,128)(2,1)S(1)}, u32[]{:S(2)}, u32[]{:S(2)}) collective-permute-start(f16[4,2,32,512]{3,2,1,0:T(8,128)(2,1)S(1)} %bitcast_dynamic-update-slice_fusion), channel_id=1, source_target_pairs={{0,4},{4,0},{8,12},{12,8},{16,20},{20,16},{24,28},{28,24},{1,5},{5... | collective-permute-start | bytes 786440 | tf_op jit(solution)/shard_map/ppermute | solution.py:142
  37.5 13.1 %collective-permute-start.8 = (bf16[256,512]{1,0:T(8,128)(2,1)S(1)}, bf16[256,512]{1,0:T(8,128)(2,1)S(1)}, u32[]{:S(2)}, u32[]{:S(2)}) collective-permute-start(bf16[256,512]{1,0:T(8,128)(2,1)S(1)} %chosen.1), channel_id=1, source_target_pairs={{0,4},{4,8},{8,12},{12,16},{16,20},{20,24},{24,28},{1,5},{5,9},{9,... | collective-permute-start | bytes 786440 | tf_op jit(solution)/shard_map/ppermute | solution.py:39
  39.4 14.3 %collective-permute-start.7 = (bf16[256,512]{1,0:T(8,128)(2,1)S(1)}, bf16[256,512]{1,0:T(8,128)(2,1)S(1)}, u32[]{:S(2)}, u32[]{:S(2)}) collective-permute-start(bf16[256,512]{1,0:T(8,128)(2,1)S(1)} %collective-permute-done.6.two_ref.refs_9_), channel_id=1, source_target_pairs={{0,8},{4,12},{8,16},{12,20},{16,24},{20,28},{1,9},{5,13},{9,17},{1... | collective-permute-start | bytes 786440 | tf_op jit(solution)/shard_map/ppermute | solution.py:39
  45.0 8.7 %copy-start.3 = (f32[1,256,512]{2,1,0:T(8,128)S(1)}, f32[1,256,512]{2,1,0:T(8,128)}, u32[]{:S(2)}) copy-start(f32[1,256,512]{2,1,0:T(8,128)} %param.12) | copy-start | bytes 1572868
  57.7 7.6 %collective-permute-start.10 = (f16[264,512]{1,0:T(8,128)(2,1)S(1)}, f16[264,512]{1,0:T(8,128)(2,1)S(1)}, u32[]{:S(2)}, u32[]{:S(2)}) collective-permute-start(f16[264,512]{1,0:T(8,128)(2,1)S(1)} %convert_element_type.26), channel_id=1, source_target_pairs={{0,1},{1,0},{2,3},{3,2},{4,5},{5,4},{6,7},{7,6},{8,9},{9,8},{10,11... | collective-permute-start | bytes 811016 | tf_op jit(solution)/shard_map/ppermute | solution.py:307

commit v6 on v4

--- a/solution.py
+++ b/solution.py
@@ -44,40 +44,51 @@
     return lax.ppermute(block, axis, route)
 
 
-def prepare_kernel(weight_ref, block_ref, out_ref, tail, block_sem, tail_sem):
+def in_squares():
+    energies = lax.axis_size("energy")
+    return energies % 2 == 0 and energies <= 16 and lax.axis_size("rep") == 2
+
+
+def share_of(place):
+    outer = lax.axis_size("energy") // 2
+    return place % 2 * outer + place // 2 if in_squares() else place
+
+
+def prepare_kernel(weight_ref, block_ref, out_ref, held_rows, read_sems, write_sems):
     energies, padded, width = out_ref.shape
     share = padded - EXTRA
-    copies = [
+    reads = [
         pltpu.make_async_copy(
-            block_ref.at[pl.ds(k * share, share), :], out_ref.at[k, pl.ds(0, share), :],
-            block_sem.at[k],
+            block_ref.at[pl.ds(share_of(k) * share, share), :],
+            held_rows.at[k, pl.ds(0, share), :], read_sems.at[k],
         )
         for k in range(energies)
     ]
-    for copy in copies:
+    for copy in reads:
         copy.start()
     weight = jnp.full((EXTRA, width), weight_ref[0], jnp.float32)
     first = weight.astype(jnp.bfloat16).astype(jnp.float32)
     second = (weight - first).astype(jnp.bfloat16).astype(jnp.float32)
     third = weight - first - second
     row = lax.broadcasted_iota(jnp.int32, (EXTRA, width), 0)
-    parts = jnp.where(row == 0, first, jnp.where(row == 1, second, third))
-    tail[...] = parts.astype(jnp.bfloat16)
-    tails = [
-        pltpu.make_async_copy(tail, out_ref.at[k, pl.ds(share, EXTRA), :], tail_sem.at[k])
+    tail = jnp.where(row == 0, first, jnp.where(row == 1, second, third)).astype(jnp.bfloat16)
+    writes = [
+        pltpu.make_async_copy(held_rows.at[k], out_ref.at[k], write_sems.at[k])
         for k in range(energies)
     ]
-    for copy in tails:
-        copy.start()
-    for copy in copies + tails:
+    for k in range(energies):
+        held_rows[k, share:, :] = tail
+    for k in range(energies):
+        reads[k].wait()
+        writes[k].start()
+    for copy in writes:
         copy.wait()
 
 
-def polar_kernel(offsets_ref, got_ref, bare_ref, out_ref, padded, bare_rows, arrived):
+def polar_kernel(offsets_ref, screen_ref, green_steps_ref, level_ref, got_ref, bare_ref, out_ref, padded, bare_rows, arrived):
     energies, tall, width = got_ref.shape
     share = tall - EXTRA
-    place = lax.axis_index("energy")
-    start = pl.multiple_of(place * share, share)
+    start = pl.multiple_of(share_of(lax.axis_index("energy")) * share, share)
     copy = pltpu.make_async_copy(bare_ref.at[pl.ds(start, share), :], bare_rows, arrived)
     copy.start()
     padded[:SHIFTS] = jnp.zeros((SHIFTS, share, width), jnp.float32)
@@ -95,7 +106,7 @@
         out_ref[f] = totals[f] * (factor * bare_rows[...])
 
 
-def polar_share(green, weight, offsets, bare):
+def polar_share(green, weight, offsets, bare, scalars):
     energies = lax.axis_size("energy")
     rows, width = green.shape
     share = rows // energies
@@ -105,7 +116,7 @@
         in_specs=[in_smem, in_hbm],
         out_specs=in_hbm,
         scratch_shapes=[
-            VMEM((EXTRA, width), green.dtype),
+            VMEM((energies, share + EXTRA, width), green.dtype),
             pltpu.SemaphoreType.DMA((energies,)),
             pltpu.SemaphoreType.DMA((energies,)),
         ],
@@ -116,7 +127,7 @@
     return pl.pallas_call(
         polar_kernel,
         out_shape=jax.ShapeDtypeStruct((FREQS, share, width), jnp.float32),
-        in_specs=[in_smem, in_vmem, in_place],
+        in_specs=[in_smem] * 4 + [in_vmem, in_place],
         out_specs=in_vmem,
         scratch_shapes=[
             VMEM((SHIFTS + energies, share, width), jnp.float32),
@@ -125,19 +136,21 @@
         ],
         compiler_params=small,
         name="polar",
-    )(offsets, got, bare)
-
-
-def polar_share_plain(green, weight, offsets, bare):
+    )(offsets, *scalars, got, bare)
+
+
+def polar_share_plain(green, weight, offsets, bare, scalars):
     energies = lax.axis_size("energy")
     rows, width = green.shape
     share = rows // energies
     weights = lax.all_gather(weight, "energy", axis=0, tiled=True)
-    got = lax.all_to_all(green.reshape(energies, share, width), "energy", 0, 0, tiled=True)
+    parts = green.reshape(energies, share, width)
+    parts = jnp.stack([parts[share_of(k)] for k in range(energies)]) if in_squares() else parts
+    got = lax.all_to_all(parts, "energy", 0, 0, tiled=True)
     wide = got.astype(jnp.float32)
     weighted = wide * weights[:, None, None]
     padded = jnp.concatenate([jnp.zeros((SHIFTS,) + wide.shape[1:], wide.dtype), wide], axis=0)
-    own = lax.dynamic_slice_in_dim(bare, lax.axis_index("energy") * share, share, 0)
+    own = lax.dynamic_slice_in_dim(bare, share_of(lax.axis_index("energy")) * share, share, 0)
     factor = -(width ** -0.5) * energies ** -0.5
     chunks = []
     for f in range(FREQS):
@@ -170,12 +183,11 @@
 
 
 def gathered(chunk):
-    energies = lax.axis_size("energy")
     chunk = chunk.astype(coded)
-    if energies % 2 or energies > 16 or lax.axis_size("rep") != 2:
+    if in_squares():
+        pieces = gather_square(gather_energy(chunk))
+    else:
         pieces = [lax.all_gather(chunk, ("rep", "energy"), axis=1, tiled=True)]
-    else:
-        pieces = gather_square(gather_energy(chunk))
     return [piece.astype(jnp.float32) for piece in pieces]
 
 
@@ -195,9 +207,11 @@
 
 def dyson_kernel(pieces, offsets_ref, steps_ref, level_ref, bare_ref, hamiltonian_ref, two_ref,
                  four_ref, odd_ref, beside_refs, screened_ref, packed_ref, step_ref, own_ref,
-                 high, low):
+                 high, low, made, hamiltonian_rows, made_sem, hamiltonian_sem):
     rows, width = bare_ref.shape
     entry_scale = width ** -0.5
+    read = pltpu.make_async_copy(hamiltonian_ref, hamiltonian_rows, hamiltonian_sem)
+    read.start()
     energy, rep = lax.axis_index("energy"), lax.axis_index("rep")
     if len(pieces) == 1:
         for f in range(FREQS):
@@ -208,7 +222,7 @@
         corners = [(x, rep), (1 - x, rep), (x, 1 - rep), (1 - x, 1 - rep)]
         for piece, (at_x, at_rep) in zip(pieces, corners):
             for z in range(outer):
-                start = pl.multiple_of(at_rep * rows + z * 2 * share + at_x * share, share)
+                start = pl.multiple_of(at_rep * rows + (at_x * outer + z) * share, share)
                 for f in range(FREQS):
                     upper, lower = halves(piece[z, f])
                     high[f, pl.ds(start, share), :] = upper
@@ -227,11 +241,14 @@
         count = steps_ref[f]
         value = jnp.where(count == 0, bare, jnp.where(count == 1, once[f], twice))
         value = value.astype(jnp.bfloat16)
-        screened_ref[f] = value
+        made[f] = value
         lowered = jnp.where(offsets_ref[f] == SHIFTS, four, less)
         energy_terms += lowered * value.astype(jnp.float32)
     beside = sum(ref[...].astype(jnp.float32) for ref in beside_refs)
-    rest = hamiltonian_ref[...] - entry_scale * energy_terms - (0.5 * entry_scale) * beside
+    write = pltpu.make_async_copy(made, screened_ref, made_sem)
+    write.start()
+    read.wait()
+    rest = hamiltonian_rows[...] - entry_scale * energy_terms - (0.5 * entry_scale) * beside
     col = lax.broadcasted_iota(jnp.int32, (rows, width), 1)
     row = lax.broadcasted_iota(jnp.int32, (rows, width), 0) + rep * rows
     on = col == row
@@ -251,6 +268,7 @@
         [*parts_of(factor_row), *parts_of(inverse_row), blank, blank], axis=0
     )
     own_ref[...] = jnp.concatenate([factor_row, inverse_row] + [blank] * 6, axis=0)
+    write.wait()
 
 
 def dyson_rows(pieces, offsets, steps, level, bare, hamiltonian, two, four, odd, beside):
@@ -270,38 +288,58 @@
             jax.ShapeDtypeStruct((rows, width), jnp.float32),
             jax.ShapeDtypeStruct((EXTRA, width), jnp.float32),
         ),
-        in_specs=[in_vmem] * count + [in_smem] * 3 + [in_vmem] * (5 + sides),
-        out_specs=(in_vmem,) * 4,
-        scratch_shapes=[VMEM((FREQS, width, width), jnp.bfloat16)] * 2,
+        in_specs=[in_vmem] * count + [in_smem] * 3 + [in_vmem, in_hbm] + [in_vmem] * (3 + sides),
+        out_specs=(in_hbm,) + (in_vmem,) * 3,
+        scratch_shapes=[VMEM((FREQS, width, width), jnp.bfloat16)] * 2
+        + [VMEM((FREQS, rows, width), jnp.bfloat16), VMEM((rows, width), jnp.float32)]
+        + [pltpu.SemaphoreType.DMA] * 2,
         compiler_params=large,
         name="dyson",
-    )(*pieces, offsets, steps, level, bare, hamiltonian, two, four, odd, *beside)
-
-
-def finish_kernel(steps_ref, step_ref, packed_ref, theirs_ref, own_ref, out_ref):
-    rows, width = step_ref.shape
+    )(*pieces, offsets, steps, level, bare, held(hamiltonian), two, four, odd, *beside)
+
+
+def columns(value, first):
+    rows = value.shape[0]
+    left, right = value[:, :rows], value[:, rows:]
+    return jnp.where(first, left, right), jnp.where(first, right, left)
+
+
+def begin_kernel(step_ref, packed_ref, own_ref, square_ref, high_ref, low_ref):
+    rows, _ = step_ref.shape
+    high, low = halves(packed_ref[:rows, :])
+    high_ref[...], low_ref[...] = high, low
+    near, _ = columns(step_ref[...] * own_ref[0:1], lax.axis_index("rep") == 0)
+    square_ref[...] = product(near, high, low)
+
+
+def finish_kernel(steps_ref, step_ref, square_ref, high_ref, low_ref, theirs_ref, own_ref, out_ref,
+                  made, sems):
+    rows, _ = step_ref.shape
     rep = lax.axis_index("rep")
     first = rep == 0
     tail = theirs_ref[rows:, :]
     factors = own_ref[0:1] + whole_of(tail[0:1], tail[1:2], tail[2:3])
     inverses = own_ref[1:2] + whole_of(tail[3:4], tail[4:5], tail[5:6])
-    mine = halves(packed_ref[:rows, :])
     theirs = halves(theirs_ref[:rows, :])
-
-    def times_all(value):
-        left, right = value[:, :rows], value[:, rows:]
-        return product(jnp.where(first, left, right), *mine) + product(
-            jnp.where(first, right, left), *theirs
+    step = step_ref[...]
+    _, far = columns(step * factors, first)
+    square = square_ref[...] + product(far, *theirs)
+    near, far = columns(square * factors, first)
+    writes = []
+    for half in range(2):
+        at = slice(half * rows, (half + 1) * rows)
+        cube = product(near, high_ref[:, at], low_ref[:, at]) + product(
+            far, theirs[0][:, at], theirs[1][:, at]
         )
-
-    step = step_ref[...]
-    square = times_all(step * factors)
-    cube = times_all(square * factors)
-    col = lax.broadcasted_iota(jnp.int32, (rows, width), 1)
-    row = lax.broadcasted_iota(jnp.int32, (rows, width), 0) + rep * rows
-    total = jnp.where(col == row, 1.0, step)
-    total = total + jnp.where(steps_ref[0] >= 2, square + cube, 0.0)
-    out_ref[...] = total * inverses
+        col = lax.broadcasted_iota(jnp.int32, (rows, rows), 1) + half * rows
+        row = lax.broadcasted_iota(jnp.int32, (rows, rows), 0) + rep * rows
+        total = jnp.where(col == row, 1.0, step[:, at])
+        total = total + jnp.where(steps_ref[0] >= 2, square[:, at] + cube, 0.0)
+        made[:, at] = total * inverses[:, at]
+        writes.append(pltpu.make_async_copy(made.at[:, at], out_ref.at[:, at], sems.at[half]))
+        writes[-1].start()
+    for write in writes:
+        write.wait()
 
 
 def body(
@@ -312,11 +350,12 @@
     rows, width = green.shape
     share = rows // lax.axis_size("energy")
     make = polar_share if share % 16 == 0 else polar_share_plain
-    pieces = gathered(make(green, occupation, offsets, bare))
+    scalars = (screen_steps, green_steps, onsite_level)
+    pieces = gathered(make(green, occupation, offsets, bare, scalars))
 
     two = shifted(green, "energy", 2)
     four = shifted(two, "energy", 2)
-    odd = shifted(chosen(offsets, (screen_steps, green_steps, onsite_level), two, green), "energy", 1)
+    odd = shifted(chosen(offsets, two, green), "energy", 1)
 
     slabs = lax.axis_size("slab")
     if slabs == 2:
@@ -330,18 +369,29 @@
         pieces, offsets, screen_steps, onsite_level, bare, hamiltonian[0], two, four, odd, beside
     )
     theirs = lax.ppermute(packed.astype(coded), "rep", [(0, 1), (1, 0)]).astype(jnp.float32)
+    wide = jax.ShapeDtypeStruct((rows, width), jnp.float32)
+    thin = jax.ShapeDtypeStruct((rows, width), jnp.bfloat16)
+    square, high, low = pl.pallas_call(
+        begin_kernel,
+        out_shape=(wide, thin, thin),
+        in_specs=[in_vmem] * 3,
+        out_specs=(in_vmem,) * 3,
+        compiler_params=small,
+        name="begin",
+    )(step, packed, own)
     green_next = pl.pallas_call(
         finish_kernel,
-        out_shape=jax.ShapeDtypeStruct((rows, width), jnp.float32),
-        in_specs=[in_smem] + [in_vmem] * 4,
-        out_specs=in_vmem,
+        out_shape=wide,
+        in_specs=[in_smem] + [in_vmem] * 6,
+        out_specs=in_hbm,
+        scratch_shapes=[VMEM((rows, width), jnp.float32), pltpu.SemaphoreType.DMA((2,))],
         compiler_params=large,
         name="finish",
-    )(green_steps, step, packed, theirs, own)
+    )(green_steps, step, square, high, low, theirs, own)
     return green_next[None, None], screened[:, None]
 
 
-def chosen_kernel(offsets_ref, screen_ref, green_steps_ref, level_ref, two_ref, green_ref, out_ref):
+def chosen_kernel(offsets_ref, two_ref, green_ref, out_ref):
     three = jnp.minimum(offsets_ref[0], offsets_ref[1]) == 3
 
     @pl.when(three)
@@ -353,15 +403,15 @@
         out_ref[...] = green_ref[...]
 
 
-def chosen(offsets, scalars, two, green):
+def chosen(offsets, two, green):
     return pl.pallas_call(
         chosen_kernel,
         out_shape=jax.ShapeDtypeStruct(green.shape, green.dtype),
-        in_specs=[in_smem] * 4 + [in_vmem] * 2,
+        in_specs=[in_smem, in_vmem, in_vmem],
         out_specs=in_vmem,
         compiler_params=small,
         name="chosen",
-    )(offsets, *scalars, two, green)
+    )(offsets, two, green)
 
 
 def solution(mesh):

time: 76 us -> 67 us (0.88)
  Pallas kernels: 16.5 us -> 9.29 us
  waiting for transfers between devices: 34 us -> 32.3 us
    pallas_call x1, Pallas kernels: 9.2 us -> 1.69 us  [polar_share(): pl.pallas_call(prepare_kernel, out_shape=jax.ShapeDtypeStruct((energies,...]
    ppermute x1, waiting for transfers between devices: 0.59 us -> 2.87 us  [gather_square(): apart = lax.ppermute(part, ('energy', 'rep'), cross)]
    ppermute x3, waiting for transfers between devices: 4.46 us -> 3.07 us  [shifted(): return lax.ppermute(block, axis, route)]
    all_to_all x1, waiting for transfers between devices: 7.92 us -> 6.59 us  [polar_share(): got = lax.all_to_all(sent, 'energy', 0, 0, tiled=True)]
    ppermute x1, waiting for transfers between devices: 4.12 us -> 3.23 us  [gather_square(): above = lax.ppermute(part, 'rep', turn)]
    pallas_call x1 -> x2, Pallas kernels: 1.96 us -> 2.16 us  [the longest x1 1.74 us: body(): pl.pallas_call(finish_kernel, out_shape=wide, in_specs=[in_smem] + [in_vm...]
where the time goes in v6:
time: 67 us; the launch traced here: 65.8 us
  waiting for transfers between devices  32.3 us (48%)
  starting transfers between devices  20.1 us (30%)
  Pallas kernels  9.29 us (14%)
  between operations  2.85 us (4%)
  local copies, waits for them, and re-layouts  0.91 us (1%)
    ppermute x3, waiting for transfers between devices, gather_energy(): got = lax.ppermute(chunk, 'energy', route)  6.78 us
    all_to_all x1, waiting for transfers between devices, polar_share(): got = lax.all_to_all(sent, 'energy', 0, 0, tiled=True)  6.59 us
    all_to_all x1, starting transfers between devices, polar_share(): got = lax.all_to_all(sent, 'energy', 0, 0, tiled=True)  6.01 us
    ppermute x1, waiting for transfers between devices, body(): lax.ppermute(packed.astype(coded), 'rep', [(0, 1), (1, 0)])  5.57 us
    ppermute x3, starting transfers between devices, gather_energy(): got = lax.ppermute(chunk, 'energy', route)  5.13 us
    ppermute x1, waiting for transfers between devices, gather_square(): beside = lax.ppermute(part, 'energy', swap)  4.19 us
    pallas_call x1, Pallas kernels, dyson_rows(): pl.pallas_call(kernel, out_shape=(jax.ShapeDtypeStruct((FREQS, rows, widt...  4.04 us
    ppermute x3, starting transfers between devices, shifted(): return lax.ppermute(block, axis, route)  3.85 us
  transfers between devices with their start and end apart: 12, of which 8 were waited for; matrix products, arithmetic and copies ran while one was open for 0% of the time, Pallas kernels for 1%

profile of v6, /device:TPU:26, one launch (start us, length us, event | category | flops | bytes accessed | tf_op | source)
XLA Modules:
  0.0 65.8 jit_solution(2099255767870255772)
XLA Ops:
  1.3 0.0 copy-start
  1.3 1.7 %prepare.1 = bf16[8,40,512]{2,1,0:T(8,128)(2,1)} custom-call(f32[1]{0:T(128)S(6)} %copy.15.weight_ref, bf16[256,512]{1,0:T(8,128)(2,1)} %bitcast.17), custom_call_target="tpu_custom_call" | custom-call | tf_op jit(solution)/shard_map/prepare/pallas_call | solution.py:113
  3.0 6.0 %all-to-all-start = ((bf16[8,40,512]{2,1,0:T(8,128)(2,1)}), bf16[8,40,512]{2,1,0:T(8,128)(2,1)S(1)}, u32[]{:S(2)}, u32[]{:S(2)}) async-start(bf16[8,40,512]{2,1,0:T(8,128)(2,1)} %prepare.1), calls=%async_computation | async-start | bytes 655360 | tf_op jit(solution)/shard_map/all_to_all | solution.py:126
  10.3 0.0 copy-start.2
  10.3 0.0 copy-start.3
  10.3 6.6 %all-to-all-done.got_ref = bf16[8,40,512]{2,1,0:T(8,128)(2,1)S(1)} async-done(((bf16[8,40,512]{2,1,0:T(8,128)(2,1)}), bf16[8,40,512]{2,1,0:T(8,128)(2,1)S(1)}, u32[]{:S(2)}, u32[]{:S(2)}) %all-to-all-start) | async-done | bytes 327712 | tf_op jit(solution)/shard_map/all_to_all | solution.py:126
  16.9 0.0 copy-done
  16.9 0.0 copy-done.2
  16.9 0.0 copy-done.3
  16.9 0.8 %polar.1 = f32[2,32,512]{2,1,0:T(8,128)S(1)} custom-call(s32[2]{0:T(128)S(1)} %copy-done.2, s32[2]{0:T(128)S(1)} %copy-done.3, s32[1]{0:T(128)S(6)} %copy.17.green_steps_ref.steps_ref, f32[1]{0:T(128)S(6)} %copy.16.level_ref.refs_6_, bf16[8,40,512]{2,1,0:T(8,128)(2,1)S(1)} %all-to-all-done.got_ref, f32[256,512]{1,0:T(8,128)S(1)} %bitcast.15), custom_call_target="tpu_custom_call" | custom-call | tf_op jit(solution)/shard_map/polar/pallas_call | solution.py:127
  17.8 0.0 copy-start.1
  17.8 0.1 collective-permute-start
  17.9 0.8 %copy-done.1 = bf16[1,1,256,512]{3,2,1,0:T(8,128)(2,1)S(1)} copy-done((bf16[1,1,256,512]{3,2,1,0:T(8,128)(2,1)S(1)}, bf16[1,1,256,512]{3,2,1,0:T(8,128)(2,1)}, u32[]{:S(2)}) %copy-start.1) | copy-done | bytes 262168
  18.7 1.3 %collective-permute-start.6 = (bf16[256,512]{1,0:T(8,128)(2,1)S(1)}, bf16[256,512]{1,0:T(8,128)(2,1)S(1)}, u32[]{:S(2)}, u32[]{:S(2)}) collective-permute-start(bf16[256,512]{1,0:T(8,128)(2,1)S(1)} %bitcast.18), channel_id=1, source_target_pairs={{0,8},{4,12},{8,16},{12,20},{16,24},{20,28},{1,9},{5,13},{9,17},{1... | collective-permute-start | bytes 786440 | tf_op jit(solution)/shard_map/ppermute | solution.py:44
  20.1 2.8 %collective-permute-start.1 = (f16[2,32,512]{2,1,0:T(8,128)(2,1)S(1)}, f16[2,32,512]{2,1,0:T(8,128)(2,1)S(1)}, u32[]{:S(2)}, u32[]{:S(2)}) collective-permute-start(f16[2,32,512]{2,1,0:T(8,128)(2,1)S(1)} %get-tuple-element.19), channel_id=1, source_target_pairs={{0,16},{4,20},{8,24},{12,28},{16,0},{20,4},{24,8},{28,12},{1,17},{... | collective-permute-start | bytes 196616 | tf_op jit(solution)/shard_map/ppermute | solution.py:169
  22.8 2.3 %collective-permute-start.2 = (f16[2,32,512]{2,1,0:T(8,128)(2,1)S(1)}, f16[2,32,512]{2,1,0:T(8,128)(2,1)S(1)}, u32[]{:S(2)}, u32[]{:S(2)}) collective-permute-start(f16[2,32,512]{2,1,0:T(8,128)(2,1)S(1)} %get-tuple-element.19), channel_id=1, source_target_pairs={{0,8},{4,12},{8,16},{12,20},{16,24},{20,28},{24,0},{28,4},{1,9},{5... | collective-permute-start | bytes 196616 | tf_op jit(solution)/shard_map/ppermute | solution.py:169
  25.1 0.0 collective-permute-done
  25.2 6.8 %collective-permute-done.1 = f16[2,32,512]{2,1,0:T(8,128)(2,1)S(1)} collective-permute-done((f16[2,32,512]{2,1,0:T(8,128)(2,1)S(1)}, f16[2,32,512]{2,1,0:T(8,128)(2,1)S(1)}, u32[]{:S(2)}, u32[]{:S(2)}) %collective-permute-start.1) | collective-permute-done | bytes 65568 | tf_op jit(solution)/shard_map/ppermute | solution.py:169
  32.0 0.0 collective-permute-done.2
  32.0 2.1 %collective-permute-start.5 = (f16[4,2,32,512]{3,2,1,0:T(8,128)(2,1)S(1)}, f16[4,2,32,512]{3,2,1,0:T(8,128)(2,1)S(1)}, u32[]{:S(2)}, u32[]{:S(2)}) collective-permute-start(f16[4,2,32,512]{3,2,1,0:T(8,128)(2,1)S(1)} %bitcast_dynamic-update-slice_fusion), channel_id=1, source_target_pairs={{0,5},{1,4},{4,1},{5,0},{8,13},{9,12},{12,9},{13,8},{16,21},{17,20... | collective-permute-start | bytes 786440 | tf_op jit(solution)/shard_map/ppermute | solution.py:179
  34.1 0.0 collective-permute-start.9
  34.1 0.5 collective-permute-start.4
  34.6 1.0 %collective-permute-start.3 = (f16[4,2,32,512]{3,2,1,0:T(8,128)(2,1)S(1)}, f16[4,2,32,512]{3,2,1,0:T(8,128)(2,1)S(1)}, u32[]{:S(2)}, u32[]{:S(2)}) collective-permute-start(f16[4,2,32,512]{3,2,1,0:T(8,128)(2,1)S(1)} %bitcast_dynamic-update-slice_fusion), channel_id=1, source_target_pairs={{0,4},{4,0},{8,12},{12,8},{16,20},{20,16},{24,28},{28,24},{1,5},{5... | collective-permute-start | bytes 786440 | tf_op jit(solution)/shard_map/ppermute | solution.py:180
  35.5 0.0 collective-permute-done.6.two_ref.refs_9_
  35.5 0.6 chosen.1
  36.1 1.3 %collective-permute-start.8 = (bf16[256,512]{1,0:T(8,128)(2,1)S(1)}, bf16[256,512]{1,0:T(8,128)(2,1)S(1)}, u32[]{:S(2)}, u32[]{:S(2)}) collective-permute-start(bf16[256,512]{1,0:T(8,128)(2,1)S(1)} %chosen.1), channel_id=1, source_target_pairs={{0,4},{4,8},{8,12},{12,16},{16,20},{20,24},{24,28},{1,5},{5,9},{9,... | collective-permute-start | bytes 786440 | tf_op jit(solution)/shard_map/ppermute | solution.py:44
  37.4 2.9 %collective-permute-done.5 = f16[4,2,32,512]{3,2,1,0:T(8,128)(2,1)S(1)} collective-permute-done((f16[4,2,32,512]{3,2,1,0:T(8,128)(2,1)S(1)}, f16[4,2,32,512]{3,2,1,0:T(8,128)(2,1)S(1)}, u32[]{:S(2)}, u32[]{:S(2)}) %collective-permute-start.5) | collective-permute-done | bytes 262176 | tf_op jit(solution)/shard_map/ppermute | solution.py:179
  40.3 1.3 %collective-permute-start.7 = (bf16[256,512]{1,0:T(8,128)(2,1)S(1)}, bf16[256,512]{1,0:T(8,128)(2,1)S(1)}, u32[]{:S(2)}, u32[]{:S(2)}) collective-permute-start(bf16[256,512]{1,0:T(8,128)(2,1)S(1)} %collective-permute-done.6.two_ref.refs_9_), channel_id=1, source_target_pairs={{0,8},{4,12},{8,16},{12,20},{16,24},{20,28},{1,9},{5,13},{9,17},{1... | collective-permute-start | bytes 786440 | tf_op jit(solution)/shard_map/ppermute | solution.py:44
  41.6 0.1 convert_element_type.22.refs_0_
  41.6 0.1 convert_element_type.25.refs_3_
  41.7 3.2 %collective-permute-done.4 = f16[4,2,32,512]{3,2,1,0:T(8,128)(2,1)S(1)} collective-permute-done((f16[4,2,32,512]{3,2,1,0:T(8,128)(2,1)S(1)}, f16[4,2,32,512]{3,2,1,0:T(8,128)(2,1)S(1)}, u32[]{:S(2)}, u32[]{:S(2)}) %collective-permute-start.4) | collective-permute-done | bytes 262176 | tf_op jit(solution)/shard_map/ppermute | solution.py:181
  44.9 0.1 convert_element_type.24.refs_2_
  45.0 4.2 %collective-permute-done.3 = f16[4,2,32,512]{3,2,1,0:T(8,128)(2,1)S(1)} collective-permute-done((f16[4,2,32,512]{3,2,1,0:T(8,128)(2,1)S(1)}, f16[4,2,32,512]{3,2,1,0:T(8,128)(2,1)S(1)}, u32[]{:S(2)}, u32[]{:S(2)}) %collective-permute-start.3) | collective-permute-done | bytes 262176 | tf_op jit(solution)/shard_map/ppermute | solution.py:180
  49.2 0.1 convert_element_type.23.refs_1_
  49.3 0.0 collective-permute-done.9.refs_12_
  49.3 1.4 %collective-permute-done.8.refs_11_ = bf16[256,512]{1,0:T(8,128)(2,1)S(1)} collective-permute-done((bf16[256,512]{1,0:T(8,128)(2,1)S(1)}, bf16[256,512]{1,0:T(8,128)(2,1)S(1)}, u32[]{:S(2)}, u32[]{:S(2)}) %collective-permute-start.8) | collective-permute-done | bytes 262176 | tf_op jit(solution)/shard_map/ppermute | solution.py:44
  50.6 1.7 %collective-permute-done.7.refs_10_ = bf16[256,512]{1,0:T(8,128)(2,1)S(1)} collective-permute-done((bf16[256,512]{1,0:T(8,128)(2,1)S(1)}, bf16[256,512]{1,0:T(8,128)(2,1)S(1)}, u32[]{:S(2)}, u32[]{:S(2)}) %collective-permute-start.7) | collective-permute-done | bytes 262176 | tf_op jit(solution)/shard_map/ppermute | solution.py:44
  52.3 4.0 %dyson.1 = (bf16[2,256,512]{2,1,0:T(8,128)(2,1)}, f32[264,512]{1,0:T(8,128)S(1)}, f32[256,512]{1,0:T(8,128)S(1)}, f32[8,512]{1,0:T(8,128)S(1)}) custom-call(f32[4,2,32,512]{3,2,1,0:T(8,128)S(1)} %convert_element_type.22.refs_0_, f32[4,2,32,512]{3,2,1,0:T(8,128)S(1)} %convert_element_type.23.refs_1_, f32[4,2,32,512]{3,2,1,0:T(8,128)S(1)} %convert_element_type.24.refs_2_, ...), custom_call_target="tpu_custom_call" | custom-call | tf_op jit(solution)/shard_map/dyson/pallas_call | solution.py:283
  56.4 1.6 %collective-permute-start.10 = (f16[264,512]{1,0:T(8,128)(2,1)S(1)}, f16[264,512]{1,0:T(8,128)(2,1)S(1)}, u32[]{:S(2)}, u32[]{:S(2)}) collective-permute-start(f16[264,512]{1,0:T(8,128)(2,1)S(1)} %convert_element_type.26), channel_id=1, source_target_pairs={{0,1},{1,0},{2,3},{3,2},{4,5},{5,4},{6,7},{7,6},{8,9},{9,8},{10,11... | collective-permute-start | bytes 811016 | tf_op jit(solution)/shard_map/ppermute | solution.py:371
  58.0 0.4 begin.1
  58.4 5.6 %collective-permute-done.10 = f16[264,512]{1,0:T(8,128)(2,1)S(1)} collective-permute-done((f16[264,512]{1,0:T(8,128)(2,1)S(1)}, f16[264,512]{1,0:T(8,128)(2,1)S(1)}, u32[]{:S(2)}, u32[]{:S(2)}) %collective-permute-start.10) | collective-permute-done | bytes 270368 | tf_op jit(solution)/shard_map/ppermute | solution.py:371
  64.0 0.1 convert_element_type.27.theirs_ref
  64.1 1.7 %finish.1 = f32[256,512]{1,0:T(8,128)} custom-call(s32[1]{0:T(128)S(6)} %copy.17.green_steps_ref.steps_ref, f32[256,512]{1,0:T(8,128)S(1)} %get-tuple-element.9.step_ref, f32[256,512]{1,0:T(8,128)S(1)} %get-tuple-element.12.square_ref, bf16[256,512]{1,0:T(8,128)(2,1)S(1)} %get-tuple-element.13.high_ref, bf16[256,512]{1,0:T(8,128)(2,1)S(1)} %get-tuple-element.14.low_ref, ...), custom_call_target="tpu_custom_call" | custom-call | tf_op jit(solution)/shard_map/finish/pallas_call | solution.py:382
  (6 shorter events, 0.1 us)
Async XLA Ops:
  1.3 15.6 %copy-start = (f32[1,256,512]{2,1,0:T(8,128)S(1)}, f32[1,256,512]{2,1,0:T(8,128)}, u32[]{:S(2)}) copy-start(f32[1,256,512]{2,1,0:T(8,128)} %param.11) | copy-start | bytes 1572868
  3.0 13.9 %all-to-all-start = ((bf16[8,40,512]{2,1,0:T(8,128)(2,1)}), bf16[8,40,512]{2,1,0:T(8,128)(2,1)S(1)}, u32[]{:S(2)}, u32[]{:S(2)}) async-start(bf16[8,40,512]{2,1,0:T(8,128)(2,1)} %prepare.1), calls=%async_computation | async-start | bytes 655360 | tf_op jit(solution)/shard_map/all_to_all | solution.py:126
  10.3 6.6 %copy-start.2 = (s32[2]{0:T(128)S(1)}, s32[2]{0:T(128)}, u32[]{:S(2)}) copy-start(s32[2]{0:T(128)} %refs_4_.1) | copy-start | bytes 28
  10.3 6.6 %copy-start.3 = (s32[2]{0:T(128)S(1)}, s32[2]{0:T(128)}, u32[]{:S(2)}) copy-start(s32[2]{0:T(128)} %refs_5_.1) | copy-start | bytes 28
  17.8 1.0 %copy-start.1 = (bf16[1,1,256,512]{3,2,1,0:T(8,128)(2,1)S(1)}, bf16[1,1,256,512]{3,2,1,0:T(8,128)(2,1)}, u32[]{:S(2)}) copy-start(bf16[1,1,256,512]{3,2,1,0:T(8,128)(2,1)} %param.8) | copy-start | bytes 786436
  17.8 7.3 %collective-permute-start = (f16[2,32,512]{2,1,0:T(8,128)(2,1)S(1)}, f16[2,32,512]{2,1,0:T(8,128)(2,1)S(1)}, u32[]{:S(2)}, u32[]{:S(2)}) collective-permute-start(f16[2,32,512]{2,1,0:T(8,128)(2,1)S(1)} %get-tuple-element.19), channel_id=1, source_target_pairs={{0,24},{4,28},{8,0},{12,4},{16,8},{20,12},{24,16},{28,20},{1,25},{... | collective-permute-start | bytes 196616 | tf_op jit(solution)/shard_map/ppermute | solution.py:169
  18.7 16.8 %collective-permute-start.6 = (bf16[256,512]{1,0:T(8,128)(2,1)S(1)}, bf16[256,512]{1,0:T(8,128)(2,1)S(1)}, u32[]{:S(2)}, u32[]{:S(2)}) collective-permute-start(bf16[256,512]{1,0:T(8,128)(2,1)S(1)} %bitcast.18), channel_id=1, source_target_pairs={{0,8},{4,12},{8,16},{12,20},{16,24},{20,28},{1,9},{5,13},{9,17},{1... | collective-permute-start | bytes 786440 | tf_op jit(solution)/shard_map/ppermute | solution.py:44
  20.1 11.9 %collective-permute-start.1 = (f16[2,32,512]{2,1,0:T(8,128)(2,1)S(1)}, f16[2,32,512]{2,1,0:T(8,128)(2,1)S(1)}, u32[]{:S(2)}, u32[]{:S(2)}) collective-permute-start(f16[2,32,512]{2,1,0:T(8,128)(2,1)S(1)} %get-tuple-element.19), channel_id=1, source_target_pairs={{0,16},{4,20},{8,24},{12,28},{16,0},{20,4},{24,8},{28,12},{1,17},{... | collective-permute-start | bytes 196616 | tf_op jit(solution)/shard_map/ppermute | solution.py:169
  22.8 9.1 %collective-permute-start.2 = (f16[2,32,512]{2,1,0:T(8,128)(2,1)S(1)}, f16[2,32,512]{2,1,0:T(8,128)(2,1)S(1)}, u32[]{:S(2)}, u32[]{:S(2)}) collective-permute-start(f16[2,32,512]{2,1,0:T(8,128)(2,1)S(1)} %get-tuple-element.19), channel_id=1, source_target_pairs={{0,8},{4,12},{8,16},{12,20},{16,24},{20,28},{24,0},{28,4},{1,9},{5... | collective-permute-start | bytes 196616 | tf_op jit(solution)/shard_map/ppermute | solution.py:169
  32.0 8.3 %collective-permute-start.5 = (f16[4,2,32,512]{3,2,1,0:T(8,128)(2,1)S(1)}, f16[4,2,32,512]{3,2,1,0:T(8,128)(2,1)S(1)}, u32[]{:S(2)}, u32[]{:S(2)}) collective-permute-start(f16[4,2,32,512]{3,2,1,0:T(8,128)(2,1)S(1)} %bitcast_dynamic-update-slice_fusion), channel_id=1, source_target_pairs={{0,5},{1,4},{4,1},{5,0},{8,13},{9,12},{12,9},{13,8},{16,21},{17,20... | collective-permute-start | bytes 786440 | tf_op jit(solution)/shard_map/ppermute | solution.py:179
  34.1 15.2 %collective-permute-start.9 = (bf16[256,512]{1,0:T(8,128)(2,1)S(1)}, bf16[256,512]{1,0:T(8,128)(2,1)S(1)}, u32[]{:S(2)}, u32[]{:S(2)}) collective-permute-start(bf16[256,512]{1,0:T(8,128)(2,1)S(1)} %bitcast.19), channel_id=1, source_target_pairs={{0,2},{2,0},{1,3},{3,1},{4,6},{6,4},{5,7},{7,5},{8,10},{10,8},{9,1... | collective-permute-start | bytes 786440 | tf_op jit(solution)/shard_map/ppermute | solution.py:362
  34.1 10.9 %collective-permute-start.4 = (f16[4,2,32,512]{3,2,1,0:T(8,128)(2,1)S(1)}, f16[4,2,32,512]{3,2,1,0:T(8,128)(2,1)S(1)}, u32[]{:S(2)}, u32[]{:S(2)}) collective-permute-start(f16[4,2,32,512]{3,2,1,0:T(8,128)(2,1)S(1)} %bitcast_dynamic-update-slice_fusion), channel_id=1, source_target_pairs={{0,1},{1,0},{2,3},{3,2},{4,5},{5,4},{6,7},{7,6},{8,9},{9,8},{10,11... | collective-permute-start | bytes 786440 | tf_op jit(solution)/shard_map/ppermute | solution.py:181
  34.6 14.6 %collective-permute-start.3 = (f16[4,2,32,512]{3,2,1,0:T(8,128)(2,1)S(1)}, f16[4,2,32,512]{3,2,1,0:T(8,128)(2,1)S(1)}, u32[]{:S(2)}, u32[]{:S(2)}) collective-permute-start(f16[4,2,32,512]{3,2,1,0:T(8,128)(2,1)S(1)} %bitcast_dynamic-update-slice_fusion), channel_id=1, source_target_pairs={{0,4},{4,0},{8,12},{12,8},{16,20},{20,16},{24,28},{28,24},{1,5},{5... | collective-permute-start | bytes 786440 | tf_op jit(solution)/shard_map/ppermute | solution.py:180
  36.1 14.5 %collective-permute-start.8 = (bf16[256,512]{1,0:T(8,128)(2,1)S(1)}, bf16[256,512]{1,0:T(8,128)(2,1)S(1)}, u32[]{:S(2)}, u32[]{:S(2)}) collective-permute-start(bf16[256,512]{1,0:T(8,128)(2,1)S(1)} %chosen.1), channel_id=1, source_target_pairs={{0,4},{4,8},{8,12},{12,16},{16,20},{20,24},{24,28},{1,5},{5,9},{9,... | collective-permute-start | bytes 786440 | tf_op jit(solution)/shard_map/ppermute | solution.py:44
  40.3 12.0 %collective-permute-start.7 = (bf16[256,512]{1,0:T(8,128)(2,1)S(1)}, bf16[256,512]{1,0:T(8,128)(2,1)S(1)}, u32[]{:S(2)}, u32[]{:S(2)}) collective-permute-start(bf16[256,512]{1,0:T(8,128)(2,1)S(1)} %collective-permute-done.6.two_ref.refs_9_), channel_id=1, source_target_pairs={{0,8},{4,12},{8,16},{12,20},{16,24},{20,28},{1,9},{5,13},{9,17},{1... | collective-permute-start | bytes 786440 | tf_op jit(solution)/shard_map/ppermute | solution.py:44
  56.4 7.6 %collective-permute-start.10 = (f16[264,512]{1,0:T(8,128)(2,1)S(1)}, f16[264,512]{1,0:T(8,128)(2,1)S(1)}, u32[]{:S(2)}, u32[]{:S(2)}) collective-permute-start(f16[264,512]{1,0:T(8,128)(2,1)S(1)} %convert_element_type.26), channel_id=1, source_target_pairs={{0,1},{1,0},{2,3},{3,2},{4,5},{5,4},{6,7},{7,6},{8,9},{9,8},{10,11... | collective-permute-start | bytes 811016 | tf_op jit(solution)/shard_map/ppermute | solution.py:371

commit v7 on v6

--- a/solution.py
+++ b/solution.py
@@ -162,24 +162,33 @@
 def gather_energy(chunk):
     outer = lax.axis_size("energy") // 2
     here = lax.axis_index("energy") // 2
-    whole = jnp.zeros((outer,) + chunk.shape, chunk.dtype)
-    whole = lax.dynamic_update_index_in_dim(whole, chunk, here, 0)
+    wholes = [
+        lax.dynamic_update_index_in_dim(jnp.zeros((outer,) + part.shape, part.dtype), part, here, 0)
+        for part in chunk
+    ]
     for k in range(outer - 1, 0, -1):
         route = [(z * 2 + x, (z + k) % outer * 2 + x) for z in range(outer) for x in range(2)]
         got = lax.ppermute(chunk, "energy", route)
-        whole = lax.dynamic_update_index_in_dim(whole, got, (here - k) % outer, 0)
-    return whole
-
-
-def gather_square(part):
+        wholes = [
+            lax.dynamic_update_index_in_dim(whole, part, (here - k) % outer, 0)
+            for whole, part in zip(wholes, got)
+        ]
+    return wholes
+
+
+def gather_square(parts):
     energies = lax.axis_size("energy")
-    swap = [(e, e ^ 1) for e in range(energies)]
-    turn = [(0, 1), (1, 0)]
-    cross = [(e * 2 + r, (e ^ 1) * 2 + 1 - r) for e in range(energies) for r in range(2)]
-    apart = lax.ppermute(part, ("energy", "rep"), cross)
-    beside = lax.ppermute(part, "energy", swap)
-    above = lax.ppermute(part, "rep", turn)
-    return [part, beside, above, apart]
+
+    def along_x(part):
+        return lax.ppermute(part, "energy", [(e, e ^ 1) for e in range(energies)])
+
+    def along_rep(part):
+        return lax.ppermute(part, "rep", [(0, 1), (1, 0)])
+
+    beside = [along_x(part) for part in parts]
+    above = [along_rep(part) for part in parts]
+    apart = [along_rep(beside[0]), along_x(above[1])]
+    return [*parts, *beside, *above, *apart]
 
 
 def gathered(chunk):
@@ -217,16 +226,16 @@
         for f in range(FREQS):
             high[f], low[f] = halves(pieces[0][f])
     else:
-        outer, _, share, _ = pieces[0].shape
+        outer, share, _ = pieces[0].shape
         x = energy % 2
         corners = [(x, rep), (1 - x, rep), (x, 1 - rep), (1 - x, 1 - rep)]
-        for piece, (at_x, at_rep) in zip(pieces, corners):
-            for z in range(outer):
-                start = pl.multiple_of(at_rep * rows + (at_x * outer + z) * share, share)
-                for f in range(FREQS):
-                    upper, lower = halves(piece[z, f])
-                    high[f, pl.ds(start, share), :] = upper
-                    low[f, pl.ds(start, share), :] = lower
+        for place, (at_x, at_rep) in enumerate(corners):
+            start = pl.multiple_of(at_rep * rows + at_x * outer * share, outer * share)
+            for f in range(FREQS):
+                piece = pieces[place * FREQS + f][...].reshape(outer * share, width)
+                upper, lower = halves(piece)
+                high[f, pl.ds(start, outer * share), :] = upper
+                low[f, pl.ds(start, outer * share), :] = lower
     bare = bare_ref[...]
     once = [bare + product(bare, high[f], low[f]) for f in range(FREQS)]
     at = jnp.where(steps_ref[1] > steps_ref[0], 1, 0)

time: 67 us -> 62 us (0.925); the launches traced: 65.8 us -> 61.7 us
  waiting for transfers between devices: 32.3 us -> 26.7 us
  starting transfers between devices: 20.1 us -> 22.3 us
  local copies, waits for them, and re-layouts: 0.91 us -> 0.12 us
    ppermute x3 -> x6, starting transfers between devices: 3.55 us -> 8.09 us  [the longest x3 4.57 us: along_rep(): return lax.ppermute(part, 'rep', [(0, 1), (1, 0)])]
    ppermute x3 -> x6, waiting for transfers between devices: 10.3 us -> 6.35 us  [the longest x3 5.68 us: along_x(): return lax.ppermute(part, 'energy', [(e, e ^ 1) for e in range(energies)])]
    ppermute x3, starting transfers between devices: 5.13 us -> 2.62 us  [gather_energy(): got = lax.ppermute(chunk, 'energy', route)]
    all_to_all x1, waiting for transfers between devices: 6.59 us -> 5.67 us  [polar_share(): got = lax.all_to_all(sent, 'energy', 0, 0, tiled=True)]
    unnamed x8, local copies, waits for them, and re-layouts: 0.84 us -> 0.02 us
    ppermute x3, waiting for transfers between devices: 3.07 us -> 2.28 us  [shifted(): return lax.ppermute(block, axis, route)]
  transfers between devices with their start and end apart: 12 -> 15, of which waited for: 8 -> 8; matrix products, arithmetic and copies ran while one was open for 0% -> 0% of each run, Pallas kernels for 1% -> 3%
where the time goes in v7:
time: 62 us; the launch traced here: 61.7 us
  waiting for transfers between devices  26.7 us (43%)
  starting transfers between devices  22.3 us (36%)
  Pallas kernels  9.34 us (15%)
  between operations  2.92 us (5%)
    ppermute x3, waiting for transfers between devices, gather_energy(): got = lax.ppermute(chunk, 'energy', route)  7.22 us
    all_to_all x1, starting transfers between devices, polar_share(): got = lax.all_to_all(sent, 'energy', 0, 0, tiled=True)  6.14 us
    ppermute x3, waiting for transfers between devices, along_x(): return lax.ppermute(part, 'energy', [(e, e ^ 1) for e in range(energies)])  5.68 us
    all_to_all x1, waiting for transfers between devices, polar_share(): got = lax.all_to_all(sent, 'energy', 0, 0, tiled=True)  5.67 us
    ppermute x1, waiting for transfers between devices, body(): lax.ppermute(packed.astype(coded), 'rep', [(0, 1), (1, 0)])  5.22 us
    ppermute x3, starting transfers between devices, along_rep(): return lax.ppermute(part, 'rep', [(0, 1), (1, 0)])  4.57 us
    pallas_call x1, Pallas kernels, dyson_rows(): pl.pallas_call(kernel, out_shape=(jax.ShapeDtypeStruct((FREQS, rows, widt...  4.11 us
    ppermute x3, starting transfers between devices, shifted(): return lax.ppermute(block, axis, route)  3.84 us
  transfers between devices with their start and end apart: 15, of which 8 were waited for; matrix products, arithmetic and copies ran while one was open for 0% of the time, Pallas kernels for 3%

profile of v7, /device:TPU:26, one launch (start us, length us, event | category | flops | bytes accessed | tf_op | source)
XLA Modules:
  0.0 61.7 jit_solution(9495737272786823995)
XLA Ops:
  1.3 0.0 copy-start.1
  1.3 1.7 %prepare.1 = bf16[8,40,512]{2,1,0:T(8,128)(2,1)} custom-call(f32[1]{0:T(128)S(6)} %copy.19.weight_ref, bf16[256,512]{1,0:T(8,128)(2,1)} %bitcast.9), custom_call_target="tpu_custom_call" | custom-call | tf_op jit(solution)/shard_map/prepare/pallas_call | solution.py:113
  3.0 0.0 copy-start
  3.0 6.1 %all-to-all-start = ((bf16[8,40,512]{2,1,0:T(8,128)(2,1)}), bf16[8,40,512]{2,1,0:T(8,128)(2,1)S(1)}, u32[]{:S(2)}, u32[]{:S(2)}) async-start(bf16[8,40,512]{2,1,0:T(8,128)(2,1)} %prepare.1), calls=%async_computation | async-start | bytes 655360 | tf_op jit(solution)/shard_map/all_to_all | solution.py:126
  9.1 0.0 copy-done.1
  9.1 1.3 %collective-permute-start.9 = (bf16[256,512]{1,0:T(8,128)(2,1)S(1)}, bf16[256,512]{1,0:T(8,128)(2,1)S(1)}, u32[]{:S(2)}, u32[]{:S(2)}) collective-permute-start(bf16[256,512]{1,0:T(8,128)(2,1)S(1)} %bitcast.10), channel_id=1, source_target_pairs={{0,8},{4,12},{8,16},{12,20},{16,24},{20,28},{1,9},{5,13},{9,17},{1... | collective-permute-start | bytes 786440 | tf_op jit(solution)/shard_map/ppermute | solution.py:44
  11.8 0.0 copy-start.2
  11.8 0.0 copy-start.3
  11.8 5.7 %all-to-all-done.got_ref = bf16[8,40,512]{2,1,0:T(8,128)(2,1)S(1)} async-done(((bf16[8,40,512]{2,1,0:T(8,128)(2,1)}), bf16[8,40,512]{2,1,0:T(8,128)(2,1)S(1)}, u32[]{:S(2)}, u32[]{:S(2)}) %all-to-all-start) | async-done | bytes 327712 | tf_op jit(solution)/shard_map/all_to_all | solution.py:126
  17.5 0.0 copy-done
  17.5 0.0 copy-done.2
  17.5 0.0 copy-done.3
  17.5 0.8 %polar.1 = f32[2,32,512]{2,1,0:T(8,128)S(1)} custom-call(s32[2]{0:T(128)S(1)} %copy-done.2, s32[2]{0:T(128)S(1)} %copy-done.3, s32[1]{0:T(128)S(6)} %copy.21.green_steps_ref.steps_ref, f32[1]{0:T(128)S(6)} %copy.20.level_ref.refs_10_, bf16[8,40,512]{2,1,0:T(8,128)(2,1)S(1)} %all-to-all-done.got_ref, f32[256,512]{1,0:T(8,128)S(1)} %bitcast.7), custom_call_target="tpu_custom_call" | custom-call | tf_op jit(solution)/shard_map/polar/pallas_call | solution.py:127
  18.3 2.0 %collective-permute-start.2 = (f16[2,32,512]{2,1,0:T(8,128)(2,1)S(1)}, f16[2,32,512]{2,1,0:T(8,128)(2,1)S(1)}, u32[]{:S(2)}, u32[]{:S(2)}) collective-permute-start(f16[2,32,512]{2,1,0:T(8,128)(2,1)S(1)} %convert_element_type.33), channel_id=1, source_target_pairs={{0,8},{4,12},{8,16},{12,20},{16,24},{20,28},{24,0},{28,4},{1,9},{5... | collective-permute-start | bytes 196616 | tf_op jit(solution)/shard_map/ppermute | solution.py:171
  20.3 0.0 collective-permute-start.1
  20.3 0.6 %collective-permute-start = (f16[2,32,512]{2,1,0:T(8,128)(2,1)S(1)}, f16[2,32,512]{2,1,0:T(8,128)(2,1)S(1)}, u32[]{:S(2)}, u32[]{:S(2)}) collective-permute-start(f16[2,32,512]{2,1,0:T(8,128)(2,1)S(1)} %convert_element_type.33), channel_id=1, source_target_pairs={{0,24},{4,28},{8,0},{12,4},{16,8},{20,12},{24,16},{28,20},{1,25},{... | collective-permute-start | bytes 196616 | tf_op jit(solution)/shard_map/ppermute | solution.py:171
  21.0 5.4 %collective-permute-done = f16[2,32,512]{2,1,0:T(8,128)(2,1)S(1)} collective-permute-done((f16[2,32,512]{2,1,0:T(8,128)(2,1)S(1)}, f16[2,32,512]{2,1,0:T(8,128)(2,1)S(1)}, u32[]{:S(2)}, u32[]{:S(2)}) %collective-permute-start) | collective-permute-done | bytes 65568 | tf_op jit(solution)/shard_map/ppermute | solution.py:171
  26.5 1.8 %collective-permute-done.1 = f16[2,32,512]{2,1,0:T(8,128)(2,1)S(1)} collective-permute-done((f16[2,32,512]{2,1,0:T(8,128)(2,1)S(1)}, f16[2,32,512]{2,1,0:T(8,128)(2,1)S(1)}, u32[]{:S(2)}, u32[]{:S(2)}) %collective-permute-start.1) | collective-permute-done | bytes 65568 | tf_op jit(solution)/shard_map/ppermute | solution.py:171
  28.3 0.0 collective-permute-done.2
  28.3 1.6 %collective-permute-start.6 = (f16[4,32,512]{2,1,0:T(8,128)(2,1)S(1)}, f16[4,32,512]{2,1,0:T(8,128)(2,1)S(1)}, u32[]{:S(2)}, u32[]{:S(2)}) collective-permute-start(f16[4,32,512]{2,1,0:T(8,128)(2,1)S(1)} %get-tuple-element.18), channel_id=1, source_target_pairs={{0,1},{1,0},{2,3},{3,2},{4,5},{5,4},{6,7},{7,6},{8,9},{9,8},{10,11... | collective-permute-start | bytes 393224 | tf_op jit(solution)/shard_map/ppermute | solution.py:186
  29.9 0.3 collective-permute-start.4
  30.2 0.0 collective-permute-start.12
  30.2 0.5 collective-permute-start.5
  30.7 0.0 collective-permute-done.9.two_ref.refs_13_
  30.7 1.8 %collective-permute-start.3 = (f16[4,32,512]{2,1,0:T(8,128)(2,1)S(1)}, f16[4,32,512]{2,1,0:T(8,128)(2,1)S(1)}, u32[]{:S(2)}, u32[]{:S(2)}) collective-permute-start(f16[4,32,512]{2,1,0:T(8,128)(2,1)S(1)} %get-tuple-element.19), channel_id=1, source_target_pairs={{0,4},{4,0},{8,12},{12,8},{16,20},{20,16},{24,28},{28,24},{1,5},{5... | collective-permute-start | bytes 393224 | tf_op jit(solution)/shard_map/ppermute | solution.py:183
  32.5 0.6 chosen.1
  33.0 0.7 %collective-permute-done.6 = f16[4,32,512]{2,1,0:T(8,128)(2,1)S(1)} collective-permute-done((f16[4,32,512]{2,1,0:T(8,128)(2,1)S(1)}, f16[4,32,512]{2,1,0:T(8,128)(2,1)S(1)}, u32[]{:S(2)}, u32[]{:S(2)}) %collective-permute-start.6) | collective-permute-done | bytes 131104 | tf_op jit(solution)/shard_map/ppermute | solution.py:186
  33.7 1.3 %collective-permute-start.11 = (bf16[256,512]{1,0:T(8,128)(2,1)S(1)}, bf16[256,512]{1,0:T(8,128)(2,1)S(1)}, u32[]{:S(2)}, u32[]{:S(2)}) collective-permute-start(bf16[256,512]{1,0:T(8,128)(2,1)S(1)} %chosen.1), channel_id=1, source_target_pairs={{0,4},{4,8},{8,12},{12,16},{16,20},{20,24},{24,28},{1,5},{5,9},{9,... | collective-permute-start | bytes 786440 | tf_op jit(solution)/shard_map/ppermute | solution.py:44
  35.0 1.2 %collective-permute-done.4 = f16[4,32,512]{2,1,0:T(8,128)(2,1)S(1)} collective-permute-done((f16[4,32,512]{2,1,0:T(8,128)(2,1)S(1)}, f16[4,32,512]{2,1,0:T(8,128)(2,1)S(1)}, u32[]{:S(2)}, u32[]{:S(2)}) %collective-permute-start.4) | collective-permute-done | bytes 131104 | tf_op jit(solution)/shard_map/ppermute | solution.py:183
  36.2 1.3 %collective-permute-start.10 = (bf16[256,512]{1,0:T(8,128)(2,1)S(1)}, bf16[256,512]{1,0:T(8,128)(2,1)S(1)}, u32[]{:S(2)}, u32[]{:S(2)}) collective-permute-start(bf16[256,512]{1,0:T(8,128)(2,1)S(1)} %collective-permute-done.9.two_ref.refs_13_), channel_id=1, source_target_pairs={{0,8},{4,12},{8,16},{12,20},{16,24},{20,28},{1,9},{5,13},{9,17},{1... | collective-permute-start | bytes 786440 | tf_op jit(solution)/shard_map/ppermute | solution.py:44
  37.5 0.0 collective-permute-done.5
  37.5 1.5 %collective-permute-start.8 = (f16[4,32,512]{2,1,0:T(8,128)(2,1)S(1)}, f16[4,32,512]{2,1,0:T(8,128)(2,1)S(1)}, u32[]{:S(2)}, u32[]{:S(2)}) collective-permute-start(f16[4,32,512]{2,1,0:T(8,128)(2,1)S(1)} %collective-permute-done.6), channel_id=1, source_target_pairs={{0,4},{4,0},{8,12},{12,8},{16,20},{20,16},{24,28},{28,24},{1,5},{5... | collective-permute-start | bytes 393224 | tf_op jit(solution)/shard_map/ppermute | solution.py:183
  39.0 0.0 collective-permute-done.3
  39.0 2.5 %collective-permute-start.7 = (f16[4,32,512]{2,1,0:T(8,128)(2,1)S(1)}, f16[4,32,512]{2,1,0:T(8,128)(2,1)S(1)}, u32[]{:S(2)}, u32[]{:S(2)}) collective-permute-start(f16[4,32,512]{2,1,0:T(8,128)(2,1)S(1)} %collective-permute-done.3), channel_id=1, source_target_pairs={{0,1},{1,0},{2,3},{3,2},{4,5},{5,4},{6,7},{7,6},{8,9},{9,8},{10,11... | collective-permute-start | bytes 393224 | tf_op jit(solution)/shard_map/ppermute | solution.py:186
  41.7 4.4 %collective-permute-done.8 = f16[4,32,512]{2,1,0:T(8,128)(2,1)S(1)} collective-permute-done((f16[4,32,512]{2,1,0:T(8,128)(2,1)S(1)}, f16[4,32,512]{2,1,0:T(8,128)(2,1)S(1)}, u32[]{:S(2)}, u32[]{:S(2)}) %collective-permute-start.8) | collective-permute-done | bytes 131104 | tf_op jit(solution)/shard_map/ppermute | solution.py:183
  46.1 0.0 collective-permute-done.7
  46.2 0.0 collective-permute-done.12.refs_16_
  46.2 0.0 collective-permute-done.11.refs_15_
  46.2 2.3 %collective-permute-done.10.refs_14_ = bf16[256,512]{1,0:T(8,128)(2,1)S(1)} collective-permute-done((bf16[256,512]{1,0:T(8,128)(2,1)S(1)}, bf16[256,512]{1,0:T(8,128)(2,1)S(1)}, u32[]{:S(2)}, u32[]{:S(2)}) %collective-permute-start.10) | collective-permute-done | bytes 262176 | tf_op jit(solution)/shard_map/ppermute | solution.py:44
  48.5 4.1 %dyson.1 = (bf16[2,256,512]{2,1,0:T(8,128)(2,1)}, f32[264,512]{1,0:T(8,128)S(1)}, f32[256,512]{1,0:T(8,128)S(1)}, f32[8,512]{1,0:T(8,128)S(1)}) custom-call(f32[4,32,512]{2,1,0:T(8,128)S(1)} %convert_element_type.34.refs_0_, f32[4,32,512]{2,1,0:T(8,128)S(1)} %convert_element_type.35.refs_1_, f32[4,32,512]{2,1,0:T(8,128)S(1)} %convert_element_type.36.refs_2_, ...), custom_call_target="tpu_custom_call" | custom-call | tf_op jit(solution)/shard_map/dyson/pallas_call | solution.py:292
  52.6 1.6 %collective-permute-start.13 = (f16[264,512]{1,0:T(8,128)(2,1)S(1)}, f16[264,512]{1,0:T(8,128)(2,1)S(1)}, u32[]{:S(2)}, u32[]{:S(2)}) collective-permute-start(f16[264,512]{1,0:T(8,128)(2,1)S(1)} %convert_element_type.42), channel_id=1, source_target_pairs={{0,1},{1,0},{2,3},{3,2},{4,5},{5,4},{6,7},{7,6},{8,9},{9,8},{10,11... | collective-permute-start | bytes 811016 | tf_op jit(solution)/shard_map/ppermute | solution.py:380
  54.2 0.4 begin.1
  54.6 5.2 %collective-permute-done.13 = f16[264,512]{1,0:T(8,128)(2,1)S(1)} collective-permute-done((f16[264,512]{1,0:T(8,128)(2,1)S(1)}, f16[264,512]{1,0:T(8,128)(2,1)S(1)}, u32[]{:S(2)}, u32[]{:S(2)}) %collective-permute-start.13) | collective-permute-done | bytes 270368 | tf_op jit(solution)/shard_map/ppermute | solution.py:380
  59.9 0.1 convert_element_type.43.theirs_ref
  59.9 1.7 %finish.1 = f32[256,512]{1,0:T(8,128)} custom-call(s32[1]{0:T(128)S(6)} %copy.21.green_steps_ref.steps_ref, f32[256,512]{1,0:T(8,128)S(1)} %get-tuple-element.9.step_ref, f32[256,512]{1,0:T(8,128)S(1)} %get-tuple-element.12.square_ref, bf16[256,512]{1,0:T(8,128)(2,1)S(1)} %get-tuple-element.13.high_ref, bf16[256,512]{1,0:T(8,128)(2,1)S(1)} %get-tuple-element.14.low_ref, ...), custom_call_target="tpu_custom_call" | custom-call | tf_op jit(solution)/shard_map/finish/pallas_call | solution.py:391
  (17 shorter events, 0.3 us)
Async XLA Ops:
  1.3 7.8 %copy-start.1 = (bf16[1,1,256,512]{3,2,1,0:T(8,128)(2,1)S(1)}, bf16[1,1,256,512]{3,2,1,0:T(8,128)(2,1)}, u32[]{:S(2)}) copy-start(bf16[1,1,256,512]{3,2,1,0:T(8,128)(2,1)} %param.8) | copy-start | bytes 786436
  3.0 14.5 %copy-start = (f32[1,256,512]{2,1,0:T(8,128)S(1)}, f32[1,256,512]{2,1,0:T(8,128)}, u32[]{:S(2)}) copy-start(f32[1,256,512]{2,1,0:T(8,128)} %param.11) | copy-start | bytes 1572868
  3.0 14.5 %all-to-all-start = ((bf16[8,40,512]{2,1,0:T(8,128)(2,1)}), bf16[8,40,512]{2,1,0:T(8,128)(2,1)S(1)}, u32[]{:S(2)}, u32[]{:S(2)}) async-start(bf16[8,40,512]{2,1,0:T(8,128)(2,1)} %prepare.1), calls=%async_computation | async-start | bytes 655360 | tf_op jit(solution)/shard_map/all_to_all | solution.py:126
  9.1 21.6 %collective-permute-start.9 = (bf16[256,512]{1,0:T(8,128)(2,1)S(1)}, bf16[256,512]{1,0:T(8,128)(2,1)S(1)}, u32[]{:S(2)}, u32[]{:S(2)}) collective-permute-start(bf16[256,512]{1,0:T(8,128)(2,1)S(1)} %bitcast.10), channel_id=1, source_target_pairs={{0,8},{4,12},{8,16},{12,20},{16,24},{20,28},{1,9},{5,13},{9,17},{1... | collective-permute-start | bytes 786440 | tf_op jit(solution)/shard_map/ppermute | solution.py:44
  11.8 5.7 %copy-start.2 = (s32[2]{0:T(128)S(1)}, s32[2]{0:T(128)}, u32[]{:S(2)}) copy-start(s32[2]{0:T(128)} %refs_8_.1) | copy-start | bytes 28
  11.8 5.7 %copy-start.3 = (s32[2]{0:T(128)S(1)}, s32[2]{0:T(128)}, u32[]{:S(2)}) copy-start(s32[2]{0:T(128)} %refs_9_.1) | copy-start | bytes 28
  18.3 9.9 %collective-permute-start.2 = (f16[2,32,512]{2,1,0:T(8,128)(2,1)S(1)}, f16[2,32,512]{2,1,0:T(8,128)(2,1)S(1)}, u32[]{:S(2)}, u32[]{:S(2)}) collective-permute-start(f16[2,32,512]{2,1,0:T(8,128)(2,1)S(1)} %convert_element_type.33), channel_id=1, source_target_pairs={{0,8},{4,12},{8,16},{12,20},{16,24},{20,28},{24,0},{28,4},{1,9},{5... | collective-permute-start | bytes 196616 | tf_op jit(solution)/shard_map/ppermute | solution.py:171
  20.3 8.0 %collective-permute-start.1 = (f16[2,32,512]{2,1,0:T(8,128)(2,1)S(1)}, f16[2,32,512]{2,1,0:T(8,128)(2,1)S(1)}, u32[]{:S(2)}, u32[]{:S(2)}) collective-permute-start(f16[2,32,512]{2,1,0:T(8,128)(2,1)S(1)} %convert_element_type.33), channel_id=1, source_target_pairs={{0,16},{4,20},{8,24},{12,28},{16,0},{20,4},{24,8},{28,12},{1,17},{... | collective-permute-start | bytes 196616 | tf_op jit(solution)/shard_map/ppermute | solution.py:171
  20.3 6.2 %collective-permute-start = (f16[2,32,512]{2,1,0:T(8,128)(2,1)S(1)}, f16[2,32,512]{2,1,0:T(8,128)(2,1)S(1)}, u32[]{:S(2)}, u32[]{:S(2)}) collective-permute-start(f16[2,32,512]{2,1,0:T(8,128)(2,1)S(1)} %convert_element_type.33), channel_id=1, source_target_pairs={{0,24},{4,28},{8,0},{12,4},{16,8},{20,12},{24,16},{28,20},{1,25},{... | collective-permute-start | bytes 196616 | tf_op jit(solution)/shard_map/ppermute | solution.py:171
  28.3 5.4 %collective-permute-start.6 = (f16[4,32,512]{2,1,0:T(8,128)(2,1)S(1)}, f16[4,32,512]{2,1,0:T(8,128)(2,1)S(1)}, u32[]{:S(2)}, u32[]{:S(2)}) collective-permute-start(f16[4,32,512]{2,1,0:T(8,128)(2,1)S(1)} %get-tuple-element.18), channel_id=1, source_target_pairs={{0,1},{1,0},{2,3},{3,2},{4,5},{5,4},{6,7},{7,6},{8,9},{9,8},{10,11... | collective-permute-start | bytes 393224 | tf_op jit(solution)/shard_map/ppermute | solution.py:186
  29.9 6.3 %collective-permute-start.4 = (f16[4,32,512]{2,1,0:T(8,128)(2,1)S(1)}, f16[4,32,512]{2,1,0:T(8,128)(2,1)S(1)}, u32[]{:S(2)}, u32[]{:S(2)}) collective-permute-start(f16[4,32,512]{2,1,0:T(8,128)(2,1)S(1)} %get-tuple-element.18), channel_id=1, source_target_pairs={{0,4},{4,0},{8,12},{12,8},{16,20},{20,16},{24,28},{28,24},{1,5},{5... | collective-permute-start | bytes 393224 | tf_op jit(solution)/shard_map/ppermute | solution.py:183
  30.2 16.0 %collective-permute-start.12 = (bf16[256,512]{1,0:T(8,128)(2,1)S(1)}, bf16[256,512]{1,0:T(8,128)(2,1)S(1)}, u32[]{:S(2)}, u32[]{:S(2)}) collective-permute-start(bf16[256,512]{1,0:T(8,128)(2,1)S(1)} %bitcast.11), channel_id=1, source_target_pairs={{0,2},{2,0},{1,3},{3,1},{4,6},{6,4},{5,7},{7,5},{8,10},{10,8},{9,1... | collective-permute-start | bytes 786440 | tf_op jit(solution)/shard_map/ppermute | solution.py:371
  30.2 7.3 %collective-permute-start.5 = (f16[4,32,512]{2,1,0:T(8,128)(2,1)S(1)}, f16[4,32,512]{2,1,0:T(8,128)(2,1)S(1)}, u32[]{:S(2)}, u32[]{:S(2)}) collective-permute-start(f16[4,32,512]{2,1,0:T(8,128)(2,1)S(1)} %get-tuple-element.19), channel_id=1, source_target_pairs={{0,1},{1,0},{2,3},{3,2},{4,5},{5,4},{6,7},{7,6},{8,9},{9,8},{10,11... | collective-permute-start | bytes 393224 | tf_op jit(solution)/shard_map/ppermute | solution.py:186
  30.7 8.3 %collective-permute-start.3 = (f16[4,32,512]{2,1,0:T(8,128)(2,1)S(1)}, f16[4,32,512]{2,1,0:T(8,128)(2,1)S(1)}, u32[]{:S(2)}, u32[]{:S(2)}) collective-permute-start(f16[4,32,512]{2,1,0:T(8,128)(2,1)S(1)} %get-tuple-element.19), channel_id=1, source_target_pairs={{0,4},{4,0},{8,12},{12,8},{16,20},{20,16},{24,28},{28,24},{1,5},{5... | collective-permute-start | bytes 393224 | tf_op jit(solution)/shard_map/ppermute | solution.py:183
  33.7 12.5 %collective-permute-start.11 = (bf16[256,512]{1,0:T(8,128)(2,1)S(1)}, bf16[256,512]{1,0:T(8,128)(2,1)S(1)}, u32[]{:S(2)}, u32[]{:S(2)}) collective-permute-start(bf16[256,512]{1,0:T(8,128)(2,1)S(1)} %chosen.1), channel_id=1, source_target_pairs={{0,4},{4,8},{8,12},{12,16},{16,20},{20,24},{24,28},{1,5},{5,9},{9,... | collective-permute-start | bytes 786440 | tf_op jit(solution)/shard_map/ppermute | solution.py:44
  36.2 12.2 %collective-permute-start.10 = (bf16[256,512]{1,0:T(8,128)(2,1)S(1)}, bf16[256,512]{1,0:T(8,128)(2,1)S(1)}, u32[]{:S(2)}, u32[]{:S(2)}) collective-permute-start(bf16[256,512]{1,0:T(8,128)(2,1)S(1)} %collective-permute-done.9.two_ref.refs_13_), channel_id=1, source_target_pairs={{0,8},{4,12},{8,16},{12,20},{16,24},{20,28},{1,9},{5,13},{9,17},{1... | collective-permute-start | bytes 786440 | tf_op jit(solution)/shard_map/ppermute | solution.py:44
  37.5 8.6 %collective-permute-start.8 = (f16[4,32,512]{2,1,0:T(8,128)(2,1)S(1)}, f16[4,32,512]{2,1,0:T(8,128)(2,1)S(1)}, u32[]{:S(2)}, u32[]{:S(2)}) collective-permute-start(f16[4,32,512]{2,1,0:T(8,128)(2,1)S(1)} %collective-permute-done.6), channel_id=1, source_target_pairs={{0,4},{4,0},{8,12},{12,8},{16,20},{20,16},{24,28},{28,24},{1,5},{5... | collective-permute-start | bytes 393224 | tf_op jit(solution)/shard_map/ppermute | solution.py:183
  39.0 7.1 %collective-permute-start.7 = (f16[4,32,512]{2,1,0:T(8,128)(2,1)S(1)}, f16[4,32,512]{2,1,0:T(8,128)(2,1)S(1)}, u32[]{:S(2)}, u32[]{:S(2)}) collective-permute-start(f16[4,32,512]{2,1,0:T(8,128)(2,1)S(1)} %collective-permute-done.3), channel_id=1, source_target_pairs={{0,1},{1,0},{2,3},{3,2},{4,5},{5,4},{6,7},{7,6},{8,9},{9,8},{10,11... | collective-permute-start | bytes 393224 | tf_op jit(solution)/shard_map/ppermute | solution.py:186
  52.6 7.2 %collective-permute-start.13 = (f16[264,512]{1,0:T(8,128)(2,1)S(1)}, f16[264,512]{1,0:T(8,128)(2,1)S(1)}, u32[]{:S(2)}, u32[]{:S(2)}) collective-permute-start(f16[264,512]{1,0:T(8,128)(2,1)S(1)} %convert_element_type.42), channel_id=1, source_target_pairs={{0,1},{1,0},{2,3},{3,2},{4,5},{5,4},{6,7},{7,6},{8,9},{9,8},{10,11... | collective-permute-start | bytes 811016 | tf_op jit(solution)/shard_map/ppermute | solution.py:380

commit v8 on v7

--- a/solution.py
+++ b/solution.py
@@ -40,8 +40,7 @@
 
 def shifted(block, axis, distance):
     count = lax.axis_size(axis)
-    route = [(i, i + distance) for i in range(count - distance)]
-    return lax.ppermute(block, axis, route)
+    return lax.ppermute(block, axis, [(i, (i + distance) % count) for i in range(count)])
 
 
 def in_squares():
@@ -214,49 +213,76 @@
     return (first + second) * jnp.exp2(exponent)
 
 
-def dyson_kernel(pieces, offsets_ref, steps_ref, level_ref, bare_ref, hamiltonian_ref, two_ref,
+def corner_start(place, block, rows):
+    x, rep = lax.axis_index("energy") % 2, lax.axis_index("rep")
+    at_x = 1 - x if place % 2 else x
+    at_rep = 1 - rep if place >= 2 else rep
+    return pl.multiple_of(at_rep * rows + at_x * block, block)
+
+
+def early_kernel(pieces, bare_ref, once_ref, high, low):
+    rows, width = bare_ref.shape
+    if len(pieces) == 1:
+        for f in range(FREQS):
+            high[f], low[f] = halves(pieces[0][f])
+    else:
+        outer, share, _ = pieces[0].shape
+        block = outer * share
+        empty = jnp.zeros((block, width), jnp.bfloat16)
+        for f in range(FREQS):
+            for place in range(4):
+                at = pl.ds(corner_start(place, block, rows), block)
+                if place == 3:
+                    high[f, at, :], low[f, at, :] = empty, empty
+                else:
+                    upper, lower = halves(pieces[place * FREQS + f][...].reshape(block, width))
+                    high[f, at, :], low[f, at, :] = upper, lower
+    bare = bare_ref[...]
+    for f in range(FREQS):
+        once_ref[f] = bare + product(bare, high[f], low[f])
+
+
+def dyson_kernel(apart, early, offsets_ref, steps_ref, level_ref, bare_ref, hamiltonian_ref, two_ref,
                  four_ref, odd_ref, beside_refs, screened_ref, packed_ref, step_ref, own_ref,
                  high, low, made, hamiltonian_rows, made_sem, hamiltonian_sem):
+    once_ref, high_ref, low_ref = early
     rows, width = bare_ref.shape
     entry_scale = width ** -0.5
     read = pltpu.make_async_copy(hamiltonian_ref, hamiltonian_rows, hamiltonian_sem)
     read.start()
     energy, rep = lax.axis_index("energy"), lax.axis_index("rep")
-    if len(pieces) == 1:
-        for f in range(FREQS):
-            high[f], low[f] = halves(pieces[0][f])
-    else:
-        outer, share, _ = pieces[0].shape
-        x = energy % 2
-        corners = [(x, rep), (1 - x, rep), (x, 1 - rep), (1 - x, 1 - rep)]
-        for place, (at_x, at_rep) in enumerate(corners):
-            start = pl.multiple_of(at_rep * rows + at_x * outer * share, outer * share)
-            for f in range(FREQS):
-                piece = pieces[place * FREQS + f][...].reshape(outer * share, width)
-                upper, lower = halves(piece)
-                high[f, pl.ds(start, outer * share), :] = upper
-                low[f, pl.ds(start, outer * share), :] = lower
     bare = bare_ref[...]
-    once = [bare + product(bare, high[f], low[f]) for f in range(FREQS)]
+    once = [once_ref[f] for f in range(FREQS)]
     at = jnp.where(steps_ref[1] > steps_ref[0], 1, 0)
+    high[...], low[...] = high_ref[at], low_ref[at]
+    if apart:
+        outer, share, _ = apart[0].shape
+        block = outer * share
+        start = corner_start(3, block, rows)
+        beyond = bare_ref[:, pl.ds(start, block)]
+        parts = [halves(ref[...].reshape(block, width)) for ref in apart]
+        once = [once[f] + product(beyond, *parts[f]) for f in range(FREQS)]
+        high[pl.ds(start, block), :] = jnp.where(at == 0, parts[0][0], parts[1][0])
+        low[pl.ds(start, block), :] = jnp.where(at == 0, parts[0][1], parts[1][1])
     last = jnp.where(at == 0, once[0], once[1])
-    upper, lower = high[at], low[at]
+    upper, lower = high[...], low[...]
     twice = last + product(product(last, upper, lower), upper, lower)
     other = jnp.minimum(offsets_ref[0], offsets_ref[1])
-    less = jnp.where(other == 2, two_ref[...].astype(jnp.float32), odd_ref[...].astype(jnp.float32))
-    four = four_ref[...].astype(jnp.float32)
+    less = jnp.where(other == 2, two_ref[...], odd_ref[...])
+    four = four_ref[...]
     energy_terms = jnp.zeros((rows, width), jnp.float32)
     for f in range(FREQS):
         count = steps_ref[f]
         value = jnp.where(count == 0, bare, jnp.where(count == 1, once[f], twice))
         value = value.astype(jnp.bfloat16)
         made[f] = value
-        lowered = jnp.where(offsets_ref[f] == SHIFTS, four, less)
+        lowered = jnp.where(offsets_ref[f] == SHIFTS, four, less).astype(jnp.float32)
+        lowered = jnp.where(energy >= offsets_ref[f], lowered, 0.0)
         energy_terms += lowered * value.astype(jnp.float32)
-    beside = sum(ref[...].astype(jnp.float32) for ref in beside_refs)
     write = pltpu.make_async_copy(made, screened_ref, made_sem)
     write.start()
     read.wait()
+    beside = sum(ref[...].astype(jnp.float32) for ref in beside_refs)
     rest = hamiltonian_rows[...] - entry_scale * energy_terms - (0.5 * entry_scale) * beside
     col = lax.broadcasted_iota(jnp.int32, (rows, width), 1)
     row = lax.broadcasted_iota(jnp.int32, (rows, width), 0) + rep * rows
@@ -282,12 +308,28 @@
 
 def dyson_rows(pieces, offsets, steps, level, bare, hamiltonian, two, four, odd, beside):
     rows, width = bare.shape
-    count, sides = len(pieces), len(beside)
+    sides = len(beside)
+    known, apart = (pieces, []) if len(pieces) == 1 else (pieces[:-FREQS], pieces[-FREQS:])
+    count = len(known)
+
+    def first_kernel(*refs):
+        early_kernel(refs[:count], *refs[count:])
+
+    early = pl.pallas_call(
+        first_kernel,
+        out_shape=(jax.ShapeDtypeStruct((FREQS, rows, width), jnp.float32),)
+        + (jax.ShapeDtypeStruct((FREQS, width, width), jnp.bfloat16),) * 2,
+        in_specs=[in_vmem] * (count + 1),
+        out_specs=(in_vmem,) * 3,
+        compiler_params=large,
+        name="early",
+    )(*known, bare)
 
     def kernel(*refs):
-        own, rest = refs[:count], refs[count:]
+        far, rest = refs[:len(apart)], refs[len(apart):]
+        done, rest = rest[:3], rest[3:]
         named, rest = rest[:8], rest[8:]
-        dyson_kernel(own, *named, rest[:sides], *rest[sides:])
+        dyson_kernel(far, done, *named, rest[:sides], *rest[sides:])
 
     return pl.pallas_call(
         kernel,
@@ -297,14 +339,15 @@
             jax.ShapeDtypeStruct((rows, width), jnp.float32),
             jax.ShapeDtypeStruct((EXTRA, width), jnp.float32),
         ),
-        in_specs=[in_vmem] * count + [in_smem] * 3 + [in_vmem, in_hbm] + [in_vmem] * (3 + sides),
+        in_specs=[in_vmem] * (len(apart) + 3) + [in_smem] * 3 + [in_vmem, in_hbm]
+        + [in_vmem] * (3 + sides),
         out_specs=(in_hbm,) + (in_vmem,) * 3,
-        scratch_shapes=[VMEM((FREQS, width, width), jnp.bfloat16)] * 2
+        scratch_shapes=[VMEM((width, width), jnp.bfloat16)] * 2
         + [VMEM((FREQS, rows, width), jnp.bfloat16), VMEM((rows, width), jnp.float32)]
         + [pltpu.SemaphoreType.DMA] * 2,
         compiler_params=large,
         name="dyson",
-    )(*pieces, offsets, steps, level, bare, held(hamiltonian), two, four, odd, *beside)
+    )(*apart, *early, offsets, steps, level, bare, held(hamiltonian), two, four, odd, *beside)
 
 
 def columns(value, first):

time: 62 us -> 69.3 us (1.12)
  the two profiles are of different devices: /device:TPU:26 before, /device:TPU:0 now
where the time goes in v8:
time: 69.3 us; the launch traced here: 69 us
  waiting for transfers between devices  31.2 us (45%)
  starting transfers between devices  24.6 us (35%)
  Pallas kernels  9.94 us (14%)
  between operations  2.85 us (4%)
    all_to_all x1, waiting for transfers between devices, polar_share(): got = lax.all_to_all(sent, 'energy', 0, 0, tiled=True)  14.8 us
    all_to_all x1, starting transfers between devices, polar_share(): got = lax.all_to_all(sent, 'energy', 0, 0, tiled=True)  7.42 us
    ppermute x1, waiting for transfers between devices, body(): lax.ppermute(packed.astype(coded), 'rep', [(0, 1), (1, 0)])  6.46 us
    ppermute x3, waiting for transfers between devices, along_x(): return lax.ppermute(part, 'energy', [(e, e ^ 1) for e in range(energies)])  5.75 us
    ppermute x3, starting transfers between devices, shifted(): lax.ppermute(block, axis, [(i, (i + distance) % count) for i in range(cou...  5.02 us
    ppermute x3, starting transfers between devices, gather_energy(): got = lax.ppermute(chunk, 'energy', route)  3.88 us
    ppermute x3, starting transfers between devices, along_rep(): return lax.ppermute(part, 'rep', [(0, 1), (1, 0)])  3.68 us
    pallas_call x1, Pallas kernels, dyson_rows(): pl.pallas_call(kernel, out_shape=(jax.ShapeDtypeStruct((FREQS, rows, widt...  3.42 us
  transfers between devices with their start and end apart: 15, of which 8 were waited for; matrix products, arithmetic and copies ran while one was open for 0% of the time, Pallas kernels for 5%

profile of v8, /device:TPU:0, one launch (start us, length us, event | category | flops | bytes accessed | tf_op | source)
XLA Modules:
  0.0 69.0 jit_solution(11473722326648335656)
XLA Ops:
  1.3 0.0 copy-start.1
  1.3 1.7 %prepare.1 = bf16[8,40,512]{2,1,0:T(8,128)(2,1)} custom-call(f32[1]{0:T(128)S(6)} %copy.19.weight_ref, bf16[256,512]{1,0:T(8,128)(2,1)} %bitcast.10), custom_call_target="tpu_custom_call" | custom-call | tf_op jit(solution)/shard_map/prepare/pallas_call | solution.py:112
  3.0 0.0 copy-start
  3.0 7.4 %all-to-all-start = ((bf16[8,40,512]{2,1,0:T(8,128)(2,1)}), bf16[8,40,512]{2,1,0:T(8,128)(2,1)S(1)}, u32[]{:S(2)}, u32[]{:S(2)}) async-start(bf16[8,40,512]{2,1,0:T(8,128)(2,1)} %prepare.1), calls=%async_computation | async-start | bytes 655360 | tf_op jit(solution)/shard_map/all_to_all | solution.py:125
  10.4 0.0 copy-done.1
  10.4 2.0 %collective-permute-start.9 = (bf16[256,512]{1,0:T(8,128)(2,1)S(1)}, bf16[256,512]{1,0:T(8,128)(2,1)S(1)}, u32[]{:S(2)}, u32[]{:S(2)}) collective-permute-start(bf16[256,512]{1,0:T(8,128)(2,1)S(1)} %bitcast.11), channel_id=1, source_target_pairs={{0,8},{4,12},{8,16},{12,20},{16,24},{20,28},{24,0},{28,4},{1,9},{5... | collective-permute-start | bytes 786440 | tf_op jit(solution)/shard_map/ppermute | solution.py:43
  13.7 0.0 copy-start.2
  13.7 0.0 copy-start.3
  13.8 14.8 %all-to-all-done.got_ref = bf16[8,40,512]{2,1,0:T(8,128)(2,1)S(1)} async-done(((bf16[8,40,512]{2,1,0:T(8,128)(2,1)}), bf16[8,40,512]{2,1,0:T(8,128)(2,1)S(1)}, u32[]{:S(2)}, u32[]{:S(2)}) %all-to-all-start) | async-done | bytes 327712 | tf_op jit(solution)/shard_map/all_to_all | solution.py:125
  28.6 0.0 copy-done
  28.6 0.0 copy-done.2
  28.6 0.0 copy-done.3
  28.6 0.8 %polar.1 = f32[2,32,512]{2,1,0:T(8,128)S(1)} custom-call(s32[2]{0:T(128)S(1)} %copy-done.2, s32[2]{0:T(128)S(1)} %copy-done.3, s32[1]{0:T(128)S(6)} %copy.21.green_steps_ref.steps_ref, f32[1]{0:T(128)S(6)} %copy.20.level_ref.refs_7_, bf16[8,40,512]{2,1,0:T(8,128)(2,1)S(1)} %all-to-all-done.got_ref, f32[256,512]{1,0:T(8,128)S(1)} %bitcast.7), custom_call_target="tpu_custom_call" | custom-call | tf_op jit(solution)/shard_map/polar/pallas_call | solution.py:126
  29.5 0.6 collective-permute-start.2
  30.1 0.0 collective-permute-start.1
  30.1 3.3 %collective-permute-start = (f16[2,32,512]{2,1,0:T(8,128)(2,1)S(1)}, f16[2,32,512]{2,1,0:T(8,128)(2,1)S(1)}, u32[]{:S(2)}, u32[]{:S(2)}) collective-permute-start(f16[2,32,512]{2,1,0:T(8,128)(2,1)S(1)} %convert_element_type.33), channel_id=1, source_target_pairs={{0,24},{4,28},{8,0},{12,4},{16,8},{20,12},{24,16},{28,20},{1,25},{... | collective-permute-start | bytes 196616 | tf_op jit(solution)/shard_map/ppermute | solution.py:170
  33.4 3.0 %collective-permute-done = f16[2,32,512]{2,1,0:T(8,128)(2,1)S(1)} collective-permute-done((f16[2,32,512]{2,1,0:T(8,128)(2,1)S(1)}, f16[2,32,512]{2,1,0:T(8,128)(2,1)S(1)}, u32[]{:S(2)}, u32[]{:S(2)}) %collective-permute-start) | collective-permute-done | bytes 65568 | tf_op jit(solution)/shard_map/ppermute | solution.py:170
  36.4 0.2 collective-permute-done.1
  36.6 0.0 collective-permute-done.2
  36.7 1.2 %collective-permute-start.7 = (f16[4,32,512]{2,1,0:T(8,128)(2,1)S(1)}, f16[4,32,512]{2,1,0:T(8,128)(2,1)S(1)}, u32[]{:S(2)}, u32[]{:S(2)}) collective-permute-start(f16[4,32,512]{2,1,0:T(8,128)(2,1)S(1)} %get-tuple-element.24), channel_id=1, source_target_pairs={{0,4},{4,0},{8,12},{12,8},{16,20},{20,16},{24,28},{28,24},{1,5},{5... | collective-permute-start | bytes 393224 | tf_op jit(solution)/shard_map/ppermute | solution.py:182
  37.9 1.5 %collective-permute-start.5 = (f16[4,32,512]{2,1,0:T(8,128)(2,1)S(1)}, f16[4,32,512]{2,1,0:T(8,128)(2,1)S(1)}, u32[]{:S(2)}, u32[]{:S(2)}) collective-permute-start(f16[4,32,512]{2,1,0:T(8,128)(2,1)S(1)} %get-tuple-element.24), channel_id=1, source_target_pairs={{0,1},{1,0},{2,3},{3,2},{4,5},{5,4},{6,7},{7,6},{8,9},{9,8},{10,11... | collective-permute-start | bytes 393224 | tf_op jit(solution)/shard_map/ppermute | solution.py:185
  39.4 0.0 collective-permute-start.12
  39.4 0.5 collective-permute-start.8
  39.9 0.0 collective-permute-done.9.two_ref.refs_10_
  39.9 0.9 %collective-permute-start.3 = (f16[4,32,512]{2,1,0:T(8,128)(2,1)S(1)}, f16[4,32,512]{2,1,0:T(8,128)(2,1)S(1)}, u32[]{:S(2)}, u32[]{:S(2)}) collective-permute-start(f16[4,32,512]{2,1,0:T(8,128)(2,1)S(1)} %get-tuple-element.25), channel_id=1, source_target_pairs={{0,4},{4,0},{8,12},{12,8},{16,20},{20,16},{24,28},{28,24},{1,5},{5... | collective-permute-start | bytes 393224 | tf_op jit(solution)/shard_map/ppermute | solution.py:182
  40.8 0.6 chosen.1
  41.4 0.3 collective-permute-done.7
  41.7 1.1 %collective-permute-start.11 = (bf16[256,512]{1,0:T(8,128)(2,1)S(1)}, bf16[256,512]{1,0:T(8,128)(2,1)S(1)}, u32[]{:S(2)}, u32[]{:S(2)}) collective-permute-start(bf16[256,512]{1,0:T(8,128)(2,1)S(1)} %chosen.1), channel_id=1, source_target_pairs={{0,4},{4,8},{8,12},{12,16},{16,20},{20,24},{24,28},{28,0},{1,5},{5... | collective-permute-start | bytes 786440 | tf_op jit(solution)/shard_map/ppermute | solution.py:43
  42.8 0.4 collective-permute-done.5
  43.2 1.9 %collective-permute-start.10 = (bf16[256,512]{1,0:T(8,128)(2,1)S(1)}, bf16[256,512]{1,0:T(8,128)(2,1)S(1)}, u32[]{:S(2)}, u32[]{:S(2)}) collective-permute-start(bf16[256,512]{1,0:T(8,128)(2,1)S(1)} %collective-permute-done.9.two_ref.refs_10_), channel_id=1, source_target_pairs={{0,8},{4,12},{8,16},{12,20},{16,24},{20,28},{24,0},{28,4},{1,9},{5... | collective-permute-start | bytes 786440 | tf_op jit(solution)/shard_map/ppermute | solution.py:43
  45.1 0.5 collective-permute-done.8
  45.6 0.9 %collective-permute-start.6 = (f16[4,32,512]{2,1,0:T(8,128)(2,1)S(1)}, f16[4,32,512]{2,1,0:T(8,128)(2,1)S(1)}, u32[]{:S(2)}, u32[]{:S(2)}) collective-permute-start(f16[4,32,512]{2,1,0:T(8,128)(2,1)S(1)} %collective-permute-done.5), channel_id=1, source_target_pairs={{0,4},{4,0},{8,12},{12,8},{16,20},{20,16},{24,28},{28,24},{1,5},{5... | collective-permute-start | bytes 393224 | tf_op jit(solution)/shard_map/ppermute | solution.py:182
  46.6 0.0 collective-permute-done.3
  46.6 1.7 %collective-permute-start.4 = (f16[4,32,512]{2,1,0:T(8,128)(2,1)S(1)}, f16[4,32,512]{2,1,0:T(8,128)(2,1)S(1)}, u32[]{:S(2)}, u32[]{:S(2)}) collective-permute-start(f16[4,32,512]{2,1,0:T(8,128)(2,1)S(1)} %collective-permute-done.3), channel_id=1, source_target_pairs={{0,1},{1,0},{2,3},{3,2},{4,5},{5,4},{6,7},{7,6},{8,9},{9,8},{10,11... | collective-permute-start | bytes 393224 | tf_op jit(solution)/shard_map/ppermute | solution.py:185
  48.4 1.3 %early.1 = (f32[2,256,512]{2,1,0:T(8,128)S(1)}, bf16[2,512,512]{2,1,0:T(8,128)(2,1)S(1)}, bf16[2,512,512]{2,1,0:T(8,128)(2,1)S(1)}) custom-call(f32[4,32,512]{2,1,0:T(8,128)S(1)} %convert_element_type.36.refs_0_, f32[4,32,512]{2,1,0:T(8,128)S(1)} %convert_element_type.37.refs_1_, f32[4,32,512]{2,1,0:T(8,128)S(1)} %convert_element_type.38.refs_2_, ...), custom_call_target="tpu_custom_call" | custom-call | tf_op jit(solution)/shard_map/early/pallas_call | solution.py:318
  49.7 5.4 %collective-permute-done.6 = f16[4,32,512]{2,1,0:T(8,128)(2,1)S(1)} collective-permute-done((f16[4,32,512]{2,1,0:T(8,128)(2,1)S(1)}, f16[4,32,512]{2,1,0:T(8,128)(2,1)S(1)}, u32[]{:S(2)}, u32[]{:S(2)}) %collective-permute-start.6) | collective-permute-done | bytes 131104 | tf_op jit(solution)/shard_map/ppermute | solution.py:182
  55.1 0.0 collective-permute-done.4
  55.2 0.0 collective-permute-done.12.refs_13_
  55.2 0.0 collective-permute-done.11.refs_12_
  55.2 0.0 collective-permute-done.10.refs_11_
  55.2 3.4 %dyson.1 = (bf16[2,256,512]{2,1,0:T(8,128)(2,1)}, f32[264,512]{1,0:T(8,128)S(1)}, f32[256,512]{1,0:T(8,128)S(1)}, f32[8,512]{1,0:T(8,128)S(1)}) custom-call(f32[4,32,512]{2,1,0:T(8,128)S(1)} %convert_element_type.34.refs_0_, f32[4,32,512]{2,1,0:T(8,128)S(1)} %convert_element_type.35.refs_1_, f32[2,256,512]{2,1,0:T(8,128)S(1)} %get-tuple-element.12.refs_2_, ...), custom_call_target="tpu_custom_call" | custom-call | tf_op jit(solution)/shard_map/dyson/pallas_call | solution.py:334
  58.7 1.6 %collective-permute-start.13 = (f16[264,512]{1,0:T(8,128)(2,1)S(1)}, f16[264,512]{1,0:T(8,128)(2,1)S(1)}, u32[]{:S(2)}, u32[]{:S(2)}) collective-permute-start(f16[264,512]{1,0:T(8,128)(2,1)S(1)} %convert_element_type.42), channel_id=1, source_target_pairs={{0,1},{1,0},{2,3},{3,2},{4,5},{5,4},{6,7},{7,6},{8,9},{9,8},{10,11... | collective-permute-start | bytes 811016 | tf_op jit(solution)/shard_map/ppermute | solution.py:423
  60.3 0.4 begin.1
  60.7 6.5 %collective-permute-done.13 = f16[264,512]{1,0:T(8,128)(2,1)S(1)} collective-permute-done((f16[264,512]{1,0:T(8,128)(2,1)S(1)}, f16[264,512]{1,0:T(8,128)(2,1)S(1)}, u32[]{:S(2)}, u32[]{:S(2)}) %collective-permute-start.13) | collective-permute-done | bytes 270368 | tf_op jit(solution)/shard_map/ppermute | solution.py:423
  67.2 0.1 convert_element_type.43.theirs_ref
  67.2 1.7 %finish.1 = f32[256,512]{1,0:T(8,128)} custom-call(s32[1]{0:T(128)S(6)} %copy.21.green_steps_ref.steps_ref, f32[256,512]{1,0:T(8,128)S(1)} %get-tuple-element.15.step_ref, f32[256,512]{1,0:T(8,128)S(1)} %get-tuple-element.18.square_ref, bf16[256,512]{1,0:T(8,128)(2,1)S(1)} %get-tuple-element.19.high_ref, bf16[256,512]{1,0:T(8,128)(2,1)S(1)} %get-tuple-element.20.low_ref, ...), custom_call_target="tpu_custom_call" | custom-call | tf_op jit(solution)/shard_map/finish/pallas_call | solution.py:434
  (17 shorter events, 0.3 us)
Async XLA Ops:
  1.3 9.1 %copy-start.1 = (bf16[1,1,256,512]{3,2,1,0:T(8,128)(2,1)S(1)}, bf16[1,1,256,512]{3,2,1,0:T(8,128)(2,1)}, u32[]{:S(2)}) copy-start(bf16[1,1,256,512]{3,2,1,0:T(8,128)(2,1)} %param.8) | copy-start | bytes 786436
  3.0 25.6 %copy-start = (f32[1,256,512]{2,1,0:T(8,128)S(1)}, f32[1,256,512]{2,1,0:T(8,128)}, u32[]{:S(2)}) copy-start(f32[1,256,512]{2,1,0:T(8,128)} %param.11) | copy-start | bytes 1572868
  3.0 25.6 %all-to-all-start = ((bf16[8,40,512]{2,1,0:T(8,128)(2,1)}), bf16[8,40,512]{2,1,0:T(8,128)(2,1)S(1)}, u32[]{:S(2)}, u32[]{:S(2)}) async-start(bf16[8,40,512]{2,1,0:T(8,128)(2,1)} %prepare.1), calls=%async_computation | async-start | bytes 655360 | tf_op jit(solution)/shard_map/all_to_all | solution.py:125
  10.4 29.5 %collective-permute-start.9 = (bf16[256,512]{1,0:T(8,128)(2,1)S(1)}, bf16[256,512]{1,0:T(8,128)(2,1)S(1)}, u32[]{:S(2)}, u32[]{:S(2)}) collective-permute-start(bf16[256,512]{1,0:T(8,128)(2,1)S(1)} %bitcast.11), channel_id=1, source_target_pairs={{0,8},{4,12},{8,16},{12,20},{16,24},{20,28},{24,0},{28,4},{1,9},{5... | collective-permute-start | bytes 786440 | tf_op jit(solution)/shard_map/ppermute | solution.py:43
  13.7 14.9 %copy-start.2 = (s32[2]{0:T(128)S(1)}, s32[2]{0:T(128)}, u32[]{:S(2)}) copy-start(s32[2]{0:T(128)} %refs_5_.1) | copy-start | bytes 28
  13.7 14.9 %copy-start.3 = (s32[2]{0:T(128)S(1)}, s32[2]{0:T(128)}, u32[]{:S(2)}) copy-start(s32[2]{0:T(128)} %refs_6_.1) | copy-start | bytes 28
  29.5 7.2 %collective-permute-start.2 = (f16[2,32,512]{2,1,0:T(8,128)(2,1)S(1)}, f16[2,32,512]{2,1,0:T(8,128)(2,1)S(1)}, u32[]{:S(2)}, u32[]{:S(2)}) collective-permute-start(f16[2,32,512]{2,1,0:T(8,128)(2,1)S(1)} %convert_element_type.33), channel_id=1, source_target_pairs={{0,8},{4,12},{8,16},{12,20},{16,24},{20,28},{24,0},{28,4},{1,9},{5... | collective-permute-start | bytes 196616 | tf_op jit(solution)/shard_map/ppermute | solution.py:170
  30.1 6.6 %collective-permute-start.1 = (f16[2,32,512]{2,1,0:T(8,128)(2,1)S(1)}, f16[2,32,512]{2,1,0:T(8,128)(2,1)S(1)}, u32[]{:S(2)}, u32[]{:S(2)}) collective-permute-start(f16[2,32,512]{2,1,0:T(8,128)(2,1)S(1)} %convert_element_type.33), channel_id=1, source_target_pairs={{0,16},{4,20},{8,24},{12,28},{16,0},{20,4},{24,8},{28,12},{1,17},{... | collective-permute-start | bytes 196616 | tf_op jit(solution)/shard_map/ppermute | solution.py:170
  30.1 6.3 %collective-permute-start = (f16[2,32,512]{2,1,0:T(8,128)(2,1)S(1)}, f16[2,32,512]{2,1,0:T(8,128)(2,1)S(1)}, u32[]{:S(2)}, u32[]{:S(2)}) collective-permute-start(f16[2,32,512]{2,1,0:T(8,128)(2,1)S(1)} %convert_element_type.33), channel_id=1, source_target_pairs={{0,24},{4,28},{8,0},{12,4},{16,8},{20,12},{24,16},{28,20},{1,25},{... | collective-permute-start | bytes 196616 | tf_op jit(solution)/shard_map/ppermute | solution.py:170
  36.7 5.0 %collective-permute-start.7 = (f16[4,32,512]{2,1,0:T(8,128)(2,1)S(1)}, f16[4,32,512]{2,1,0:T(8,128)(2,1)S(1)}, u32[]{:S(2)}, u32[]{:S(2)}) collective-permute-start(f16[4,32,512]{2,1,0:T(8,128)(2,1)S(1)} %get-tuple-element.24), channel_id=1, source_target_pairs={{0,4},{4,0},{8,12},{12,8},{16,20},{20,16},{24,28},{28,24},{1,5},{5... | collective-permute-start | bytes 393224 | tf_op jit(solution)/shard_map/ppermute | solution.py:182
  37.9 5.4 %collective-permute-start.5 = (f16[4,32,512]{2,1,0:T(8,128)(2,1)S(1)}, f16[4,32,512]{2,1,0:T(8,128)(2,1)S(1)}, u32[]{:S(2)}, u32[]{:S(2)}) collective-permute-start(f16[4,32,512]{2,1,0:T(8,128)(2,1)S(1)} %get-tuple-element.24), channel_id=1, source_target_pairs={{0,1},{1,0},{2,3},{3,2},{4,5},{5,4},{6,7},{7,6},{8,9},{9,8},{10,11... | collective-permute-start | bytes 393224 | tf_op jit(solution)/shard_map/ppermute | solution.py:185
  39.4 15.8 %collective-permute-start.12 = (bf16[256,512]{1,0:T(8,128)(2,1)S(1)}, bf16[256,512]{1,0:T(8,128)(2,1)S(1)}, u32[]{:S(2)}, u32[]{:S(2)}) collective-permute-start(bf16[256,512]{1,0:T(8,128)(2,1)S(1)} %bitcast.12), channel_id=1, source_target_pairs={{0,2},{2,0},{1,3},{3,1},{4,6},{6,4},{5,7},{7,5},{8,10},{10,8},{9,1... | collective-permute-start | bytes 786440 | tf_op jit(solution)/shard_map/ppermute | solution.py:414
  39.4 6.3 %collective-permute-start.8 = (f16[4,32,512]{2,1,0:T(8,128)(2,1)S(1)}, f16[4,32,512]{2,1,0:T(8,128)(2,1)S(1)}, u32[]{:S(2)}, u32[]{:S(2)}) collective-permute-start(f16[4,32,512]{2,1,0:T(8,128)(2,1)S(1)} %get-tuple-element.25), channel_id=1, source_target_pairs={{0,1},{1,0},{2,3},{3,2},{4,5},{5,4},{6,7},{7,6},{8,9},{9,8},{10,11... | collective-permute-start | bytes 393224 | tf_op jit(solution)/shard_map/ppermute | solution.py:185
  39.9 6.7 %collective-permute-start.3 = (f16[4,32,512]{2,1,0:T(8,128)(2,1)S(1)}, f16[4,32,512]{2,1,0:T(8,128)(2,1)S(1)}, u32[]{:S(2)}, u32[]{:S(2)}) collective-permute-start(f16[4,32,512]{2,1,0:T(8,128)(2,1)S(1)} %get-tuple-element.25), channel_id=1, source_target_pairs={{0,4},{4,0},{8,12},{12,8},{16,20},{20,16},{24,28},{28,24},{1,5},{5... | collective-permute-start | bytes 393224 | tf_op jit(solution)/shard_map/ppermute | solution.py:182
  41.7 13.5 %collective-permute-start.11 = (bf16[256,512]{1,0:T(8,128)(2,1)S(1)}, bf16[256,512]{1,0:T(8,128)(2,1)S(1)}, u32[]{:S(2)}, u32[]{:S(2)}) collective-permute-start(bf16[256,512]{1,0:T(8,128)(2,1)S(1)} %chosen.1), channel_id=1, source_target_pairs={{0,4},{4,8},{8,12},{12,16},{16,20},{20,24},{24,28},{28,0},{1,5},{5... | collective-permute-start | bytes 786440 | tf_op jit(solution)/shard_map/ppermute | solution.py:43
  43.2 12.0 %collective-permute-start.10 = (bf16[256,512]{1,0:T(8,128)(2,1)S(1)}, bf16[256,512]{1,0:T(8,128)(2,1)S(1)}, u32[]{:S(2)}, u32[]{:S(2)}) collective-permute-start(bf16[256,512]{1,0:T(8,128)(2,1)S(1)} %collective-permute-done.9.two_ref.refs_10_), channel_id=1, source_target_pairs={{0,8},{4,12},{8,16},{12,20},{16,24},{20,28},{24,0},{28,4},{1,9},{5... | collective-permute-start | bytes 786440 | tf_op jit(solution)/shard_map/ppermute | solution.py:43
  45.6 9.5 %collective-permute-start.6 = (f16[4,32,512]{2,1,0:T(8,128)(2,1)S(1)}, f16[4,32,512]{2,1,0:T(8,128)(2,1)S(1)}, u32[]{:S(2)}, u32[]{:S(2)}) collective-permute-start(f16[4,32,512]{2,1,0:T(8,128)(2,1)S(1)} %collective-permute-done.5), channel_id=1, source_target_pairs={{0,4},{4,0},{8,12},{12,8},{16,20},{20,16},{24,28},{28,24},{1,5},{5... | collective-permute-start | bytes 393224 | tf_op jit(solution)/shard_map/ppermute | solution.py:182
  46.6 8.6 %collective-permute-start.4 = (f16[4,32,512]{2,1,0:T(8,128)(2,1)S(1)}, f16[4,32,512]{2,1,0:T(8,128)(2,1)S(1)}, u32[]{:S(2)}, u32[]{:S(2)}) collective-permute-start(f16[4,32,512]{2,1,0:T(8,128)(2,1)S(1)} %collective-permute-done.3), channel_id=1, source_target_pairs={{0,1},{1,0},{2,3},{3,2},{4,5},{5,4},{6,7},{7,6},{8,9},{9,8},{10,11... | collective-permute-start | bytes 393224 | tf_op jit(solution)/shard_map/ppermute | solution.py:185
  58.7 8.5 %collective-permute-start.13 = (f16[264,512]{1,0:T(8,128)(2,1)S(1)}, f16[264,512]{1,0:T(8,128)(2,1)S(1)}, u32[]{:S(2)}, u32[]{:S(2)}) collective-permute-start(f16[264,512]{1,0:T(8,128)(2,1)S(1)} %convert_element_type.42), channel_id=1, source_target_pairs={{0,1},{1,0},{2,3},{3,2},{4,5},{5,4},{6,7},{7,6},{8,9},{9,8},{10,11... | collective-permute-start | bytes 811016 | tf_op jit(solution)/shard_map/ppermute | solution.py:423

commit v9 on v8

--- a/solution.py
+++ b/solution.py
@@ -38,9 +38,10 @@
     return dot(top, high) + dot(top, low) + dot(rest, high)
 
 
-def shifted(block, axis, distance):
+def shifted(block, axis, distance, around=True):
     count = lax.axis_size(axis)
-    return lax.ppermute(block, axis, [(i, (i + distance) % count) for i in range(count)])
+    route = [(i, (i + distance) % count) for i in range(count if around else count - distance)]
+    return lax.ppermute(block, axis, route)
 
 
 def in_squares():
@@ -405,7 +406,7 @@
     scalars = (screen_steps, green_steps, onsite_level)
     pieces = gathered(make(green, occupation, offsets, bare, scalars))
 
-    two = shifted(green, "energy", 2)
+    two = shifted(green, "energy", 2, around=False)
     four = shifted(two, "energy", 2)
     odd = shifted(chosen(offsets, two, green), "energy", 1)
 

time: 69.3 us -> 62.5 us (0.902)
  waiting for transfers between devices: 31.2 us -> 23 us
  starting transfers between devices: 24.6 us -> 25.9 us
    all_to_all x1, waiting for transfers between devices: 14.8 us -> 4.96 us  [polar_share(): got = lax.all_to_all(sent, 'energy', 0, 0, tiled=True)]
    ppermute x3, starting transfers between devices: 5.02 us -> 6.86 us  [shifted(): return lax.ppermute(block, axis, route)]
    ppermute x3, waiting for transfers between devices: 5.75 us -> 6.64 us  [along_x(): return lax.ppermute(part, 'energy', [(e, e ^ 1) for e in range(energies)])]
where the time goes in v9:
time: 62.5 us; the launch traced here: 62.2 us
  starting transfers between devices  25.9 us (41%)
  waiting for transfers between devices  23 us (37%)
  Pallas kernels  9.94 us (16%)
  between operations  2.92 us (5%)
    all_to_all x1, starting transfers between devices, polar_share(): got = lax.all_to_all(sent, 'energy', 0, 0, tiled=True)  7.42 us
    ppermute x1, waiting for transfers between devices, body(): lax.ppermute(packed.astype(coded), 'rep', [(0, 1), (1, 0)])  7.04 us
    ppermute x3, starting transfers between devices, shifted(): return lax.ppermute(block, axis, route)  6.86 us
    ppermute x3, waiting for transfers between devices, along_x(): return lax.ppermute(part, 'energy', [(e, e ^ 1) for e in range(energies)])  6.64 us
    all_to_all x1, waiting for transfers between devices, polar_share(): got = lax.all_to_all(sent, 'energy', 0, 0, tiled=True)  4.96 us
    ppermute x3, starting transfers between devices, gather_energy(): got = lax.ppermute(chunk, 'energy', route)  3.88 us
    ppermute x3, waiting for transfers between devices, gather_energy(): got = lax.ppermute(chunk, 'energy', route)  3.55 us
    ppermute x3, starting transfers between devices, along_rep(): return lax.ppermute(part, 'rep', [(0, 1), (1, 0)])  3.55 us
  transfers between devices with their start and end apart: 15, of which 8 were waited for; matrix products, arithmetic and copies ran while one was open for 0% of the time, Pallas kernels for 5%

profile of v9, /device:TPU:0, one launch (start us, length us, event | category | flops | bytes accessed | tf_op | source)
XLA Modules:
  0.0 62.2 jit_solution(6934128920033196173)
XLA Ops:
  1.3 0.0 copy-start.1
  1.3 1.7 %prepare.1 = bf16[8,40,512]{2,1,0:T(8,128)(2,1)} custom-call(f32[1]{0:T(128)S(6)} %copy.19.weight_ref, bf16[256,512]{1,0:T(8,128)(2,1)} %bitcast.10), custom_call_target="tpu_custom_call" | custom-call | tf_op jit(solution)/shard_map/prepare/pallas_call | solution.py:113
  3.0 0.0 copy-start
  3.0 7.4 %all-to-all-start = ((bf16[8,40,512]{2,1,0:T(8,128)(2,1)}), bf16[8,40,512]{2,1,0:T(8,128)(2,1)S(1)}, u32[]{:S(2)}, u32[]{:S(2)}) async-start(bf16[8,40,512]{2,1,0:T(8,128)(2,1)} %prepare.1), calls=%async_computation | async-start | bytes 655360 | tf_op jit(solution)/shard_map/all_to_all | solution.py:126
  10.4 0.0 copy-done.1
  10.4 3.9 %collective-permute-start.9 = (bf16[256,512]{1,0:T(8,128)(2,1)S(1)}, bf16[256,512]{1,0:T(8,128)(2,1)S(1)}, u32[]{:S(2)}, u32[]{:S(2)}) collective-permute-start(bf16[256,512]{1,0:T(8,128)(2,1)S(1)} %bitcast.11), channel_id=1, source_target_pairs={{0,8},{4,12},{8,16},{12,20},{16,24},{20,28},{1,9},{5,13},{9,17},{1... | collective-permute-start | bytes 786440 | tf_op jit(solution)/shard_map/ppermute | solution.py:44
  15.7 0.0 copy-start.2
  15.7 0.0 copy-start.3
  15.7 5.0 %all-to-all-done.got_ref = bf16[8,40,512]{2,1,0:T(8,128)(2,1)S(1)} async-done(((bf16[8,40,512]{2,1,0:T(8,128)(2,1)}), bf16[8,40,512]{2,1,0:T(8,128)(2,1)S(1)}, u32[]{:S(2)}, u32[]{:S(2)}) %all-to-all-start) | async-done | bytes 327712 | tf_op jit(solution)/shard_map/all_to_all | solution.py:126
  20.7 0.0 copy-done
  20.7 0.0 copy-done.2
  20.7 0.0 copy-done.3
  20.7 0.8 %polar.1 = f32[2,32,512]{2,1,0:T(8,128)S(1)} custom-call(s32[2]{0:T(128)S(1)} %copy-done.2, s32[2]{0:T(128)S(1)} %copy-done.3, s32[1]{0:T(128)S(6)} %copy.21.green_steps_ref.steps_ref, f32[1]{0:T(128)S(6)} %copy.20.level_ref.refs_7_, bf16[8,40,512]{2,1,0:T(8,128)(2,1)S(1)} %all-to-all-done.got_ref, f32[256,512]{1,0:T(8,128)S(1)} %bitcast.7), custom_call_target="tpu_custom_call" | custom-call | tf_op jit(solution)/shard_map/polar/pallas_call | solution.py:127
  21.6 1.1 %collective-permute-start.2 = (f16[2,32,512]{2,1,0:T(8,128)(2,1)S(1)}, f16[2,32,512]{2,1,0:T(8,128)(2,1)S(1)}, u32[]{:S(2)}, u32[]{:S(2)}) collective-permute-start(f16[2,32,512]{2,1,0:T(8,128)(2,1)S(1)} %convert_element_type.33), channel_id=1, source_target_pairs={{0,8},{4,12},{8,16},{12,20},{16,24},{20,28},{24,0},{28,4},{1,9},{5... | collective-permute-start | bytes 196616 | tf_op jit(solution)/shard_map/ppermute | solution.py:171
  22.6 1.3 %collective-permute-start.1 = (f16[2,32,512]{2,1,0:T(8,128)(2,1)S(1)}, f16[2,32,512]{2,1,0:T(8,128)(2,1)S(1)}, u32[]{:S(2)}, u32[]{:S(2)}) collective-permute-start(f16[2,32,512]{2,1,0:T(8,128)(2,1)S(1)} %convert_element_type.33), channel_id=1, source_target_pairs={{0,16},{4,20},{8,24},{12,28},{16,0},{20,4},{24,8},{28,12},{1,17},{... | collective-permute-start | bytes 196616 | tf_op jit(solution)/shard_map/ppermute | solution.py:171
  23.9 1.6 %collective-permute-start = (f16[2,32,512]{2,1,0:T(8,128)(2,1)S(1)}, f16[2,32,512]{2,1,0:T(8,128)(2,1)S(1)}, u32[]{:S(2)}, u32[]{:S(2)}) collective-permute-start(f16[2,32,512]{2,1,0:T(8,128)(2,1)S(1)} %convert_element_type.33), channel_id=1, source_target_pairs={{0,24},{4,28},{8,0},{12,4},{16,8},{20,12},{24,16},{28,20},{1,25},{... | collective-permute-start | bytes 196616 | tf_op jit(solution)/shard_map/ppermute | solution.py:171
  25.5 3.0 %collective-permute-done = f16[2,32,512]{2,1,0:T(8,128)(2,1)S(1)} collective-permute-done((f16[2,32,512]{2,1,0:T(8,128)(2,1)S(1)}, f16[2,32,512]{2,1,0:T(8,128)(2,1)S(1)}, u32[]{:S(2)}, u32[]{:S(2)}) %collective-permute-start) | collective-permute-done | bytes 65568 | tf_op jit(solution)/shard_map/ppermute | solution.py:171
  28.5 0.6 collective-permute-done.1
  29.1 0.0 collective-permute-done.2
  29.1 1.0 %collective-permute-start.7 = (f16[4,32,512]{2,1,0:T(8,128)(2,1)S(1)}, f16[4,32,512]{2,1,0:T(8,128)(2,1)S(1)}, u32[]{:S(2)}, u32[]{:S(2)}) collective-permute-start(f16[4,32,512]{2,1,0:T(8,128)(2,1)S(1)} %get-tuple-element.24), channel_id=1, source_target_pairs={{0,4},{4,0},{8,12},{12,8},{16,20},{20,16},{24,28},{28,24},{1,5},{5... | collective-permute-start | bytes 393224 | tf_op jit(solution)/shard_map/ppermute | solution.py:183
  30.2 1.5 %collective-permute-start.5 = (f16[4,32,512]{2,1,0:T(8,128)(2,1)S(1)}, f16[4,32,512]{2,1,0:T(8,128)(2,1)S(1)}, u32[]{:S(2)}, u32[]{:S(2)}) collective-permute-start(f16[4,32,512]{2,1,0:T(8,128)(2,1)S(1)} %get-tuple-element.24), channel_id=1, source_target_pairs={{0,1},{1,0},{2,3},{3,2},{4,5},{5,4},{6,7},{7,6},{8,9},{9,8},{10,11... | collective-permute-start | bytes 393224 | tf_op jit(solution)/shard_map/ppermute | solution.py:186
  31.7 0.0 collective-permute-start.12
  31.7 0.5 collective-permute-start.8
  32.2 0.0 collective-permute-done.9.two_ref.refs_10_
  32.2 1.1 %collective-permute-start.3 = (f16[4,32,512]{2,1,0:T(8,128)(2,1)S(1)}, f16[4,32,512]{2,1,0:T(8,128)(2,1)S(1)}, u32[]{:S(2)}, u32[]{:S(2)}) collective-permute-start(f16[4,32,512]{2,1,0:T(8,128)(2,1)S(1)} %get-tuple-element.25), channel_id=1, source_target_pairs={{0,4},{4,0},{8,12},{12,8},{16,20},{20,16},{24,28},{28,24},{1,5},{5... | collective-permute-start | bytes 393224 | tf_op jit(solution)/shard_map/ppermute | solution.py:183
  33.3 0.6 chosen.1
  33.8 0.3 collective-permute-done.7
  34.2 1.0 %collective-permute-start.11 = (bf16[256,512]{1,0:T(8,128)(2,1)S(1)}, bf16[256,512]{1,0:T(8,128)(2,1)S(1)}, u32[]{:S(2)}, u32[]{:S(2)}) collective-permute-start(bf16[256,512]{1,0:T(8,128)(2,1)S(1)} %chosen.1), channel_id=1, source_target_pairs={{0,4},{4,8},{8,12},{12,16},{16,20},{20,24},{24,28},{28,0},{1,5},{5... | collective-permute-start | bytes 786440 | tf_op jit(solution)/shard_map/ppermute | solution.py:44
  35.2 0.4 collective-permute-done.5
  35.5 2.0 %collective-permute-start.10 = (bf16[256,512]{1,0:T(8,128)(2,1)S(1)}, bf16[256,512]{1,0:T(8,128)(2,1)S(1)}, u32[]{:S(2)}, u32[]{:S(2)}) collective-permute-start(bf16[256,512]{1,0:T(8,128)(2,1)S(1)} %collective-permute-done.9.two_ref.refs_10_), channel_id=1, source_target_pairs={{0,8},{4,12},{8,16},{12,20},{16,24},{20,28},{24,0},{28,4},{1,9},{5... | collective-permute-start | bytes 786440 | tf_op jit(solution)/shard_map/ppermute | solution.py:44
  37.5 0.5 collective-permute-done.8
  38.0 1.1 %collective-permute-start.6 = (f16[4,32,512]{2,1,0:T(8,128)(2,1)S(1)}, f16[4,32,512]{2,1,0:T(8,128)(2,1)S(1)}, u32[]{:S(2)}, u32[]{:S(2)}) collective-permute-start(f16[4,32,512]{2,1,0:T(8,128)(2,1)S(1)} %collective-permute-done.5), channel_id=1, source_target_pairs={{0,4},{4,0},{8,12},{12,8},{16,20},{20,16},{24,28},{28,24},{1,5},{5... | collective-permute-start | bytes 393224 | tf_op jit(solution)/shard_map/ppermute | solution.py:183
  39.0 0.0 collective-permute-done.3
  39.0 1.5 %collective-permute-start.4 = (f16[4,32,512]{2,1,0:T(8,128)(2,1)S(1)}, f16[4,32,512]{2,1,0:T(8,128)(2,1)S(1)}, u32[]{:S(2)}, u32[]{:S(2)}) collective-permute-start(f16[4,32,512]{2,1,0:T(8,128)(2,1)S(1)} %collective-permute-done.3), channel_id=1, source_target_pairs={{0,1},{1,0},{2,3},{3,2},{4,5},{5,4},{6,7},{7,6},{8,9},{9,8},{10,11... | collective-permute-start | bytes 393224 | tf_op jit(solution)/shard_map/ppermute | solution.py:186
  40.7 1.3 %early.1 = (f32[2,256,512]{2,1,0:T(8,128)S(1)}, bf16[2,512,512]{2,1,0:T(8,128)(2,1)S(1)}, bf16[2,512,512]{2,1,0:T(8,128)(2,1)S(1)}) custom-call(f32[4,32,512]{2,1,0:T(8,128)S(1)} %convert_element_type.36.refs_0_, f32[4,32,512]{2,1,0:T(8,128)S(1)} %convert_element_type.37.refs_1_, f32[4,32,512]{2,1,0:T(8,128)S(1)} %convert_element_type.38.refs_2_, ...), custom_call_target="tpu_custom_call" | custom-call | tf_op jit(solution)/shard_map/early/pallas_call | solution.py:319
  42.0 6.3 %collective-permute-done.6 = f16[4,32,512]{2,1,0:T(8,128)(2,1)S(1)} collective-permute-done((f16[4,32,512]{2,1,0:T(8,128)(2,1)S(1)}, f16[4,32,512]{2,1,0:T(8,128)(2,1)S(1)}, u32[]{:S(2)}, u32[]{:S(2)}) %collective-permute-start.6) | collective-permute-done | bytes 131104 | tf_op jit(solution)/shard_map/ppermute | solution.py:183
  48.4 0.0 collective-permute-done.4
  48.4 0.0 collective-permute-done.12.refs_13_
  48.4 0.0 collective-permute-done.11.refs_12_
  48.4 0.0 collective-permute-done.10.refs_11_
  48.4 3.4 %dyson.1 = (bf16[2,256,512]{2,1,0:T(8,128)(2,1)}, f32[264,512]{1,0:T(8,128)S(1)}, f32[256,512]{1,0:T(8,128)S(1)}, f32[8,512]{1,0:T(8,128)S(1)}) custom-call(f32[4,32,512]{2,1,0:T(8,128)S(1)} %convert_element_type.34.refs_0_, f32[4,32,512]{2,1,0:T(8,128)S(1)} %convert_element_type.35.refs_1_, f32[2,256,512]{2,1,0:T(8,128)S(1)} %get-tuple-element.12.refs_2_, ...), custom_call_target="tpu_custom_call" | custom-call | tf_op jit(solution)/shard_map/dyson/pallas_call | solution.py:335
  51.9 1.0 %collective-permute-start.13 = (f16[264,512]{1,0:T(8,128)(2,1)S(1)}, f16[264,512]{1,0:T(8,128)(2,1)S(1)}, u32[]{:S(2)}, u32[]{:S(2)}) collective-permute-start(f16[264,512]{1,0:T(8,128)(2,1)S(1)} %convert_element_type.42), channel_id=1, source_target_pairs={{0,1},{1,0},{2,3},{3,2},{4,5},{5,4},{6,7},{7,6},{8,9},{9,8},{10,11... | collective-permute-start | bytes 811016 | tf_op jit(solution)/shard_map/ppermute | solution.py:424
  52.9 0.4 begin.1
  53.3 7.0 %collective-permute-done.13 = f16[264,512]{1,0:T(8,128)(2,1)S(1)} collective-permute-done((f16[264,512]{1,0:T(8,128)(2,1)S(1)}, f16[264,512]{1,0:T(8,128)(2,1)S(1)}, u32[]{:S(2)}, u32[]{:S(2)}) %collective-permute-start.13) | collective-permute-done | bytes 270368 | tf_op jit(solution)/shard_map/ppermute | solution.py:424
  60.4 0.1 convert_element_type.43.theirs_ref
  60.4 1.7 %finish.1 = f32[256,512]{1,0:T(8,128)} custom-call(s32[1]{0:T(128)S(6)} %copy.21.green_steps_ref.steps_ref, f32[256,512]{1,0:T(8,128)S(1)} %get-tuple-element.15.step_ref, f32[256,512]{1,0:T(8,128)S(1)} %get-tuple-element.18.square_ref, bf16[256,512]{1,0:T(8,128)(2,1)S(1)} %get-tuple-element.19.high_ref, bf16[256,512]{1,0:T(8,128)(2,1)S(1)} %get-tuple-element.20.low_ref, ...), custom_call_target="tpu_custom_call" | custom-call | tf_op jit(solution)/shard_map/finish/pallas_call | solution.py:435
  (17 shorter events, 0.3 us)
Async XLA Ops:
  1.3 9.1 %copy-start.1 = (bf16[1,1,256,512]{3,2,1,0:T(8,128)(2,1)S(1)}, bf16[1,1,256,512]{3,2,1,0:T(8,128)(2,1)}, u32[]{:S(2)}) copy-start(bf16[1,1,256,512]{3,2,1,0:T(8,128)(2,1)} %param.8) | copy-start | bytes 786436
  3.0 17.7 %copy-start = (f32[1,256,512]{2,1,0:T(8,128)S(1)}, f32[1,256,512]{2,1,0:T(8,128)}, u32[]{:S(2)}) copy-start(f32[1,256,512]{2,1,0:T(8,128)} %param.11) | copy-start | bytes 1572868
  3.0 17.7 %all-to-all-start = ((bf16[8,40,512]{2,1,0:T(8,128)(2,1)}), bf16[8,40,512]{2,1,0:T(8,128)(2,1)S(1)}, u32[]{:S(2)}, u32[]{:S(2)}) async-start(bf16[8,40,512]{2,1,0:T(8,128)(2,1)} %prepare.1), calls=%async_computation | async-start | bytes 655360 | tf_op jit(solution)/shard_map/all_to_all | solution.py:126
  10.4 21.8 %collective-permute-start.9 = (bf16[256,512]{1,0:T(8,128)(2,1)S(1)}, bf16[256,512]{1,0:T(8,128)(2,1)S(1)}, u32[]{:S(2)}, u32[]{:S(2)}) collective-permute-start(bf16[256,512]{1,0:T(8,128)(2,1)S(1)} %bitcast.11), channel_id=1, source_target_pairs={{0,8},{4,12},{8,16},{12,20},{16,24},{20,28},{1,9},{5,13},{9,17},{1... | collective-permute-start | bytes 786440 | tf_op jit(solution)/shard_map/ppermute | solution.py:44
  15.7 5.0 %copy-start.2 = (s32[2]{0:T(128)S(1)}, s32[2]{0:T(128)}, u32[]{:S(2)}) copy-start(s32[2]{0:T(128)} %refs_5_.1) | copy-start | bytes 28
  15.7 5.0 %copy-start.3 = (s32[2]{0:T(128)S(1)}, s32[2]{0:T(128)}, u32[]{:S(2)}) copy-start(s32[2]{0:T(128)} %refs_6_.1) | copy-start | bytes 28
  21.6 7.5 %collective-permute-start.2 = (f16[2,32,512]{2,1,0:T(8,128)(2,1)S(1)}, f16[2,32,512]{2,1,0:T(8,128)(2,1)S(1)}, u32[]{:S(2)}, u32[]{:S(2)}) collective-permute-start(f16[2,32,512]{2,1,0:T(8,128)(2,1)S(1)} %convert_element_type.33), channel_id=1, source_target_pairs={{0,8},{4,12},{8,16},{12,20},{16,24},{20,28},{24,0},{28,4},{1,9},{5... | collective-permute-start | bytes 196616 | tf_op jit(solution)/shard_map/ppermute | solution.py:171
  22.6 6.5 %collective-permute-start.1 = (f16[2,32,512]{2,1,0:T(8,128)(2,1)S(1)}, f16[2,32,512]{2,1,0:T(8,128)(2,1)S(1)}, u32[]{:S(2)}, u32[]{:S(2)}) collective-permute-start(f16[2,32,512]{2,1,0:T(8,128)(2,1)S(1)} %convert_element_type.33), channel_id=1, source_target_pairs={{0,16},{4,20},{8,24},{12,28},{16,0},{20,4},{24,8},{28,12},{1,17},{... | collective-permute-start | bytes 196616 | tf_op jit(solution)/shard_map/ppermute | solution.py:171
  23.9 4.6 %collective-permute-start = (f16[2,32,512]{2,1,0:T(8,128)(2,1)S(1)}, f16[2,32,512]{2,1,0:T(8,128)(2,1)S(1)}, u32[]{:S(2)}, u32[]{:S(2)}) collective-permute-start(f16[2,32,512]{2,1,0:T(8,128)(2,1)S(1)} %convert_element_type.33), channel_id=1, source_target_pairs={{0,24},{4,28},{8,0},{12,4},{16,8},{20,12},{24,16},{28,20},{1,25},{... | collective-permute-start | bytes 196616 | tf_op jit(solution)/shard_map/ppermute | solution.py:171
  29.1 5.0 %collective-permute-start.7 = (f16[4,32,512]{2,1,0:T(8,128)(2,1)S(1)}, f16[4,32,512]{2,1,0:T(8,128)(2,1)S(1)}, u32[]{:S(2)}, u32[]{:S(2)}) collective-permute-start(f16[4,32,512]{2,1,0:T(8,128)(2,1)S(1)} %get-tuple-element.24), channel_id=1, source_target_pairs={{0,4},{4,0},{8,12},{12,8},{16,20},{20,16},{24,28},{28,24},{1,5},{5... | collective-permute-start | bytes 393224 | tf_op jit(solution)/shard_map/ppermute | solution.py:183
  30.2 5.4 %collective-permute-start.5 = (f16[4,32,512]{2,1,0:T(8,128)(2,1)S(1)}, f16[4,32,512]{2,1,0:T(8,128)(2,1)S(1)}, u32[]{:S(2)}, u32[]{:S(2)}) collective-permute-start(f16[4,32,512]{2,1,0:T(8,128)(2,1)S(1)} %get-tuple-element.24), channel_id=1, source_target_pairs={{0,1},{1,0},{2,3},{3,2},{4,5},{5,4},{6,7},{7,6},{8,9},{9,8},{10,11... | collective-permute-start | bytes 393224 | tf_op jit(solution)/shard_map/ppermute | solution.py:186
  31.7 16.7 %collective-permute-start.12 = (bf16[256,512]{1,0:T(8,128)(2,1)S(1)}, bf16[256,512]{1,0:T(8,128)(2,1)S(1)}, u32[]{:S(2)}, u32[]{:S(2)}) collective-permute-start(bf16[256,512]{1,0:T(8,128)(2,1)S(1)} %bitcast.12), channel_id=1, source_target_pairs={{0,2},{2,0},{1,3},{3,1},{4,6},{6,4},{5,7},{7,5},{8,10},{10,8},{9,1... | collective-permute-start | bytes 786440 | tf_op jit(solution)/shard_map/ppermute | solution.py:415
  31.7 6.3 %collective-permute-start.8 = (f16[4,32,512]{2,1,0:T(8,128)(2,1)S(1)}, f16[4,32,512]{2,1,0:T(8,128)(2,1)S(1)}, u32[]{:S(2)}, u32[]{:S(2)}) collective-permute-start(f16[4,32,512]{2,1,0:T(8,128)(2,1)S(1)} %get-tuple-element.25), channel_id=1, source_target_pairs={{0,1},{1,0},{2,3},{3,2},{4,5},{5,4},{6,7},{7,6},{8,9},{9,8},{10,11... | collective-permute-start | bytes 393224 | tf_op jit(solution)/shard_map/ppermute | solution.py:186
  32.2 6.8 %collective-permute-start.3 = (f16[4,32,512]{2,1,0:T(8,128)(2,1)S(1)}, f16[4,32,512]{2,1,0:T(8,128)(2,1)S(1)}, u32[]{:S(2)}, u32[]{:S(2)}) collective-permute-start(f16[4,32,512]{2,1,0:T(8,128)(2,1)S(1)} %get-tuple-element.25), channel_id=1, source_target_pairs={{0,4},{4,0},{8,12},{12,8},{16,20},{20,16},{24,28},{28,24},{1,5},{5... | collective-permute-start | bytes 393224 | tf_op jit(solution)/shard_map/ppermute | solution.py:183
  34.2 14.2 %collective-permute-start.11 = (bf16[256,512]{1,0:T(8,128)(2,1)S(1)}, bf16[256,512]{1,0:T(8,128)(2,1)S(1)}, u32[]{:S(2)}, u32[]{:S(2)}) collective-permute-start(bf16[256,512]{1,0:T(8,128)(2,1)S(1)} %chosen.1), channel_id=1, source_target_pairs={{0,4},{4,8},{8,12},{12,16},{16,20},{20,24},{24,28},{28,0},{1,5},{5... | collective-permute-start | bytes 786440 | tf_op jit(solution)/shard_map/ppermute | solution.py:44
  35.5 12.9 %collective-permute-start.10 = (bf16[256,512]{1,0:T(8,128)(2,1)S(1)}, bf16[256,512]{1,0:T(8,128)(2,1)S(1)}, u32[]{:S(2)}, u32[]{:S(2)}) collective-permute-start(bf16[256,512]{1,0:T(8,128)(2,1)S(1)} %collective-permute-done.9.two_ref.refs_10_), channel_id=1, source_target_pairs={{0,8},{4,12},{8,16},{12,20},{16,24},{20,28},{24,0},{28,4},{1,9},{5... | collective-permute-start | bytes 786440 | tf_op jit(solution)/shard_map/ppermute | solution.py:44
  38.0 10.4 %collective-permute-start.6 = (f16[4,32,512]{2,1,0:T(8,128)(2,1)S(1)}, f16[4,32,512]{2,1,0:T(8,128)(2,1)S(1)}, u32[]{:S(2)}, u32[]{:S(2)}) collective-permute-start(f16[4,32,512]{2,1,0:T(8,128)(2,1)S(1)} %collective-permute-done.5), channel_id=1, source_target_pairs={{0,4},{4,0},{8,12},{12,8},{16,20},{20,16},{24,28},{28,24},{1,5},{5... | collective-permute-start | bytes 393224 | tf_op jit(solution)/shard_map/ppermute | solution.py:183
  39.0 9.3 %collective-permute-start.4 = (f16[4,32,512]{2,1,0:T(8,128)(2,1)S(1)}, f16[4,32,512]{2,1,0:T(8,128)(2,1)S(1)}, u32[]{:S(2)}, u32[]{:S(2)}) collective-permute-start(f16[4,32,512]{2,1,0:T(8,128)(2,1)S(1)} %collective-permute-done.3), channel_id=1, source_target_pairs={{0,1},{1,0},{2,3},{3,2},{4,5},{5,4},{6,7},{7,6},{8,9},{9,8},{10,11... | collective-permute-start | bytes 393224 | tf_op jit(solution)/shard_map/ppermute | solution.py:186
  51.9 8.5 %collective-permute-start.13 = (f16[264,512]{1,0:T(8,128)(2,1)S(1)}, f16[264,512]{1,0:T(8,128)(2,1)S(1)}, u32[]{:S(2)}, u32[]{:S(2)}) collective-permute-start(f16[264,512]{1,0:T(8,128)(2,1)S(1)} %convert_element_type.42), channel_id=1, source_target_pairs={{0,1},{1,0},{2,3},{3,2},{4,5},{5,4},{6,7},{7,6},{8,9},{9,8},{10,11... | collective-permute-start | bytes 811016 | tf_op jit(solution)/shard_map/ppermute | solution.py:424

commit v10 on v8

--- a/solution.py
+++ b/solution.py
@@ -40,7 +40,8 @@
 
 def shifted(block, axis, distance):
     count = lax.axis_size(axis)
-    return lax.ppermute(block, axis, [(i, (i + distance) % count) for i in range(count)])
+    route = [(i, i + distance) for i in range(count - distance)]
+    return lax.ppermute(block, axis, route)
 
 
 def in_squares():
@@ -250,7 +251,7 @@
     entry_scale = width ** -0.5
     read = pltpu.make_async_copy(hamiltonian_ref, hamiltonian_rows, hamiltonian_sem)
     read.start()
-    energy, rep = lax.axis_index("energy"), lax.axis_index("rep")
+    rep = lax.axis_index("rep")
     bare = bare_ref[...]
     once = [once_ref[f] for f in range(FREQS)]
     at = jnp.where(steps_ref[1] > steps_ref[0], 1, 0)
@@ -277,7 +278,6 @@
         value = value.astype(jnp.bfloat16)
         made[f] = value
         lowered = jnp.where(offsets_ref[f] == SHIFTS, four, less).astype(jnp.float32)
-        lowered = jnp.where(energy >= offsets_ref[f], lowered, 0.0)
         energy_terms += lowered * value.astype(jnp.float32)
     write = pltpu.make_async_copy(made, screened_ref, made_sem)
     write.start()

time: 69.3 us -> 60.9 us (0.88)
  the two profiles are of different devices: /device:TPU:0 before, /device:TPU:26 now
where the time goes in v10:
time: 60.9 us; the launch traced here: 60.6 us
  waiting for transfers between devices  25.4 us (42%)
  starting transfers between devices  22.2 us (36%)
  Pallas kernels  9.69 us (16%)
  between operations  2.93 us (5%)
    ppermute x3, waiting for transfers between devices, gather_energy(): got = lax.ppermute(chunk, 'energy', route)  7.22 us
    all_to_all x1, starting transfers between devices, polar_share(): got = lax.all_to_all(sent, 'energy', 0, 0, tiled=True)  6.14 us
    all_to_all x1, waiting for transfers between devices, polar_share(): got = lax.all_to_all(sent, 'energy', 0, 0, tiled=True)  5.67 us
    ppermute x1, waiting for transfers between devices, body(): lax.ppermute(packed.astype(coded), 'rep', [(0, 1), (1, 0)])  5.1 us
    ppermute x3, waiting for transfers between devices, along_x(): return lax.ppermute(part, 'energy', [(e, e ^ 1) for e in range(energies)])  4.56 us
    ppermute x3, starting transfers between devices, along_x(): return lax.ppermute(part, 'energy', [(e, e ^ 1) for e in range(energies)])  4.43 us
    ppermute x3, starting transfers between devices, shifted(): return lax.ppermute(block, axis, route)  3.85 us
    ppermute x3, starting transfers between devices, along_rep(): return lax.ppermute(part, 'rep', [(0, 1), (1, 0)])  3.55 us
  transfers between devices with their start and end apart: 15, of which 8 were waited for; matrix products, arithmetic and copies ran while one was open for 0% of the time, Pallas kernels for 5%

profile of v10, /device:TPU:26, one launch (start us, length us, event | category | flops | bytes accessed | tf_op | source)
XLA Modules:
  0.0 60.6 jit_solution(15515016501549304925)
XLA Ops:
  1.3 0.0 copy-start.1
  1.3 1.7 %prepare.1 = bf16[8,40,512]{2,1,0:T(8,128)(2,1)} custom-call(f32[1]{0:T(128)S(6)} %copy.19.weight_ref, bf16[256,512]{1,0:T(8,128)(2,1)} %bitcast.10), custom_call_target="tpu_custom_call" | custom-call | tf_op jit(solution)/shard_map/prepare/pallas_call | solution.py:113
  3.0 0.0 copy-start
  3.0 6.1 %all-to-all-start = ((bf16[8,40,512]{2,1,0:T(8,128)(2,1)}), bf16[8,40,512]{2,1,0:T(8,128)(2,1)S(1)}, u32[]{:S(2)}, u32[]{:S(2)}) async-start(bf16[8,40,512]{2,1,0:T(8,128)(2,1)} %prepare.1), calls=%async_computation | async-start | bytes 655360 | tf_op jit(solution)/shard_map/all_to_all | solution.py:126
  9.1 0.0 copy-done.1
  9.1 1.3 %collective-permute-start.9 = (bf16[256,512]{1,0:T(8,128)(2,1)S(1)}, bf16[256,512]{1,0:T(8,128)(2,1)S(1)}, u32[]{:S(2)}, u32[]{:S(2)}) collective-permute-start(bf16[256,512]{1,0:T(8,128)(2,1)S(1)} %bitcast.11), channel_id=1, source_target_pairs={{0,8},{4,12},{8,16},{12,20},{16,24},{20,28},{1,9},{5,13},{9,17},{1... | collective-permute-start | bytes 786440 | tf_op jit(solution)/shard_map/ppermute | solution.py:44
  11.8 0.0 copy-start.2
  11.8 0.0 copy-start.3
  11.8 5.7 %all-to-all-done.got_ref = bf16[8,40,512]{2,1,0:T(8,128)(2,1)S(1)} async-done(((bf16[8,40,512]{2,1,0:T(8,128)(2,1)}), bf16[8,40,512]{2,1,0:T(8,128)(2,1)S(1)}, u32[]{:S(2)}, u32[]{:S(2)}) %all-to-all-start) | async-done | bytes 327712 | tf_op jit(solution)/shard_map/all_to_all | solution.py:126
  17.5 0.0 copy-done
  17.5 0.0 copy-done.2
  17.5 0.0 copy-done.3
  17.5 0.8 %polar.1 = f32[2,32,512]{2,1,0:T(8,128)S(1)} custom-call(s32[2]{0:T(128)S(1)} %copy-done.2, s32[2]{0:T(128)S(1)} %copy-done.3, s32[1]{0:T(128)S(6)} %copy.21.green_steps_ref.steps_ref, f32[1]{0:T(128)S(6)} %copy.20.level_ref.refs_7_, bf16[8,40,512]{2,1,0:T(8,128)(2,1)S(1)} %all-to-all-done.got_ref, f32[256,512]{1,0:T(8,128)S(1)} %bitcast.7), custom_call_target="tpu_custom_call" | custom-call | tf_op jit(solution)/shard_map/polar/pallas_call | solution.py:127
  18.3 2.0 %collective-permute-start.2 = (f16[2,32,512]{2,1,0:T(8,128)(2,1)S(1)}, f16[2,32,512]{2,1,0:T(8,128)(2,1)S(1)}, u32[]{:S(2)}, u32[]{:S(2)}) collective-permute-start(f16[2,32,512]{2,1,0:T(8,128)(2,1)S(1)} %convert_element_type.33), channel_id=1, source_target_pairs={{0,8},{4,12},{8,16},{12,20},{16,24},{20,28},{24,0},{28,4},{1,9},{5... | collective-permute-start | bytes 196616 | tf_op jit(solution)/shard_map/ppermute | solution.py:171
  20.3 0.0 collective-permute-start.1
  20.3 0.6 %collective-permute-start = (f16[2,32,512]{2,1,0:T(8,128)(2,1)S(1)}, f16[2,32,512]{2,1,0:T(8,128)(2,1)S(1)}, u32[]{:S(2)}, u32[]{:S(2)}) collective-permute-start(f16[2,32,512]{2,1,0:T(8,128)(2,1)S(1)} %convert_element_type.33), channel_id=1, source_target_pairs={{0,24},{4,28},{8,0},{12,4},{16,8},{20,12},{24,16},{28,20},{1,25},{... | collective-permute-start | bytes 196616 | tf_op jit(solution)/shard_map/ppermute | solution.py:171
  21.0 5.4 %collective-permute-done = f16[2,32,512]{2,1,0:T(8,128)(2,1)S(1)} collective-permute-done((f16[2,32,512]{2,1,0:T(8,128)(2,1)S(1)}, f16[2,32,512]{2,1,0:T(8,128)(2,1)S(1)}, u32[]{:S(2)}, u32[]{:S(2)}) %collective-permute-start) | collective-permute-done | bytes 65568 | tf_op jit(solution)/shard_map/ppermute | solution.py:171
  26.5 1.8 %collective-permute-done.1 = f16[2,32,512]{2,1,0:T(8,128)(2,1)S(1)} collective-permute-done((f16[2,32,512]{2,1,0:T(8,128)(2,1)S(1)}, f16[2,32,512]{2,1,0:T(8,128)(2,1)S(1)}, u32[]{:S(2)}, u32[]{:S(2)}) %collective-permute-start.1) | collective-permute-done | bytes 65568 | tf_op jit(solution)/shard_map/ppermute | solution.py:171
  28.3 0.0 collective-permute-done.2
  28.3 0.3 collective-permute-start.7
  28.7 1.5 %collective-permute-start.5 = (f16[4,32,512]{2,1,0:T(8,128)(2,1)S(1)}, f16[4,32,512]{2,1,0:T(8,128)(2,1)S(1)}, u32[]{:S(2)}, u32[]{:S(2)}) collective-permute-start(f16[4,32,512]{2,1,0:T(8,128)(2,1)S(1)} %get-tuple-element.24), channel_id=1, source_target_pairs={{0,1},{1,0},{2,3},{3,2},{4,5},{5,4},{6,7},{7,6},{8,9},{9,8},{10,11... | collective-permute-start | bytes 393224 | tf_op jit(solution)/shard_map/ppermute | solution.py:186
  30.2 0.0 collective-permute-start.12
  30.2 0.5 collective-permute-start.8
  30.7 0.0 collective-permute-done.9.two_ref.refs_10_
  30.7 1.8 %collective-permute-start.3 = (f16[4,32,512]{2,1,0:T(8,128)(2,1)S(1)}, f16[4,32,512]{2,1,0:T(8,128)(2,1)S(1)}, u32[]{:S(2)}, u32[]{:S(2)}) collective-permute-start(f16[4,32,512]{2,1,0:T(8,128)(2,1)S(1)} %get-tuple-element.25), channel_id=1, source_target_pairs={{0,4},{4,0},{8,12},{12,8},{16,20},{20,16},{24,28},{28,24},{1,5},{5... | collective-permute-start | bytes 393224 | tf_op jit(solution)/shard_map/ppermute | solution.py:183
  32.5 0.6 chosen.1
  33.0 0.4 collective-permute-done.7
  33.5 1.3 %collective-permute-start.11 = (bf16[256,512]{1,0:T(8,128)(2,1)S(1)}, bf16[256,512]{1,0:T(8,128)(2,1)S(1)}, u32[]{:S(2)}, u32[]{:S(2)}) collective-permute-start(bf16[256,512]{1,0:T(8,128)(2,1)S(1)} %chosen.1), channel_id=1, source_target_pairs={{0,4},{4,8},{8,12},{12,16},{16,20},{20,24},{24,28},{1,5},{5,9},{9,... | collective-permute-start | bytes 786440 | tf_op jit(solution)/shard_map/ppermute | solution.py:44
  34.8 0.0 collective-permute-done.5
  34.8 1.3 %collective-permute-start.10 = (bf16[256,512]{1,0:T(8,128)(2,1)S(1)}, bf16[256,512]{1,0:T(8,128)(2,1)S(1)}, u32[]{:S(2)}, u32[]{:S(2)}) collective-permute-start(bf16[256,512]{1,0:T(8,128)(2,1)S(1)} %collective-permute-done.9.two_ref.refs_10_), channel_id=1, source_target_pairs={{0,8},{4,12},{8,16},{12,20},{16,24},{20,28},{1,9},{5,13},{9,17},{1... | collective-permute-start | bytes 786440 | tf_op jit(solution)/shard_map/ppermute | solution.py:44
  36.1 0.4 collective-permute-done.8
  36.4 2.3 %collective-permute-start.6 = (f16[4,32,512]{2,1,0:T(8,128)(2,1)S(1)}, f16[4,32,512]{2,1,0:T(8,128)(2,1)S(1)}, u32[]{:S(2)}, u32[]{:S(2)}) collective-permute-start(f16[4,32,512]{2,1,0:T(8,128)(2,1)S(1)} %collective-permute-done.5), channel_id=1, source_target_pairs={{0,4},{4,0},{8,12},{12,8},{16,20},{20,16},{24,28},{28,24},{1,5},{5... | collective-permute-start | bytes 393224 | tf_op jit(solution)/shard_map/ppermute | solution.py:183
  38.8 0.0 collective-permute-done.3
  38.8 1.5 %collective-permute-start.4 = (f16[4,32,512]{2,1,0:T(8,128)(2,1)S(1)}, f16[4,32,512]{2,1,0:T(8,128)(2,1)S(1)}, u32[]{:S(2)}, u32[]{:S(2)}) collective-permute-start(f16[4,32,512]{2,1,0:T(8,128)(2,1)S(1)} %collective-permute-done.3), channel_id=1, source_target_pairs={{0,1},{1,0},{2,3},{3,2},{4,5},{5,4},{6,7},{7,6},{8,9},{9,8},{10,11... | collective-permute-start | bytes 393224 | tf_op jit(solution)/shard_map/ppermute | solution.py:186
  40.5 1.3 %early.1 = (f32[2,256,512]{2,1,0:T(8,128)S(1)}, bf16[2,512,512]{2,1,0:T(8,128)(2,1)S(1)}, bf16[2,512,512]{2,1,0:T(8,128)(2,1)S(1)}) custom-call(f32[4,32,512]{2,1,0:T(8,128)S(1)} %convert_element_type.36.refs_0_, f32[4,32,512]{2,1,0:T(8,128)S(1)} %convert_element_type.37.refs_1_, f32[4,32,512]{2,1,0:T(8,128)S(1)} %convert_element_type.38.refs_2_, ...), custom_call_target="tpu_custom_call" | custom-call | tf_op jit(solution)/shard_map/early/pallas_call | solution.py:318
  41.8 4.1 %collective-permute-done.6 = f16[4,32,512]{2,1,0:T(8,128)(2,1)S(1)} collective-permute-done((f16[4,32,512]{2,1,0:T(8,128)(2,1)S(1)}, f16[4,32,512]{2,1,0:T(8,128)(2,1)S(1)}, u32[]{:S(2)}, u32[]{:S(2)}) %collective-permute-start.6) | collective-permute-done | bytes 131104 | tf_op jit(solution)/shard_map/ppermute | solution.py:183
  45.9 0.0 collective-permute-done.4
  46.0 0.0 collective-permute-done.12.refs_13_
  46.0 0.0 collective-permute-done.11.refs_12_
  46.0 2.5 %collective-permute-done.10.refs_11_ = bf16[256,512]{1,0:T(8,128)(2,1)S(1)} collective-permute-done((bf16[256,512]{1,0:T(8,128)(2,1)S(1)}, bf16[256,512]{1,0:T(8,128)(2,1)S(1)}, u32[]{:S(2)}, u32[]{:S(2)}) %collective-permute-start.10) | collective-permute-done | bytes 262176 | tf_op jit(solution)/shard_map/ppermute | solution.py:44
  48.5 3.2 %dyson.1 = (bf16[2,256,512]{2,1,0:T(8,128)(2,1)}, f32[264,512]{1,0:T(8,128)S(1)}, f32[256,512]{1,0:T(8,128)S(1)}, f32[8,512]{1,0:T(8,128)S(1)}) custom-call(f32[4,32,512]{2,1,0:T(8,128)S(1)} %convert_element_type.34.refs_0_, f32[4,32,512]{2,1,0:T(8,128)S(1)} %convert_element_type.35.refs_1_, f32[2,256,512]{2,1,0:T(8,128)S(1)} %get-tuple-element.12.refs_2_, ...), custom_call_target="tpu_custom_call" | custom-call | tf_op jit(solution)/shard_map/dyson/pallas_call | solution.py:334
  51.7 1.6 %collective-permute-start.13 = (f16[264,512]{1,0:T(8,128)(2,1)S(1)}, f16[264,512]{1,0:T(8,128)(2,1)S(1)}, u32[]{:S(2)}, u32[]{:S(2)}) collective-permute-start(f16[264,512]{1,0:T(8,128)(2,1)S(1)} %convert_element_type.42), channel_id=1, source_target_pairs={{0,1},{1,0},{2,3},{3,2},{4,5},{5,4},{6,7},{7,6},{8,9},{9,8},{10,11... | collective-permute-start | bytes 811016 | tf_op jit(solution)/shard_map/ppermute | solution.py:423
  53.3 0.4 begin.1
  53.7 5.1 %collective-permute-done.13 = f16[264,512]{1,0:T(8,128)(2,1)S(1)} collective-permute-done((f16[264,512]{1,0:T(8,128)(2,1)S(1)}, f16[264,512]{1,0:T(8,128)(2,1)S(1)}, u32[]{:S(2)}, u32[]{:S(2)}) %collective-permute-start.13) | collective-permute-done | bytes 270368 | tf_op jit(solution)/shard_map/ppermute | solution.py:423
  58.8 0.1 convert_element_type.43.theirs_ref
  58.9 1.7 %finish.1 = f32[256,512]{1,0:T(8,128)} custom-call(s32[1]{0:T(128)S(6)} %copy.21.green_steps_ref.steps_ref, f32[256,512]{1,0:T(8,128)S(1)} %get-tuple-element.15.step_ref, f32[256,512]{1,0:T(8,128)S(1)} %get-tuple-element.18.square_ref, bf16[256,512]{1,0:T(8,128)(2,1)S(1)} %get-tuple-element.19.high_ref, bf16[256,512]{1,0:T(8,128)(2,1)S(1)} %get-tuple-element.20.low_ref, ...), custom_call_target="tpu_custom_call" | custom-call | tf_op jit(solution)/shard_map/finish/pallas_call | solution.py:434
  (17 shorter events, 0.3 us)
Async XLA Ops:
  1.3 7.8 %copy-start.1 = (bf16[1,1,256,512]{3,2,1,0:T(8,128)(2,1)S(1)}, bf16[1,1,256,512]{3,2,1,0:T(8,128)(2,1)}, u32[]{:S(2)}) copy-start(bf16[1,1,256,512]{3,2,1,0:T(8,128)(2,1)} %param.8) | copy-start | bytes 786436
  3.0 14.5 %copy-start = (f32[1,256,512]{2,1,0:T(8,128)S(1)}, f32[1,256,512]{2,1,0:T(8,128)}, u32[]{:S(2)}) copy-start(f32[1,256,512]{2,1,0:T(8,128)} %param.11) | copy-start | bytes 1572868
  3.0 14.5 %all-to-all-start = ((bf16[8,40,512]{2,1,0:T(8,128)(2,1)}), bf16[8,40,512]{2,1,0:T(8,128)(2,1)S(1)}, u32[]{:S(2)}, u32[]{:S(2)}) async-start(bf16[8,40,512]{2,1,0:T(8,128)(2,1)} %prepare.1), calls=%async_computation | async-start | bytes 655360 | tf_op jit(solution)/shard_map/all_to_all | solution.py:126
  9.1 21.6 %collective-permute-start.9 = (bf16[256,512]{1,0:T(8,128)(2,1)S(1)}, bf16[256,512]{1,0:T(8,128)(2,1)S(1)}, u32[]{:S(2)}, u32[]{:S(2)}) collective-permute-start(bf16[256,512]{1,0:T(8,128)(2,1)S(1)} %bitcast.11), channel_id=1, source_target_pairs={{0,8},{4,12},{8,16},{12,20},{16,24},{20,28},{1,9},{5,13},{9,17},{1... | collective-permute-start | bytes 786440 | tf_op jit(solution)/shard_map/ppermute | solution.py:44
  11.8 5.7 %copy-start.2 = (s32[2]{0:T(128)S(1)}, s32[2]{0:T(128)}, u32[]{:S(2)}) copy-start(s32[2]{0:T(128)} %refs_5_.1) | copy-start | bytes 28
  11.8 5.7 %copy-start.3 = (s32[2]{0:T(128)S(1)}, s32[2]{0:T(128)}, u32[]{:S(2)}) copy-start(s32[2]{0:T(128)} %refs_6_.1) | copy-start | bytes 28
  18.3 9.9 %collective-permute-start.2 = (f16[2,32,512]{2,1,0:T(8,128)(2,1)S(1)}, f16[2,32,512]{2,1,0:T(8,128)(2,1)S(1)}, u32[]{:S(2)}, u32[]{:S(2)}) collective-permute-start(f16[2,32,512]{2,1,0:T(8,128)(2,1)S(1)} %convert_element_type.33), channel_id=1, source_target_pairs={{0,8},{4,12},{8,16},{12,20},{16,24},{20,28},{24,0},{28,4},{1,9},{5... | collective-permute-start | bytes 196616 | tf_op jit(solution)/shard_map/ppermute | solution.py:171
  20.3 8.0 %collective-permute-start.1 = (f16[2,32,512]{2,1,0:T(8,128)(2,1)S(1)}, f16[2,32,512]{2,1,0:T(8,128)(2,1)S(1)}, u32[]{:S(2)}, u32[]{:S(2)}) collective-permute-start(f16[2,32,512]{2,1,0:T(8,128)(2,1)S(1)} %convert_element_type.33), channel_id=1, source_target_pairs={{0,16},{4,20},{8,24},{12,28},{16,0},{20,4},{24,8},{28,12},{1,17},{... | collective-permute-start | bytes 196616 | tf_op jit(solution)/shard_map/ppermute | solution.py:171
  20.3 6.2 %collective-permute-start = (f16[2,32,512]{2,1,0:T(8,128)(2,1)S(1)}, f16[2,32,512]{2,1,0:T(8,128)(2,1)S(1)}, u32[]{:S(2)}, u32[]{:S(2)}) collective-permute-start(f16[2,32,512]{2,1,0:T(8,128)(2,1)S(1)} %convert_element_type.33), channel_id=1, source_target_pairs={{0,24},{4,28},{8,0},{12,4},{16,8},{20,12},{24,16},{28,20},{1,25},{... | collective-permute-start | bytes 196616 | tf_op jit(solution)/shard_map/ppermute | solution.py:171
  28.3 5.1 %collective-permute-start.7 = (f16[4,32,512]{2,1,0:T(8,128)(2,1)S(1)}, f16[4,32,512]{2,1,0:T(8,128)(2,1)S(1)}, u32[]{:S(2)}, u32[]{:S(2)}) collective-permute-start(f16[4,32,512]{2,1,0:T(8,128)(2,1)S(1)} %get-tuple-element.24), channel_id=1, source_target_pairs={{0,4},{4,0},{8,12},{12,8},{16,20},{20,16},{24,28},{28,24},{1,5},{5... | collective-permute-start | bytes 393224 | tf_op jit(solution)/shard_map/ppermute | solution.py:183
  28.7 6.1 %collective-permute-start.5 = (f16[4,32,512]{2,1,0:T(8,128)(2,1)S(1)}, f16[4,32,512]{2,1,0:T(8,128)(2,1)S(1)}, u32[]{:S(2)}, u32[]{:S(2)}) collective-permute-start(f16[4,32,512]{2,1,0:T(8,128)(2,1)S(1)} %get-tuple-element.24), channel_id=1, source_target_pairs={{0,1},{1,0},{2,3},{3,2},{4,5},{5,4},{6,7},{7,6},{8,9},{9,8},{10,11... | collective-permute-start | bytes 393224 | tf_op jit(solution)/shard_map/ppermute | solution.py:186
  30.2 15.8 %collective-permute-start.12 = (bf16[256,512]{1,0:T(8,128)(2,1)S(1)}, bf16[256,512]{1,0:T(8,128)(2,1)S(1)}, u32[]{:S(2)}, u32[]{:S(2)}) collective-permute-start(bf16[256,512]{1,0:T(8,128)(2,1)S(1)} %bitcast.12), channel_id=1, source_target_pairs={{0,2},{2,0},{1,3},{3,1},{4,6},{6,4},{5,7},{7,5},{8,10},{10,8},{9,1... | collective-permute-start | bytes 786440 | tf_op jit(solution)/shard_map/ppermute | solution.py:414
  30.2 6.3 %collective-permute-start.8 = (f16[4,32,512]{2,1,0:T(8,128)(2,1)S(1)}, f16[4,32,512]{2,1,0:T(8,128)(2,1)S(1)}, u32[]{:S(2)}, u32[]{:S(2)}) collective-permute-start(f16[4,32,512]{2,1,0:T(8,128)(2,1)S(1)} %get-tuple-element.25), channel_id=1, source_target_pairs={{0,1},{1,0},{2,3},{3,2},{4,5},{5,4},{6,7},{7,6},{8,9},{9,8},{10,11... | collective-permute-start | bytes 393224 | tf_op jit(solution)/shard_map/ppermute | solution.py:186
  30.7 8.1 %collective-permute-start.3 = (f16[4,32,512]{2,1,0:T(8,128)(2,1)S(1)}, f16[4,32,512]{2,1,0:T(8,128)(2,1)S(1)}, u32[]{:S(2)}, u32[]{:S(2)}) collective-permute-start(f16[4,32,512]{2,1,0:T(8,128)(2,1)S(1)} %get-tuple-element.25), channel_id=1, source_target_pairs={{0,4},{4,0},{8,12},{12,8},{16,20},{20,16},{24,28},{28,24},{1,5},{5... | collective-permute-start | bytes 393224 | tf_op jit(solution)/shard_map/ppermute | solution.py:183
  33.5 12.5 %collective-permute-start.11 = (bf16[256,512]{1,0:T(8,128)(2,1)S(1)}, bf16[256,512]{1,0:T(8,128)(2,1)S(1)}, u32[]{:S(2)}, u32[]{:S(2)}) collective-permute-start(bf16[256,512]{1,0:T(8,128)(2,1)S(1)} %chosen.1), channel_id=1, source_target_pairs={{0,4},{4,8},{8,12},{12,16},{16,20},{20,24},{24,28},{1,5},{5,9},{9,... | collective-permute-start | bytes 786440 | tf_op jit(solution)/shard_map/ppermute | solution.py:44
  34.8 13.7 %collective-permute-start.10 = (bf16[256,512]{1,0:T(8,128)(2,1)S(1)}, bf16[256,512]{1,0:T(8,128)(2,1)S(1)}, u32[]{:S(2)}, u32[]{:S(2)}) collective-permute-start(bf16[256,512]{1,0:T(8,128)(2,1)S(1)} %collective-permute-done.9.two_ref.refs_10_), channel_id=1, source_target_pairs={{0,8},{4,12},{8,16},{12,20},{16,24},{20,28},{1,9},{5,13},{9,17},{1... | collective-permute-start | bytes 786440 | tf_op jit(solution)/shard_map/ppermute | solution.py:44
  36.4 9.5 %collective-permute-start.6 = (f16[4,32,512]{2,1,0:T(8,128)(2,1)S(1)}, f16[4,32,512]{2,1,0:T(8,128)(2,1)S(1)}, u32[]{:S(2)}, u32[]{:S(2)}) collective-permute-start(f16[4,32,512]{2,1,0:T(8,128)(2,1)S(1)} %collective-permute-done.5), channel_id=1, source_target_pairs={{0,4},{4,0},{8,12},{12,8},{16,20},{20,16},{24,28},{28,24},{1,5},{5... | collective-permute-start | bytes 393224 | tf_op jit(solution)/shard_map/ppermute | solution.py:183
  38.8 7.1 %collective-permute-start.4 = (f16[4,32,512]{2,1,0:T(8,128)(2,1)S(1)}, f16[4,32,512]{2,1,0:T(8,128)(2,1)S(1)}, u32[]{:S(2)}, u32[]{:S(2)}) collective-permute-start(f16[4,32,512]{2,1,0:T(8,128)(2,1)S(1)} %collective-permute-done.3), channel_id=1, source_target_pairs={{0,1},{1,0},{2,3},{3,2},{4,5},{5,4},{6,7},{7,6},{8,9},{9,8},{10,11... | collective-permute-start | bytes 393224 | tf_op jit(solution)/shard_map/ppermute | solution.py:186
  51.7 7.1 %collective-permute-start.13 = (f16[264,512]{1,0:T(8,128)(2,1)S(1)}, f16[264,512]{1,0:T(8,128)(2,1)S(1)}, u32[]{:S(2)}, u32[]{:S(2)}) collective-permute-start(f16[264,512]{1,0:T(8,128)(2,1)S(1)} %convert_element_type.42), channel_id=1, source_target_pairs={{0,1},{1,0},{2,3},{3,2},{4,5},{5,4},{6,7},{7,6},{8,9},{9,8},{10,11... | collective-permute-start | bytes 811016 | tf_op jit(solution)/shard_map/ppermute | solution.py:423

commit v11 on v10

--- a/solution.py
+++ b/solution.py
@@ -54,52 +54,80 @@
     return place % 2 * outer + place // 2 if in_squares() else place
 
 
-def prepare_kernel(weight_ref, block_ref, out_ref, held_rows, read_sems, write_sems):
-    energies, padded, width = out_ref.shape
-    share = padded - EXTRA
-    reads = [
-        pltpu.make_async_copy(
-            block_ref.at[pl.ds(share_of(k) * share, share), :],
-            held_rows.at[k, pl.ds(0, share), :], read_sems.at[k],
-        )
-        for k in range(energies)
-    ]
-    for copy in reads:
-        copy.start()
-    weight = jnp.full((EXTRA, width), weight_ref[0], jnp.float32)
+def weight_rows(weight, first_row, width):
+    weight = jnp.full((EXTRA, width), weight, jnp.float32)
     first = weight.astype(jnp.bfloat16).astype(jnp.float32)
     second = (weight - first).astype(jnp.bfloat16).astype(jnp.float32)
     third = weight - first - second
-    row = lax.broadcasted_iota(jnp.int32, (EXTRA, width), 0)
-    tail = jnp.where(row == 0, first, jnp.where(row == 1, second, third)).astype(jnp.bfloat16)
-    writes = [
-        pltpu.make_async_copy(held_rows.at[k], out_ref.at[k], write_sems.at[k])
-        for k in range(energies)
-    ]
-    for k in range(energies):
-        held_rows[k, share:, :] = tail
-    for k in range(energies):
-        reads[k].wait()
-        writes[k].start()
-    for copy in writes:
-        copy.wait()
-
-
-def polar_kernel(offsets_ref, screen_ref, green_steps_ref, level_ref, got_ref, bare_ref, out_ref, padded, bare_rows, arrived):
-    energies, tall, width = got_ref.shape
-    share = tall - EXTRA
-    start = pl.multiple_of(share_of(lax.axis_index("energy")) * share, share)
+    row = lax.broadcasted_iota(jnp.int32, (EXTRA, width), 0) - first_row
+    later = jnp.where(row == 1, second, jnp.where(row == 2, third, 0.0))
+    return jnp.where(row == 0, first, later)
+
+
+def prepare_kernel(weight_ref, block_ref, out_ref, arrived):
+    half, width = out_ref.shape[0] - EXTRA, out_ref.shape[1]
+    x = lax.axis_index("energy") % 2
+    start = pl.multiple_of((1 - x) * half, half)
+    copy = pltpu.make_async_copy(
+        block_ref.at[pl.ds(start, half), :], out_ref.at[pl.ds(0, half), :], arrived
+    )
+    copy.start()
+    out_ref[half:, :] = weight_rows(weight_ref[0], 3, width).astype(out_ref.dtype)
+    copy.wait()
+
+
+def arrange_kernel(weight_ref, block_ref, got_ref, *out_refs):
+    outer = len(out_refs) + 1
+    half, width = got_ref.shape[0] - EXTRA, got_ref.shape[1]
+    share = half // outer
+    x, z = lax.axis_index("energy") % 2, lax.axis_index("energy") // 2
+    tail = weight_rows(weight_ref[0], 0, width) + got_ref[half:, :].astype(jnp.float32)
+    tail = tail.astype(got_ref.dtype)
+    for k, out_ref in enumerate(out_refs, 1):
+        at = (z + k) % outer * share
+        mine = pl.ds(pl.multiple_of(x * half + at, share), share)
+        out_ref[:share, :] = block_ref[mine, :]
+        out_ref[share:2 * share, :] = got_ref[pl.ds(pl.multiple_of(at, share), share), :]
+        out_ref[2 * share:, :] = tail
+
+
+def polar_kernel(received, weight_ref, offsets_ref, block_ref, got_ref, bare_ref, out_ref,
+                 padded, weighted, bare_rows, arrived):
+    _, share, width = out_ref.shape
+    energies = weighted.shape[0]
+    outer = energies // 2
+    half = outer * share
+    energy = lax.axis_index("energy")
+    x, z = energy % 2, energy // 2
+    start = pl.multiple_of(x * half + z * share, share)
     copy = pltpu.make_async_copy(bare_ref.at[pl.ds(start, share), :], bare_rows, arrived)
     copy.start()
     padded[:SHIFTS] = jnp.zeros((SHIFTS, share, width), jnp.float32)
-    for e in range(energies):
-        padded[SHIFTS + e] = got_ref[e, :share, :].astype(jnp.float32)
+
+    def place(at, rows, weight):
+        rows = rows.astype(jnp.float32)
+        padded[SHIFTS + at] = rows
+        weighted[at] = rows * weight
+
+    def total(tail, row):
+        return tail[row:row + 1] + tail[row + 1:row + 2] + tail[row + 2:row + 3]
+
+    place(energy, block_ref[pl.ds(start, share), :], weight_ref[0])
+    place(
+        z * 2 + 1 - x,
+        got_ref[pl.ds(pl.multiple_of(z * share, share), share), :],
+        total(got_ref[half:, :].astype(jnp.float32), 3),
+    )
+    for k, ref in enumerate(received, 1):
+        behind = (z + outer - k) % outer * 2
+        tail = ref[2 * share:, :].astype(jnp.float32)
+        place(behind + x, ref[:share, :], total(tail, 0))
+        place(behind + 1 - x, ref[share:2 * share, :], total(tail, 3))
     totals = [jnp.zeros((share, width), jnp.float32) for _ in range(FREQS)]
     for e in range(energies):
-        tail = got_ref[e, share:, :].astype(jnp.float32)
-        weighted = padded[SHIFTS + e] * (tail[0:1] + tail[1:2] + tail[2:3])
+        own = weighted[e]
         for f in range(FREQS):
-            totals[f] += weighted * padded[SHIFTS + e - offsets_ref[f]]
+            totals[f] += own * padded[SHIFTS + e - offsets_ref[f]]
     copy.wait()
     factor = -(width ** -0.5) * energies ** -0.5
     for f in range(FREQS):
@@ -109,34 +137,50 @@
 def polar_share(green, weight, offsets, bare, scalars):
     energies = lax.axis_size("energy")
     rows, width = green.shape
+    outer = energies // 2
     share = rows // energies
+    half = rows // 2
     sent = pl.pallas_call(
         prepare_kernel,
-        out_shape=jax.ShapeDtypeStruct((energies, share + EXTRA, width), green.dtype),
+        out_shape=jax.ShapeDtypeStruct((half + EXTRA, width), green.dtype),
         in_specs=[in_smem, in_hbm],
-        out_specs=in_hbm,
-        scratch_shapes=[
-            VMEM((energies, share + EXTRA, width), green.dtype),
-            pltpu.SemaphoreType.DMA((energies,)),
-            pltpu.SemaphoreType.DMA((energies,)),
-        ],
+        out_specs=in_vmem,
+        scratch_shapes=[pltpu.SemaphoreType.DMA],
         compiler_params=small,
         name="prepare",
     )(weight, held(green))
-    got = lax.all_to_all(sent, "energy", 0, 0, tiled=True)
+    got = lax.ppermute(sent, "energy", [(e, e ^ 1) for e in range(energies)])
+    shares = pl.pallas_call(
+        arrange_kernel,
+        out_shape=(jax.ShapeDtypeStruct((2 * share + EXTRA, width), green.dtype),) * (outer - 1),
+        in_specs=[in_smem, in_vmem, in_vmem],
+        out_specs=(in_vmem,) * (outer - 1),
+        compiler_params=small,
+        name="arrange",
+    )(weight, green, got)
+    received = [None] * (outer - 1)
+    for k in range(outer - 1, 0, -1):
+        route = [(z * 2 + x, (z + k) % outer * 2 + x) for z in range(outer) for x in range(2)]
+        received[k - 1] = lax.ppermute(shares[k - 1], "energy", route)
+
+    def kernel(*refs):
+        count = outer - 1
+        polar_kernel(refs[:count], *refs[count:count + 2], *refs[count + 5:])
+
     return pl.pallas_call(
-        polar_kernel,
+        kernel,
         out_shape=jax.ShapeDtypeStruct((FREQS, share, width), jnp.float32),
-        in_specs=[in_smem] * 4 + [in_vmem, in_place],
+        in_specs=[in_vmem] * (outer - 1) + [in_smem] * 5 + [in_vmem, in_vmem, in_place],
         out_specs=in_vmem,
         scratch_shapes=[
             VMEM((SHIFTS + energies, share, width), jnp.float32),
+            VMEM((energies, share, width), jnp.float32),
             VMEM((share, width), jnp.float32),
             pltpu.SemaphoreType.DMA,
         ],
         compiler_params=small,
         name="polar",
-    )(offsets, *scalars, got, bare)
+    )(*received, weight, offsets, *scalars, green, got, bare)
 
 
 def polar_share_plain(green, weight, offsets, bare, scalars):
@@ -401,7 +445,7 @@
     bare = coulomb[0]
     rows, width = green.shape
     share = rows // lax.axis_size("energy")
-    make = polar_share if share % 16 == 0 else polar_share_plain
+    make = polar_share if in_squares() and share % 16 == 0 else polar_share_plain
     scalars = (screen_steps, green_steps, onsite_level)
     pieces = gathered(make(green, occupation, offsets, bare, scalars))
 

time: 60.9 us -> 60.2 us (0.989)
  starting transfers between devices: 22.2 us -> 18.3 us
  waiting for transfers between devices: 25.4 us -> 29.2 us
  Pallas kernels: 9.69 us -> 8.98 us
    ppermute x0 -> x4, waiting for transfers between devices: none -> 8.72 us  [the longest x1 4.88 us: polar_share(): got = lax.ppermute(sent, 'energy', [(e, e ^ 1) for e in range(energies)])]
    all_to_all x1 -> x0, starting transfers between devices: 6.14 us -> none  [polar_share(): got = lax.all_to_all(sent, 'energy', 0, 0, tiled=True)]
    all_to_all x1 -> x0, waiting for transfers between devices: 5.67 us -> none  [polar_share(): got = lax.all_to_all(sent, 'energy', 0, 0, tiled=True)]
    ppermute x0 -> x4, starting transfers between devices: none -> 3.01 us  [the longest x3 2.41 us: polar_share(): received[k - 1] = lax.ppermute(shares[k - 1], 'energy', route)]
    pallas_call x2 -> x3, Pallas kernels: 2.51 us -> 1.8 us  [the longest x1 0.93 us: polar_share(): pl.pallas_call(prepare_kernel, out_shape=jax.ShapeDtypeStruct((half + EXT...]
  transfers between devices with their start and end apart: 15 -> 18, of which waited for: 8 -> 9; matrix products, arithmetic and copies ran while one was open for 0% -> 0% of each run, Pallas kernels for 5% -> 5%
where the time goes in v11:
time: 60.2 us; the launch traced here: 60 us
  waiting for transfers between devices  29.2 us (49%)
  starting transfers between devices  18.3 us (30%)
  Pallas kernels  8.98 us (15%)
  between operations  3.03 us (5%)
    ppermute x3, waiting for transfers between devices, gather_energy(): got = lax.ppermute(chunk, 'energy', route)  7.26 us
    ppermute x1, waiting for transfers between devices, body(): lax.ppermute(packed.astype(coded), 'rep', [(0, 1), (1, 0)])  5.22 us
    ppermute x1, waiting for transfers between devices, polar_share(): got = lax.ppermute(sent, 'energy', [(e, e ^ 1) for e in range(energies)])  4.88 us
    ppermute x3, waiting for transfers between devices, along_x(): return lax.ppermute(part, 'energy', [(e, e ^ 1) for e in range(energies)])  4.55 us
    ppermute x3, starting transfers between devices, along_x(): return lax.ppermute(part, 'energy', [(e, e ^ 1) for e in range(energies)])  4.06 us
    ppermute x3, starting transfers between devices, shifted(): return lax.ppermute(block, axis, route)  3.85 us
    ppermute x3, waiting for transfers between devices, polar_share(): received[k - 1] = lax.ppermute(shares[k - 1], 'energy', route)  3.85 us
    ppermute x3, starting transfers between devices, along_rep(): return lax.ppermute(part, 'rep', [(0, 1), (1, 0)])  3.55 us
  transfers between devices with their start and end apart: 18, of which 9 were waited for; matrix products, arithmetic and copies ran while one was open for 0% of the time, Pallas kernels for 5%

profile of v11, /device:TPU:26, one launch (start us, length us, event | category | flops | bytes accessed | tf_op | source)
XLA Modules:
  0.0 60.0 jit_solution(6642733073722247315)
XLA Ops:
  0.6 0.0 copy-start.1
  0.6 0.0 copy-start
  1.4 0.9 %prepare.1 = bf16[136,512]{1,0:T(8,128)(2,1)S(1)} custom-call(f32[1]{0:T(128)S(6)} %copy.19.weight_ref.refs_3_, bf16[256,512]{1,0:T(8,128)(2,1)} %bitcast.10), custom_call_target="tpu_custom_call" | custom-call | tf_op jit(solution)/shard_map/prepare/pallas_call | solution.py:143
  2.3 0.6 %collective-permute-start = (bf16[136,512]{1,0:T(8,128)(2,1)S(1)}, bf16[136,512]{1,0:T(8,128)(2,1)S(1)}, u32[]{:S(2)}, u32[]{:S(2)}) collective-permute-start(bf16[136,512]{1,0:T(8,128)(2,1)S(1)} %prepare.1), channel_id=1, source_target_pairs={{0,4},{4,0},{8,12},{12,8},{16,20},{20,16},{24,28},{28,24},{1,5},{5... | collective-permute-start | bytes 417800 | tf_op jit(solution)/shard_map/ppermute | solution.py:152
  2.9 4.9 %collective-permute-done.got_ref.refs_9_ = bf16[136,512]{1,0:T(8,128)(2,1)S(1)} collective-permute-done((bf16[136,512]{1,0:T(8,128)(2,1)S(1)}, bf16[136,512]{1,0:T(8,128)(2,1)S(1)}, u32[]{:S(2)}, u32[]{:S(2)}) %collective-permute-start) | collective-permute-done | bytes 139296 | tf_op jit(solution)/shard_map/ppermute | solution.py:152
  7.8 0.0 copy-done.1
  7.8 0.3 collective-permute-start.1
  8.1 1.7 %collective-permute-start.2 = (bf16[72,512]{1,0:T(8,128)(2,1)S(1)}, bf16[72,512]{1,0:T(8,128)(2,1)S(1)}, u32[]{:S(2)}, u32[]{:S(2)}) collective-permute-start(bf16[72,512]{1,0:T(8,128)(2,1)S(1)} %get-tuple-element.16), channel_id=1, source_target_pairs={{0,16},{4,20},{8,24},{12,28},{16,0},{20,4},{24,8},{28,12},{1,17},{... | collective-permute-start | bytes 221192 | tf_op jit(solution)/shard_map/ppermute | solution.py:164
  9.8 0.4 collective-permute-start.3
  10.2 1.3 %collective-permute-start.13 = (bf16[256,512]{1,0:T(8,128)(2,1)S(1)}, bf16[256,512]{1,0:T(8,128)(2,1)S(1)}, u32[]{:S(2)}, u32[]{:S(2)}) collective-permute-start(bf16[256,512]{1,0:T(8,128)(2,1)S(1)} %bitcast.12), channel_id=1, source_target_pairs={{0,8},{4,12},{8,16},{12,20},{16,24},{20,28},{1,9},{5,13},{9,17},{1... | collective-permute-start | bytes 786440 | tf_op jit(solution)/shard_map/ppermute | solution.py:44
  12.9 0.0 copy-start.2
  12.9 0.0 copy-start.3
  12.9 0.0 collective-permute-done.1.refs_0_
  12.9 3.8 %collective-permute-done.2.refs_1_ = bf16[72,512]{1,0:T(8,128)(2,1)S(1)} collective-permute-done((bf16[72,512]{1,0:T(8,128)(2,1)S(1)}, bf16[72,512]{1,0:T(8,128)(2,1)S(1)}, u32[]{:S(2)}, u32[]{:S(2)}) %collective-permute-start.2) | collective-permute-done | bytes 73760 | tf_op jit(solution)/shard_map/ppermute | solution.py:164
  16.8 0.0 collective-permute-done.3.refs_2_
  16.8 0.0 copy-done
  16.8 0.0 copy-done.2
  16.8 0.0 copy-done.3
  16.8 0.8 %polar.1 = f32[2,32,512]{2,1,0:T(8,128)S(1)} custom-call(bf16[72,512]{1,0:T(8,128)(2,1)S(1)} %collective-permute-done.1.refs_0_, bf16[72,512]{1,0:T(8,128)(2,1)S(1)} %collective-permute-done.2.refs_1_, bf16[72,512]{1,0:T(8,128)(2,1)S(1)} %collective-permute-done.3.refs_2_, f32[1]{0:T(128)S(6)} %copy.19.weight_ref.refs_3_, s32[2]{0:T(128)S(1)} %copy-done.2, ...), custom_call_target="tpu_custom_call" | custom-call | tf_op jit(solution)/shard_map/polar/pallas_call | solution.py:170
  17.7 1.5 %collective-permute-start.6 = (f16[2,32,512]{2,1,0:T(8,128)(2,1)S(1)}, f16[2,32,512]{2,1,0:T(8,128)(2,1)S(1)}, u32[]{:S(2)}, u32[]{:S(2)}) collective-permute-start(f16[2,32,512]{2,1,0:T(8,128)(2,1)S(1)} %convert_element_type.33), channel_id=1, source_target_pairs={{0,8},{4,12},{8,16},{12,20},{16,24},{20,28},{24,0},{28,4},{1,9},{5... | collective-permute-start | bytes 196616 | tf_op jit(solution)/shard_map/ppermute | solution.py:215
  19.2 0.0 collective-permute-start.5
  19.2 0.8 %collective-permute-start.4 = (f16[2,32,512]{2,1,0:T(8,128)(2,1)S(1)}, f16[2,32,512]{2,1,0:T(8,128)(2,1)S(1)}, u32[]{:S(2)}, u32[]{:S(2)}) collective-permute-start(f16[2,32,512]{2,1,0:T(8,128)(2,1)S(1)} %convert_element_type.33), channel_id=1, source_target_pairs={{0,24},{4,28},{8,0},{12,4},{16,8},{20,12},{24,16},{28,20},{1,25},{... | collective-permute-start | bytes 196616 | tf_op jit(solution)/shard_map/ppermute | solution.py:215
  20.0 5.6 %collective-permute-done.4 = f16[2,32,512]{2,1,0:T(8,128)(2,1)S(1)} collective-permute-done((f16[2,32,512]{2,1,0:T(8,128)(2,1)S(1)}, f16[2,32,512]{2,1,0:T(8,128)(2,1)S(1)}, u32[]{:S(2)}, u32[]{:S(2)}) %collective-permute-start.4) | collective-permute-done | bytes 65568 | tf_op jit(solution)/shard_map/ppermute | solution.py:215
  25.6 1.7 %collective-permute-done.5 = f16[2,32,512]{2,1,0:T(8,128)(2,1)S(1)} collective-permute-done((f16[2,32,512]{2,1,0:T(8,128)(2,1)S(1)}, f16[2,32,512]{2,1,0:T(8,128)(2,1)S(1)}, u32[]{:S(2)}, u32[]{:S(2)}) %collective-permute-start.5) | collective-permute-done | bytes 65568 | tf_op jit(solution)/shard_map/ppermute | solution.py:215
  27.3 0.0 collective-permute-done.6
  27.4 0.6 %collective-permute-start.11 = (f16[4,32,512]{2,1,0:T(8,128)(2,1)S(1)}, f16[4,32,512]{2,1,0:T(8,128)(2,1)S(1)}, u32[]{:S(2)}, u32[]{:S(2)}) collective-permute-start(f16[4,32,512]{2,1,0:T(8,128)(2,1)S(1)} %get-tuple-element.30), channel_id=1, source_target_pairs={{0,4},{4,0},{8,12},{12,8},{16,20},{20,16},{24,28},{28,24},{1,5},{5... | collective-permute-start | bytes 393224 | tf_op jit(solution)/shard_map/ppermute | solution.py:227
  28.0 1.5 %collective-permute-start.9 = (f16[4,32,512]{2,1,0:T(8,128)(2,1)S(1)}, f16[4,32,512]{2,1,0:T(8,128)(2,1)S(1)}, u32[]{:S(2)}, u32[]{:S(2)}) collective-permute-start(f16[4,32,512]{2,1,0:T(8,128)(2,1)S(1)} %get-tuple-element.30), channel_id=1, source_target_pairs={{0,1},{1,0},{2,3},{3,2},{4,5},{5,4},{6,7},{7,6},{8,9},{9,8},{10,11... | collective-permute-start | bytes 393224 | tf_op jit(solution)/shard_map/ppermute | solution.py:230
  29.5 0.0 collective-permute-start.16
  29.5 0.5 collective-permute-start.12
  30.0 0.0 collective-permute-done.13.two_ref.refs_10_
  30.0 1.5 %collective-permute-start.7 = (f16[4,32,512]{2,1,0:T(8,128)(2,1)S(1)}, f16[4,32,512]{2,1,0:T(8,128)(2,1)S(1)}, u32[]{:S(2)}, u32[]{:S(2)}) collective-permute-start(f16[4,32,512]{2,1,0:T(8,128)(2,1)S(1)} %get-tuple-element.31), channel_id=1, source_target_pairs={{0,4},{4,0},{8,12},{12,8},{16,20},{20,16},{24,28},{28,24},{1,5},{5... | collective-permute-start | bytes 393224 | tf_op jit(solution)/shard_map/ppermute | solution.py:227
  31.5 0.6 chosen.1
  32.1 0.3 collective-permute-done.11
  32.4 1.3 %collective-permute-start.15 = (bf16[256,512]{1,0:T(8,128)(2,1)S(1)}, bf16[256,512]{1,0:T(8,128)(2,1)S(1)}, u32[]{:S(2)}, u32[]{:S(2)}) collective-permute-start(bf16[256,512]{1,0:T(8,128)(2,1)S(1)} %chosen.1), channel_id=1, source_target_pairs={{0,4},{4,8},{8,12},{12,16},{16,20},{20,24},{24,28},{1,5},{5,9},{9,... | collective-permute-start | bytes 786440 | tf_op jit(solution)/shard_map/ppermute | solution.py:44
  33.7 0.0 collective-permute-done.9
  33.7 1.3 %collective-permute-start.14 = (bf16[256,512]{1,0:T(8,128)(2,1)S(1)}, bf16[256,512]{1,0:T(8,128)(2,1)S(1)}, u32[]{:S(2)}, u32[]{:S(2)}) collective-permute-start(bf16[256,512]{1,0:T(8,128)(2,1)S(1)} %collective-permute-done.13.two_ref.refs_10_), channel_id=1, source_target_pairs={{0,8},{4,12},{8,16},{12,20},{16,24},{20,28},{1,9},{5,13},{9,17},{1... | collective-permute-start | bytes 786440 | tf_op jit(solution)/shard_map/ppermute | solution.py:44
  35.0 0.7 %collective-permute-done.12 = f16[4,32,512]{2,1,0:T(8,128)(2,1)S(1)} collective-permute-done((f16[4,32,512]{2,1,0:T(8,128)(2,1)S(1)}, f16[4,32,512]{2,1,0:T(8,128)(2,1)S(1)}, u32[]{:S(2)}, u32[]{:S(2)}) %collective-permute-start.12) | collective-permute-done | bytes 131104 | tf_op jit(solution)/shard_map/ppermute | solution.py:230
  35.7 2.0 %collective-permute-start.10 = (f16[4,32,512]{2,1,0:T(8,128)(2,1)S(1)}, f16[4,32,512]{2,1,0:T(8,128)(2,1)S(1)}, u32[]{:S(2)}, u32[]{:S(2)}) collective-permute-start(f16[4,32,512]{2,1,0:T(8,128)(2,1)S(1)} %collective-permute-done.9), channel_id=1, source_target_pairs={{0,4},{4,0},{8,12},{12,8},{16,20},{20,16},{24,28},{28,24},{1,5},{5... | collective-permute-start | bytes 393224 | tf_op jit(solution)/shard_map/ppermute | solution.py:227
  37.7 0.0 collective-permute-done.7
  37.7 1.5 %collective-permute-start.8 = (f16[4,32,512]{2,1,0:T(8,128)(2,1)S(1)}, f16[4,32,512]{2,1,0:T(8,128)(2,1)S(1)}, u32[]{:S(2)}, u32[]{:S(2)}) collective-permute-start(f16[4,32,512]{2,1,0:T(8,128)(2,1)S(1)} %collective-permute-done.7), channel_id=1, source_target_pairs={{0,1},{1,0},{2,3},{3,2},{4,5},{5,4},{6,7},{7,6},{8,9},{9,8},{10,11... | collective-permute-start | bytes 393224 | tf_op jit(solution)/shard_map/ppermute | solution.py:230
  39.4 1.3 %early.1 = (f32[2,256,512]{2,1,0:T(8,128)S(1)}, bf16[2,512,512]{2,1,0:T(8,128)(2,1)S(1)}, bf16[2,512,512]{2,1,0:T(8,128)(2,1)S(1)}) custom-call(f32[4,32,512]{2,1,0:T(8,128)S(1)} %convert_element_type.36.refs_0_, f32[4,32,512]{2,1,0:T(8,128)S(1)} %convert_element_type.37.refs_1_, f32[4,32,512]{2,1,0:T(8,128)S(1)} %convert_element_type.38.refs_2_, ...), custom_call_target="tpu_custom_call" | custom-call | tf_op jit(solution)/shard_map/early/pallas_call | solution.py:362
  40.7 4.2 %collective-permute-done.10 = f16[4,32,512]{2,1,0:T(8,128)(2,1)S(1)} collective-permute-done((f16[4,32,512]{2,1,0:T(8,128)(2,1)S(1)}, f16[4,32,512]{2,1,0:T(8,128)(2,1)S(1)}, u32[]{:S(2)}, u32[]{:S(2)}) %collective-permute-start.10) | collective-permute-done | bytes 131104 | tf_op jit(solution)/shard_map/ppermute | solution.py:227
  45.0 0.0 collective-permute-done.8
  45.0 0.0 collective-permute-done.16.refs_13_
  45.0 0.0 collective-permute-done.15.refs_12_
  45.0 2.7 %collective-permute-done.14.refs_11_ = bf16[256,512]{1,0:T(8,128)(2,1)S(1)} collective-permute-done((bf16[256,512]{1,0:T(8,128)(2,1)S(1)}, bf16[256,512]{1,0:T(8,128)(2,1)S(1)}, u32[]{:S(2)}, u32[]{:S(2)}) %collective-permute-start.14) | collective-permute-done | bytes 262176 | tf_op jit(solution)/shard_map/ppermute | solution.py:44
  47.8 3.2 %dyson.1 = (bf16[2,256,512]{2,1,0:T(8,128)(2,1)}, f32[264,512]{1,0:T(8,128)S(1)}, f32[256,512]{1,0:T(8,128)S(1)}, f32[8,512]{1,0:T(8,128)S(1)}) custom-call(f32[4,32,512]{2,1,0:T(8,128)S(1)} %convert_element_type.34.refs_0_, f32[4,32,512]{2,1,0:T(8,128)S(1)} %convert_element_type.35.refs_1_, f32[2,256,512]{2,1,0:T(8,128)S(1)} %get-tuple-element.18.refs_2_, ...), custom_call_target="tpu_custom_call" | custom-call | tf_op jit(solution)/shard_map/dyson/pallas_call | solution.py:378
  51.0 1.6 %collective-permute-start.17 = (f16[264,512]{1,0:T(8,128)(2,1)S(1)}, f16[264,512]{1,0:T(8,128)(2,1)S(1)}, u32[]{:S(2)}, u32[]{:S(2)}) collective-permute-start(f16[264,512]{1,0:T(8,128)(2,1)S(1)} %convert_element_type.42), channel_id=1, source_target_pairs={{0,1},{1,0},{2,3},{3,2},{4,5},{5,4},{6,7},{7,6},{8,9},{9,8},{10,11... | collective-permute-start | bytes 811016 | tf_op jit(solution)/shard_map/ppermute | solution.py:467
  52.5 0.4 begin.1
  53.0 5.2 %collective-permute-done.17 = f16[264,512]{1,0:T(8,128)(2,1)S(1)} collective-permute-done((f16[264,512]{1,0:T(8,128)(2,1)S(1)}, f16[264,512]{1,0:T(8,128)(2,1)S(1)}, u32[]{:S(2)}, u32[]{:S(2)}) %collective-permute-start.17) | collective-permute-done | bytes 270368 | tf_op jit(solution)/shard_map/ppermute | solution.py:467
  58.2 0.1 convert_element_type.43.theirs_ref
  58.3 1.7 %finish.1 = f32[256,512]{1,0:T(8,128)} custom-call(s32[1]{0:T(128)S(6)} %copy.21.refs_6_.steps_ref, f32[256,512]{1,0:T(8,128)S(1)} %get-tuple-element.21.step_ref, f32[256,512]{1,0:T(8,128)S(1)} %get-tuple-element.24.square_ref, bf16[256,512]{1,0:T(8,128)(2,1)S(1)} %get-tuple-element.25.high_ref, bf16[256,512]{1,0:T(8,128)(2,1)S(1)} %get-tuple-element.26.low_ref, ...), custom_call_target="tpu_custom_call" | custom-call | tf_op jit(solution)/shard_map/finish/pallas_call | solution.py:478
  (18 shorter events, 0.4 us)
Async XLA Ops:
  0.6 7.2 %copy-start.1 = (bf16[1,1,256,512]{3,2,1,0:T(8,128)(2,1)S(1)}, bf16[1,1,256,512]{3,2,1,0:T(8,128)(2,1)}, u32[]{:S(2)}) copy-start(bf16[1,1,256,512]{3,2,1,0:T(8,128)(2,1)} %param.8) | copy-start | bytes 786436
  0.6 16.1 %copy-start = (f32[1,256,512]{2,1,0:T(8,128)S(1)}, f32[1,256,512]{2,1,0:T(8,128)}, u32[]{:S(2)}) copy-start(f32[1,256,512]{2,1,0:T(8,128)} %param.11) | copy-start | bytes 1572868
  2.3 5.5 %collective-permute-start = (bf16[136,512]{1,0:T(8,128)(2,1)S(1)}, bf16[136,512]{1,0:T(8,128)(2,1)S(1)}, u32[]{:S(2)}, u32[]{:S(2)}) collective-permute-start(bf16[136,512]{1,0:T(8,128)(2,1)S(1)} %prepare.1), channel_id=1, source_target_pairs={{0,4},{4,0},{8,12},{12,8},{16,20},{20,16},{24,28},{28,24},{1,5},{5... | collective-permute-start | bytes 417800 | tf_op jit(solution)/shard_map/ppermute | solution.py:152
  7.8 5.1 %collective-permute-start.1 = (bf16[72,512]{1,0:T(8,128)(2,1)S(1)}, bf16[72,512]{1,0:T(8,128)(2,1)S(1)}, u32[]{:S(2)}, u32[]{:S(2)}) collective-permute-start(bf16[72,512]{1,0:T(8,128)(2,1)S(1)} %get-tuple-element.15), channel_id=1, source_target_pairs={{0,8},{4,12},{8,16},{12,20},{16,24},{20,28},{24,0},{28,4},{1,9},{5... | collective-permute-start | bytes 221192 | tf_op jit(solution)/shard_map/ppermute | solution.py:164
  8.1 8.7 %collective-permute-start.2 = (bf16[72,512]{1,0:T(8,128)(2,1)S(1)}, bf16[72,512]{1,0:T(8,128)(2,1)S(1)}, u32[]{:S(2)}, u32[]{:S(2)}) collective-permute-start(bf16[72,512]{1,0:T(8,128)(2,1)S(1)} %get-tuple-element.16), channel_id=1, source_target_pairs={{0,16},{4,20},{8,24},{12,28},{16,0},{20,4},{24,8},{28,12},{1,17},{... | collective-permute-start | bytes 221192 | tf_op jit(solution)/shard_map/ppermute | solution.py:164
  9.8 7.0 %collective-permute-start.3 = (bf16[72,512]{1,0:T(8,128)(2,1)S(1)}, bf16[72,512]{1,0:T(8,128)(2,1)S(1)}, u32[]{:S(2)}, u32[]{:S(2)}) collective-permute-start(bf16[72,512]{1,0:T(8,128)(2,1)S(1)} %get-tuple-element.17), channel_id=1, source_target_pairs={{0,24},{4,28},{8,0},{12,4},{16,8},{20,12},{24,16},{28,20},{1,25},{... | collective-permute-start | bytes 221192 | tf_op jit(solution)/shard_map/ppermute | solution.py:164
  10.2 19.7 %collective-permute-start.13 = (bf16[256,512]{1,0:T(8,128)(2,1)S(1)}, bf16[256,512]{1,0:T(8,128)(2,1)S(1)}, u32[]{:S(2)}, u32[]{:S(2)}) collective-permute-start(bf16[256,512]{1,0:T(8,128)(2,1)S(1)} %bitcast.12), channel_id=1, source_target_pairs={{0,8},{4,12},{8,16},{12,20},{16,24},{20,28},{1,9},{5,13},{9,17},{1... | collective-permute-start | bytes 786440 | tf_op jit(solution)/shard_map/ppermute | solution.py:44
  12.9 3.9 %copy-start.2 = (s32[2]{0:T(128)S(1)}, s32[2]{0:T(128)}, u32[]{:S(2)}) copy-start(s32[2]{0:T(128)} %refs_5_.3) | copy-start | bytes 28
  12.9 3.9 %copy-start.3 = (s32[2]{0:T(128)S(1)}, s32[2]{0:T(128)}, u32[]{:S(2)}) copy-start(s32[2]{0:T(128)} %refs_6_.2) | copy-start | bytes 28
  17.7 9.7 %collective-permute-start.6 = (f16[2,32,512]{2,1,0:T(8,128)(2,1)S(1)}, f16[2,32,512]{2,1,0:T(8,128)(2,1)S(1)}, u32[]{:S(2)}, u32[]{:S(2)}) collective-permute-start(f16[2,32,512]{2,1,0:T(8,128)(2,1)S(1)} %convert_element_type.33), channel_id=1, source_target_pairs={{0,8},{4,12},{8,16},{12,20},{16,24},{20,28},{24,0},{28,4},{1,9},{5... | collective-permute-start | bytes 196616 | tf_op jit(solution)/shard_map/ppermute | solution.py:215
  19.2 8.1 %collective-permute-start.5 = (f16[2,32,512]{2,1,0:T(8,128)(2,1)S(1)}, f16[2,32,512]{2,1,0:T(8,128)(2,1)S(1)}, u32[]{:S(2)}, u32[]{:S(2)}) collective-permute-start(f16[2,32,512]{2,1,0:T(8,128)(2,1)S(1)} %convert_element_type.33), channel_id=1, source_target_pairs={{0,16},{4,20},{8,24},{12,28},{16,0},{20,4},{24,8},{28,12},{1,17},{... | collective-permute-start | bytes 196616 | tf_op jit(solution)/shard_map/ppermute | solution.py:215
  19.2 6.4 %collective-permute-start.4 = (f16[2,32,512]{2,1,0:T(8,128)(2,1)S(1)}, f16[2,32,512]{2,1,0:T(8,128)(2,1)S(1)}, u32[]{:S(2)}, u32[]{:S(2)}) collective-permute-start(f16[2,32,512]{2,1,0:T(8,128)(2,1)S(1)} %convert_element_type.33), channel_id=1, source_target_pairs={{0,24},{4,28},{8,0},{12,4},{16,8},{20,12},{24,16},{28,20},{1,25},{... | collective-permute-start | bytes 196616 | tf_op jit(solution)/shard_map/ppermute | solution.py:215
  27.4 5.0 %collective-permute-start.11 = (f16[4,32,512]{2,1,0:T(8,128)(2,1)S(1)}, f16[4,32,512]{2,1,0:T(8,128)(2,1)S(1)}, u32[]{:S(2)}, u32[]{:S(2)}) collective-permute-start(f16[4,32,512]{2,1,0:T(8,128)(2,1)S(1)} %get-tuple-element.30), channel_id=1, source_target_pairs={{0,4},{4,0},{8,12},{12,8},{16,20},{20,16},{24,28},{28,24},{1,5},{5... | collective-permute-start | bytes 393224 | tf_op jit(solution)/shard_map/ppermute | solution.py:227
  28.0 5.7 %collective-permute-start.9 = (f16[4,32,512]{2,1,0:T(8,128)(2,1)S(1)}, f16[4,32,512]{2,1,0:T(8,128)(2,1)S(1)}, u32[]{:S(2)}, u32[]{:S(2)}) collective-permute-start(f16[4,32,512]{2,1,0:T(8,128)(2,1)S(1)} %get-tuple-element.30), channel_id=1, source_target_pairs={{0,1},{1,0},{2,3},{3,2},{4,5},{5,4},{6,7},{7,6},{8,9},{9,8},{10,11... | collective-permute-start | bytes 393224 | tf_op jit(solution)/shard_map/ppermute | solution.py:230
  29.5 15.5 %collective-permute-start.16 = (bf16[256,512]{1,0:T(8,128)(2,1)S(1)}, bf16[256,512]{1,0:T(8,128)(2,1)S(1)}, u32[]{:S(2)}, u32[]{:S(2)}) collective-permute-start(bf16[256,512]{1,0:T(8,128)(2,1)S(1)} %bitcast.14), channel_id=1, source_target_pairs={{0,2},{2,0},{1,3},{3,1},{4,6},{6,4},{5,7},{7,5},{8,10},{10,8},{9,1... | collective-permute-start | bytes 786440 | tf_op jit(solution)/shard_map/ppermute | solution.py:458
  29.5 6.3 %collective-permute-start.12 = (f16[4,32,512]{2,1,0:T(8,128)(2,1)S(1)}, f16[4,32,512]{2,1,0:T(8,128)(2,1)S(1)}, u32[]{:S(2)}, u32[]{:S(2)}) collective-permute-start(f16[4,32,512]{2,1,0:T(8,128)(2,1)S(1)} %get-tuple-element.31), channel_id=1, source_target_pairs={{0,1},{1,0},{2,3},{3,2},{4,5},{5,4},{6,7},{7,6},{8,9},{9,8},{10,11... | collective-permute-start | bytes 393224 | tf_op jit(solution)/shard_map/ppermute | solution.py:230
  30.0 7.7 %collective-permute-start.7 = (f16[4,32,512]{2,1,0:T(8,128)(2,1)S(1)}, f16[4,32,512]{2,1,0:T(8,128)(2,1)S(1)}, u32[]{:S(2)}, u32[]{:S(2)}) collective-permute-start(f16[4,32,512]{2,1,0:T(8,128)(2,1)S(1)} %get-tuple-element.31), channel_id=1, source_target_pairs={{0,4},{4,0},{8,12},{12,8},{16,20},{20,16},{24,28},{28,24},{1,5},{5... | collective-permute-start | bytes 393224 | tf_op jit(solution)/shard_map/ppermute | solution.py:227
  32.4 12.6 %collective-permute-start.15 = (bf16[256,512]{1,0:T(8,128)(2,1)S(1)}, bf16[256,512]{1,0:T(8,128)(2,1)S(1)}, u32[]{:S(2)}, u32[]{:S(2)}) collective-permute-start(bf16[256,512]{1,0:T(8,128)(2,1)S(1)} %chosen.1), channel_id=1, source_target_pairs={{0,4},{4,8},{8,12},{12,16},{16,20},{20,24},{24,28},{1,5},{5,9},{9,... | collective-permute-start | bytes 786440 | tf_op jit(solution)/shard_map/ppermute | solution.py:44
  33.7 14.1 %collective-permute-start.14 = (bf16[256,512]{1,0:T(8,128)(2,1)S(1)}, bf16[256,512]{1,0:T(8,128)(2,1)S(1)}, u32[]{:S(2)}, u32[]{:S(2)}) collective-permute-start(bf16[256,512]{1,0:T(8,128)(2,1)S(1)} %collective-permute-done.13.two_ref.refs_10_), channel_id=1, source_target_pairs={{0,8},{4,12},{8,16},{12,20},{16,24},{20,28},{1,9},{5,13},{9,17},{1... | collective-permute-start | bytes 786440 | tf_op jit(solution)/shard_map/ppermute | solution.py:44
  35.7 9.2 %collective-permute-start.10 = (f16[4,32,512]{2,1,0:T(8,128)(2,1)S(1)}, f16[4,32,512]{2,1,0:T(8,128)(2,1)S(1)}, u32[]{:S(2)}, u32[]{:S(2)}) collective-permute-start(f16[4,32,512]{2,1,0:T(8,128)(2,1)S(1)} %collective-permute-done.9), channel_id=1, source_target_pairs={{0,4},{4,0},{8,12},{12,8},{16,20},{20,16},{24,28},{28,24},{1,5},{5... | collective-permute-start | bytes 393224 | tf_op jit(solution)/shard_map/ppermute | solution.py:227
  37.7 7.2 %collective-permute-start.8 = (f16[4,32,512]{2,1,0:T(8,128)(2,1)S(1)}, f16[4,32,512]{2,1,0:T(8,128)(2,1)S(1)}, u32[]{:S(2)}, u32[]{:S(2)}) collective-permute-start(f16[4,32,512]{2,1,0:T(8,128)(2,1)S(1)} %collective-permute-done.7), channel_id=1, source_target_pairs={{0,1},{1,0},{2,3},{3,2},{4,5},{5,4},{6,7},{7,6},{8,9},{9,8},{10,11... | collective-permute-start | bytes 393224 | tf_op jit(solution)/shard_map/ppermute | solution.py:230
  51.0 7.2 %collective-permute-start.17 = (f16[264,512]{1,0:T(8,128)(2,1)S(1)}, f16[264,512]{1,0:T(8,128)(2,1)S(1)}, u32[]{:S(2)}, u32[]{:S(2)}) collective-permute-start(f16[264,512]{1,0:T(8,128)(2,1)S(1)} %convert_element_type.42), channel_id=1, source_target_pairs={{0,1},{1,0},{2,3},{3,2},{4,5},{5,4},{6,7},{7,6},{8,9},{9,8},{10,11... | collective-permute-start | bytes 811016 | tf_op jit(solution)/shard_map/ppermute | solution.py:467

commit v12 on v11

--- a/solution.py
+++ b/solution.py
@@ -76,7 +76,7 @@
     copy.wait()
 
 
-def arrange_kernel(weight_ref, block_ref, got_ref, *out_refs):
+def arrange_kernel(weight_ref, screen_ref, green_steps_ref, level_ref, block_ref, got_ref, *out_refs):
     outer = len(out_refs) + 1
     half, width = got_ref.shape[0] - EXTRA, got_ref.shape[1]
     share = half // outer
@@ -153,11 +153,11 @@
     shares = pl.pallas_call(
         arrange_kernel,
         out_shape=(jax.ShapeDtypeStruct((2 * share + EXTRA, width), green.dtype),) * (outer - 1),
-        in_specs=[in_smem, in_vmem, in_vmem],
+        in_specs=[in_smem] * 4 + [in_vmem] * 2,
         out_specs=(in_vmem,) * (outer - 1),
         compiler_params=small,
         name="arrange",
-    )(weight, green, got)
+    )(weight, *scalars, green, got)
     received = [None] * (outer - 1)
     for k in range(outer - 1, 0, -1):
         route = [(z * 2 + x, (z + k) % outer * 2 + x) for z in range(outer) for x in range(2)]
@@ -165,12 +165,12 @@
 
     def kernel(*refs):
         count = outer - 1
-        polar_kernel(refs[:count], *refs[count:count + 2], *refs[count + 5:])
+        polar_kernel(refs[:count], *refs[count:])
 
     return pl.pallas_call(
         kernel,
         out_shape=jax.ShapeDtypeStruct((FREQS, share, width), jnp.float32),
-        in_specs=[in_vmem] * (outer - 1) + [in_smem] * 5 + [in_vmem, in_vmem, in_place],
+        in_specs=[in_vmem] * (outer - 1) + [in_smem] * 2 + [in_vmem, in_vmem, in_place],
         out_specs=in_vmem,
         scratch_shapes=[
             VMEM((SHIFTS + energies, share, width), jnp.float32),
@@ -180,7 +180,7 @@
         ],
         compiler_params=small,
         name="polar",
-    )(*received, weight, offsets, *scalars, green, got, bare)
+    )(*received, weight, offsets, green, got, bare)
 
 
 def polar_share_plain(green, weight, offsets, bare, scalars):

time: 60.2 us -> 62.1 us (1.032)
  local copies, waits for them, and re-layouts: 0.12 us -> 1.43 us
    ppermute x3, waiting for transfers between devices: 3.85 us -> 5.16 us  [polar_share(): received[k - 1] = lax.ppermute(shares[k - 1], 'energy', route)]
    unnamed x8 -> x10, local copies, waits for them, and re-layouts: 0.02 us -> 1.33 us
    ppermute x1, waiting for transfers between devices: 4.88 us -> 3.58 us  [polar_share(): got = lax.ppermute(sent, 'energy', [(e, e ^ 1) for e in range(energies)])]
  transfers between devices with their start and end apart: 18 -> 18, of which waited for: 9 -> 10; matrix products, arithmetic and copies ran while one was open for 0% -> 0% of each run, Pallas kernels for 5% -> 5%
where the time goes in v12:
time: 62.1 us; the launch traced here: 61.9 us
  waiting for transfers between devices  29.3 us (47%)
  starting transfers between devices  18.3 us (29%)
  Pallas kernels  9.52 us (15%)
  between operations  3.01 us (5%)
  local copies, waits for them, and re-layouts  1.43 us (2%)
    ppermute x3, waiting for transfers between devices, gather_energy(): got = lax.ppermute(chunk, 'energy', route)  7.31 us
    ppermute x1, waiting for transfers between devices, body(): lax.ppermute(packed.astype(coded), 'rep', [(0, 1), (1, 0)])  5.21 us
    ppermute x3, waiting for transfers between devices, polar_share(): received[k - 1] = lax.ppermute(shares[k - 1], 'energy', route)  5.16 us
    ppermute x3, waiting for transfers between devices, along_x(): return lax.ppermute(part, 'energy', [(e, e ^ 1) for e in range(energies)])  4.55 us
    ppermute x3, starting transfers between devices, along_x(): return lax.ppermute(part, 'energy', [(e, e ^ 1) for e in range(energies)])  4.06 us
    ppermute x3, starting transfers between devices, shifted(): return lax.ppermute(block, axis, route)  3.85 us
    ppermute x1, waiting for transfers between devices, polar_share(): got = lax.ppermute(sent, 'energy', [(e, e ^ 1) for e in range(energies)])  3.58 us
    ppermute x3, starting transfers between devices, along_rep(): return lax.ppermute(part, 'rep', [(0, 1), (1, 0)])  3.55 us
  transfers between devices with their start and end apart: 18, of which 10 were waited for; matrix products, arithmetic and copies ran while one was open for 0% of the time, Pallas kernels for 5%

profile of v12, /device:TPU:26, one launch (start us, length us, event | category | flops | bytes accessed | tf_op | source)
XLA Modules:
  0.0 61.9 jit_solution(7866878871830736364)
XLA Ops:
  0.6 0.0 copy-start.1
  0.6 0.0 copy-start
  1.4 0.9 %prepare.1 = bf16[136,512]{1,0:T(8,128)(2,1)S(1)} custom-call(f32[1]{0:T(128)S(6)} %copy.19.weight_ref.refs_3_, bf16[256,512]{1,0:T(8,128)(2,1)} %bitcast.10), custom_call_target="tpu_custom_call" | custom-call | tf_op jit(solution)/shard_map/prepare/pallas_call | solution.py:143
  2.3 0.6 collective-permute-start
  4.2 3.6 %collective-permute-done.got_ref.refs_6_ = bf16[136,512]{1,0:T(8,128)(2,1)S(1)} collective-permute-done((bf16[136,512]{1,0:T(8,128)(2,1)S(1)}, bf16[136,512]{1,0:T(8,128)(2,1)S(1)}, u32[]{:S(2)}, u32[]{:S(2)}) %collective-permute-start) | collective-permute-done | bytes 139296 | tf_op jit(solution)/shard_map/ppermute | solution.py:152
  7.8 0.0 copy-done.1
  7.8 0.0 copy-start.3
  7.8 0.7 %copy-done.3 = s32[2]{0:T(128)S(1)} copy-done((s32[2]{0:T(128)S(1)}, s32[2]{0:T(128)}, u32[]{:S(2)}) %copy-start.3) | copy-done | bytes 32
  8.4 0.6 arrange.1
  9.0 0.3 collective-permute-start.1
  9.3 1.7 %collective-permute-start.2 = (bf16[72,512]{1,0:T(8,128)(2,1)S(1)}, bf16[72,512]{1,0:T(8,128)(2,1)S(1)}, u32[]{:S(2)}, u32[]{:S(2)}) collective-permute-start(bf16[72,512]{1,0:T(8,128)(2,1)S(1)} %get-tuple-element.16), channel_id=1, source_target_pairs={{0,16},{4,20},{8,24},{12,28},{16,0},{20,4},{24,8},{28,12},{1,17},{... | collective-permute-start | bytes 221192 | tf_op jit(solution)/shard_map/ppermute | solution.py:164
  11.0 0.4 collective-permute-start.3
  11.4 1.3 %collective-permute-start.13 = (bf16[256,512]{1,0:T(8,128)(2,1)S(1)}, bf16[256,512]{1,0:T(8,128)(2,1)S(1)}, u32[]{:S(2)}, u32[]{:S(2)}) collective-permute-start(bf16[256,512]{1,0:T(8,128)(2,1)S(1)} %bitcast.12), channel_id=1, source_target_pairs={{0,8},{4,12},{8,16},{12,20},{16,24},{20,28},{1,9},{5,13},{9,17},{1... | collective-permute-start | bytes 786440 | tf_op jit(solution)/shard_map/ppermute | solution.py:44
  12.8 0.0 copy-start.2
  12.8 0.6 collective-permute-done.1.refs_0_
  13.4 4.5 %collective-permute-done.2.refs_1_ = bf16[72,512]{1,0:T(8,128)(2,1)S(1)} collective-permute-done((bf16[72,512]{1,0:T(8,128)(2,1)S(1)}, bf16[72,512]{1,0:T(8,128)(2,1)S(1)}, u32[]{:S(2)}, u32[]{:S(2)}) %collective-permute-start.2) | collective-permute-done | bytes 73760 | tf_op jit(solution)/shard_map/ppermute | solution.py:164
  18.0 0.0 collective-permute-done.3.refs_2_
  18.0 0.0 copy-done
  18.0 0.0 copy-done.2
  18.0 0.8 %polar.1 = f32[2,32,512]{2,1,0:T(8,128)S(1)} custom-call(bf16[72,512]{1,0:T(8,128)(2,1)S(1)} %collective-permute-done.1.refs_0_, bf16[72,512]{1,0:T(8,128)(2,1)S(1)} %collective-permute-done.2.refs_1_, bf16[72,512]{1,0:T(8,128)(2,1)S(1)} %collective-permute-done.3.refs_2_, f32[1]{0:T(128)S(6)} %copy.19.weight_ref.refs_3_, s32[2]{0:T(128)S(1)} %copy-done.2, ...), custom_call_target="tpu_custom_call" | custom-call | tf_op jit(solution)/shard_map/polar/pallas_call | solution.py:170
  18.9 0.3 collective-permute-start.6
  19.2 0.0 collective-permute-start.5
  19.2 1.9 %collective-permute-start.4 = (f16[2,32,512]{2,1,0:T(8,128)(2,1)S(1)}, f16[2,32,512]{2,1,0:T(8,128)(2,1)S(1)}, u32[]{:S(2)}, u32[]{:S(2)}) collective-permute-start(f16[2,32,512]{2,1,0:T(8,128)(2,1)S(1)} %convert_element_type.33), channel_id=1, source_target_pairs={{0,24},{4,28},{8,0},{12,4},{16,8},{20,12},{24,16},{28,20},{1,25},{... | collective-permute-start | bytes 196616 | tf_op jit(solution)/shard_map/ppermute | solution.py:215
  21.2 5.6 %collective-permute-done.4 = f16[2,32,512]{2,1,0:T(8,128)(2,1)S(1)} collective-permute-done((f16[2,32,512]{2,1,0:T(8,128)(2,1)S(1)}, f16[2,32,512]{2,1,0:T(8,128)(2,1)S(1)}, u32[]{:S(2)}, u32[]{:S(2)}) %collective-permute-start.4) | collective-permute-done | bytes 65568 | tf_op jit(solution)/shard_map/ppermute | solution.py:215
  26.8 1.7 %collective-permute-done.5 = f16[2,32,512]{2,1,0:T(8,128)(2,1)S(1)} collective-permute-done((f16[2,32,512]{2,1,0:T(8,128)(2,1)S(1)}, f16[2,32,512]{2,1,0:T(8,128)(2,1)S(1)}, u32[]{:S(2)}, u32[]{:S(2)}) %collective-permute-start.5) | collective-permute-done | bytes 65568 | tf_op jit(solution)/shard_map/ppermute | solution.py:215
  28.5 0.0 collective-permute-done.6
  28.6 0.6 collective-permute-start.11
  29.2 1.5 %collective-permute-start.9 = (f16[4,32,512]{2,1,0:T(8,128)(2,1)S(1)}, f16[4,32,512]{2,1,0:T(8,128)(2,1)S(1)}, u32[]{:S(2)}, u32[]{:S(2)}) collective-permute-start(f16[4,32,512]{2,1,0:T(8,128)(2,1)S(1)} %get-tuple-element.30), channel_id=1, source_target_pairs={{0,1},{1,0},{2,3},{3,2},{4,5},{5,4},{6,7},{7,6},{8,9},{9,8},{10,11... | collective-permute-start | bytes 393224 | tf_op jit(solution)/shard_map/ppermute | solution.py:230
  30.7 0.0 collective-permute-start.16
  30.7 0.5 collective-permute-start.12
  31.2 0.0 collective-permute-done.13.two_ref.refs_10_
  31.2 1.5 %collective-permute-start.7 = (f16[4,32,512]{2,1,0:T(8,128)(2,1)S(1)}, f16[4,32,512]{2,1,0:T(8,128)(2,1)S(1)}, u32[]{:S(2)}, u32[]{:S(2)}) collective-permute-start(f16[4,32,512]{2,1,0:T(8,128)(2,1)S(1)} %get-tuple-element.31), channel_id=1, source_target_pairs={{0,4},{4,0},{8,12},{12,8},{16,20},{20,16},{24,28},{28,24},{1,5},{5... | collective-permute-start | bytes 393224 | tf_op jit(solution)/shard_map/ppermute | solution.py:227
  32.7 0.6 chosen.1
  33.3 0.3 collective-permute-done.11
  33.6 1.3 %collective-permute-start.15 = (bf16[256,512]{1,0:T(8,128)(2,1)S(1)}, bf16[256,512]{1,0:T(8,128)(2,1)S(1)}, u32[]{:S(2)}, u32[]{:S(2)}) collective-permute-start(bf16[256,512]{1,0:T(8,128)(2,1)S(1)} %chosen.1), channel_id=1, source_target_pairs={{0,4},{4,8},{8,12},{12,16},{16,20},{20,24},{24,28},{1,5},{5,9},{9,... | collective-permute-start | bytes 786440 | tf_op jit(solution)/shard_map/ppermute | solution.py:44
  34.9 0.0 collective-permute-done.9
  34.9 1.3 %collective-permute-start.14 = (bf16[256,512]{1,0:T(8,128)(2,1)S(1)}, bf16[256,512]{1,0:T(8,128)(2,1)S(1)}, u32[]{:S(2)}, u32[]{:S(2)}) collective-permute-start(bf16[256,512]{1,0:T(8,128)(2,1)S(1)} %collective-permute-done.13.two_ref.refs_10_), channel_id=1, source_target_pairs={{0,8},{4,12},{8,16},{12,20},{16,24},{20,28},{1,9},{5,13},{9,17},{1... | collective-permute-start | bytes 786440 | tf_op jit(solution)/shard_map/ppermute | solution.py:44
  36.2 0.7 %collective-permute-done.12 = f16[4,32,512]{2,1,0:T(8,128)(2,1)S(1)} collective-permute-done((f16[4,32,512]{2,1,0:T(8,128)(2,1)S(1)}, f16[4,32,512]{2,1,0:T(8,128)(2,1)S(1)}, u32[]{:S(2)}, u32[]{:S(2)}) %collective-permute-start.12) | collective-permute-done | bytes 131104 | tf_op jit(solution)/shard_map/ppermute | solution.py:230
  36.9 2.0 %collective-permute-start.10 = (f16[4,32,512]{2,1,0:T(8,128)(2,1)S(1)}, f16[4,32,512]{2,1,0:T(8,128)(2,1)S(1)}, u32[]{:S(2)}, u32[]{:S(2)}) collective-permute-start(f16[4,32,512]{2,1,0:T(8,128)(2,1)S(1)} %collective-permute-done.9), channel_id=1, source_target_pairs={{0,4},{4,0},{8,12},{12,8},{16,20},{20,16},{24,28},{28,24},{1,5},{5... | collective-permute-start | bytes 393224 | tf_op jit(solution)/shard_map/ppermute | solution.py:227
  38.9 0.0 collective-permute-done.7
  38.9 1.5 %collective-permute-start.8 = (f16[4,32,512]{2,1,0:T(8,128)(2,1)S(1)}, f16[4,32,512]{2,1,0:T(8,128)(2,1)S(1)}, u32[]{:S(2)}, u32[]{:S(2)}) collective-permute-start(f16[4,32,512]{2,1,0:T(8,128)(2,1)S(1)} %collective-permute-done.7), channel_id=1, source_target_pairs={{0,1},{1,0},{2,3},{3,2},{4,5},{5,4},{6,7},{7,6},{8,9},{9,8},{10,11... | collective-permute-start | bytes 393224 | tf_op jit(solution)/shard_map/ppermute | solution.py:230
  40.6 1.3 %early.1 = (f32[2,256,512]{2,1,0:T(8,128)S(1)}, bf16[2,512,512]{2,1,0:T(8,128)(2,1)S(1)}, bf16[2,512,512]{2,1,0:T(8,128)(2,1)S(1)}) custom-call(f32[4,32,512]{2,1,0:T(8,128)S(1)} %convert_element_type.36.refs_0_, f32[4,32,512]{2,1,0:T(8,128)S(1)} %convert_element_type.37.refs_1_, f32[4,32,512]{2,1,0:T(8,128)S(1)} %convert_element_type.38.refs_2_, ...), custom_call_target="tpu_custom_call" | custom-call | tf_op jit(solution)/shard_map/early/pallas_call | solution.py:362
  41.9 4.2 %collective-permute-done.10 = f16[4,32,512]{2,1,0:T(8,128)(2,1)S(1)} collective-permute-done((f16[4,32,512]{2,1,0:T(8,128)(2,1)S(1)}, f16[4,32,512]{2,1,0:T(8,128)(2,1)S(1)}, u32[]{:S(2)}, u32[]{:S(2)}) %collective-permute-start.10) | collective-permute-done | bytes 131104 | tf_op jit(solution)/shard_map/ppermute | solution.py:227
  46.2 0.0 collective-permute-done.8
  46.2 0.0 collective-permute-done.16.refs_13_
  46.2 0.0 collective-permute-done.15.refs_12_
  46.2 2.7 %collective-permute-done.14.refs_11_ = bf16[256,512]{1,0:T(8,128)(2,1)S(1)} collective-permute-done((bf16[256,512]{1,0:T(8,128)(2,1)S(1)}, bf16[256,512]{1,0:T(8,128)(2,1)S(1)}, u32[]{:S(2)}, u32[]{:S(2)}) %collective-permute-start.14) | collective-permute-done | bytes 262176 | tf_op jit(solution)/shard_map/ppermute | solution.py:44
  49.0 0.0 copy-start.4
  49.0 0.7 %copy-done.4 = s32[2]{0:T(128)S(1)} copy-done((s32[2]{0:T(128)S(1)}, s32[2]{0:T(128)}, u32[]{:S(2)}) %copy-start.4) | copy-done | bytes 32
  49.6 3.2 %dyson.1 = (bf16[2,256,512]{2,1,0:T(8,128)(2,1)}, f32[264,512]{1,0:T(8,128)S(1)}, f32[256,512]{1,0:T(8,128)S(1)}, f32[8,512]{1,0:T(8,128)S(1)}) custom-call(f32[4,32,512]{2,1,0:T(8,128)S(1)} %convert_element_type.34.refs_0_, f32[4,32,512]{2,1,0:T(8,128)S(1)} %convert_element_type.35.refs_1_, f32[2,256,512]{2,1,0:T(8,128)S(1)} %get-tuple-element.18.refs_2_, ...), custom_call_target="tpu_custom_call" | custom-call | tf_op jit(solution)/shard_map/dyson/pallas_call | solution.py:378
  52.8 1.6 %collective-permute-start.17 = (f16[264,512]{1,0:T(8,128)(2,1)S(1)}, f16[264,512]{1,0:T(8,128)(2,1)S(1)}, u32[]{:S(2)}, u32[]{:S(2)}) collective-permute-start(f16[264,512]{1,0:T(8,128)(2,1)S(1)} %convert_element_type.42), channel_id=1, source_target_pairs={{0,1},{1,0},{2,3},{3,2},{4,5},{5,4},{6,7},{7,6},{8,9},{9,8},{10,11... | collective-permute-start | bytes 811016 | tf_op jit(solution)/shard_map/ppermute | solution.py:467
  54.4 0.4 begin.1
  54.8 5.2 %collective-permute-done.17 = f16[264,512]{1,0:T(8,128)(2,1)S(1)} collective-permute-done((f16[264,512]{1,0:T(8,128)(2,1)S(1)}, f16[264,512]{1,0:T(8,128)(2,1)S(1)}, u32[]{:S(2)}, u32[]{:S(2)}) %collective-permute-start.17) | collective-permute-done | bytes 270368 | tf_op jit(solution)/shard_map/ppermute | solution.py:467
  60.1 0.1 convert_element_type.43.theirs_ref
  60.1 1.7 %finish.1 = f32[256,512]{1,0:T(8,128)} custom-call(s32[1]{0:T(128)S(6)} %copy.21.green_steps_ref.steps_ref, f32[256,512]{1,0:T(8,128)S(1)} %get-tuple-element.21.step_ref, f32[256,512]{1,0:T(8,128)S(1)} %get-tuple-element.24.square_ref, bf16[256,512]{1,0:T(8,128)(2,1)S(1)} %get-tuple-element.25.high_ref, bf16[256,512]{1,0:T(8,128)(2,1)S(1)} %get-tuple-element.26.low_ref, ...), custom_call_target="tpu_custom_call" | custom-call | tf_op jit(solution)/shard_map/finish/pallas_call | solution.py:478
  (17 shorter events, 0.3 us)
Async XLA Ops:
  0.6 7.2 %copy-start.1 = (bf16[1,1,256,512]{3,2,1,0:T(8,128)(2,1)S(1)}, bf16[1,1,256,512]{3,2,1,0:T(8,128)(2,1)}, u32[]{:S(2)}) copy-start(bf16[1,1,256,512]{3,2,1,0:T(8,128)(2,1)} %param.8) | copy-start | bytes 786436
  0.6 17.3 %copy-start = (f32[1,256,512]{2,1,0:T(8,128)S(1)}, f32[1,256,512]{2,1,0:T(8,128)}, u32[]{:S(2)}) copy-start(f32[1,256,512]{2,1,0:T(8,128)} %param.11) | copy-start | bytes 1572868
  2.3 5.5 %collective-permute-start = (bf16[136,512]{1,0:T(8,128)(2,1)S(1)}, bf16[136,512]{1,0:T(8,128)(2,1)S(1)}, u32[]{:S(2)}, u32[]{:S(2)}) collective-permute-start(bf16[136,512]{1,0:T(8,128)(2,1)S(1)} %prepare.1), channel_id=1, source_target_pairs={{0,4},{4,0},{8,12},{12,8},{16,20},{20,16},{24,28},{28,24},{1,5},{5... | collective-permute-start | bytes 417800 | tf_op jit(solution)/shard_map/ppermute | solution.py:152
  7.8 0.7 %copy-start.3 = (s32[2]{0:T(128)S(1)}, s32[2]{0:T(128)}, u32[]{:S(2)}) copy-start(s32[2]{0:T(128)} %refs_6_.1) | copy-start | bytes 28
  9.0 4.4 %collective-permute-start.1 = (bf16[72,512]{1,0:T(8,128)(2,1)S(1)}, bf16[72,512]{1,0:T(8,128)(2,1)S(1)}, u32[]{:S(2)}, u32[]{:S(2)}) collective-permute-start(bf16[72,512]{1,0:T(8,128)(2,1)S(1)} %get-tuple-element.15), channel_id=1, source_target_pairs={{0,8},{4,12},{8,16},{12,20},{16,24},{20,28},{24,0},{28,4},{1,9},{5... | collective-permute-start | bytes 221192 | tf_op jit(solution)/shard_map/ppermute | solution.py:164
  9.3 8.7 %collective-permute-start.2 = (bf16[72,512]{1,0:T(8,128)(2,1)S(1)}, bf16[72,512]{1,0:T(8,128)(2,1)S(1)}, u32[]{:S(2)}, u32[]{:S(2)}) collective-permute-start(bf16[72,512]{1,0:T(8,128)(2,1)S(1)} %get-tuple-element.16), channel_id=1, source_target_pairs={{0,16},{4,20},{8,24},{12,28},{16,0},{20,4},{24,8},{28,12},{1,17},{... | collective-permute-start | bytes 221192 | tf_op jit(solution)/shard_map/ppermute | solution.py:164
  11.0 7.0 %collective-permute-start.3 = (bf16[72,512]{1,0:T(8,128)(2,1)S(1)}, bf16[72,512]{1,0:T(8,128)(2,1)S(1)}, u32[]{:S(2)}, u32[]{:S(2)}) collective-permute-start(bf16[72,512]{1,0:T(8,128)(2,1)S(1)} %get-tuple-element.17), channel_id=1, source_target_pairs={{0,24},{4,28},{8,0},{12,4},{16,8},{20,12},{24,16},{28,20},{1,25},{... | collective-permute-start | bytes 221192 | tf_op jit(solution)/shard_map/ppermute | solution.py:164
  11.4 19.7 %collective-permute-start.13 = (bf16[256,512]{1,0:T(8,128)(2,1)S(1)}, bf16[256,512]{1,0:T(8,128)(2,1)S(1)}, u32[]{:S(2)}, u32[]{:S(2)}) collective-permute-start(bf16[256,512]{1,0:T(8,128)(2,1)S(1)} %bitcast.12), channel_id=1, source_target_pairs={{0,8},{4,12},{8,16},{12,20},{16,24},{20,28},{1,9},{5,13},{9,17},{1... | collective-permute-start | bytes 786440 | tf_op jit(solution)/shard_map/ppermute | solution.py:44
  12.8 5.2 %copy-start.2 = (s32[2]{0:T(128)S(1)}, s32[2]{0:T(128)}, u32[]{:S(2)}) copy-start(s32[2]{0:T(128)} %refs_5_.1) | copy-start | bytes 28
  18.9 9.7 %collective-permute-start.6 = (f16[2,32,512]{2,1,0:T(8,128)(2,1)S(1)}, f16[2,32,512]{2,1,0:T(8,128)(2,1)S(1)}, u32[]{:S(2)}, u32[]{:S(2)}) collective-permute-start(f16[2,32,512]{2,1,0:T(8,128)(2,1)S(1)} %convert_element_type.33), channel_id=1, source_target_pairs={{0,8},{4,12},{8,16},{12,20},{16,24},{20,28},{24,0},{28,4},{1,9},{5... | collective-permute-start | bytes 196616 | tf_op jit(solution)/shard_map/ppermute | solution.py:215
  19.2 9.3 %collective-permute-start.5 = (f16[2,32,512]{2,1,0:T(8,128)(2,1)S(1)}, f16[2,32,512]{2,1,0:T(8,128)(2,1)S(1)}, u32[]{:S(2)}, u32[]{:S(2)}) collective-permute-start(f16[2,32,512]{2,1,0:T(8,128)(2,1)S(1)} %convert_element_type.33), channel_id=1, source_target_pairs={{0,16},{4,20},{8,24},{12,28},{16,0},{20,4},{24,8},{28,12},{1,17},{... | collective-permute-start | bytes 196616 | tf_op jit(solution)/shard_map/ppermute | solution.py:215
  19.2 7.6 %collective-permute-start.4 = (f16[2,32,512]{2,1,0:T(8,128)(2,1)S(1)}, f16[2,32,512]{2,1,0:T(8,128)(2,1)S(1)}, u32[]{:S(2)}, u32[]{:S(2)}) collective-permute-start(f16[2,32,512]{2,1,0:T(8,128)(2,1)S(1)} %convert_element_type.33), channel_id=1, source_target_pairs={{0,24},{4,28},{8,0},{12,4},{16,8},{20,12},{24,16},{28,20},{1,25},{... | collective-permute-start | bytes 196616 | tf_op jit(solution)/shard_map/ppermute | solution.py:215
  28.6 5.0 %collective-permute-start.11 = (f16[4,32,512]{2,1,0:T(8,128)(2,1)S(1)}, f16[4,32,512]{2,1,0:T(8,128)(2,1)S(1)}, u32[]{:S(2)}, u32[]{:S(2)}) collective-permute-start(f16[4,32,512]{2,1,0:T(8,128)(2,1)S(1)} %get-tuple-element.30), channel_id=1, source_target_pairs={{0,4},{4,0},{8,12},{12,8},{16,20},{20,16},{24,28},{28,24},{1,5},{5... | collective-permute-start | bytes 393224 | tf_op jit(solution)/shard_map/ppermute | solution.py:227
  29.2 5.7 %collective-permute-start.9 = (f16[4,32,512]{2,1,0:T(8,128)(2,1)S(1)}, f16[4,32,512]{2,1,0:T(8,128)(2,1)S(1)}, u32[]{:S(2)}, u32[]{:S(2)}) collective-permute-start(f16[4,32,512]{2,1,0:T(8,128)(2,1)S(1)} %get-tuple-element.30), channel_id=1, source_target_pairs={{0,1},{1,0},{2,3},{3,2},{4,5},{5,4},{6,7},{7,6},{8,9},{9,8},{10,11... | collective-permute-start | bytes 393224 | tf_op jit(solution)/shard_map/ppermute | solution.py:230
  30.7 15.5 %collective-permute-start.16 = (bf16[256,512]{1,0:T(8,128)(2,1)S(1)}, bf16[256,512]{1,0:T(8,128)(2,1)S(1)}, u32[]{:S(2)}, u32[]{:S(2)}) collective-permute-start(bf16[256,512]{1,0:T(8,128)(2,1)S(1)} %bitcast.14), channel_id=1, source_target_pairs={{0,2},{2,0},{1,3},{3,1},{4,6},{6,4},{5,7},{7,5},{8,10},{10,8},{9,1... | collective-permute-start | bytes 786440 | tf_op jit(solution)/shard_map/ppermute | solution.py:458
  30.7 6.3 %collective-permute-start.12 = (f16[4,32,512]{2,1,0:T(8,128)(2,1)S(1)}, f16[4,32,512]{2,1,0:T(8,128)(2,1)S(1)}, u32[]{:S(2)}, u32[]{:S(2)}) collective-permute-start(f16[4,32,512]{2,1,0:T(8,128)(2,1)S(1)} %get-tuple-element.31), channel_id=1, source_target_pairs={{0,1},{1,0},{2,3},{3,2},{4,5},{5,4},{6,7},{7,6},{8,9},{9,8},{10,11... | collective-permute-start | bytes 393224 | tf_op jit(solution)/shard_map/ppermute | solution.py:230
  31.2 7.7 %collective-permute-start.7 = (f16[4,32,512]{2,1,0:T(8,128)(2,1)S(1)}, f16[4,32,512]{2,1,0:T(8,128)(2,1)S(1)}, u32[]{:S(2)}, u32[]{:S(2)}) collective-permute-start(f16[4,32,512]{2,1,0:T(8,128)(2,1)S(1)} %get-tuple-element.31), channel_id=1, source_target_pairs={{0,4},{4,0},{8,12},{12,8},{16,20},{20,16},{24,28},{28,24},{1,5},{5... | collective-permute-start | bytes 393224 | tf_op jit(solution)/shard_map/ppermute | solution.py:227
  33.6 12.6 %collective-permute-start.15 = (bf16[256,512]{1,0:T(8,128)(2,1)S(1)}, bf16[256,512]{1,0:T(8,128)(2,1)S(1)}, u32[]{:S(2)}, u32[]{:S(2)}) collective-permute-start(bf16[256,512]{1,0:T(8,128)(2,1)S(1)} %chosen.1), channel_id=1, source_target_pairs={{0,4},{4,8},{8,12},{12,16},{16,20},{20,24},{24,28},{1,5},{5,9},{9,... | collective-permute-start | bytes 786440 | tf_op jit(solution)/shard_map/ppermute | solution.py:44
  34.9 14.1 %collective-permute-start.14 = (bf16[256,512]{1,0:T(8,128)(2,1)S(1)}, bf16[256,512]{1,0:T(8,128)(2,1)S(1)}, u32[]{:S(2)}, u32[]{:S(2)}) collective-permute-start(bf16[256,512]{1,0:T(8,128)(2,1)S(1)} %collective-permute-done.13.two_ref.refs_10_), channel_id=1, source_target_pairs={{0,8},{4,12},{8,16},{12,20},{16,24},{20,28},{1,9},{5,13},{9,17},{1... | collective-permute-start | bytes 786440 | tf_op jit(solution)/shard_map/ppermute | solution.py:44
  36.9 9.2 %collective-permute-start.10 = (f16[4,32,512]{2,1,0:T(8,128)(2,1)S(1)}, f16[4,32,512]{2,1,0:T(8,128)(2,1)S(1)}, u32[]{:S(2)}, u32[]{:S(2)}) collective-permute-start(f16[4,32,512]{2,1,0:T(8,128)(2,1)S(1)} %collective-permute-done.9), channel_id=1, source_target_pairs={{0,4},{4,0},{8,12},{12,8},{16,20},{20,16},{24,28},{28,24},{1,5},{5... | collective-permute-start | bytes 393224 | tf_op jit(solution)/shard_map/ppermute | solution.py:227
  38.9 7.2 %collective-permute-start.8 = (f16[4,32,512]{2,1,0:T(8,128)(2,1)S(1)}, f16[4,32,512]{2,1,0:T(8,128)(2,1)S(1)}, u32[]{:S(2)}, u32[]{:S(2)}) collective-permute-start(f16[4,32,512]{2,1,0:T(8,128)(2,1)S(1)} %collective-permute-done.7), channel_id=1, source_target_pairs={{0,1},{1,0},{2,3},{3,2},{4,5},{5,4},{6,7},{7,6},{8,9},{9,8},{10,11... | collective-permute-start | bytes 393224 | tf_op jit(solution)/shard_map/ppermute | solution.py:230
  49.0 0.7 %copy-start.4 = (s32[2]{0:T(128)S(1)}, s32[2]{0:T(128)}, u32[]{:S(2)}) copy-start(s32[2]{0:T(128)} %refs_6_.1) | copy-start | bytes 28
  52.8 7.2 %collective-permute-start.17 = (f16[264,512]{1,0:T(8,128)(2,1)S(1)}, f16[264,512]{1,0:T(8,128)(2,1)S(1)}, u32[]{:S(2)}, u32[]{:S(2)}) collective-permute-start(f16[264,512]{1,0:T(8,128)(2,1)S(1)} %convert_element_type.42), channel_id=1, source_target_pairs={{0,1},{1,0},{2,3},{3,2},{4,5},{5,4},{6,7},{7,6},{8,9},{9,8},{10,11... | collective-permute-start | bytes 811016 | tf_op jit(solution)/shard_map/ppermute | solution.py:467

commit v13 on v11

--- a/solution.py
+++ b/solution.py
@@ -231,7 +231,7 @@
 
     beside = [along_x(part) for part in parts]
     above = [along_rep(part) for part in parts]
-    apart = [along_rep(beside[0]), along_x(above[1])]
+    apart = [along_rep(part) for part in beside]
     return [*parts, *beside, *above, *apart]
 
 
@@ -287,15 +287,8 @@
         once_ref[f] = bare + product(bare, high[f], low[f])
 
 
-def dyson_kernel(apart, early, offsets_ref, steps_ref, level_ref, bare_ref, hamiltonian_ref, two_ref,
-                 four_ref, odd_ref, beside_refs, screened_ref, packed_ref, step_ref, own_ref,
-                 high, low, made, hamiltonian_rows, made_sem, hamiltonian_sem):
-    once_ref, high_ref, low_ref = early
+def twice_kernel(apart, once_ref, high_ref, low_ref, steps_ref, bare_ref, made_ref, high, low):
     rows, width = bare_ref.shape
-    entry_scale = width ** -0.5
-    read = pltpu.make_async_copy(hamiltonian_ref, hamiltonian_rows, hamiltonian_sem)
-    read.start()
-    rep = lax.axis_index("rep")
     bare = bare_ref[...]
     once = [once_ref[f] for f in range(FREQS)]
     at = jnp.where(steps_ref[1] > steps_ref[0], 1, 0)
@@ -312,21 +305,31 @@
     last = jnp.where(at == 0, once[0], once[1])
     upper, lower = high[...], low[...]
     twice = last + product(product(last, upper, lower), upper, lower)
+    for f in range(FREQS):
+        count = steps_ref[f]
+        value = jnp.where(count == 0, bare, jnp.where(count == 1, once[f], twice))
+        made_ref[f] = value.astype(jnp.bfloat16)
+
+
+def dyson_kernel(made_ref, offsets_ref, level_ref, hamiltonian_ref, two_ref, four_ref, odd_ref,
+                 beside_refs, screened_ref, packed_ref, step_ref, own_ref,
+                 hamiltonian_rows, made_sem, hamiltonian_sem):
+    rows, width = step_ref.shape
+    entry_scale = width ** -0.5
+    read = pltpu.make_async_copy(hamiltonian_ref, hamiltonian_rows, hamiltonian_sem)
+    read.start()
+    write = pltpu.make_async_copy(made_ref, screened_ref, made_sem)
+    write.start()
+    rep = lax.axis_index("rep")
     other = jnp.minimum(offsets_ref[0], offsets_ref[1])
     less = jnp.where(other == 2, two_ref[...], odd_ref[...])
     four = four_ref[...]
     energy_terms = jnp.zeros((rows, width), jnp.float32)
     for f in range(FREQS):
-        count = steps_ref[f]
-        value = jnp.where(count == 0, bare, jnp.where(count == 1, once[f], twice))
-        value = value.astype(jnp.bfloat16)
-        made[f] = value
         lowered = jnp.where(offsets_ref[f] == SHIFTS, four, less).astype(jnp.float32)
-        energy_terms += lowered * value.astype(jnp.float32)
-    write = pltpu.make_async_copy(made, screened_ref, made_sem)
-    write.start()
+        energy_terms += lowered * made_ref[f].astype(jnp.float32)
+    beside = sum(ref[...].astype(jnp.float32) for ref in beside_refs)
     read.wait()
-    beside = sum(ref[...].astype(jnp.float32) for ref in beside_refs)
     rest = hamiltonian_rows[...] - entry_scale * energy_terms - (0.5 * entry_scale) * beside
     col = lax.broadcasted_iota(jnp.int32, (rows, width), 1)
     row = lax.broadcasted_iota(jnp.int32, (rows, width), 0) + rep * rows
@@ -369,11 +372,22 @@
         name="early",
     )(*known, bare)
 
+    def second_kernel(*refs):
+        far, rest = refs[:len(apart)], refs[len(apart):]
+        twice_kernel(far, *rest)
+
+    made = pl.pallas_call(
+        second_kernel,
+        out_shape=jax.ShapeDtypeStruct((FREQS, rows, width), jnp.bfloat16),
+        in_specs=[in_vmem] * (len(apart) + 3) + [in_smem, in_vmem],
+        out_specs=in_vmem,
+        scratch_shapes=[VMEM((width, width), jnp.bfloat16)] * 2,
+        compiler_params=large,
+        name="twice",
+    )(*apart, *early, steps, bare)
+
     def kernel(*refs):
-        far, rest = refs[:len(apart)], refs[len(apart):]
-        done, rest = rest[:3], rest[3:]
-        named, rest = rest[:8], rest[8:]
-        dyson_kernel(far, done, *named, rest[:sides], *rest[sides:])
+        dyson_kernel(*refs[:7], refs[7:7 + sides], *refs[7 + sides:])
 
     return pl.pallas_call(
         kernel,
@@ -383,15 +397,12 @@
             jax.ShapeDtypeStruct((rows, width), jnp.float32),
             jax.ShapeDtypeStruct((EXTRA, width), jnp.float32),
         ),
-        in_specs=[in_vmem] * (len(apart) + 3) + [in_smem] * 3 + [in_vmem, in_hbm]
-        + [in_vmem] * (3 + sides),
+        in_specs=[in_vmem] + [in_smem] * 2 + [in_hbm] + [in_vmem] * (3 + sides),
         out_specs=(in_hbm,) + (in_vmem,) * 3,
-        scratch_shapes=[VMEM((width, width), jnp.bfloat16)] * 2
-        + [VMEM((FREQS, rows, width), jnp.bfloat16), VMEM((rows, width), jnp.float32)]
-        + [pltpu.SemaphoreType.DMA] * 2,
+        scratch_shapes=[VMEM((rows, width), jnp.float32)] + [pltpu.SemaphoreType.DMA] * 2,
         compiler_params=large,
         name="dyson",
-    )(*apart, *early, offsets, steps, level, bare, held(hamiltonian), two, four, odd, *beside)
+    )(made, offsets, level, held(hamiltonian), two, four, odd, *beside)
 
 
 def columns(value, first):

time: 60.2 us -> 61 us (1.013)
  the two profiles are of different devices: /device:TPU:26 before, /device:TPU:0 now
where the time goes in v13:
time: 61 us; the launch traced here: 60.7 us
  starting transfers between devices  29.5 us (48%)
  waiting for transfers between devices  16.9 us (28%)
  Pallas kernels  10.2 us (17%)
  between operations  3.04 us (5%)
  local copies, waits for them, and re-layouts  0.72 us (1%)
    ppermute x3, starting transfers between devices, shifted(): return lax.ppermute(block, axis, route)  9.83 us
    ppermute x3, starting transfers between devices, polar_share(): received[k - 1] = lax.ppermute(shares[k - 1], 'energy', route)  5.82 us
    ppermute x3, waiting for transfers between devices, gather_energy(): got = lax.ppermute(chunk, 'energy', route)  5.31 us
    ppermute x1, waiting for transfers between devices, body(): lax.ppermute(packed.astype(coded), 'rep', [(0, 1), (1, 0)])  4.51 us
    ppermute x4, starting transfers between devices, along_rep(): return lax.ppermute(part, 'rep', [(0, 1), (1, 0)])  4.12 us
    ppermute x1, waiting for transfers between devices, polar_share(): got = lax.ppermute(sent, 'energy', [(e, e ^ 1) for e in range(energies)])  3.67 us
    ppermute x3, starting transfers between devices, gather_energy(): got = lax.ppermute(chunk, 'energy', route)  3.07 us
    ppermute x4, waiting for transfers between devices, along_rep(): return lax.ppermute(part, 'rep', [(0, 1), (1, 0)])  3.07 us
  transfers between devices with their start and end apart: 18, of which 8 were waited for; matrix products, arithmetic and copies ran while one was open for 0% of the time, Pallas kernels for 9%

profile of v13, /device:TPU:0, one launch (start us, length us, event | category | flops | bytes accessed | tf_op | source)
XLA Modules:
  0.0 60.7 jit_solution(14797763322426961057)
XLA Ops:
  0.6 0.0 copy-start.1
  0.6 0.0 copy-start
  1.4 0.9 %prepare.1 = bf16[136,512]{1,0:T(8,128)(2,1)S(1)} custom-call(f32[1]{0:T(128)S(6)} %copy.19.weight_ref.refs_3_, bf16[256,512]{1,0:T(8,128)(2,1)} %bitcast.10), custom_call_target="tpu_custom_call" | custom-call | tf_op jit(solution)/shard_map/prepare/pallas_call | solution.py:143
  2.3 3.0 %collective-permute-start = (bf16[136,512]{1,0:T(8,128)(2,1)S(1)}, bf16[136,512]{1,0:T(8,128)(2,1)S(1)}, u32[]{:S(2)}, u32[]{:S(2)}) collective-permute-start(bf16[136,512]{1,0:T(8,128)(2,1)S(1)} %prepare.1), channel_id=1, source_target_pairs={{0,4},{4,0},{8,12},{12,8},{16,20},{20,16},{24,28},{28,24},{1,5},{5... | collective-permute-start | bytes 417800 | tf_op jit(solution)/shard_map/ppermute | solution.py:152
  5.3 3.7 %collective-permute-done.got_ref.refs_9_ = bf16[136,512]{1,0:T(8,128)(2,1)S(1)} collective-permute-done((bf16[136,512]{1,0:T(8,128)(2,1)S(1)}, bf16[136,512]{1,0:T(8,128)(2,1)S(1)}, u32[]{:S(2)}, u32[]{:S(2)}) %collective-permute-start) | collective-permute-done | bytes 139296 | tf_op jit(solution)/shard_map/ppermute | solution.py:152
  9.0 0.0 copy-done.1
  9.0 1.9 %collective-permute-start.1 = (bf16[72,512]{1,0:T(8,128)(2,1)S(1)}, bf16[72,512]{1,0:T(8,128)(2,1)S(1)}, u32[]{:S(2)}, u32[]{:S(2)}) collective-permute-start(bf16[72,512]{1,0:T(8,128)(2,1)S(1)} %get-tuple-element.15), channel_id=1, source_target_pairs={{0,8},{4,12},{8,16},{12,20},{16,24},{20,28},{24,0},{28,4},{1,9},{5... | collective-permute-start | bytes 221192 | tf_op jit(solution)/shard_map/ppermute | solution.py:164
  10.9 2.6 %collective-permute-start.2 = (bf16[72,512]{1,0:T(8,128)(2,1)S(1)}, bf16[72,512]{1,0:T(8,128)(2,1)S(1)}, u32[]{:S(2)}, u32[]{:S(2)}) collective-permute-start(bf16[72,512]{1,0:T(8,128)(2,1)S(1)} %get-tuple-element.16), channel_id=1, source_target_pairs={{0,16},{4,20},{8,24},{12,28},{16,0},{20,4},{24,8},{28,12},{1,17},{... | collective-permute-start | bytes 221192 | tf_op jit(solution)/shard_map/ppermute | solution.py:164
  13.5 1.3 %collective-permute-start.3 = (bf16[72,512]{1,0:T(8,128)(2,1)S(1)}, bf16[72,512]{1,0:T(8,128)(2,1)S(1)}, u32[]{:S(2)}, u32[]{:S(2)}) collective-permute-start(bf16[72,512]{1,0:T(8,128)(2,1)S(1)} %get-tuple-element.17), channel_id=1, source_target_pairs={{0,24},{4,28},{8,0},{12,4},{16,8},{20,12},{24,16},{28,20},{1,25},{... | collective-permute-start | bytes 221192 | tf_op jit(solution)/shard_map/ppermute | solution.py:164
  14.9 2.6 %collective-permute-start.13 = (bf16[256,512]{1,0:T(8,128)(2,1)S(1)}, bf16[256,512]{1,0:T(8,128)(2,1)S(1)}, u32[]{:S(2)}, u32[]{:S(2)}) collective-permute-start(bf16[256,512]{1,0:T(8,128)(2,1)S(1)} %bitcast.12), channel_id=1, source_target_pairs={{0,8},{4,12},{8,16},{12,20},{16,24},{20,28},{1,9},{5,13},{9,17},{1... | collective-permute-start | bytes 786440 | tf_op jit(solution)/shard_map/ppermute | solution.py:44
  18.8 0.0 copy-start.2
  18.8 0.0 copy-start.3
  18.9 0.0 collective-permute-done.1.refs_0_
  18.9 0.0 collective-permute-done.2.refs_1_
  18.9 0.0 collective-permute-done.3.refs_2_
  18.9 0.0 copy-done
  18.9 0.6 copy-done.2
  19.5 0.0 copy-done.3
  19.5 0.8 %polar.1 = f32[2,32,512]{2,1,0:T(8,128)S(1)} custom-call(bf16[72,512]{1,0:T(8,128)(2,1)S(1)} %collective-permute-done.1.refs_0_, bf16[72,512]{1,0:T(8,128)(2,1)S(1)} %collective-permute-done.2.refs_1_, bf16[72,512]{1,0:T(8,128)(2,1)S(1)} %collective-permute-done.3.refs_2_, f32[1]{0:T(128)S(6)} %copy.19.weight_ref.refs_3_, s32[2]{0:T(128)S(1)} %copy-done.2, ...), custom_call_target="tpu_custom_call" | custom-call | tf_op jit(solution)/shard_map/polar/pallas_call | solution.py:170
  20.4 2.4 %collective-permute-start.4 = (f16[2,32,512]{2,1,0:T(8,128)(2,1)S(1)}, f16[2,32,512]{2,1,0:T(8,128)(2,1)S(1)}, u32[]{:S(2)}, u32[]{:S(2)}) collective-permute-start(f16[2,32,512]{2,1,0:T(8,128)(2,1)S(1)} %convert_element_type.33), channel_id=1, source_target_pairs={{0,24},{4,28},{8,0},{12,4},{16,8},{20,12},{24,16},{28,20},{1,25},{... | collective-permute-start | bytes 196616 | tf_op jit(solution)/shard_map/ppermute | solution.py:215
  22.8 0.0 collective-permute-start.5
  22.8 0.6 %collective-permute-start.6 = (f16[2,32,512]{2,1,0:T(8,128)(2,1)S(1)}, f16[2,32,512]{2,1,0:T(8,128)(2,1)S(1)}, u32[]{:S(2)}, u32[]{:S(2)}) collective-permute-start(f16[2,32,512]{2,1,0:T(8,128)(2,1)S(1)} %convert_element_type.33), channel_id=1, source_target_pairs={{0,8},{4,12},{8,16},{12,20},{16,24},{20,28},{24,0},{28,4},{1,9},{5... | collective-permute-start | bytes 196616 | tf_op jit(solution)/shard_map/ppermute | solution.py:215
  23.5 1.5 %collective-permute-done.4 = f16[2,32,512]{2,1,0:T(8,128)(2,1)S(1)} collective-permute-done((f16[2,32,512]{2,1,0:T(8,128)(2,1)S(1)}, f16[2,32,512]{2,1,0:T(8,128)(2,1)S(1)}, u32[]{:S(2)}, u32[]{:S(2)}) %collective-permute-start.4) | collective-permute-done | bytes 65568 | tf_op jit(solution)/shard_map/ppermute | solution.py:215
  25.0 2.9 %collective-permute-done.5 = f16[2,32,512]{2,1,0:T(8,128)(2,1)S(1)} collective-permute-done((f16[2,32,512]{2,1,0:T(8,128)(2,1)S(1)}, f16[2,32,512]{2,1,0:T(8,128)(2,1)S(1)}, u32[]{:S(2)}, u32[]{:S(2)}) %collective-permute-start.5) | collective-permute-done | bytes 65568 | tf_op jit(solution)/shard_map/ppermute | solution.py:215
  28.0 0.9 %collective-permute-done.6 = f16[2,32,512]{2,1,0:T(8,128)(2,1)S(1)} collective-permute-done((f16[2,32,512]{2,1,0:T(8,128)(2,1)S(1)}, f16[2,32,512]{2,1,0:T(8,128)(2,1)S(1)}, u32[]{:S(2)}, u32[]{:S(2)}) %collective-permute-start.6) | collective-permute-done | bytes 65568 | tf_op jit(solution)/shard_map/ppermute | solution.py:215
  28.9 1.6 %collective-permute-start.7 = (f16[4,32,512]{2,1,0:T(8,128)(2,1)S(1)}, f16[4,32,512]{2,1,0:T(8,128)(2,1)S(1)}, u32[]{:S(2)}, u32[]{:S(2)}) collective-permute-start(f16[4,32,512]{2,1,0:T(8,128)(2,1)S(1)} %get-tuple-element.31), channel_id=1, source_target_pairs={{0,4},{4,0},{8,12},{12,8},{16,20},{20,16},{24,28},{28,24},{1,5},{5... | collective-permute-start | bytes 393224 | tf_op jit(solution)/shard_map/ppermute | solution.py:227
  30.4 0.5 collective-permute-start.9
  31.0 1.5 %collective-permute-start.11 = (f16[4,32,512]{2,1,0:T(8,128)(2,1)S(1)}, f16[4,32,512]{2,1,0:T(8,128)(2,1)S(1)}, u32[]{:S(2)}, u32[]{:S(2)}) collective-permute-start(f16[4,32,512]{2,1,0:T(8,128)(2,1)S(1)} %get-tuple-element.31), channel_id=1, source_target_pairs={{0,1},{1,0},{2,3},{3,2},{4,5},{5,4},{6,7},{7,6},{8,9},{9,8},{10,11... | collective-permute-start | bytes 393224 | tf_op jit(solution)/shard_map/ppermute | solution.py:230
  32.5 0.5 collective-permute-start.12
  33.0 0.0 collective-permute-done.13.two_ref.refs_4_
  33.0 0.0 collective-permute-start.16
  33.0 0.6 chosen.1
  33.6 0.3 collective-permute-done.7
  33.9 3.4 %collective-permute-start.15 = (bf16[256,512]{1,0:T(8,128)(2,1)S(1)}, bf16[256,512]{1,0:T(8,128)(2,1)S(1)}, u32[]{:S(2)}, u32[]{:S(2)}) collective-permute-start(bf16[256,512]{1,0:T(8,128)(2,1)S(1)} %chosen.1), channel_id=1, source_target_pairs={{0,4},{4,8},{8,12},{12,16},{16,20},{20,24},{24,28},{1,5},{5,9},{9,... | collective-permute-start | bytes 786440 | tf_op jit(solution)/shard_map/ppermute | solution.py:44
  37.3 0.0 collective-permute-done.9
  37.3 3.8 %collective-permute-start.14 = (bf16[256,512]{1,0:T(8,128)(2,1)S(1)}, bf16[256,512]{1,0:T(8,128)(2,1)S(1)}, u32[]{:S(2)}, u32[]{:S(2)}) collective-permute-start(bf16[256,512]{1,0:T(8,128)(2,1)S(1)} %collective-permute-done.13.two_ref.refs_4_), channel_id=1, source_target_pairs={{0,8},{4,12},{8,16},{12,20},{16,24},{20,28},{1,9},{5,13},{9,17},{1... | collective-permute-start | bytes 786440 | tf_op jit(solution)/shard_map/ppermute | solution.py:44
  41.2 0.0 collective-permute-done.11
  41.2 1.6 %collective-permute-start.8 = (f16[4,32,512]{2,1,0:T(8,128)(2,1)S(1)}, f16[4,32,512]{2,1,0:T(8,128)(2,1)S(1)}, u32[]{:S(2)}, u32[]{:S(2)}) collective-permute-start(f16[4,32,512]{2,1,0:T(8,128)(2,1)S(1)} %collective-permute-done.7), channel_id=1, source_target_pairs={{0,1},{1,0},{2,3},{3,2},{4,5},{5,4},{6,7},{7,6},{8,9},{9,8},{10,11... | collective-permute-start | bytes 393224 | tf_op jit(solution)/shard_map/ppermute | solution.py:230
  42.8 0.0 collective-permute-done.12
  42.8 0.5 collective-permute-start.10
  43.5 1.3 %early.1 = (f32[2,256,512]{2,1,0:T(8,128)S(1)}, bf16[2,512,512]{2,1,0:T(8,128)(2,1)S(1)}, bf16[2,512,512]{2,1,0:T(8,128)(2,1)S(1)}) custom-call(f32[4,32,512]{2,1,0:T(8,128)S(1)} %convert_element_type.36.refs_0_, f32[4,32,512]{2,1,0:T(8,128)S(1)} %convert_element_type.37.refs_1_, f32[4,32,512]{2,1,0:T(8,128)S(1)} %convert_element_type.38.refs_2_, ...), custom_call_target="tpu_custom_call" | custom-call | tf_op jit(solution)/shard_map/early/pallas_call | solution.py:365
  44.8 1.7 %collective-permute-done.8 = f16[4,32,512]{2,1,0:T(8,128)(2,1)S(1)} collective-permute-done((f16[4,32,512]{2,1,0:T(8,128)(2,1)S(1)}, f16[4,32,512]{2,1,0:T(8,128)(2,1)S(1)}, u32[]{:S(2)}, u32[]{:S(2)}) %collective-permute-start.8) | collective-permute-done | bytes 131104 | tf_op jit(solution)/shard_map/ppermute | solution.py:230
  46.5 1.4 %collective-permute-done.10 = f16[4,32,512]{2,1,0:T(8,128)(2,1)S(1)} collective-permute-done((f16[4,32,512]{2,1,0:T(8,128)(2,1)S(1)}, f16[4,32,512]{2,1,0:T(8,128)(2,1)S(1)}, u32[]{:S(2)}, u32[]{:S(2)}) %collective-permute-start.10) | collective-permute-done | bytes 131104 | tf_op jit(solution)/shard_map/ppermute | solution.py:230
  47.9 2.2 %twice.1.refs_0_ = bf16[2,256,512]{2,1,0:T(8,128)(2,1)S(1)} custom-call(f32[4,32,512]{2,1,0:T(8,128)S(1)} %convert_element_type.34.refs_0_, f32[4,32,512]{2,1,0:T(8,128)S(1)} %convert_element_type.35.refs_1_, f32[2,256,512]{2,1,0:T(8,128)S(1)} %get-tuple-element.18.refs_2_, bf16[2,512,512]{2,1,0:T(8,128)(2,1)S(1)} %get-tuple-element.19.refs_3_, ...), custom_call_target="tpu_custom_call" | custom-call | tf_op jit(solution)/shard_map/twice/pallas_call | solution.py:379
  50.1 0.0 collective-permute-done.16.refs_7_
  50.1 0.0 collective-permute-done.15.refs_6_
  50.1 0.0 collective-permute-done.14.refs_5_
  50.1 2.2 %dyson.1 = (bf16[2,256,512]{2,1,0:T(8,128)(2,1)}, f32[264,512]{1,0:T(8,128)S(1)}, f32[256,512]{1,0:T(8,128)S(1)}, f32[8,512]{1,0:T(8,128)S(1)}) custom-call(bf16[2,256,512]{2,1,0:T(8,128)(2,1)S(1)} %twice.1.refs_0_, s32[2]{0:T(128)S(1)} %copy-done.2, f32[1]{0:T(128)S(6)} %copy.20.refs_7_.refs_2_, f32[256,512]{1,0:T(8,128)} %bitcast.16, ...), custom_call_target="tpu_custom_call" | custom-call | tf_op jit(solution)/shard_map/dyson/pallas_call | solution.py:392
  52.4 1.6 %collective-permute-start.17 = (f16[264,512]{1,0:T(8,128)(2,1)S(1)}, f16[264,512]{1,0:T(8,128)(2,1)S(1)}, u32[]{:S(2)}, u32[]{:S(2)}) collective-permute-start(f16[264,512]{1,0:T(8,128)(2,1)S(1)} %convert_element_type.42), channel_id=1, source_target_pairs={{0,1},{1,0},{2,3},{3,2},{4,5},{5,4},{6,7},{7,6},{8,9},{9,8},{10,11... | collective-permute-start | bytes 811016 | tf_op jit(solution)/shard_map/ppermute | solution.py:478
  53.9 0.4 begin.1
  54.4 4.5 %collective-permute-done.17 = f16[264,512]{1,0:T(8,128)(2,1)S(1)} collective-permute-done((f16[264,512]{1,0:T(8,128)(2,1)S(1)}, f16[264,512]{1,0:T(8,128)(2,1)S(1)}, u32[]{:S(2)}, u32[]{:S(2)}) %collective-permute-start.17) | collective-permute-done | bytes 270368 | tf_op jit(solution)/shard_map/ppermute | solution.py:478
  58.9 0.1 convert_element_type.43.theirs_ref
  58.9 1.7 %finish.1 = f32[256,512]{1,0:T(8,128)} custom-call(s32[1]{0:T(128)S(6)} %copy.21.refs_6_.steps_ref, f32[256,512]{1,0:T(8,128)S(1)} %get-tuple-element.21.step_ref, f32[256,512]{1,0:T(8,128)S(1)} %get-tuple-element.24.square_ref, bf16[256,512]{1,0:T(8,128)(2,1)S(1)} %get-tuple-element.25.high_ref, bf16[256,512]{1,0:T(8,128)(2,1)S(1)} %get-tuple-element.26.low_ref, ...), custom_call_target="tpu_custom_call" | custom-call | tf_op jit(solution)/shard_map/finish/pallas_call | solution.py:489
  (18 shorter events, 0.4 us)
Async XLA Ops:
  0.6 8.4 %copy-start.1 = (bf16[1,1,256,512]{3,2,1,0:T(8,128)(2,1)S(1)}, bf16[1,1,256,512]{3,2,1,0:T(8,128)(2,1)}, u32[]{:S(2)}) copy-start(bf16[1,1,256,512]{3,2,1,0:T(8,128)(2,1)} %param.8) | copy-start | bytes 786436
  0.6 18.3 %copy-start = (f32[1,256,512]{2,1,0:T(8,128)S(1)}, f32[1,256,512]{2,1,0:T(8,128)}, u32[]{:S(2)}) copy-start(f32[1,256,512]{2,1,0:T(8,128)} %param.11) | copy-start | bytes 1572868
  2.3 6.7 %collective-permute-start = (bf16[136,512]{1,0:T(8,128)(2,1)S(1)}, bf16[136,512]{1,0:T(8,128)(2,1)S(1)}, u32[]{:S(2)}, u32[]{:S(2)}) collective-permute-start(bf16[136,512]{1,0:T(8,128)(2,1)S(1)} %prepare.1), channel_id=1, source_target_pairs={{0,4},{4,0},{8,12},{12,8},{16,20},{20,16},{24,28},{28,24},{1,5},{5... | collective-permute-start | bytes 417800 | tf_op jit(solution)/shard_map/ppermute | solution.py:152
  9.0 9.8 %collective-permute-start.1 = (bf16[72,512]{1,0:T(8,128)(2,1)S(1)}, bf16[72,512]{1,0:T(8,128)(2,1)S(1)}, u32[]{:S(2)}, u32[]{:S(2)}) collective-permute-start(bf16[72,512]{1,0:T(8,128)(2,1)S(1)} %get-tuple-element.15), channel_id=1, source_target_pairs={{0,8},{4,12},{8,16},{12,20},{16,24},{20,28},{24,0},{28,4},{1,9},{5... | collective-permute-start | bytes 221192 | tf_op jit(solution)/shard_map/ppermute | solution.py:164
  10.9 7.9 %collective-permute-start.2 = (bf16[72,512]{1,0:T(8,128)(2,1)S(1)}, bf16[72,512]{1,0:T(8,128)(2,1)S(1)}, u32[]{:S(2)}, u32[]{:S(2)}) collective-permute-start(bf16[72,512]{1,0:T(8,128)(2,1)S(1)} %get-tuple-element.16), channel_id=1, source_target_pairs={{0,16},{4,20},{8,24},{12,28},{16,0},{20,4},{24,8},{28,12},{1,17},{... | collective-permute-start | bytes 221192 | tf_op jit(solution)/shard_map/ppermute | solution.py:164
  13.5 5.4 %collective-permute-start.3 = (bf16[72,512]{1,0:T(8,128)(2,1)S(1)}, bf16[72,512]{1,0:T(8,128)(2,1)S(1)}, u32[]{:S(2)}, u32[]{:S(2)}) collective-permute-start(bf16[72,512]{1,0:T(8,128)(2,1)S(1)} %get-tuple-element.17), channel_id=1, source_target_pairs={{0,24},{4,28},{8,0},{12,4},{16,8},{20,12},{24,16},{28,20},{1,25},{... | collective-permute-start | bytes 221192 | tf_op jit(solution)/shard_map/ppermute | solution.py:164
  14.9 18.1 %collective-permute-start.13 = (bf16[256,512]{1,0:T(8,128)(2,1)S(1)}, bf16[256,512]{1,0:T(8,128)(2,1)S(1)}, u32[]{:S(2)}, u32[]{:S(2)}) collective-permute-start(bf16[256,512]{1,0:T(8,128)(2,1)S(1)} %bitcast.12), channel_id=1, source_target_pairs={{0,8},{4,12},{8,16},{12,20},{16,24},{20,28},{1,9},{5,13},{9,17},{1... | collective-permute-start | bytes 786440 | tf_op jit(solution)/shard_map/ppermute | solution.py:44
  18.8 0.7 %copy-start.2 = (s32[2]{0:T(128)S(1)}, s32[2]{0:T(128)}, u32[]{:S(2)}) copy-start(s32[2]{0:T(128)} %refs_1_.1) | copy-start | bytes 28
  18.8 0.7 %copy-start.3 = (s32[2]{0:T(128)S(1)}, s32[2]{0:T(128)}, u32[]{:S(2)}) copy-start(s32[2]{0:T(128)} %refs_5_.3) | copy-start | bytes 28
  20.4 4.6 %collective-permute-start.4 = (f16[2,32,512]{2,1,0:T(8,128)(2,1)S(1)}, f16[2,32,512]{2,1,0:T(8,128)(2,1)S(1)}, u32[]{:S(2)}, u32[]{:S(2)}) collective-permute-start(f16[2,32,512]{2,1,0:T(8,128)(2,1)S(1)} %convert_element_type.33), channel_id=1, source_target_pairs={{0,24},{4,28},{8,0},{12,4},{16,8},{20,12},{24,16},{28,20},{1,25},{... | collective-permute-start | bytes 196616 | tf_op jit(solution)/shard_map/ppermute | solution.py:215
  22.8 5.2 %collective-permute-start.5 = (f16[2,32,512]{2,1,0:T(8,128)(2,1)S(1)}, f16[2,32,512]{2,1,0:T(8,128)(2,1)S(1)}, u32[]{:S(2)}, u32[]{:S(2)}) collective-permute-start(f16[2,32,512]{2,1,0:T(8,128)(2,1)S(1)} %convert_element_type.33), channel_id=1, source_target_pairs={{0,16},{4,20},{8,24},{12,28},{16,0},{20,4},{24,8},{28,12},{1,17},{... | collective-permute-start | bytes 196616 | tf_op jit(solution)/shard_map/ppermute | solution.py:215
  22.8 6.1 %collective-permute-start.6 = (f16[2,32,512]{2,1,0:T(8,128)(2,1)S(1)}, f16[2,32,512]{2,1,0:T(8,128)(2,1)S(1)}, u32[]{:S(2)}, u32[]{:S(2)}) collective-permute-start(f16[2,32,512]{2,1,0:T(8,128)(2,1)S(1)} %convert_element_type.33), channel_id=1, source_target_pairs={{0,8},{4,12},{8,16},{12,20},{16,24},{20,28},{24,0},{28,4},{1,9},{5... | collective-permute-start | bytes 196616 | tf_op jit(solution)/shard_map/ppermute | solution.py:215
  28.9 5.0 %collective-permute-start.7 = (f16[4,32,512]{2,1,0:T(8,128)(2,1)S(1)}, f16[4,32,512]{2,1,0:T(8,128)(2,1)S(1)}, u32[]{:S(2)}, u32[]{:S(2)}) collective-permute-start(f16[4,32,512]{2,1,0:T(8,128)(2,1)S(1)} %get-tuple-element.31), channel_id=1, source_target_pairs={{0,4},{4,0},{8,12},{12,8},{16,20},{20,16},{24,28},{28,24},{1,5},{5... | collective-permute-start | bytes 393224 | tf_op jit(solution)/shard_map/ppermute | solution.py:227
  30.4 6.9 %collective-permute-start.9 = (f16[4,32,512]{2,1,0:T(8,128)(2,1)S(1)}, f16[4,32,512]{2,1,0:T(8,128)(2,1)S(1)}, u32[]{:S(2)}, u32[]{:S(2)}) collective-permute-start(f16[4,32,512]{2,1,0:T(8,128)(2,1)S(1)} %get-tuple-element.30), channel_id=1, source_target_pairs={{0,4},{4,0},{8,12},{12,8},{16,20},{20,16},{24,28},{28,24},{1,5},{5... | collective-permute-start | bytes 393224 | tf_op jit(solution)/shard_map/ppermute | solution.py:227
  31.0 10.2 %collective-permute-start.11 = (f16[4,32,512]{2,1,0:T(8,128)(2,1)S(1)}, f16[4,32,512]{2,1,0:T(8,128)(2,1)S(1)}, u32[]{:S(2)}, u32[]{:S(2)}) collective-permute-start(f16[4,32,512]{2,1,0:T(8,128)(2,1)S(1)} %get-tuple-element.31), channel_id=1, source_target_pairs={{0,1},{1,0},{2,3},{3,2},{4,5},{5,4},{6,7},{7,6},{8,9},{9,8},{10,11... | collective-permute-start | bytes 393224 | tf_op jit(solution)/shard_map/ppermute | solution.py:230
  32.5 10.3 %collective-permute-start.12 = (f16[4,32,512]{2,1,0:T(8,128)(2,1)S(1)}, f16[4,32,512]{2,1,0:T(8,128)(2,1)S(1)}, u32[]{:S(2)}, u32[]{:S(2)}) collective-permute-start(f16[4,32,512]{2,1,0:T(8,128)(2,1)S(1)} %get-tuple-element.30), channel_id=1, source_target_pairs={{0,1},{1,0},{2,3},{3,2},{4,5},{5,4},{6,7},{7,6},{8,9},{9,8},{10,11... | collective-permute-start | bytes 393224 | tf_op jit(solution)/shard_map/ppermute | solution.py:230
  33.0 17.1 %collective-permute-start.16 = (bf16[256,512]{1,0:T(8,128)(2,1)S(1)}, bf16[256,512]{1,0:T(8,128)(2,1)S(1)}, u32[]{:S(2)}, u32[]{:S(2)}) collective-permute-start(bf16[256,512]{1,0:T(8,128)(2,1)S(1)} %bitcast.14), channel_id=1, source_target_pairs={{0,2},{2,0},{1,3},{3,1},{4,6},{6,4},{5,7},{7,5},{8,10},{10,8},{9,1... | collective-permute-start | bytes 786440 | tf_op jit(solution)/shard_map/ppermute | solution.py:469
  33.9 16.2 %collective-permute-start.15 = (bf16[256,512]{1,0:T(8,128)(2,1)S(1)}, bf16[256,512]{1,0:T(8,128)(2,1)S(1)}, u32[]{:S(2)}, u32[]{:S(2)}) collective-permute-start(bf16[256,512]{1,0:T(8,128)(2,1)S(1)} %chosen.1), channel_id=1, source_target_pairs={{0,4},{4,8},{8,12},{12,16},{16,20},{20,24},{24,28},{1,5},{5,9},{9,... | collective-permute-start | bytes 786440 | tf_op jit(solution)/shard_map/ppermute | solution.py:44
  37.3 12.8 %collective-permute-start.14 = (bf16[256,512]{1,0:T(8,128)(2,1)S(1)}, bf16[256,512]{1,0:T(8,128)(2,1)S(1)}, u32[]{:S(2)}, u32[]{:S(2)}) collective-permute-start(bf16[256,512]{1,0:T(8,128)(2,1)S(1)} %collective-permute-done.13.two_ref.refs_4_), channel_id=1, source_target_pairs={{0,8},{4,12},{8,16},{12,20},{16,24},{20,28},{1,9},{5,13},{9,17},{1... | collective-permute-start | bytes 786440 | tf_op jit(solution)/shard_map/ppermute | solution.py:44
  41.2 5.3 %collective-permute-start.8 = (f16[4,32,512]{2,1,0:T(8,128)(2,1)S(1)}, f16[4,32,512]{2,1,0:T(8,128)(2,1)S(1)}, u32[]{:S(2)}, u32[]{:S(2)}) collective-permute-start(f16[4,32,512]{2,1,0:T(8,128)(2,1)S(1)} %collective-permute-done.7), channel_id=1, source_target_pairs={{0,1},{1,0},{2,3},{3,2},{4,5},{5,4},{6,7},{7,6},{8,9},{9,8},{10,11... | collective-permute-start | bytes 393224 | tf_op jit(solution)/shard_map/ppermute | solution.py:230
  42.8 5.1 %collective-permute-start.10 = (f16[4,32,512]{2,1,0:T(8,128)(2,1)S(1)}, f16[4,32,512]{2,1,0:T(8,128)(2,1)S(1)}, u32[]{:S(2)}, u32[]{:S(2)}) collective-permute-start(f16[4,32,512]{2,1,0:T(8,128)(2,1)S(1)} %collective-permute-done.9), channel_id=1, source_target_pairs={{0,1},{1,0},{2,3},{3,2},{4,5},{5,4},{6,7},{7,6},{8,9},{9,8},{10,11... | collective-permute-start | bytes 393224 | tf_op jit(solution)/shard_map/ppermute | solution.py:230
  52.4 6.5 %collective-permute-start.17 = (f16[264,512]{1,0:T(8,128)(2,1)S(1)}, f16[264,512]{1,0:T(8,128)(2,1)S(1)}, u32[]{:S(2)}, u32[]{:S(2)}) collective-permute-start(f16[264,512]{1,0:T(8,128)(2,1)S(1)} %convert_element_type.42), channel_id=1, source_target_pairs={{0,1},{1,0},{2,3},{3,2},{4,5},{5,4},{6,7},{7,6},{8,9},{9,8},{10,11... | collective-permute-start | bytes 811016 | tf_op jit(solution)/shard_map/ppermute | solution.py:478

commit v14 on v11

--- a/solution.py
+++ b/solution.py
@@ -42,6 +42,14 @@
     count = lax.axis_size(axis)
     route = [(i, i + distance) for i in range(count - distance)]
     return lax.ppermute(block, axis, route)
+
+
+def partner(z, k, outer):
+    return z ^ k if outer & (outer - 1) == 0 else (z + k) % outer
+
+
+def origin(z, k, outer):
+    return z ^ k if outer & (outer - 1) == 0 else (z + outer - k) % outer
 
 
 def in_squares():
@@ -84,7 +92,7 @@
     tail = weight_rows(weight_ref[0], 0, width) + got_ref[half:, :].astype(jnp.float32)
     tail = tail.astype(got_ref.dtype)
     for k, out_ref in enumerate(out_refs, 1):
-        at = (z + k) % outer * share
+        at = partner(z, k, outer) * share
         mine = pl.ds(pl.multiple_of(x * half + at, share), share)
         out_ref[:share, :] = block_ref[mine, :]
         out_ref[share:2 * share, :] = got_ref[pl.ds(pl.multiple_of(at, share), share), :]
@@ -119,7 +127,7 @@
         total(got_ref[half:, :].astype(jnp.float32), 3),
     )
     for k, ref in enumerate(received, 1):
-        behind = (z + outer - k) % outer * 2
+        behind = origin(z, k, outer) * 2
         tail = ref[2 * share:, :].astype(jnp.float32)
         place(behind + x, ref[:share, :], total(tail, 0))
         place(behind + 1 - x, ref[share:2 * share, :], total(tail, 3))
@@ -159,8 +167,8 @@
         name="arrange",
     )(weight, green, got)
     received = [None] * (outer - 1)
-    for k in range(outer - 1, 0, -1):
-        route = [(z * 2 + x, (z + k) % outer * 2 + x) for z in range(outer) for x in range(2)]
+    for k in range(1, outer):
+        route = [(z * 2 + x, partner(z, k, outer) * 2 + x) for z in range(outer) for x in range(2)]
         received[k - 1] = lax.ppermute(shares[k - 1], "energy", route)
 
     def kernel(*refs):
@@ -210,11 +218,11 @@
         lax.dynamic_update_index_in_dim(jnp.zeros((outer,) + part.shape, part.dtype), part, here, 0)
         for part in chunk
     ]
-    for k in range(outer - 1, 0, -1):
-        route = [(z * 2 + x, (z + k) % outer * 2 + x) for z in range(outer) for x in range(2)]
+    for k in range(1, outer):
+        route = [(z * 2 + x, partner(z, k, outer) * 2 + x) for z in range(outer) for x in range(2)]
         got = lax.ppermute(chunk, "energy", route)
         wholes = [
-            lax.dynamic_update_index_in_dim(whole, part, (here - k) % outer, 0)
+            lax.dynamic_update_index_in_dim(whole, part, origin(here, k, outer), 0)
             for whole, part in zip(wholes, got)
         ]
     return wholes

time: 60.2 us -> 61 us (1.013)
  starting transfers between devices: 18.3 us -> 22.6 us
  waiting for transfers between devices: 29.2 us -> 25.9 us
    ppermute x3, starting transfers between devices: 2.28 us -> 4.45 us  [gather_energy(): got = lax.ppermute(chunk, 'energy', route)]
    ppermute x3, starting transfers between devices: 2.41 us -> 4.45 us  [polar_share(): received[k - 1] = lax.ppermute(shares[k - 1], 'energy', route)]
    ppermute x3, waiting for transfers between devices: 3.85 us -> 2.05 us  [polar_share(): received[k - 1] = lax.ppermute(shares[k - 1], 'energy', route)]
    ppermute x3, waiting for transfers between devices: 7.26 us -> 5.69 us  [gather_energy(): got = lax.ppermute(chunk, 'energy', route)]
  transfers between devices with their start and end apart: 18 -> 18, of which waited for: 9 -> 10; matrix products, arithmetic and copies ran while one was open for 0% -> 0% of each run, Pallas kernels for 5% -> 5%
where the time goes in v14:
time: 61 us; the launch traced here: 60.8 us
  waiting for transfers between devices  25.9 us (42%)
  starting transfers between devices  22.6 us (37%)
  Pallas kernels  8.97 us (15%)
  between operations  2.97 us (5%)
    ppermute x3, waiting for transfers between devices, gather_energy(): got = lax.ppermute(chunk, 'energy', route)  5.69 us
    ppermute x1, waiting for transfers between devices, body(): lax.ppermute(packed.astype(coded), 'rep', [(0, 1), (1, 0)])  5.21 us
    ppermute x1, waiting for transfers between devices, polar_share(): got = lax.ppermute(sent, 'energy', [(e, e ^ 1) for e in range(energies)])  4.88 us
    ppermute x3, waiting for transfers between devices, along_x(): return lax.ppermute(part, 'energy', [(e, e ^ 1) for e in range(energies)])  4.55 us
    ppermute x3, starting transfers between devices, polar_share(): received[k - 1] = lax.ppermute(shares[k - 1], 'energy', route)  4.45 us
    ppermute x3, starting transfers between devices, gather_energy(): got = lax.ppermute(chunk, 'energy', route)  4.45 us
    ppermute x3, starting transfers between devices, along_x(): return lax.ppermute(part, 'energy', [(e, e ^ 1) for e in range(energies)])  4.06 us
    ppermute x3, starting transfers between devices, shifted(): return lax.ppermute(block, axis, route)  3.85 us
  transfers between devices with their start and end apart: 18, of which 10 were waited for; matrix products, arithmetic and copies ran while one was open for 0% of the time, Pallas kernels for 5%

profile of v14, /device:TPU:26, one launch (start us, length us, event | category | flops | bytes accessed | tf_op | source)
XLA Modules:
  0.0 60.8 jit_solution(11934389307008825188)
XLA Ops:
  0.6 0.0 copy-start.1
  0.6 0.0 copy-start
  1.4 0.9 %prepare.1 = bf16[136,512]{1,0:T(8,128)(2,1)S(1)} custom-call(f32[1]{0:T(128)S(6)} %copy.19.weight_ref.refs_3_, bf16[256,512]{1,0:T(8,128)(2,1)} %bitcast.10), custom_call_target="tpu_custom_call" | custom-call | tf_op jit(solution)/shard_map/prepare/pallas_call | solution.py:151
  2.3 0.6 collective-permute-start
  2.9 4.9 %collective-permute-done.got_ref.refs_9_ = bf16[136,512]{1,0:T(8,128)(2,1)S(1)} collective-permute-done((bf16[136,512]{1,0:T(8,128)(2,1)S(1)}, bf16[136,512]{1,0:T(8,128)(2,1)S(1)}, u32[]{:S(2)}, u32[]{:S(2)}) %collective-permute-start) | collective-permute-done | bytes 139296 | tf_op jit(solution)/shard_map/ppermute | solution.py:160
  7.8 0.0 copy-done.1
  7.8 0.5 collective-permute-start.1
  8.3 0.3 collective-permute-start.2
  8.7 3.6 %collective-permute-start.3 = (bf16[72,512]{1,0:T(8,128)(2,1)S(1)}, bf16[72,512]{1,0:T(8,128)(2,1)S(1)}, u32[]{:S(2)}, u32[]{:S(2)}) collective-permute-start(bf16[72,512]{1,0:T(8,128)(2,1)S(1)} %get-tuple-element.17), channel_id=1, source_target_pairs={{0,24},{4,28},{8,16},{12,20},{16,8},{20,12},{24,0},{28,4},{1,25},{... | collective-permute-start | bytes 221192 | tf_op jit(solution)/shard_map/ppermute | solution.py:172
  12.3 1.3 %collective-permute-start.13 = (bf16[256,512]{1,0:T(8,128)(2,1)S(1)}, bf16[256,512]{1,0:T(8,128)(2,1)S(1)}, u32[]{:S(2)}, u32[]{:S(2)}) collective-permute-start(bf16[256,512]{1,0:T(8,128)(2,1)S(1)} %bitcast.12), channel_id=1, source_target_pairs={{0,8},{4,12},{8,16},{12,20},{16,24},{20,28},{1,9},{5,13},{9,17},{1... | collective-permute-start | bytes 786440 | tf_op jit(solution)/shard_map/ppermute | solution.py:44
  14.9 0.0 copy-start.2
  14.9 0.0 copy-start.3
  14.9 0.0 collective-permute-done.1.refs_0_
  14.9 1.5 %collective-permute-done.2.refs_1_ = bf16[72,512]{1,0:T(8,128)(2,1)S(1)} collective-permute-done((bf16[72,512]{1,0:T(8,128)(2,1)S(1)}, bf16[72,512]{1,0:T(8,128)(2,1)S(1)}, u32[]{:S(2)}, u32[]{:S(2)}) %collective-permute-start.2) | collective-permute-done | bytes 73760 | tf_op jit(solution)/shard_map/ppermute | solution.py:172
  16.4 0.6 collective-permute-done.3.refs_2_
  17.0 0.0 copy-done
  17.0 0.0 copy-done.2
  17.0 0.0 copy-done.3
  17.0 0.8 %polar.1 = f32[2,32,512]{2,1,0:T(8,128)S(1)} custom-call(bf16[72,512]{1,0:T(8,128)(2,1)S(1)} %collective-permute-done.1.refs_0_, bf16[72,512]{1,0:T(8,128)(2,1)S(1)} %collective-permute-done.2.refs_1_, bf16[72,512]{1,0:T(8,128)(2,1)S(1)} %collective-permute-done.3.refs_2_, f32[1]{0:T(128)S(6)} %copy.19.weight_ref.refs_3_, s32[2]{0:T(128)S(1)} %copy-done.2, ...), custom_call_target="tpu_custom_call" | custom-call | tf_op jit(solution)/shard_map/polar/pallas_call | solution.py:178
  17.8 1.5 %collective-permute-start.6 = (f16[2,32,512]{2,1,0:T(8,128)(2,1)S(1)}, f16[2,32,512]{2,1,0:T(8,128)(2,1)S(1)}, u32[]{:S(2)}, u32[]{:S(2)}) collective-permute-start(f16[2,32,512]{2,1,0:T(8,128)(2,1)S(1)} %convert_element_type.33), channel_id=1, source_target_pairs={{0,24},{4,28},{8,16},{12,20},{16,8},{20,12},{24,0},{28,4},{1,25},{... | collective-permute-start | bytes 196616 | tf_op jit(solution)/shard_map/ppermute | solution.py:223
  19.4 1.9 %collective-permute-start.5 = (f16[2,32,512]{2,1,0:T(8,128)(2,1)S(1)}, f16[2,32,512]{2,1,0:T(8,128)(2,1)S(1)}, u32[]{:S(2)}, u32[]{:S(2)}) collective-permute-start(f16[2,32,512]{2,1,0:T(8,128)(2,1)S(1)} %convert_element_type.33), channel_id=1, source_target_pairs={{0,16},{4,20},{8,24},{12,28},{16,0},{20,4},{24,8},{28,12},{1,17},{... | collective-permute-start | bytes 196616 | tf_op jit(solution)/shard_map/ppermute | solution.py:223
  21.2 1.1 %collective-permute-start.4 = (f16[2,32,512]{2,1,0:T(8,128)(2,1)S(1)}, f16[2,32,512]{2,1,0:T(8,128)(2,1)S(1)}, u32[]{:S(2)}, u32[]{:S(2)}) collective-permute-start(f16[2,32,512]{2,1,0:T(8,128)(2,1)S(1)} %convert_element_type.33), channel_id=1, source_target_pairs={{0,8},{4,12},{8,0},{12,4},{16,24},{20,28},{24,16},{28,20},{1,9},{5... | collective-permute-start | bytes 196616 | tf_op jit(solution)/shard_map/ppermute | solution.py:223
  22.4 3.4 %collective-permute-done.4 = f16[2,32,512]{2,1,0:T(8,128)(2,1)S(1)} collective-permute-done((f16[2,32,512]{2,1,0:T(8,128)(2,1)S(1)}, f16[2,32,512]{2,1,0:T(8,128)(2,1)S(1)}, u32[]{:S(2)}, u32[]{:S(2)}) %collective-permute-start.4) | collective-permute-done | bytes 65568 | tf_op jit(solution)/shard_map/ppermute | solution.py:223
  25.8 2.3 %collective-permute-done.5 = f16[2,32,512]{2,1,0:T(8,128)(2,1)S(1)} collective-permute-done((f16[2,32,512]{2,1,0:T(8,128)(2,1)S(1)}, f16[2,32,512]{2,1,0:T(8,128)(2,1)S(1)}, u32[]{:S(2)}, u32[]{:S(2)}) %collective-permute-start.5) | collective-permute-done | bytes 65568 | tf_op jit(solution)/shard_map/ppermute | solution.py:223
  28.1 0.0 collective-permute-done.6
  28.1 0.6 collective-permute-start.11
  28.7 1.5 %collective-permute-start.9 = (f16[4,32,512]{2,1,0:T(8,128)(2,1)S(1)}, f16[4,32,512]{2,1,0:T(8,128)(2,1)S(1)}, u32[]{:S(2)}, u32[]{:S(2)}) collective-permute-start(f16[4,32,512]{2,1,0:T(8,128)(2,1)S(1)} %get-tuple-element.30), channel_id=1, source_target_pairs={{0,1},{1,0},{2,3},{3,2},{4,5},{5,4},{6,7},{7,6},{8,9},{9,8},{10,11... | collective-permute-start | bytes 393224 | tf_op jit(solution)/shard_map/ppermute | solution.py:238
  30.3 0.0 collective-permute-start.16
  30.3 0.5 collective-permute-start.12
  30.8 0.0 collective-permute-done.13.two_ref.refs_10_
  30.8 1.5 %collective-permute-start.7 = (f16[4,32,512]{2,1,0:T(8,128)(2,1)S(1)}, f16[4,32,512]{2,1,0:T(8,128)(2,1)S(1)}, u32[]{:S(2)}, u32[]{:S(2)}) collective-permute-start(f16[4,32,512]{2,1,0:T(8,128)(2,1)S(1)} %get-tuple-element.31), channel_id=1, source_target_pairs={{0,4},{4,0},{8,12},{12,8},{16,20},{20,16},{24,28},{28,24},{1,5},{5... | collective-permute-start | bytes 393224 | tf_op jit(solution)/shard_map/ppermute | solution.py:235
  32.3 0.6 chosen.1
  32.8 0.3 collective-permute-done.11
  33.2 1.3 %collective-permute-start.15 = (bf16[256,512]{1,0:T(8,128)(2,1)S(1)}, bf16[256,512]{1,0:T(8,128)(2,1)S(1)}, u32[]{:S(2)}, u32[]{:S(2)}) collective-permute-start(bf16[256,512]{1,0:T(8,128)(2,1)S(1)} %chosen.1), channel_id=1, source_target_pairs={{0,4},{4,8},{8,12},{12,16},{16,20},{20,24},{24,28},{1,5},{5,9},{9,... | collective-permute-start | bytes 786440 | tf_op jit(solution)/shard_map/ppermute | solution.py:44
  34.5 0.0 collective-permute-done.9
  34.5 1.3 %collective-permute-start.14 = (bf16[256,512]{1,0:T(8,128)(2,1)S(1)}, bf16[256,512]{1,0:T(8,128)(2,1)S(1)}, u32[]{:S(2)}, u32[]{:S(2)}) collective-permute-start(bf16[256,512]{1,0:T(8,128)(2,1)S(1)} %collective-permute-done.13.two_ref.refs_10_), channel_id=1, source_target_pairs={{0,8},{4,12},{8,16},{12,20},{16,24},{20,28},{1,9},{5,13},{9,17},{1... | collective-permute-start | bytes 786440 | tf_op jit(solution)/shard_map/ppermute | solution.py:44
  35.8 0.7 %collective-permute-done.12 = f16[4,32,512]{2,1,0:T(8,128)(2,1)S(1)} collective-permute-done((f16[4,32,512]{2,1,0:T(8,128)(2,1)S(1)}, f16[4,32,512]{2,1,0:T(8,128)(2,1)S(1)}, u32[]{:S(2)}, u32[]{:S(2)}) %collective-permute-start.12) | collective-permute-done | bytes 131104 | tf_op jit(solution)/shard_map/ppermute | solution.py:238
  36.5 2.0 %collective-permute-start.10 = (f16[4,32,512]{2,1,0:T(8,128)(2,1)S(1)}, f16[4,32,512]{2,1,0:T(8,128)(2,1)S(1)}, u32[]{:S(2)}, u32[]{:S(2)}) collective-permute-start(f16[4,32,512]{2,1,0:T(8,128)(2,1)S(1)} %collective-permute-done.9), channel_id=1, source_target_pairs={{0,4},{4,0},{8,12},{12,8},{16,20},{20,16},{24,28},{28,24},{1,5},{5... | collective-permute-start | bytes 393224 | tf_op jit(solution)/shard_map/ppermute | solution.py:235
  38.5 0.0 collective-permute-done.7
  38.5 1.5 %collective-permute-start.8 = (f16[4,32,512]{2,1,0:T(8,128)(2,1)S(1)}, f16[4,32,512]{2,1,0:T(8,128)(2,1)S(1)}, u32[]{:S(2)}, u32[]{:S(2)}) collective-permute-start(f16[4,32,512]{2,1,0:T(8,128)(2,1)S(1)} %collective-permute-done.7), channel_id=1, source_target_pairs={{0,1},{1,0},{2,3},{3,2},{4,5},{5,4},{6,7},{7,6},{8,9},{9,8},{10,11... | collective-permute-start | bytes 393224 | tf_op jit(solution)/shard_map/ppermute | solution.py:238
  40.2 1.3 %early.1 = (f32[2,256,512]{2,1,0:T(8,128)S(1)}, bf16[2,512,512]{2,1,0:T(8,128)(2,1)S(1)}, bf16[2,512,512]{2,1,0:T(8,128)(2,1)S(1)}) custom-call(f32[4,32,512]{2,1,0:T(8,128)S(1)} %convert_element_type.36.refs_0_, f32[4,32,512]{2,1,0:T(8,128)S(1)} %convert_element_type.37.refs_1_, f32[4,32,512]{2,1,0:T(8,128)S(1)} %convert_element_type.38.refs_2_, ...), custom_call_target="tpu_custom_call" | custom-call | tf_op jit(solution)/shard_map/early/pallas_call | solution.py:370
  41.5 4.2 %collective-permute-done.10 = f16[4,32,512]{2,1,0:T(8,128)(2,1)S(1)} collective-permute-done((f16[4,32,512]{2,1,0:T(8,128)(2,1)S(1)}, f16[4,32,512]{2,1,0:T(8,128)(2,1)S(1)}, u32[]{:S(2)}, u32[]{:S(2)}) %collective-permute-start.10) | collective-permute-done | bytes 131104 | tf_op jit(solution)/shard_map/ppermute | solution.py:235
  45.7 0.0 collective-permute-done.8
  45.8 0.0 collective-permute-done.16.refs_13_
  45.8 0.0 collective-permute-done.15.refs_12_
  45.8 2.7 %collective-permute-done.14.refs_11_ = bf16[256,512]{1,0:T(8,128)(2,1)S(1)} collective-permute-done((bf16[256,512]{1,0:T(8,128)(2,1)S(1)}, bf16[256,512]{1,0:T(8,128)(2,1)S(1)}, u32[]{:S(2)}, u32[]{:S(2)}) %collective-permute-start.14) | collective-permute-done | bytes 262176 | tf_op jit(solution)/shard_map/ppermute | solution.py:44
  48.5 3.2 %dyson.1 = (bf16[2,256,512]{2,1,0:T(8,128)(2,1)}, f32[264,512]{1,0:T(8,128)S(1)}, f32[256,512]{1,0:T(8,128)S(1)}, f32[8,512]{1,0:T(8,128)S(1)}) custom-call(f32[4,32,512]{2,1,0:T(8,128)S(1)} %convert_element_type.34.refs_0_, f32[4,32,512]{2,1,0:T(8,128)S(1)} %convert_element_type.35.refs_1_, f32[2,256,512]{2,1,0:T(8,128)S(1)} %get-tuple-element.18.refs_2_, ...), custom_call_target="tpu_custom_call" | custom-call | tf_op jit(solution)/shard_map/dyson/pallas_call | solution.py:386
  51.7 1.6 %collective-permute-start.17 = (f16[264,512]{1,0:T(8,128)(2,1)S(1)}, f16[264,512]{1,0:T(8,128)(2,1)S(1)}, u32[]{:S(2)}, u32[]{:S(2)}) collective-permute-start(f16[264,512]{1,0:T(8,128)(2,1)S(1)} %convert_element_type.42), channel_id=1, source_target_pairs={{0,1},{1,0},{2,3},{3,2},{4,5},{5,4},{6,7},{7,6},{8,9},{9,8},{10,11... | collective-permute-start | bytes 811016 | tf_op jit(solution)/shard_map/ppermute | solution.py:475
  53.3 0.4 begin.1
  53.8 5.2 %collective-permute-done.17 = f16[264,512]{1,0:T(8,128)(2,1)S(1)} collective-permute-done((f16[264,512]{1,0:T(8,128)(2,1)S(1)}, f16[264,512]{1,0:T(8,128)(2,1)S(1)}, u32[]{:S(2)}, u32[]{:S(2)}) %collective-permute-start.17) | collective-permute-done | bytes 270368 | tf_op jit(solution)/shard_map/ppermute | solution.py:475
  59.0 0.1 convert_element_type.43.theirs_ref
  59.0 1.7 %finish.1 = f32[256,512]{1,0:T(8,128)} custom-call(s32[1]{0:T(128)S(6)} %copy.21.refs_6_.steps_ref, f32[256,512]{1,0:T(8,128)S(1)} %get-tuple-element.21.step_ref, f32[256,512]{1,0:T(8,128)S(1)} %get-tuple-element.24.square_ref, bf16[256,512]{1,0:T(8,128)(2,1)S(1)} %get-tuple-element.25.high_ref, bf16[256,512]{1,0:T(8,128)(2,1)S(1)} %get-tuple-element.26.low_ref, ...), custom_call_target="tpu_custom_call" | custom-call | tf_op jit(solution)/shard_map/finish/pallas_call | solution.py:486
  (18 shorter events, 0.4 us)
Async XLA Ops:
  0.6 7.2 %copy-start.1 = (bf16[1,1,256,512]{3,2,1,0:T(8,128)(2,1)S(1)}, bf16[1,1,256,512]{3,2,1,0:T(8,128)(2,1)}, u32[]{:S(2)}) copy-start(bf16[1,1,256,512]{3,2,1,0:T(8,128)(2,1)} %param.8) | copy-start | bytes 786436
  0.6 16.3 %copy-start = (f32[1,256,512]{2,1,0:T(8,128)S(1)}, f32[1,256,512]{2,1,0:T(8,128)}, u32[]{:S(2)}) copy-start(f32[1,256,512]{2,1,0:T(8,128)} %param.11) | copy-start | bytes 1572868
  2.3 5.5 %collective-permute-start = (bf16[136,512]{1,0:T(8,128)(2,1)S(1)}, bf16[136,512]{1,0:T(8,128)(2,1)S(1)}, u32[]{:S(2)}, u32[]{:S(2)}) collective-permute-start(bf16[136,512]{1,0:T(8,128)(2,1)S(1)} %prepare.1), channel_id=1, source_target_pairs={{0,4},{4,0},{8,12},{12,8},{16,20},{20,16},{24,28},{28,24},{1,5},{5... | collective-permute-start | bytes 417800 | tf_op jit(solution)/shard_map/ppermute | solution.py:160
  7.8 7.1 %collective-permute-start.1 = (bf16[72,512]{1,0:T(8,128)(2,1)S(1)}, bf16[72,512]{1,0:T(8,128)(2,1)S(1)}, u32[]{:S(2)}, u32[]{:S(2)}) collective-permute-start(bf16[72,512]{1,0:T(8,128)(2,1)S(1)} %get-tuple-element.15), channel_id=1, source_target_pairs={{0,8},{4,12},{8,0},{12,4},{16,24},{20,28},{24,16},{28,20},{1,9},{5... | collective-permute-start | bytes 221192 | tf_op jit(solution)/shard_map/ppermute | solution.py:172
  8.3 8.1 %collective-permute-start.2 = (bf16[72,512]{1,0:T(8,128)(2,1)S(1)}, bf16[72,512]{1,0:T(8,128)(2,1)S(1)}, u32[]{:S(2)}, u32[]{:S(2)}) collective-permute-start(bf16[72,512]{1,0:T(8,128)(2,1)S(1)} %get-tuple-element.16), channel_id=1, source_target_pairs={{0,16},{4,20},{8,24},{12,28},{16,0},{20,4},{24,8},{28,12},{1,17},{... | collective-permute-start | bytes 221192 | tf_op jit(solution)/shard_map/ppermute | solution.py:172
  8.7 8.3 %collective-permute-start.3 = (bf16[72,512]{1,0:T(8,128)(2,1)S(1)}, bf16[72,512]{1,0:T(8,128)(2,1)S(1)}, u32[]{:S(2)}, u32[]{:S(2)}) collective-permute-start(bf16[72,512]{1,0:T(8,128)(2,1)S(1)} %get-tuple-element.17), channel_id=1, source_target_pairs={{0,24},{4,28},{8,16},{12,20},{16,8},{20,12},{24,0},{28,4},{1,25},{... | collective-permute-start | bytes 221192 | tf_op jit(solution)/shard_map/ppermute | solution.py:172
  12.3 18.5 %collective-permute-start.13 = (bf16[256,512]{1,0:T(8,128)(2,1)S(1)}, bf16[256,512]{1,0:T(8,128)(2,1)S(1)}, u32[]{:S(2)}, u32[]{:S(2)}) collective-permute-start(bf16[256,512]{1,0:T(8,128)(2,1)S(1)} %bitcast.12), channel_id=1, source_target_pairs={{0,8},{4,12},{8,16},{12,20},{16,24},{20,28},{1,9},{5,13},{9,17},{1... | collective-permute-start | bytes 786440 | tf_op jit(solution)/shard_map/ppermute | solution.py:44
  14.9 2.1 %copy-start.2 = (s32[2]{0:T(128)S(1)}, s32[2]{0:T(128)}, u32[]{:S(2)}) copy-start(s32[2]{0:T(128)} %refs_5_.3) | copy-start | bytes 28
  14.9 2.1 %copy-start.3 = (s32[2]{0:T(128)S(1)}, s32[2]{0:T(128)}, u32[]{:S(2)}) copy-start(s32[2]{0:T(128)} %refs_6_.2) | copy-start | bytes 28
  17.8 10.3 %collective-permute-start.6 = (f16[2,32,512]{2,1,0:T(8,128)(2,1)S(1)}, f16[2,32,512]{2,1,0:T(8,128)(2,1)S(1)}, u32[]{:S(2)}, u32[]{:S(2)}) collective-permute-start(f16[2,32,512]{2,1,0:T(8,128)(2,1)S(1)} %convert_element_type.33), channel_id=1, source_target_pairs={{0,24},{4,28},{8,16},{12,20},{16,8},{20,12},{24,0},{28,4},{1,25},{... | collective-permute-start | bytes 196616 | tf_op jit(solution)/shard_map/ppermute | solution.py:223
  19.4 8.7 %collective-permute-start.5 = (f16[2,32,512]{2,1,0:T(8,128)(2,1)S(1)}, f16[2,32,512]{2,1,0:T(8,128)(2,1)S(1)}, u32[]{:S(2)}, u32[]{:S(2)}) collective-permute-start(f16[2,32,512]{2,1,0:T(8,128)(2,1)S(1)} %convert_element_type.33), channel_id=1, source_target_pairs={{0,16},{4,20},{8,24},{12,28},{16,0},{20,4},{24,8},{28,12},{1,17},{... | collective-permute-start | bytes 196616 | tf_op jit(solution)/shard_map/ppermute | solution.py:223
  21.2 4.5 %collective-permute-start.4 = (f16[2,32,512]{2,1,0:T(8,128)(2,1)S(1)}, f16[2,32,512]{2,1,0:T(8,128)(2,1)S(1)}, u32[]{:S(2)}, u32[]{:S(2)}) collective-permute-start(f16[2,32,512]{2,1,0:T(8,128)(2,1)S(1)} %convert_element_type.33), channel_id=1, source_target_pairs={{0,8},{4,12},{8,0},{12,4},{16,24},{20,28},{24,16},{28,20},{1,9},{5... | collective-permute-start | bytes 196616 | tf_op jit(solution)/shard_map/ppermute | solution.py:223
  28.1 5.0 %collective-permute-start.11 = (f16[4,32,512]{2,1,0:T(8,128)(2,1)S(1)}, f16[4,32,512]{2,1,0:T(8,128)(2,1)S(1)}, u32[]{:S(2)}, u32[]{:S(2)}) collective-permute-start(f16[4,32,512]{2,1,0:T(8,128)(2,1)S(1)} %get-tuple-element.30), channel_id=1, source_target_pairs={{0,4},{4,0},{8,12},{12,8},{16,20},{20,16},{24,28},{28,24},{1,5},{5... | collective-permute-start | bytes 393224 | tf_op jit(solution)/shard_map/ppermute | solution.py:235
  28.7 5.7 %collective-permute-start.9 = (f16[4,32,512]{2,1,0:T(8,128)(2,1)S(1)}, f16[4,32,512]{2,1,0:T(8,128)(2,1)S(1)}, u32[]{:S(2)}, u32[]{:S(2)}) collective-permute-start(f16[4,32,512]{2,1,0:T(8,128)(2,1)S(1)} %get-tuple-element.30), channel_id=1, source_target_pairs={{0,1},{1,0},{2,3},{3,2},{4,5},{5,4},{6,7},{7,6},{8,9},{9,8},{10,11... | collective-permute-start | bytes 393224 | tf_op jit(solution)/shard_map/ppermute | solution.py:238
  30.3 15.5 %collective-permute-start.16 = (bf16[256,512]{1,0:T(8,128)(2,1)S(1)}, bf16[256,512]{1,0:T(8,128)(2,1)S(1)}, u32[]{:S(2)}, u32[]{:S(2)}) collective-permute-start(bf16[256,512]{1,0:T(8,128)(2,1)S(1)} %bitcast.14), channel_id=1, source_target_pairs={{0,2},{2,0},{1,3},{3,1},{4,6},{6,4},{5,7},{7,5},{8,10},{10,8},{9,1... | collective-permute-start | bytes 786440 | tf_op jit(solution)/shard_map/ppermute | solution.py:466
  30.3 6.3 %collective-permute-start.12 = (f16[4,32,512]{2,1,0:T(8,128)(2,1)S(1)}, f16[4,32,512]{2,1,0:T(8,128)(2,1)S(1)}, u32[]{:S(2)}, u32[]{:S(2)}) collective-permute-start(f16[4,32,512]{2,1,0:T(8,128)(2,1)S(1)} %get-tuple-element.31), channel_id=1, source_target_pairs={{0,1},{1,0},{2,3},{3,2},{4,5},{5,4},{6,7},{7,6},{8,9},{9,8},{10,11... | collective-permute-start | bytes 393224 | tf_op jit(solution)/shard_map/ppermute | solution.py:238
  30.8 7.7 %collective-permute-start.7 = (f16[4,32,512]{2,1,0:T(8,128)(2,1)S(1)}, f16[4,32,512]{2,1,0:T(8,128)(2,1)S(1)}, u32[]{:S(2)}, u32[]{:S(2)}) collective-permute-start(f16[4,32,512]{2,1,0:T(8,128)(2,1)S(1)} %get-tuple-element.31), channel_id=1, source_target_pairs={{0,4},{4,0},{8,12},{12,8},{16,20},{20,16},{24,28},{28,24},{1,5},{5... | collective-permute-start | bytes 393224 | tf_op jit(solution)/shard_map/ppermute | solution.py:235
  33.2 12.6 %collective-permute-start.15 = (bf16[256,512]{1,0:T(8,128)(2,1)S(1)}, bf16[256,512]{1,0:T(8,128)(2,1)S(1)}, u32[]{:S(2)}, u32[]{:S(2)}) collective-permute-start(bf16[256,512]{1,0:T(8,128)(2,1)S(1)} %chosen.1), channel_id=1, source_target_pairs={{0,4},{4,8},{8,12},{12,16},{16,20},{20,24},{24,28},{1,5},{5,9},{9,... | collective-permute-start | bytes 786440 | tf_op jit(solution)/shard_map/ppermute | solution.py:44
  34.5 14.1 %collective-permute-start.14 = (bf16[256,512]{1,0:T(8,128)(2,1)S(1)}, bf16[256,512]{1,0:T(8,128)(2,1)S(1)}, u32[]{:S(2)}, u32[]{:S(2)}) collective-permute-start(bf16[256,512]{1,0:T(8,128)(2,1)S(1)} %collective-permute-done.13.two_ref.refs_10_), channel_id=1, source_target_pairs={{0,8},{4,12},{8,16},{12,20},{16,24},{20,28},{1,9},{5,13},{9,17},{1... | collective-permute-start | bytes 786440 | tf_op jit(solution)/shard_map/ppermute | solution.py:44
  36.5 9.2 %collective-permute-start.10 = (f16[4,32,512]{2,1,0:T(8,128)(2,1)S(1)}, f16[4,32,512]{2,1,0:T(8,128)(2,1)S(1)}, u32[]{:S(2)}, u32[]{:S(2)}) collective-permute-start(f16[4,32,512]{2,1,0:T(8,128)(2,1)S(1)} %collective-permute-done.9), channel_id=1, source_target_pairs={{0,4},{4,0},{8,12},{12,8},{16,20},{20,16},{24,28},{28,24},{1,5},{5... | collective-permute-start | bytes 393224 | tf_op jit(solution)/shard_map/ppermute | solution.py:235
  38.5 7.2 %collective-permute-start.8 = (f16[4,32,512]{2,1,0:T(8,128)(2,1)S(1)}, f16[4,32,512]{2,1,0:T(8,128)(2,1)S(1)}, u32[]{:S(2)}, u32[]{:S(2)}) collective-permute-start(f16[4,32,512]{2,1,0:T(8,128)(2,1)S(1)} %collective-permute-done.7), channel_id=1, source_target_pairs={{0,1},{1,0},{2,3},{3,2},{4,5},{5,4},{6,7},{7,6},{8,9},{9,8},{10,11... | collective-permute-start | bytes 393224 | tf_op jit(solution)/shard_map/ppermute | solution.py:238
  51.7 7.2 %collective-permute-start.17 = (f16[264,512]{1,0:T(8,128)(2,1)S(1)}, f16[264,512]{1,0:T(8,128)(2,1)S(1)}, u32[]{:S(2)}, u32[]{:S(2)}) collective-permute-start(f16[264,512]{1,0:T(8,128)(2,1)S(1)} %convert_element_type.42), channel_id=1, source_target_pairs={{0,1},{1,0},{2,3},{3,2},{4,5},{5,4},{6,7},{7,6},{8,9},{9,8},{10,11... | collective-permute-start | bytes 811016 | tf_op jit(solution)/shard_map/ppermute | solution.py:475

commit v15 on v14

--- a/solution.py
+++ b/solution.py
@@ -54,7 +54,7 @@
 
 def in_squares():
     energies = lax.axis_size("energy")
-    return energies % 2 == 0 and energies <= 16 and lax.axis_size("rep") == 2
+    return energies % 2 == 0 and energies <= 10 and lax.axis_size("rep") == 2
 
 
 def share_of(place):
@@ -62,41 +62,58 @@
     return place % 2 * outer + place // 2 if in_squares() else place
 
 
-def weight_rows(weight, first_row, width):
-    weight = jnp.full((EXTRA, width), weight, jnp.float32)
+def weight_parts(weight):
     first = weight.astype(jnp.bfloat16).astype(jnp.float32)
     second = (weight - first).astype(jnp.bfloat16).astype(jnp.float32)
-    third = weight - first - second
-    row = lax.broadcasted_iota(jnp.int32, (EXTRA, width), 0) - first_row
-    later = jnp.where(row == 1, second, jnp.where(row == 2, third, 0.0))
-    return jnp.where(row == 0, first, later)
-
-
-def prepare_kernel(weight_ref, block_ref, out_ref, arrived):
-    half, width = out_ref.shape[0] - EXTRA, out_ref.shape[1]
-    x = lax.axis_index("energy") % 2
-    start = pl.multiple_of((1 - x) * half, half)
-    copy = pltpu.make_async_copy(
-        block_ref.at[pl.ds(start, half), :], out_ref.at[pl.ds(0, half), :], arrived
-    )
-    copy.start()
-    out_ref[half:, :] = weight_rows(weight_ref[0], 3, width).astype(out_ref.dtype)
-    copy.wait()
-
-
-def arrange_kernel(weight_ref, block_ref, got_ref, *out_refs):
+    return first, second, weight - first - second
+
+
+def in_rows(parts, first_row, rows, width):
+    row = lax.broadcasted_iota(jnp.int32, (rows, width), 0) - first_row
+    total = jnp.zeros((rows, width), jnp.float32)
+    for k, part in enumerate(parts):
+        total = total + jnp.where(row == k, part, 0.0)
+    return total
+
+
+def split_kernel(weight_ref, block_ref, *refs):
+    out_refs, arrived = refs[:-1], refs[-1]
     outer = len(out_refs) + 1
-    half, width = got_ref.shape[0] - EXTRA, got_ref.shape[1]
-    share = half // outer
+    tall, width = out_refs[0].shape
+    share = (tall - EXTRA) // 2
+    z = lax.axis_index("energy") // 2
+    copies = []
+    for k, out_ref in enumerate(out_refs, 1):
+        for x in range(2):
+            at = pl.multiple_of((x * outer + partner(z, k, outer)) * share, share)
+            copies.append(pltpu.make_async_copy(
+                block_ref.at[pl.ds(at, share), :], out_ref.at[pl.ds(x * share, share), :],
+                arrived.at[len(copies)],
+            ))
+            copies[-1].start()
+    weight = jnp.full((EXTRA, width), weight_ref[0], jnp.float32)
+    tail = in_rows(weight_parts(weight), 0, EXTRA, width).astype(out_refs[0].dtype)
+    for out_ref in out_refs:
+        out_ref[2 * share:, :] = tail
+    for copy in copies:
+        copy.wait()
+
+
+def collect_kernel(received, weight_ref, block_ref, out_ref):
+    outer = len(received) + 1
+    tall, width = out_ref.shape
+    share = (tall - 2 * EXTRA) // outer
     x, z = lax.axis_index("energy") % 2, lax.axis_index("energy") // 2
-    tail = weight_rows(weight_ref[0], 0, width) + got_ref[half:, :].astype(jnp.float32)
-    tail = tail.astype(got_ref.dtype)
-    for k, out_ref in enumerate(out_refs, 1):
-        at = partner(z, k, outer) * share
-        mine = pl.ds(pl.multiple_of(x * half + at, share), share)
-        out_ref[:share, :] = block_ref[mine, :]
-        out_ref[share:2 * share, :] = got_ref[pl.ds(pl.multiple_of(at, share), share), :]
-        out_ref[2 * share:, :] = tail
+    at = pl.multiple_of(((1 - x) * outer + z) * share, share)
+    out_ref[:share, :] = block_ref[pl.ds(at, share), :]
+    weight = jnp.full((1, width), weight_ref[0], jnp.float32)
+    tail = in_rows(weight_parts(weight), 0, 2 * EXTRA, width)
+    for k, ref in enumerate(received, 1):
+        at = pl.multiple_of((1 - x) * share, share)
+        out_ref[k * share:(k + 1) * share, :] = ref[pl.ds(at, share), :]
+        parts = ref[2 * share:, :].astype(jnp.float32)
+        tail = tail + in_rows([parts[i:i + 1] for i in range(3)], 3 * k, 2 * EXTRA, width)
+    out_ref[outer * share:, :] = tail.astype(out_ref.dtype)
 
 
 def polar_kernel(received, weight_ref, offsets_ref, block_ref, got_ref, bare_ref, out_ref,
@@ -104,10 +121,9 @@
     _, share, width = out_ref.shape
     energies = weighted.shape[0]
     outer = energies // 2
-    half = outer * share
     energy = lax.axis_index("energy")
     x, z = energy % 2, energy // 2
-    start = pl.multiple_of(x * half + z * share, share)
+    start = pl.multiple_of((x * outer + z) * share, share)
     copy = pltpu.make_async_copy(bare_ref.at[pl.ds(start, share), :], bare_rows, arrived)
     copy.start()
     padded[:SHIFTS] = jnp.zeros((SHIFTS, share, width), jnp.float32)
@@ -121,16 +137,13 @@
         return tail[row:row + 1] + tail[row + 1:row + 2] + tail[row + 2:row + 3]
 
     place(energy, block_ref[pl.ds(start, share), :], weight_ref[0])
-    place(
-        z * 2 + 1 - x,
-        got_ref[pl.ds(pl.multiple_of(z * share, share), share), :],
-        total(got_ref[half:, :].astype(jnp.float32), 3),
-    )
     for k, ref in enumerate(received, 1):
-        behind = origin(z, k, outer) * 2
-        tail = ref[2 * share:, :].astype(jnp.float32)
-        place(behind + x, ref[:share, :], total(tail, 0))
-        place(behind + 1 - x, ref[share:2 * share, :], total(tail, 3))
+        rows = ref[pl.ds(pl.multiple_of(x * share, share), share), :]
+        place(origin(z, k, outer) * 2 + x, rows, total(ref[2 * share:, :].astype(jnp.float32), 0))
+    tail = got_ref[outer * share:, :].astype(jnp.float32)
+    for k in range(outer):
+        rows = got_ref[k * share:(k + 1) * share, :]
+        place((origin(z, k, outer) if k else z) * 2 + 1 - x, rows, total(tail, 3 * k))
     totals = [jnp.zeros((share, width), jnp.float32) for _ in range(FREQS)]
     for e in range(energies):
         own = weighted[e]
@@ -147,38 +160,41 @@
     rows, width = green.shape
     outer = energies // 2
     share = rows // energies
-    half = rows // 2
-    sent = pl.pallas_call(
-        prepare_kernel,
-        out_shape=jax.ShapeDtypeStruct((half + EXTRA, width), green.dtype),
+    count = outer - 1
+    shares = pl.pallas_call(
+        split_kernel,
+        out_shape=(jax.ShapeDtypeStruct((2 * share + EXTRA, width), green.dtype),) * count,
         in_specs=[in_smem, in_hbm],
-        out_specs=in_vmem,
-        scratch_shapes=[pltpu.SemaphoreType.DMA],
+        out_specs=(in_vmem,) * count,
+        scratch_shapes=[pltpu.SemaphoreType.DMA((2 * count,))],
         compiler_params=small,
-        name="prepare",
+        name="split",
     )(weight, held(green))
-    got = lax.ppermute(sent, "energy", [(e, e ^ 1) for e in range(energies)])
-    shares = pl.pallas_call(
-        arrange_kernel,
-        out_shape=(jax.ShapeDtypeStruct((2 * share + EXTRA, width), green.dtype),) * (outer - 1),
-        in_specs=[in_smem, in_vmem, in_vmem],
-        out_specs=(in_vmem,) * (outer - 1),
-        compiler_params=small,
-        name="arrange",
-    )(weight, green, got)
-    received = [None] * (outer - 1)
-    for k in range(1, outer):
+    received = [None] * count
+    for k in range(count, 0, -1):
         route = [(z * 2 + x, partner(z, k, outer) * 2 + x) for z in range(outer) for x in range(2)]
         received[k - 1] = lax.ppermute(shares[k - 1], "energy", route)
 
+    def second_kernel(*refs):
+        collect_kernel(refs[:count], refs[count], *refs[count + 4:])
+
+    sent = pl.pallas_call(
+        second_kernel,
+        out_shape=jax.ShapeDtypeStruct((outer * share + 2 * EXTRA, width), green.dtype),
+        in_specs=[in_vmem] * count + [in_smem] * 4 + [in_vmem],
+        out_specs=in_vmem,
+        compiler_params=small,
+        name="collect",
+    )(*received, weight, *scalars, green)
+    got = lax.ppermute(sent, "energy", [(e, e ^ 1) for e in range(energies)])
+
     def kernel(*refs):
-        count = outer - 1
-        polar_kernel(refs[:count], *refs[count:count + 2], *refs[count + 5:])
+        polar_kernel(refs[:count], *refs[count:])
 
     return pl.pallas_call(
         kernel,
         out_shape=jax.ShapeDtypeStruct((FREQS, share, width), jnp.float32),
-        in_specs=[in_vmem] * (outer - 1) + [in_smem] * 5 + [in_vmem, in_vmem, in_place],
+        in_specs=[in_vmem] * count + [in_smem] * 2 + [in_vmem, in_vmem, in_place],
         out_specs=in_vmem,
         scratch_shapes=[
             VMEM((SHIFTS + energies, share, width), jnp.float32),
@@ -188,7 +204,7 @@
         ],
         compiler_params=small,
         name="polar",
-    )(*received, weight, offsets, *scalars, green, got, bare)
+    )(*received, weight, offsets, green, got, bare)
 
 
 def polar_share_plain(green, weight, offsets, bare, scalars):
@@ -218,7 +234,7 @@
         lax.dynamic_update_index_in_dim(jnp.zeros((outer,) + part.shape, part.dtype), part, here, 0)
         for part in chunk
     ]
-    for k in range(1, outer):
+    for k in range(outer - 1, 0, -1):
         route = [(z * 2 + x, partner(z, k, outer) * 2 + x) for z in range(outer) for x in range(2)]
         got = lax.ppermute(chunk, "energy", route)
         wholes = [

time: 61 us -> 62.9 us (1.031); the launches traced: 60.8 us -> 61.7 us
  local copies, waits for them, and re-layouts: 0.12 us -> 1.42 us
  starting transfers between devices: 22.6 us -> 21.6 us
    ppermute x1, waiting for transfers between devices: 4.88 us -> 3.27 us  [polar_share(): got = lax.ppermute(sent, 'energy', [(e, e ^ 1) for e in range(energies)])]
    ppermute x3, waiting for transfers between devices: 5.69 us -> 4.2 us  [gather_energy(): got = lax.ppermute(chunk, 'energy', route)]
    unnamed x8 -> x10, local copies, waits for them, and re-layouts: 0.02 us -> 1.32 us
    ppermute x3, waiting for transfers between devices: 2.05 us -> 3.33 us  [polar_share(): received[k - 1] = lax.ppermute(shares[k - 1], 'energy', route)]
    ppermute x3, waiting for transfers between devices: 0.75 us -> 1.73 us  [along_rep(): return lax.ppermute(part, 'rep', [(0, 1), (1, 0)])]
    ppermute x3, starting transfers between devices: 4.06 us -> 3.11 us  [along_x(): return lax.ppermute(part, 'energy', [(e, e ^ 1) for e in range(energies)])]
    ppermute x3, waiting for transfers between devices: 2.74 us -> 3.62 us  [shifted(): return lax.ppermute(block, axis, route)]
where the time goes in v15:
time: 62.9 us; the launch traced here: 61.7 us
  waiting for transfers between devices  26 us (41%)
  starting transfers between devices  21.6 us (34%)
  Pallas kernels  9.49 us (15%)
  between operations  2.96 us (5%)
  local copies, waits for them, and re-layouts  1.42 us (2%)
    ppermute x1, waiting for transfers between devices, body(): lax.ppermute(packed.astype(coded), 'rep', [(0, 1), (1, 0)])  5.21 us
    ppermute x3, waiting for transfers between devices, along_x(): return lax.ppermute(part, 'energy', [(e, e ^ 1) for e in range(energies)])  4.62 us
    ppermute x3, starting transfers between devices, gather_energy(): got = lax.ppermute(chunk, 'energy', route)  4.45 us
    ppermute x3, starting transfers between devices, polar_share(): received[k - 1] = lax.ppermute(shares[k - 1], 'energy', route)  4.45 us
    ppermute x3, waiting for transfers between devices, gather_energy(): got = lax.ppermute(chunk, 'energy', route)  4.2 us
    ppermute x3, starting transfers between devices, shifted(): return lax.ppermute(block, axis, route)  3.84 us
    ppermute x3, waiting for transfers between devices, shifted(): return lax.ppermute(block, axis, route)  3.62 us
    ppermute x3, starting transfers between devices, along_rep(): return lax.ppermute(part, 'rep', [(0, 1), (1, 0)])  3.55 us
  transfers between devices with their start and end apart: 18, of which 10 were waited for; matrix products, arithmetic and copies ran while one was open for 0% of the time, Pallas kernels for 5%

profile of v15, /device:TPU:26, one launch (start us, length us, event | category | flops | bytes accessed | tf_op | source)
XLA Modules:
  0.0 61.7 jit_solution(6833751486166622814)
XLA Ops:
  0.6 0.0 copy-start.1
  0.6 0.0 copy-start
  1.4 0.9 %split.1 = (bf16[72,512]{1,0:T(8,128)(2,1)S(1)}, bf16[72,512]{1,0:T(8,128)(2,1)S(1)}, bf16[72,512]{1,0:T(8,128)(2,1)S(1)}) custom-call(f32[1]{0:T(128)S(6)} %copy.19.weight_ref.refs_3_, bf16[256,512]{1,0:T(8,128)(2,1)} %bitcast.10), custom_call_target="tpu_custom_call" | custom-call | tf_op jit(solution)/shard_map/split/pallas_call | solution.py:164
  2.3 0.5 collective-permute-start
  2.8 0.3 collective-permute-start.1
  3.1 3.6 %collective-permute-start.2 = (bf16[72,512]{1,0:T(8,128)(2,1)S(1)}, bf16[72,512]{1,0:T(8,128)(2,1)S(1)}, u32[]{:S(2)}, u32[]{:S(2)}) collective-permute-start(bf16[72,512]{1,0:T(8,128)(2,1)S(1)} %get-tuple-element.17), channel_id=1, source_target_pairs={{0,24},{4,28},{8,16},{12,20},{16,8},{20,12},{24,0},{28,4},{1,25},{... | collective-permute-start | bytes 221192 | tf_op jit(solution)/shard_map/ppermute | solution.py:176
  8.0 0.0 collective-permute-done.refs_0_
  8.0 3.3 %collective-permute-done.1.refs_1_ = bf16[72,512]{1,0:T(8,128)(2,1)S(1)} collective-permute-done((bf16[72,512]{1,0:T(8,128)(2,1)S(1)}, bf16[72,512]{1,0:T(8,128)(2,1)S(1)}, u32[]{:S(2)}, u32[]{:S(2)}) %collective-permute-start.1) | collective-permute-done | bytes 73760 | tf_op jit(solution)/shard_map/ppermute | solution.py:176
  11.4 0.0 collective-permute-done.2.refs_2_
  11.4 0.0 copy-done.1
  11.4 0.0 copy-start.3
  11.4 0.7 %copy-done.3 = s32[2]{0:T(128)S(1)} copy-done((s32[2]{0:T(128)S(1)}, s32[2]{0:T(128)}, u32[]{:S(2)}) %copy-start.3) | copy-done | bytes 32
  12.0 0.6 collect.1
  12.6 0.6 collective-permute-start.3
  13.2 1.3 %collective-permute-start.13 = (bf16[256,512]{1,0:T(8,128)(2,1)S(1)}, bf16[256,512]{1,0:T(8,128)(2,1)S(1)}, u32[]{:S(2)}, u32[]{:S(2)}) collective-permute-start(bf16[256,512]{1,0:T(8,128)(2,1)S(1)} %bitcast.12), channel_id=1, source_target_pairs={{0,8},{4,12},{8,16},{12,20},{16,24},{20,28},{1,9},{5,13},{9,17},{1... | collective-permute-start | bytes 786440 | tf_op jit(solution)/shard_map/ppermute | solution.py:44
  14.5 0.0 copy-start.2
  14.6 3.3 %collective-permute-done.3.refs_6_ = bf16[144,512]{1,0:T(8,128)(2,1)S(1)} collective-permute-done((bf16[144,512]{1,0:T(8,128)(2,1)S(1)}, bf16[144,512]{1,0:T(8,128)(2,1)S(1)}, u32[]{:S(2)}, u32[]{:S(2)}) %collective-permute-start.3) | collective-permute-done | bytes 147488 | tf_op jit(solution)/shard_map/ppermute | solution.py:189
  17.8 0.0 copy-done
  17.8 0.0 copy-done.2
  17.8 0.8 %polar.1 = f32[2,32,512]{2,1,0:T(8,128)S(1)} custom-call(bf16[72,512]{1,0:T(8,128)(2,1)S(1)} %collective-permute-done.refs_0_, bf16[72,512]{1,0:T(8,128)(2,1)S(1)} %collective-permute-done.1.refs_1_, bf16[72,512]{1,0:T(8,128)(2,1)S(1)} %collective-permute-done.2.refs_2_, f32[1]{0:T(128)S(6)} %copy.19.weight_ref.refs_3_, s32[2]{0:T(128)S(1)} %copy-done.2, ...), custom_call_target="tpu_custom_call" | custom-call | tf_op jit(solution)/shard_map/polar/pallas_call | solution.py:194
  18.7 1.4 %collective-permute-start.6 = (f16[2,32,512]{2,1,0:T(8,128)(2,1)S(1)}, f16[2,32,512]{2,1,0:T(8,128)(2,1)S(1)}, u32[]{:S(2)}, u32[]{:S(2)}) collective-permute-start(f16[2,32,512]{2,1,0:T(8,128)(2,1)S(1)} %convert_element_type.33), channel_id=1, source_target_pairs={{0,8},{4,12},{8,0},{12,4},{16,24},{20,28},{24,16},{28,20},{1,9},{5... | collective-permute-start | bytes 196616 | tf_op jit(solution)/shard_map/ppermute | solution.py:239
  20.1 0.8 %collective-permute-start.5 = (f16[2,32,512]{2,1,0:T(8,128)(2,1)S(1)}, f16[2,32,512]{2,1,0:T(8,128)(2,1)S(1)}, u32[]{:S(2)}, u32[]{:S(2)}) collective-permute-start(f16[2,32,512]{2,1,0:T(8,128)(2,1)S(1)} %convert_element_type.33), channel_id=1, source_target_pairs={{0,16},{4,20},{8,24},{12,28},{16,0},{20,4},{24,8},{28,12},{1,17},{... | collective-permute-start | bytes 196616 | tf_op jit(solution)/shard_map/ppermute | solution.py:239
  20.9 2.2 %collective-permute-start.4 = (f16[2,32,512]{2,1,0:T(8,128)(2,1)S(1)}, f16[2,32,512]{2,1,0:T(8,128)(2,1)S(1)}, u32[]{:S(2)}, u32[]{:S(2)}) collective-permute-start(f16[2,32,512]{2,1,0:T(8,128)(2,1)S(1)} %convert_element_type.33), channel_id=1, source_target_pairs={{0,24},{4,28},{8,16},{12,20},{16,8},{20,12},{24,0},{28,4},{1,25},{... | collective-permute-start | bytes 196616 | tf_op jit(solution)/shard_map/ppermute | solution.py:239
  23.2 3.9 %collective-permute-done.4 = f16[2,32,512]{2,1,0:T(8,128)(2,1)S(1)} collective-permute-done((f16[2,32,512]{2,1,0:T(8,128)(2,1)S(1)}, f16[2,32,512]{2,1,0:T(8,128)(2,1)S(1)}, u32[]{:S(2)}, u32[]{:S(2)}) %collective-permute-start.4) | collective-permute-done | bytes 65568 | tf_op jit(solution)/shard_map/ppermute | solution.py:239
  27.1 0.3 collective-permute-done.5
  27.5 0.0 collective-permute-done.6
  27.5 1.6 %collective-permute-start.11 = (f16[4,32,512]{2,1,0:T(8,128)(2,1)S(1)}, f16[4,32,512]{2,1,0:T(8,128)(2,1)S(1)}, u32[]{:S(2)}, u32[]{:S(2)}) collective-permute-start(f16[4,32,512]{2,1,0:T(8,128)(2,1)S(1)} %get-tuple-element.30), channel_id=1, source_target_pairs={{0,4},{4,0},{8,12},{12,8},{16,20},{20,16},{24,28},{28,24},{1,5},{5... | collective-permute-start | bytes 393224 | tf_op jit(solution)/shard_map/ppermute | solution.py:251
  29.0 1.5 %collective-permute-start.9 = (f16[4,32,512]{2,1,0:T(8,128)(2,1)S(1)}, f16[4,32,512]{2,1,0:T(8,128)(2,1)S(1)}, u32[]{:S(2)}, u32[]{:S(2)}) collective-permute-start(f16[4,32,512]{2,1,0:T(8,128)(2,1)S(1)} %get-tuple-element.30), channel_id=1, source_target_pairs={{0,1},{1,0},{2,3},{3,2},{4,5},{5,4},{6,7},{7,6},{8,9},{9,8},{10,11... | collective-permute-start | bytes 393224 | tf_op jit(solution)/shard_map/ppermute | solution.py:254
  30.6 0.0 collective-permute-start.16
  30.6 0.5 collective-permute-start.12
  31.1 0.0 collective-permute-done.13.two_ref.refs_10_
  31.1 0.5 collective-permute-start.7
  31.6 0.6 chosen.1
  32.2 0.3 collective-permute-done.11
  32.5 1.3 %collective-permute-start.15 = (bf16[256,512]{1,0:T(8,128)(2,1)S(1)}, bf16[256,512]{1,0:T(8,128)(2,1)S(1)}, u32[]{:S(2)}, u32[]{:S(2)}) collective-permute-start(bf16[256,512]{1,0:T(8,128)(2,1)S(1)} %chosen.1), channel_id=1, source_target_pairs={{0,4},{4,8},{8,12},{12,16},{16,20},{20,24},{24,28},{1,5},{5,9},{9,... | collective-permute-start | bytes 786440 | tf_op jit(solution)/shard_map/ppermute | solution.py:44
  33.8 0.6 collective-permute-done.9
  34.4 1.3 %collective-permute-start.14 = (bf16[256,512]{1,0:T(8,128)(2,1)S(1)}, bf16[256,512]{1,0:T(8,128)(2,1)S(1)}, u32[]{:S(2)}, u32[]{:S(2)}) collective-permute-start(bf16[256,512]{1,0:T(8,128)(2,1)S(1)} %collective-permute-done.13.two_ref.refs_10_), channel_id=1, source_target_pairs={{0,8},{4,12},{8,16},{12,20},{16,24},{20,28},{1,9},{5,13},{9,17},{1... | collective-permute-start | bytes 786440 | tf_op jit(solution)/shard_map/ppermute | solution.py:44
  35.7 1.1 %collective-permute-done.12 = f16[4,32,512]{2,1,0:T(8,128)(2,1)S(1)} collective-permute-done((f16[4,32,512]{2,1,0:T(8,128)(2,1)S(1)}, f16[4,32,512]{2,1,0:T(8,128)(2,1)S(1)}, u32[]{:S(2)}, u32[]{:S(2)}) %collective-permute-start.12) | collective-permute-done | bytes 131104 | tf_op jit(solution)/shard_map/ppermute | solution.py:254
  36.8 1.0 %collective-permute-start.10 = (f16[4,32,512]{2,1,0:T(8,128)(2,1)S(1)}, f16[4,32,512]{2,1,0:T(8,128)(2,1)S(1)}, u32[]{:S(2)}, u32[]{:S(2)}) collective-permute-start(f16[4,32,512]{2,1,0:T(8,128)(2,1)S(1)} %collective-permute-done.9), channel_id=1, source_target_pairs={{0,4},{4,0},{8,12},{12,8},{16,20},{20,16},{24,28},{28,24},{1,5},{5... | collective-permute-start | bytes 393224 | tf_op jit(solution)/shard_map/ppermute | solution.py:251
  37.8 0.0 collective-permute-done.7
  37.8 1.5 %collective-permute-start.8 = (f16[4,32,512]{2,1,0:T(8,128)(2,1)S(1)}, f16[4,32,512]{2,1,0:T(8,128)(2,1)S(1)}, u32[]{:S(2)}, u32[]{:S(2)}) collective-permute-start(f16[4,32,512]{2,1,0:T(8,128)(2,1)S(1)} %collective-permute-done.7), channel_id=1, source_target_pairs={{0,1},{1,0},{2,3},{3,2},{4,5},{5,4},{6,7},{7,6},{8,9},{9,8},{10,11... | collective-permute-start | bytes 393224 | tf_op jit(solution)/shard_map/ppermute | solution.py:254
  39.5 1.3 %early.1 = (f32[2,256,512]{2,1,0:T(8,128)S(1)}, bf16[2,512,512]{2,1,0:T(8,128)(2,1)S(1)}, bf16[2,512,512]{2,1,0:T(8,128)(2,1)S(1)}) custom-call(f32[4,32,512]{2,1,0:T(8,128)S(1)} %convert_element_type.36.refs_0_, f32[4,32,512]{2,1,0:T(8,128)S(1)} %convert_element_type.37.refs_1_, f32[4,32,512]{2,1,0:T(8,128)S(1)} %convert_element_type.38.refs_2_, ...), custom_call_target="tpu_custom_call" | custom-call | tf_op jit(solution)/shard_map/early/pallas_call | solution.py:386
  40.9 4.3 %collective-permute-done.10 = f16[4,32,512]{2,1,0:T(8,128)(2,1)S(1)} collective-permute-done((f16[4,32,512]{2,1,0:T(8,128)(2,1)S(1)}, f16[4,32,512]{2,1,0:T(8,128)(2,1)S(1)}, u32[]{:S(2)}, u32[]{:S(2)}) %collective-permute-start.10) | collective-permute-done | bytes 131104 | tf_op jit(solution)/shard_map/ppermute | solution.py:251
  45.2 0.0 collective-permute-done.8
  45.2 0.0 collective-permute-done.16.refs_13_
  45.2 0.0 collective-permute-done.15.refs_12_
  45.2 3.6 %collective-permute-done.14.refs_11_ = bf16[256,512]{1,0:T(8,128)(2,1)S(1)} collective-permute-done((bf16[256,512]{1,0:T(8,128)(2,1)S(1)}, bf16[256,512]{1,0:T(8,128)(2,1)S(1)}, u32[]{:S(2)}, u32[]{:S(2)}) %collective-permute-start.14) | collective-permute-done | bytes 262176 | tf_op jit(solution)/shard_map/ppermute | solution.py:44
  48.8 0.0 copy-start.4
  48.8 0.7 %copy-done.4 = s32[2]{0:T(128)S(1)} copy-done((s32[2]{0:T(128)S(1)}, s32[2]{0:T(128)}, u32[]{:S(2)}) %copy-start.4) | copy-done | bytes 32
  49.5 3.2 %dyson.1 = (bf16[2,256,512]{2,1,0:T(8,128)(2,1)}, f32[264,512]{1,0:T(8,128)S(1)}, f32[256,512]{1,0:T(8,128)S(1)}, f32[8,512]{1,0:T(8,128)S(1)}) custom-call(f32[4,32,512]{2,1,0:T(8,128)S(1)} %convert_element_type.34.refs_0_, f32[4,32,512]{2,1,0:T(8,128)S(1)} %convert_element_type.35.refs_1_, f32[2,256,512]{2,1,0:T(8,128)S(1)} %get-tuple-element.18.refs_2_, ...), custom_call_target="tpu_custom_call" | custom-call | tf_op jit(solution)/shard_map/dyson/pallas_call | solution.py:402
  52.7 1.6 %collective-permute-start.17 = (f16[264,512]{1,0:T(8,128)(2,1)S(1)}, f16[264,512]{1,0:T(8,128)(2,1)S(1)}, u32[]{:S(2)}, u32[]{:S(2)}) collective-permute-start(f16[264,512]{1,0:T(8,128)(2,1)S(1)} %convert_element_type.42), channel_id=1, source_target_pairs={{0,1},{1,0},{2,3},{3,2},{4,5},{5,4},{6,7},{7,6},{8,9},{9,8},{10,11... | collective-permute-start | bytes 811016 | tf_op jit(solution)/shard_map/ppermute | solution.py:491
  54.3 0.4 begin.1
  54.7 5.2 %collective-permute-done.17 = f16[264,512]{1,0:T(8,128)(2,1)S(1)} collective-permute-done((f16[264,512]{1,0:T(8,128)(2,1)S(1)}, f16[264,512]{1,0:T(8,128)(2,1)S(1)}, u32[]{:S(2)}, u32[]{:S(2)}) %collective-permute-start.17) | collective-permute-done | bytes 270368 | tf_op jit(solution)/shard_map/ppermute | solution.py:491
  59.9 0.1 convert_element_type.43.theirs_ref
  60.0 1.7 %finish.1 = f32[256,512]{1,0:T(8,128)} custom-call(s32[1]{0:T(128)S(6)} %copy.21.refs_5_.steps_ref, f32[256,512]{1,0:T(8,128)S(1)} %get-tuple-element.21.step_ref, f32[256,512]{1,0:T(8,128)S(1)} %get-tuple-element.24.square_ref, bf16[256,512]{1,0:T(8,128)(2,1)S(1)} %get-tuple-element.25.high_ref, bf16[256,512]{1,0:T(8,128)(2,1)S(1)} %get-tuple-element.26.low_ref, ...), custom_call_target="tpu_custom_call" | custom-call | tf_op jit(solution)/shard_map/finish/pallas_call | solution.py:502
  (17 shorter events, 0.3 us)
Async XLA Ops:
  0.6 10.8 %copy-start.1 = (bf16[1,1,256,512]{3,2,1,0:T(8,128)(2,1)S(1)}, bf16[1,1,256,512]{3,2,1,0:T(8,128)(2,1)}, u32[]{:S(2)}) copy-start(bf16[1,1,256,512]{3,2,1,0:T(8,128)(2,1)} %param.8) | copy-start | bytes 786436
  0.6 17.2 %copy-start = (f32[1,256,512]{2,1,0:T(8,128)S(1)}, f32[1,256,512]{2,1,0:T(8,128)}, u32[]{:S(2)}) copy-start(f32[1,256,512]{2,1,0:T(8,128)} %param.11) | copy-start | bytes 1572868
  2.3 5.8 %collective-permute-start = (bf16[72,512]{1,0:T(8,128)(2,1)S(1)}, bf16[72,512]{1,0:T(8,128)(2,1)S(1)}, u32[]{:S(2)}, u32[]{:S(2)}) collective-permute-start(bf16[72,512]{1,0:T(8,128)(2,1)S(1)} %get-tuple-element.15), channel_id=1, source_target_pairs={{0,8},{4,12},{8,0},{12,4},{16,24},{20,28},{24,16},{28,20},{1,9},{5... | collective-permute-start | bytes 221192 | tf_op jit(solution)/shard_map/ppermute | solution.py:176
  2.8 8.6 %collective-permute-start.1 = (bf16[72,512]{1,0:T(8,128)(2,1)S(1)}, bf16[72,512]{1,0:T(8,128)(2,1)S(1)}, u32[]{:S(2)}, u32[]{:S(2)}) collective-permute-start(bf16[72,512]{1,0:T(8,128)(2,1)S(1)} %get-tuple-element.16), channel_id=1, source_target_pairs={{0,16},{4,20},{8,24},{12,28},{16,0},{20,4},{24,8},{28,12},{1,17},{... | collective-permute-start | bytes 221192 | tf_op jit(solution)/shard_map/ppermute | solution.py:176
  3.1 8.2 %collective-permute-start.2 = (bf16[72,512]{1,0:T(8,128)(2,1)S(1)}, bf16[72,512]{1,0:T(8,128)(2,1)S(1)}, u32[]{:S(2)}, u32[]{:S(2)}) collective-permute-start(bf16[72,512]{1,0:T(8,128)(2,1)S(1)} %get-tuple-element.17), channel_id=1, source_target_pairs={{0,24},{4,28},{8,16},{12,20},{16,8},{20,12},{24,0},{28,4},{1,25},{... | collective-permute-start | bytes 221192 | tf_op jit(solution)/shard_map/ppermute | solution.py:176
  11.4 0.7 %copy-start.3 = (s32[2]{0:T(128)S(1)}, s32[2]{0:T(128)}, u32[]{:S(2)}) copy-start(s32[2]{0:T(128)} %refs_6_.2) | copy-start | bytes 28
  12.6 5.2 %collective-permute-start.3 = (bf16[144,512]{1,0:T(8,128)(2,1)S(1)}, bf16[144,512]{1,0:T(8,128)(2,1)S(1)}, u32[]{:S(2)}, u32[]{:S(2)}) collective-permute-start(bf16[144,512]{1,0:T(8,128)(2,1)S(1)} %collect.1), channel_id=1, source_target_pairs={{0,4},{4,0},{8,12},{12,8},{16,20},{20,16},{24,28},{28,24},{1,5},{5... | collective-permute-start | bytes 442376 | tf_op jit(solution)/shard_map/ppermute | solution.py:189
  13.2 17.9 %collective-permute-start.13 = (bf16[256,512]{1,0:T(8,128)(2,1)S(1)}, bf16[256,512]{1,0:T(8,128)(2,1)S(1)}, u32[]{:S(2)}, u32[]{:S(2)}) collective-permute-start(bf16[256,512]{1,0:T(8,128)(2,1)S(1)} %bitcast.12), channel_id=1, source_target_pairs={{0,8},{4,12},{8,16},{12,20},{16,24},{20,28},{1,9},{5,13},{9,17},{1... | collective-permute-start | bytes 786440 | tf_op jit(solution)/shard_map/ppermute | solution.py:44
  14.5 3.3 %copy-start.2 = (s32[2]{0:T(128)S(1)}, s32[2]{0:T(128)}, u32[]{:S(2)}) copy-start(s32[2]{0:T(128)} %refs_5_.2) | copy-start | bytes 28
  18.7 8.8 %collective-permute-start.6 = (f16[2,32,512]{2,1,0:T(8,128)(2,1)S(1)}, f16[2,32,512]{2,1,0:T(8,128)(2,1)S(1)}, u32[]{:S(2)}, u32[]{:S(2)}) collective-permute-start(f16[2,32,512]{2,1,0:T(8,128)(2,1)S(1)} %convert_element_type.33), channel_id=1, source_target_pairs={{0,8},{4,12},{8,0},{12,4},{16,24},{20,28},{24,16},{28,20},{1,9},{5... | collective-permute-start | bytes 196616 | tf_op jit(solution)/shard_map/ppermute | solution.py:239
  20.1 7.3 %collective-permute-start.5 = (f16[2,32,512]{2,1,0:T(8,128)(2,1)S(1)}, f16[2,32,512]{2,1,0:T(8,128)(2,1)S(1)}, u32[]{:S(2)}, u32[]{:S(2)}) collective-permute-start(f16[2,32,512]{2,1,0:T(8,128)(2,1)S(1)} %convert_element_type.33), channel_id=1, source_target_pairs={{0,16},{4,20},{8,24},{12,28},{16,0},{20,4},{24,8},{28,12},{1,17},{... | collective-permute-start | bytes 196616 | tf_op jit(solution)/shard_map/ppermute | solution.py:239
  20.9 6.2 %collective-permute-start.4 = (f16[2,32,512]{2,1,0:T(8,128)(2,1)S(1)}, f16[2,32,512]{2,1,0:T(8,128)(2,1)S(1)}, u32[]{:S(2)}, u32[]{:S(2)}) collective-permute-start(f16[2,32,512]{2,1,0:T(8,128)(2,1)S(1)} %convert_element_type.33), channel_id=1, source_target_pairs={{0,24},{4,28},{8,16},{12,20},{16,8},{20,12},{24,0},{28,4},{1,25},{... | collective-permute-start | bytes 196616 | tf_op jit(solution)/shard_map/ppermute | solution.py:239
  27.5 5.0 %collective-permute-start.11 = (f16[4,32,512]{2,1,0:T(8,128)(2,1)S(1)}, f16[4,32,512]{2,1,0:T(8,128)(2,1)S(1)}, u32[]{:S(2)}, u32[]{:S(2)}) collective-permute-start(f16[4,32,512]{2,1,0:T(8,128)(2,1)S(1)} %get-tuple-element.30), channel_id=1, source_target_pairs={{0,4},{4,0},{8,12},{12,8},{16,20},{20,16},{24,28},{28,24},{1,5},{5... | collective-permute-start | bytes 393224 | tf_op jit(solution)/shard_map/ppermute | solution.py:251
  29.0 5.4 %collective-permute-start.9 = (f16[4,32,512]{2,1,0:T(8,128)(2,1)S(1)}, f16[4,32,512]{2,1,0:T(8,128)(2,1)S(1)}, u32[]{:S(2)}, u32[]{:S(2)}) collective-permute-start(f16[4,32,512]{2,1,0:T(8,128)(2,1)S(1)} %get-tuple-element.30), channel_id=1, source_target_pairs={{0,1},{1,0},{2,3},{3,2},{4,5},{5,4},{6,7},{7,6},{8,9},{9,8},{10,11... | collective-permute-start | bytes 393224 | tf_op jit(solution)/shard_map/ppermute | solution.py:254
  30.6 14.6 %collective-permute-start.16 = (bf16[256,512]{1,0:T(8,128)(2,1)S(1)}, bf16[256,512]{1,0:T(8,128)(2,1)S(1)}, u32[]{:S(2)}, u32[]{:S(2)}) collective-permute-start(bf16[256,512]{1,0:T(8,128)(2,1)S(1)} %bitcast.14), channel_id=1, source_target_pairs={{0,2},{2,0},{1,3},{3,1},{4,6},{6,4},{5,7},{7,5},{8,10},{10,8},{9,1... | collective-permute-start | bytes 786440 | tf_op jit(solution)/shard_map/ppermute | solution.py:482
  30.6 6.3 %collective-permute-start.12 = (f16[4,32,512]{2,1,0:T(8,128)(2,1)S(1)}, f16[4,32,512]{2,1,0:T(8,128)(2,1)S(1)}, u32[]{:S(2)}, u32[]{:S(2)}) collective-permute-start(f16[4,32,512]{2,1,0:T(8,128)(2,1)S(1)} %get-tuple-element.31), channel_id=1, source_target_pairs={{0,1},{1,0},{2,3},{3,2},{4,5},{5,4},{6,7},{7,6},{8,9},{9,8},{10,11... | collective-permute-start | bytes 393224 | tf_op jit(solution)/shard_map/ppermute | solution.py:254
  31.1 6.8 %collective-permute-start.7 = (f16[4,32,512]{2,1,0:T(8,128)(2,1)S(1)}, f16[4,32,512]{2,1,0:T(8,128)(2,1)S(1)}, u32[]{:S(2)}, u32[]{:S(2)}) collective-permute-start(f16[4,32,512]{2,1,0:T(8,128)(2,1)S(1)} %get-tuple-element.31), channel_id=1, source_target_pairs={{0,4},{4,0},{8,12},{12,8},{16,20},{20,16},{24,28},{28,24},{1,5},{5... | collective-permute-start | bytes 393224 | tf_op jit(solution)/shard_map/ppermute | solution.py:251
  32.5 12.7 %collective-permute-start.15 = (bf16[256,512]{1,0:T(8,128)(2,1)S(1)}, bf16[256,512]{1,0:T(8,128)(2,1)S(1)}, u32[]{:S(2)}, u32[]{:S(2)}) collective-permute-start(bf16[256,512]{1,0:T(8,128)(2,1)S(1)} %chosen.1), channel_id=1, source_target_pairs={{0,4},{4,8},{8,12},{12,16},{16,20},{20,24},{24,28},{1,5},{5,9},{9,... | collective-permute-start | bytes 786440 | tf_op jit(solution)/shard_map/ppermute | solution.py:44
  34.4 14.4 %collective-permute-start.14 = (bf16[256,512]{1,0:T(8,128)(2,1)S(1)}, bf16[256,512]{1,0:T(8,128)(2,1)S(1)}, u32[]{:S(2)}, u32[]{:S(2)}) collective-permute-start(bf16[256,512]{1,0:T(8,128)(2,1)S(1)} %collective-permute-done.13.two_ref.refs_10_), channel_id=1, source_target_pairs={{0,8},{4,12},{8,16},{12,20},{16,24},{20,28},{1,9},{5,13},{9,17},{1... | collective-permute-start | bytes 786440 | tf_op jit(solution)/shard_map/ppermute | solution.py:44
  36.8 8.3 %collective-permute-start.10 = (f16[4,32,512]{2,1,0:T(8,128)(2,1)S(1)}, f16[4,32,512]{2,1,0:T(8,128)(2,1)S(1)}, u32[]{:S(2)}, u32[]{:S(2)}) collective-permute-start(f16[4,32,512]{2,1,0:T(8,128)(2,1)S(1)} %collective-permute-done.9), channel_id=1, source_target_pairs={{0,4},{4,0},{8,12},{12,8},{16,20},{20,16},{24,28},{28,24},{1,5},{5... | collective-permute-start | bytes 393224 | tf_op jit(solution)/shard_map/ppermute | solution.py:251
  37.8 7.3 %collective-permute-start.8 = (f16[4,32,512]{2,1,0:T(8,128)(2,1)S(1)}, f16[4,32,512]{2,1,0:T(8,128)(2,1)S(1)}, u32[]{:S(2)}, u32[]{:S(2)}) collective-permute-start(f16[4,32,512]{2,1,0:T(8,128)(2,1)S(1)} %collective-permute-done.7), channel_id=1, source_target_pairs={{0,1},{1,0},{2,3},{3,2},{4,5},{5,4},{6,7},{7,6},{8,9},{9,8},{10,11... | collective-permute-start | bytes 393224 | tf_op jit(solution)/shard_map/ppermute | solution.py:254
  48.8 0.7 %copy-start.4 = (s32[2]{0:T(128)S(1)}, s32[2]{0:T(128)}, u32[]{:S(2)}) copy-start(s32[2]{0:T(128)} %refs_6_.2) | copy-start | bytes 28
  52.7 7.2 %collective-permute-start.17 = (f16[264,512]{1,0:T(8,128)(2,1)S(1)}, f16[264,512]{1,0:T(8,128)(2,1)S(1)}, u32[]{:S(2)}, u32[]{:S(2)}) collective-permute-start(f16[264,512]{1,0:T(8,128)(2,1)S(1)} %convert_element_type.42), channel_id=1, source_target_pairs={{0,1},{1,0},{2,3},{3,2},{4,5},{5,4},{6,7},{7,6},{8,9},{9,8},{10,11... | collective-permute-start | bytes 811016 | tf_op jit(solution)/shard_map/ppermute | solution.py:491

commit v16 on v14

--- a/solution.py
+++ b/solution.py
@@ -72,16 +72,11 @@
     return jnp.where(row == 0, first, later)
 
 
-def prepare_kernel(weight_ref, block_ref, out_ref, arrived):
+def prepare_kernel(weight_ref, block_ref, out_ref):
     half, width = out_ref.shape[0] - EXTRA, out_ref.shape[1]
     x = lax.axis_index("energy") % 2
-    start = pl.multiple_of((1 - x) * half, half)
-    copy = pltpu.make_async_copy(
-        block_ref.at[pl.ds(start, half), :], out_ref.at[pl.ds(0, half), :], arrived
-    )
-    copy.start()
+    out_ref[:half, :] = block_ref[pl.ds(pl.multiple_of((1 - x) * half, half), half), :]
     out_ref[half:, :] = weight_rows(weight_ref[0], 3, width).astype(out_ref.dtype)
-    copy.wait()
 
 
 def arrange_kernel(weight_ref, block_ref, got_ref, *out_refs):
@@ -151,12 +146,11 @@
     sent = pl.pallas_call(
         prepare_kernel,
         out_shape=jax.ShapeDtypeStruct((half + EXTRA, width), green.dtype),
-        in_specs=[in_smem, in_hbm],
+        in_specs=[in_smem, in_vmem],
         out_specs=in_vmem,
-        scratch_shapes=[pltpu.SemaphoreType.DMA],
         compiler_params=small,
         name="prepare",
-    )(weight, held(green))
+    )(weight, green)
     got = lax.ppermute(sent, "energy", [(e, e ^ 1) for e in range(energies)])
     shares = pl.pallas_call(
         arrange_kernel,
@@ -167,7 +161,7 @@
         name="arrange",
     )(weight, green, got)
     received = [None] * (outer - 1)
-    for k in range(1, outer):
+    for k in range(outer - 1, 0, -1):
         route = [(z * 2 + x, partner(z, k, outer) * 2 + x) for z in range(outer) for x in range(2)]
         received[k - 1] = lax.ppermute(shares[k - 1], "energy", route)
 
@@ -218,7 +212,7 @@
         lax.dynamic_update_index_in_dim(jnp.zeros((outer,) + part.shape, part.dtype), part, here, 0)
         for part in chunk
     ]
-    for k in range(1, outer):
+    for k in range(outer - 1, 0, -1):
         route = [(z * 2 + x, partner(z, k, outer) * 2 + x) for z in range(outer) for x in range(2)]
         got = lax.ppermute(chunk, "energy", route)
         wholes = [
@@ -338,17 +332,26 @@
     rest = hamiltonian_rows[...] - entry_scale * energy_terms - (0.5 * entry_scale) * beside
     col = lax.broadcasted_iota(jnp.int32, (rows, width), 1)
     row = lax.broadcasted_iota(jnp.int32, (rows, width), 0) + rep * rows
-    on = col == row
-    diagonal = level_ref[0] + jnp.sum(jnp.where(on, rest, 0.0), axis=1, keepdims=True)
-    off = jnp.where(on, 0.0, rest)
-    largest = jnp.max(jnp.abs(off), axis=1, keepdims=True)
+    off = jnp.where(col == row, 0.0, rest)
+    first = rep == 0
+    own = jnp.where(first, rest[:, :rows], rest[:, rows:])
+    on = lax.broadcasted_iota(jnp.int32, (rows, rows), 0) == lax.broadcasted_iota(
+        jnp.int32, (rows, rows), 1
+    )
+    diagonal = level_ref[0] + jnp.sum(jnp.where(on, own, 0.0), axis=1, keepdims=True)
+    largest = jnp.max(jnp.max(jnp.abs(off), axis=0, keepdims=True), axis=1, keepdims=True)
     largest = jnp.where(largest > 0.0, largest, 1.0)
     unit = off * (1.0 / largest)
     inverse = 1.0 / diagonal
     factor = -largest * inverse
     step_ref[...] = unit * factor
-    factor_row = jnp.sum(jnp.where(on, factor, 0.0), axis=0, keepdims=True)
-    inverse_row = jnp.sum(jnp.where(on, inverse, 0.0), axis=0, keepdims=True)
+
+    def in_own_columns(column):
+        line = jnp.sum(jnp.where(on, column, 0.0), axis=0, keepdims=True)
+        return jnp.concatenate([jnp.where(first, line, 0.0), jnp.where(first, 0.0, line)], axis=1)
+
+    inverse_row = in_own_columns(inverse)
+    factor_row = -largest * inverse_row
     blank = jnp.zeros((1, width), jnp.float32)
     packed_ref[:rows, :] = unit
     packed_ref[rows:, :] = jnp.concatenate(

time: 61 us -> 62.9 us (1.031); the launches traced: 60.8 us -> 61.8 us
  Pallas kernels: 8.97 us -> 10.8 us
  waiting for transfers between devices: 25.9 us -> 24.9 us
    ppermute x3, waiting for transfers between devices: 5.69 us -> 4.67 us  [gather_energy(): got = lax.ppermute(chunk, 'energy', route)]
    pallas_call x1, Pallas kernels: 0.03 us -> 0.98 us  [polar_share(): pl.pallas_call(arrange_kernel, out_shape=(jax.ShapeDtypeStruct((2 * share...]
  transfers between devices with their start and end apart: 18 -> 18, of which waited for: 10 -> 9; matrix products, arithmetic and copies ran while one was open for 0% -> 0% of each run, Pallas kernels for 5% -> 6%
where the time goes in v16:
time: 62.9 us; the launch traced here: 61.8 us
  waiting for transfers between devices  24.9 us (40%)
  starting transfers between devices  22.7 us (36%)
  Pallas kernels  10.8 us (17%)
  between operations  2.95 us (5%)
    ppermute x1, waiting for transfers between devices, body(): lax.ppermute(packed.astype(coded), 'rep', [(0, 1), (1, 0)])  5.52 us
    ppermute x1, waiting for transfers between devices, polar_share(): got = lax.ppermute(sent, 'energy', [(e, e ^ 1) for e in range(energies)])  4.88 us
    ppermute x3, waiting for transfers between devices, gather_energy(): got = lax.ppermute(chunk, 'energy', route)  4.67 us
    ppermute x3, waiting for transfers between devices, along_x(): return lax.ppermute(part, 'energy', [(e, e ^ 1) for e in range(energies)])  4.53 us
    ppermute x3, starting transfers between devices, gather_energy(): got = lax.ppermute(chunk, 'energy', route)  4.5 us
    ppermute x3, starting transfers between devices, polar_share(): received[k - 1] = lax.ppermute(shares[k - 1], 'energy', route)  4.45 us
    ppermute x3, starting transfers between devices, along_x(): return lax.ppermute(part, 'energy', [(e, e ^ 1) for e in range(energies)])  4.17 us
    ppermute x3, starting transfers between devices, shifted(): return lax.ppermute(block, axis, route)  3.86 us
  transfers between devices with their start and end apart: 18, of which 9 were waited for; matrix products, arithmetic and copies ran while one was open for 0% of the time, Pallas kernels for 6%

profile of v16, /device:TPU:26, one launch (start us, length us, event | category | flops | bytes accessed | tf_op | source)
XLA Modules:
  0.0 61.8 jit_solution(16081851825536706604)
XLA Ops:
  0.6 0.0 copy-start
  1.3 1.0 %prepare.1 = bf16[136,512]{1,0:T(8,128)(2,1)S(1)} custom-call(f32[1]{0:T(128)S(6)} %copy.19.weight_ref.refs_3_, bf16[256,512]{1,0:T(8,128)(2,1)} %bitcast.block_ref.refs_8_.green_ref), custom_call_target="tpu_custom_call" | custom-call | tf_op jit(solution)/shard_map/prepare/pallas_call | solution.py:146
  2.3 0.6 collective-permute-start
  2.9 4.9 %collective-permute-done.got_ref.refs_9_ = bf16[136,512]{1,0:T(8,128)(2,1)S(1)} collective-permute-done((bf16[136,512]{1,0:T(8,128)(2,1)S(1)}, bf16[136,512]{1,0:T(8,128)(2,1)S(1)}, u32[]{:S(2)}, u32[]{:S(2)}) %collective-permute-start) | collective-permute-done | bytes 139296 | tf_op jit(solution)/shard_map/ppermute | solution.py:154
  7.8 1.0 %arrange.1 = (bf16[72,512]{1,0:T(8,128)(2,1)S(1)}, bf16[72,512]{1,0:T(8,128)(2,1)S(1)}, bf16[72,512]{1,0:T(8,128)(2,1)S(1)}) custom-call(f32[1]{0:T(128)S(6)} %copy.19.weight_ref.refs_3_, bf16[256,512]{1,0:T(8,128)(2,1)} %bitcast.block_ref.refs_8_.green_ref, bf16[136,512]{1,0:T(8,128)(2,1)S(1)} %collective-permute-done.got_ref.refs_9_), custom_call_target="tpu_custom_call" | custom-call | tf_op jit(solution)/shard_map/arrange/pallas_call | solution.py:155
  8.8 0.5 collective-permute-start.1
  9.3 0.3 collective-permute-start.2
  9.6 3.6 %collective-permute-start.3 = (bf16[72,512]{1,0:T(8,128)(2,1)S(1)}, bf16[72,512]{1,0:T(8,128)(2,1)S(1)}, u32[]{:S(2)}, u32[]{:S(2)}) collective-permute-start(bf16[72,512]{1,0:T(8,128)(2,1)S(1)} %get-tuple-element.17), channel_id=1, source_target_pairs={{0,24},{4,28},{8,16},{12,20},{16,8},{20,12},{24,0},{28,4},{1,25},{... | collective-permute-start | bytes 221192 | tf_op jit(solution)/shard_map/ppermute | solution.py:166
  13.2 1.3 %collective-permute-start.13 = (bf16[256,512]{1,0:T(8,128)(2,1)}, bf16[256,512]{1,0:T(8,128)(2,1)S(1)}, u32[]{:S(2)}, u32[]{:S(2)}) collective-permute-start(bf16[256,512]{1,0:T(8,128)(2,1)} %bitcast.block_ref.refs_8_.green_ref), channel_id=1, source_target_pairs={{0,8},{4,12},{8,16},{12,20},{16,24},{20,28},{1,9},{5,13},{9,17},{1... | collective-permute-start | bytes 786440 | tf_op jit(solution)/shard_map/ppermute | solution.py:44
  15.8 0.0 copy-start.1
  15.9 0.0 copy-start.2
  15.9 0.0 collective-permute-done.1.refs_0_
  15.9 1.6 %collective-permute-done.2.refs_1_ = bf16[72,512]{1,0:T(8,128)(2,1)S(1)} collective-permute-done((bf16[72,512]{1,0:T(8,128)(2,1)S(1)}, bf16[72,512]{1,0:T(8,128)(2,1)S(1)}, u32[]{:S(2)}, u32[]{:S(2)}) %collective-permute-start.2) | collective-permute-done | bytes 73760 | tf_op jit(solution)/shard_map/ppermute | solution.py:166
  17.5 0.3 collective-permute-done.3.refs_2_
  17.8 0.0 copy-done
  17.8 0.0 copy-done.1
  17.8 0.0 copy-done.2
  17.8 1.3 %polar.1 = f32[2,32,512]{2,1,0:T(8,128)S(1)} custom-call(bf16[72,512]{1,0:T(8,128)(2,1)S(1)} %collective-permute-done.1.refs_0_, bf16[72,512]{1,0:T(8,128)(2,1)S(1)} %collective-permute-done.2.refs_1_, bf16[72,512]{1,0:T(8,128)(2,1)S(1)} %collective-permute-done.3.refs_2_, f32[1]{0:T(128)S(6)} %copy.19.weight_ref.refs_3_, s32[2]{0:T(128)S(1)} %copy-done.1, ...), custom_call_target="tpu_custom_call" | custom-call | tf_op jit(solution)/shard_map/polar/pallas_call | solution.py:172
  19.1 2.1 %collective-permute-start.6 = (f16[2,32,512]{2,1,0:T(8,128)(2,1)S(1)}, f16[2,32,512]{2,1,0:T(8,128)(2,1)S(1)}, u32[]{:S(2)}, u32[]{:S(2)}) collective-permute-start(f16[2,32,512]{2,1,0:T(8,128)(2,1)S(1)} %convert_element_type.33), channel_id=1, source_target_pairs={{0,8},{4,12},{8,0},{12,4},{16,24},{20,28},{24,16},{28,20},{1,9},{5... | collective-permute-start | bytes 196616 | tf_op jit(solution)/shard_map/ppermute | solution.py:217
  21.1 0.2 collective-permute-start.5
  21.3 2.3 %collective-permute-start.4 = (f16[2,32,512]{2,1,0:T(8,128)(2,1)S(1)}, f16[2,32,512]{2,1,0:T(8,128)(2,1)S(1)}, u32[]{:S(2)}, u32[]{:S(2)}) collective-permute-start(f16[2,32,512]{2,1,0:T(8,128)(2,1)S(1)} %convert_element_type.33), channel_id=1, source_target_pairs={{0,24},{4,28},{8,16},{12,20},{16,8},{20,12},{24,0},{28,4},{1,25},{... | collective-permute-start | bytes 196616 | tf_op jit(solution)/shard_map/ppermute | solution.py:217
  23.6 3.8 %collective-permute-done.4 = f16[2,32,512]{2,1,0:T(8,128)(2,1)S(1)} collective-permute-done((f16[2,32,512]{2,1,0:T(8,128)(2,1)S(1)}, f16[2,32,512]{2,1,0:T(8,128)(2,1)S(1)}, u32[]{:S(2)}, u32[]{:S(2)}) %collective-permute-start.4) | collective-permute-done | bytes 65568 | tf_op jit(solution)/shard_map/ppermute | solution.py:217
  27.5 0.8 %collective-permute-done.5 = f16[2,32,512]{2,1,0:T(8,128)(2,1)S(1)} collective-permute-done((f16[2,32,512]{2,1,0:T(8,128)(2,1)S(1)}, f16[2,32,512]{2,1,0:T(8,128)(2,1)S(1)}, u32[]{:S(2)}, u32[]{:S(2)}) %collective-permute-start.5) | collective-permute-done | bytes 65568 | tf_op jit(solution)/shard_map/ppermute | solution.py:217
  28.4 0.0 collective-permute-done.6
  28.4 0.6 collective-permute-start.11
  29.0 1.5 %collective-permute-start.9 = (f16[4,32,512]{2,1,0:T(8,128)(2,1)S(1)}, f16[4,32,512]{2,1,0:T(8,128)(2,1)S(1)}, u32[]{:S(2)}, u32[]{:S(2)}) collective-permute-start(f16[4,32,512]{2,1,0:T(8,128)(2,1)S(1)} %get-tuple-element.30), channel_id=1, source_target_pairs={{0,1},{1,0},{2,3},{3,2},{4,5},{5,4},{6,7},{7,6},{8,9},{9,8},{10,11... | collective-permute-start | bytes 393224 | tf_op jit(solution)/shard_map/ppermute | solution.py:232
  30.5 0.0 collective-permute-start.16
  30.5 0.5 collective-permute-start.12
  31.0 0.0 collective-permute-done.13.two_ref.refs_10_
  31.0 1.5 %collective-permute-start.7 = (f16[4,32,512]{2,1,0:T(8,128)(2,1)S(1)}, f16[4,32,512]{2,1,0:T(8,128)(2,1)S(1)}, u32[]{:S(2)}, u32[]{:S(2)}) collective-permute-start(f16[4,32,512]{2,1,0:T(8,128)(2,1)S(1)} %get-tuple-element.31), channel_id=1, source_target_pairs={{0,4},{4,0},{8,12},{12,8},{16,20},{20,16},{24,28},{28,24},{1,5},{5... | collective-permute-start | bytes 393224 | tf_op jit(solution)/shard_map/ppermute | solution.py:229
  32.5 1.0 %chosen.1 = bf16[256,512]{1,0:T(8,128)(2,1)S(1)} custom-call(s32[2]{0:T(128)S(1)} %copy-done.1, bf16[256,512]{1,0:T(8,128)(2,1)S(1)} %collective-permute-done.13.two_ref.refs_10_, bf16[256,512]{1,0:T(8,128)(2,1)} %bitcast.block_ref.refs_8_.green_ref), custom_call_target="tpu_custom_call" | custom-call | tf_op jit(solution)/shard_map/chosen/pallas_call | solution.py:514
  33.5 0.0 collective-permute-done.11
  33.5 1.3 %collective-permute-start.15 = (bf16[256,512]{1,0:T(8,128)(2,1)S(1)}, bf16[256,512]{1,0:T(8,128)(2,1)S(1)}, u32[]{:S(2)}, u32[]{:S(2)}) collective-permute-start(bf16[256,512]{1,0:T(8,128)(2,1)S(1)} %chosen.1), channel_id=1, source_target_pairs={{0,4},{4,8},{8,12},{12,16},{16,20},{20,24},{24,28},{1,5},{5,9},{9,... | collective-permute-start | bytes 786440 | tf_op jit(solution)/shard_map/ppermute | solution.py:44
  34.8 0.0 collective-permute-done.9
  34.8 1.3 %collective-permute-start.14 = (bf16[256,512]{1,0:T(8,128)(2,1)S(1)}, bf16[256,512]{1,0:T(8,128)(2,1)S(1)}, u32[]{:S(2)}, u32[]{:S(2)}) collective-permute-start(bf16[256,512]{1,0:T(8,128)(2,1)S(1)} %collective-permute-done.13.two_ref.refs_10_), channel_id=1, source_target_pairs={{0,8},{4,12},{8,16},{12,20},{16,24},{20,28},{1,9},{5,13},{9,17},{1... | collective-permute-start | bytes 786440 | tf_op jit(solution)/shard_map/ppermute | solution.py:44
  36.1 0.6 %collective-permute-done.12 = f16[4,32,512]{2,1,0:T(8,128)(2,1)S(1)} collective-permute-done((f16[4,32,512]{2,1,0:T(8,128)(2,1)S(1)}, f16[4,32,512]{2,1,0:T(8,128)(2,1)S(1)}, u32[]{:S(2)}, u32[]{:S(2)}) %collective-permute-start.12) | collective-permute-done | bytes 131104 | tf_op jit(solution)/shard_map/ppermute | solution.py:232
  36.8 2.1 %collective-permute-start.10 = (f16[4,32,512]{2,1,0:T(8,128)(2,1)S(1)}, f16[4,32,512]{2,1,0:T(8,128)(2,1)S(1)}, u32[]{:S(2)}, u32[]{:S(2)}) collective-permute-start(f16[4,32,512]{2,1,0:T(8,128)(2,1)S(1)} %collective-permute-done.9), channel_id=1, source_target_pairs={{0,4},{4,0},{8,12},{12,8},{16,20},{20,16},{24,28},{28,24},{1,5},{5... | collective-permute-start | bytes 393224 | tf_op jit(solution)/shard_map/ppermute | solution.py:229
  38.8 0.0 collective-permute-done.7
  38.9 1.5 %collective-permute-start.8 = (f16[4,32,512]{2,1,0:T(8,128)(2,1)S(1)}, f16[4,32,512]{2,1,0:T(8,128)(2,1)S(1)}, u32[]{:S(2)}, u32[]{:S(2)}) collective-permute-start(f16[4,32,512]{2,1,0:T(8,128)(2,1)S(1)} %collective-permute-done.7), channel_id=1, source_target_pairs={{0,1},{1,0},{2,3},{3,2},{4,5},{5,4},{6,7},{7,6},{8,9},{9,8},{10,11... | collective-permute-start | bytes 393224 | tf_op jit(solution)/shard_map/ppermute | solution.py:232
  40.6 1.3 %early.1 = (f32[2,256,512]{2,1,0:T(8,128)S(1)}, bf16[2,512,512]{2,1,0:T(8,128)(2,1)S(1)}, bf16[2,512,512]{2,1,0:T(8,128)(2,1)S(1)}) custom-call(f32[4,32,512]{2,1,0:T(8,128)S(1)} %convert_element_type.36.refs_0_, f32[4,32,512]{2,1,0:T(8,128)S(1)} %convert_element_type.37.refs_1_, f32[4,32,512]{2,1,0:T(8,128)S(1)} %convert_element_type.38.refs_2_, ...), custom_call_target="tpu_custom_call" | custom-call | tf_op jit(solution)/shard_map/early/pallas_call | solution.py:373
  41.9 4.5 %collective-permute-done.10 = f16[4,32,512]{2,1,0:T(8,128)(2,1)S(1)} collective-permute-done((f16[4,32,512]{2,1,0:T(8,128)(2,1)S(1)}, f16[4,32,512]{2,1,0:T(8,128)(2,1)S(1)}, u32[]{:S(2)}, u32[]{:S(2)}) %collective-permute-start.10) | collective-permute-done | bytes 131104 | tf_op jit(solution)/shard_map/ppermute | solution.py:229
  46.4 0.0 collective-permute-done.8
  46.4 0.0 collective-permute-done.16.refs_13_
  46.5 0.0 collective-permute-done.15.refs_12_
  46.5 2.7 %collective-permute-done.14.refs_11_ = bf16[256,512]{1,0:T(8,128)(2,1)S(1)} collective-permute-done((bf16[256,512]{1,0:T(8,128)(2,1)S(1)}, bf16[256,512]{1,0:T(8,128)(2,1)S(1)}, u32[]{:S(2)}, u32[]{:S(2)}) %collective-permute-start.14) | collective-permute-done | bytes 262176 | tf_op jit(solution)/shard_map/ppermute | solution.py:44
  49.2 3.2 %dyson.1 = (bf16[2,256,512]{2,1,0:T(8,128)(2,1)}, f32[264,512]{1,0:T(8,128)S(1)}, f32[256,512]{1,0:T(8,128)S(1)}, f32[8,512]{1,0:T(8,128)S(1)}) custom-call(f32[4,32,512]{2,1,0:T(8,128)S(1)} %convert_element_type.34.refs_0_, f32[4,32,512]{2,1,0:T(8,128)S(1)} %convert_element_type.35.refs_1_, f32[2,256,512]{2,1,0:T(8,128)S(1)} %get-tuple-element.18.refs_2_, ...), custom_call_target="tpu_custom_call" | custom-call | tf_op jit(solution)/shard_map/dyson/pallas_call | solution.py:389
  52.4 1.6 %collective-permute-start.17 = (f16[264,512]{1,0:T(8,128)(2,1)S(1)}, f16[264,512]{1,0:T(8,128)(2,1)S(1)}, u32[]{:S(2)}, u32[]{:S(2)}) collective-permute-start(f16[264,512]{1,0:T(8,128)(2,1)S(1)} %convert_element_type.42), channel_id=1, source_target_pairs={{0,1},{1,0},{2,3},{3,2},{4,5},{5,4},{6,7},{7,6},{8,9},{9,8},{10,11... | collective-permute-start | bytes 811016 | tf_op jit(solution)/shard_map/ppermute | solution.py:478
  54.0 0.4 begin.1
  54.4 5.5 %collective-permute-done.17 = f16[264,512]{1,0:T(8,128)(2,1)S(1)} collective-permute-done((f16[264,512]{1,0:T(8,128)(2,1)S(1)}, f16[264,512]{1,0:T(8,128)(2,1)S(1)}, u32[]{:S(2)}, u32[]{:S(2)}) %collective-permute-start.17) | collective-permute-done | bytes 270368 | tf_op jit(solution)/shard_map/ppermute | solution.py:478
  60.0 0.1 convert_element_type.43.theirs_ref
  60.0 1.7 %finish.1 = f32[256,512]{1,0:T(8,128)} custom-call(s32[1]{0:T(128)S(6)} %copy.21.refs_6_.steps_ref, f32[256,512]{1,0:T(8,128)S(1)} %get-tuple-element.21.step_ref, f32[256,512]{1,0:T(8,128)S(1)} %get-tuple-element.24.square_ref, bf16[256,512]{1,0:T(8,128)(2,1)S(1)} %get-tuple-element.25.high_ref, bf16[256,512]{1,0:T(8,128)(2,1)S(1)} %get-tuple-element.26.low_ref, ...), custom_call_target="tpu_custom_call" | custom-call | tf_op jit(solution)/shard_map/finish/pallas_call | solution.py:489
  (17 shorter events, 0.3 us)
Async XLA Ops:
  0.6 17.1 %copy-start = (f32[1,256,512]{2,1,0:T(8,128)S(1)}, f32[1,256,512]{2,1,0:T(8,128)}, u32[]{:S(2)}) copy-start(f32[1,256,512]{2,1,0:T(8,128)} %param.11) | copy-start | bytes 1572868
  2.3 5.5 %collective-permute-start = (bf16[136,512]{1,0:T(8,128)(2,1)S(1)}, bf16[136,512]{1,0:T(8,128)(2,1)S(1)}, u32[]{:S(2)}, u32[]{:S(2)}) collective-permute-start(bf16[136,512]{1,0:T(8,128)(2,1)S(1)} %prepare.1), channel_id=1, source_target_pairs={{0,4},{4,0},{8,12},{12,8},{16,20},{20,16},{24,28},{28,24},{1,5},{5... | collective-permute-start | bytes 417800 | tf_op jit(solution)/shard_map/ppermute | solution.py:154
  8.8 7.1 %collective-permute-start.1 = (bf16[72,512]{1,0:T(8,128)(2,1)S(1)}, bf16[72,512]{1,0:T(8,128)(2,1)S(1)}, u32[]{:S(2)}, u32[]{:S(2)}) collective-permute-start(bf16[72,512]{1,0:T(8,128)(2,1)S(1)} %get-tuple-element.15), channel_id=1, source_target_pairs={{0,8},{4,12},{8,0},{12,4},{16,24},{20,28},{24,16},{28,20},{1,9},{5... | collective-permute-start | bytes 221192 | tf_op jit(solution)/shard_map/ppermute | solution.py:166
  9.3 8.2 %collective-permute-start.2 = (bf16[72,512]{1,0:T(8,128)(2,1)S(1)}, bf16[72,512]{1,0:T(8,128)(2,1)S(1)}, u32[]{:S(2)}, u32[]{:S(2)}) collective-permute-start(bf16[72,512]{1,0:T(8,128)(2,1)S(1)} %get-tuple-element.16), channel_id=1, source_target_pairs={{0,16},{4,20},{8,24},{12,28},{16,0},{20,4},{24,8},{28,12},{1,17},{... | collective-permute-start | bytes 221192 | tf_op jit(solution)/shard_map/ppermute | solution.py:166
  9.6 8.1 %collective-permute-start.3 = (bf16[72,512]{1,0:T(8,128)(2,1)S(1)}, bf16[72,512]{1,0:T(8,128)(2,1)S(1)}, u32[]{:S(2)}, u32[]{:S(2)}) collective-permute-start(bf16[72,512]{1,0:T(8,128)(2,1)S(1)} %get-tuple-element.17), channel_id=1, source_target_pairs={{0,24},{4,28},{8,16},{12,20},{16,8},{20,12},{24,0},{28,4},{1,25},{... | collective-permute-start | bytes 221192 | tf_op jit(solution)/shard_map/ppermute | solution.py:166
  13.2 17.8 %collective-permute-start.13 = (bf16[256,512]{1,0:T(8,128)(2,1)}, bf16[256,512]{1,0:T(8,128)(2,1)S(1)}, u32[]{:S(2)}, u32[]{:S(2)}) collective-permute-start(bf16[256,512]{1,0:T(8,128)(2,1)} %bitcast.block_ref.refs_8_.green_ref), channel_id=1, source_target_pairs={{0,8},{4,12},{8,16},{12,20},{16,24},{20,28},{1,9},{5,13},{9,17},{1... | collective-permute-start | bytes 786440 | tf_op jit(solution)/shard_map/ppermute | solution.py:44
  15.8 1.9 %copy-start.1 = (s32[2]{0:T(128)S(1)}, s32[2]{0:T(128)}, u32[]{:S(2)}) copy-start(s32[2]{0:T(128)} %refs_5_.3) | copy-start | bytes 28
  15.9 1.9 %copy-start.2 = (s32[2]{0:T(128)S(1)}, s32[2]{0:T(128)}, u32[]{:S(2)}) copy-start(s32[2]{0:T(128)} %refs_6_.2) | copy-start | bytes 28
  19.1 9.3 %collective-permute-start.6 = (f16[2,32,512]{2,1,0:T(8,128)(2,1)S(1)}, f16[2,32,512]{2,1,0:T(8,128)(2,1)S(1)}, u32[]{:S(2)}, u32[]{:S(2)}) collective-permute-start(f16[2,32,512]{2,1,0:T(8,128)(2,1)S(1)} %convert_element_type.33), channel_id=1, source_target_pairs={{0,8},{4,12},{8,0},{12,4},{16,24},{20,28},{24,16},{28,20},{1,9},{5... | collective-permute-start | bytes 196616 | tf_op jit(solution)/shard_map/ppermute | solution.py:217
  21.1 7.2 %collective-permute-start.5 = (f16[2,32,512]{2,1,0:T(8,128)(2,1)S(1)}, f16[2,32,512]{2,1,0:T(8,128)(2,1)S(1)}, u32[]{:S(2)}, u32[]{:S(2)}) collective-permute-start(f16[2,32,512]{2,1,0:T(8,128)(2,1)S(1)} %convert_element_type.33), channel_id=1, source_target_pairs={{0,16},{4,20},{8,24},{12,28},{16,0},{20,4},{24,8},{28,12},{1,17},{... | collective-permute-start | bytes 196616 | tf_op jit(solution)/shard_map/ppermute | solution.py:217
  21.3 6.2 %collective-permute-start.4 = (f16[2,32,512]{2,1,0:T(8,128)(2,1)S(1)}, f16[2,32,512]{2,1,0:T(8,128)(2,1)S(1)}, u32[]{:S(2)}, u32[]{:S(2)}) collective-permute-start(f16[2,32,512]{2,1,0:T(8,128)(2,1)S(1)} %convert_element_type.33), channel_id=1, source_target_pairs={{0,24},{4,28},{8,16},{12,20},{16,8},{20,12},{24,0},{28,4},{1,25},{... | collective-permute-start | bytes 196616 | tf_op jit(solution)/shard_map/ppermute | solution.py:217
  28.4 5.1 %collective-permute-start.11 = (f16[4,32,512]{2,1,0:T(8,128)(2,1)S(1)}, f16[4,32,512]{2,1,0:T(8,128)(2,1)S(1)}, u32[]{:S(2)}, u32[]{:S(2)}) collective-permute-start(f16[4,32,512]{2,1,0:T(8,128)(2,1)S(1)} %get-tuple-element.30), channel_id=1, source_target_pairs={{0,4},{4,0},{8,12},{12,8},{16,20},{20,16},{24,28},{28,24},{1,5},{5... | collective-permute-start | bytes 393224 | tf_op jit(solution)/shard_map/ppermute | solution.py:229
  29.0 5.8 %collective-permute-start.9 = (f16[4,32,512]{2,1,0:T(8,128)(2,1)S(1)}, f16[4,32,512]{2,1,0:T(8,128)(2,1)S(1)}, u32[]{:S(2)}, u32[]{:S(2)}) collective-permute-start(f16[4,32,512]{2,1,0:T(8,128)(2,1)S(1)} %get-tuple-element.30), channel_id=1, source_target_pairs={{0,1},{1,0},{2,3},{3,2},{4,5},{5,4},{6,7},{7,6},{8,9},{9,8},{10,11... | collective-permute-start | bytes 393224 | tf_op jit(solution)/shard_map/ppermute | solution.py:232
  30.5 15.9 %collective-permute-start.16 = (bf16[256,512]{1,0:T(8,128)(2,1)}, bf16[256,512]{1,0:T(8,128)(2,1)S(1)}, u32[]{:S(2)}, u32[]{:S(2)}) collective-permute-start(bf16[256,512]{1,0:T(8,128)(2,1)} %bitcast.block_ref.refs_8_.green_ref), channel_id=1, source_target_pairs={{0,2},{2,0},{1,3},{3,1},{4,6},{6,4},{5,7},{7,5},{8,10},{10,8},{9,1... | collective-permute-start | bytes 786440 | tf_op jit(solution)/shard_map/ppermute | solution.py:469
  30.5 6.3 %collective-permute-start.12 = (f16[4,32,512]{2,1,0:T(8,128)(2,1)S(1)}, f16[4,32,512]{2,1,0:T(8,128)(2,1)S(1)}, u32[]{:S(2)}, u32[]{:S(2)}) collective-permute-start(f16[4,32,512]{2,1,0:T(8,128)(2,1)S(1)} %get-tuple-element.31), channel_id=1, source_target_pairs={{0,1},{1,0},{2,3},{3,2},{4,5},{5,4},{6,7},{7,6},{8,9},{9,8},{10,11... | collective-permute-start | bytes 393224 | tf_op jit(solution)/shard_map/ppermute | solution.py:232
  31.0 7.8 %collective-permute-start.7 = (f16[4,32,512]{2,1,0:T(8,128)(2,1)S(1)}, f16[4,32,512]{2,1,0:T(8,128)(2,1)S(1)}, u32[]{:S(2)}, u32[]{:S(2)}) collective-permute-start(f16[4,32,512]{2,1,0:T(8,128)(2,1)S(1)} %get-tuple-element.31), channel_id=1, source_target_pairs={{0,4},{4,0},{8,12},{12,8},{16,20},{20,16},{24,28},{28,24},{1,5},{5... | collective-permute-start | bytes 393224 | tf_op jit(solution)/shard_map/ppermute | solution.py:229
  33.5 12.9 %collective-permute-start.15 = (bf16[256,512]{1,0:T(8,128)(2,1)S(1)}, bf16[256,512]{1,0:T(8,128)(2,1)S(1)}, u32[]{:S(2)}, u32[]{:S(2)}) collective-permute-start(bf16[256,512]{1,0:T(8,128)(2,1)S(1)} %chosen.1), channel_id=1, source_target_pairs={{0,4},{4,8},{8,12},{12,16},{16,20},{20,24},{24,28},{1,5},{5,9},{9,... | collective-permute-start | bytes 786440 | tf_op jit(solution)/shard_map/ppermute | solution.py:44
  34.8 14.4 %collective-permute-start.14 = (bf16[256,512]{1,0:T(8,128)(2,1)S(1)}, bf16[256,512]{1,0:T(8,128)(2,1)S(1)}, u32[]{:S(2)}, u32[]{:S(2)}) collective-permute-start(bf16[256,512]{1,0:T(8,128)(2,1)S(1)} %collective-permute-done.13.two_ref.refs_10_), channel_id=1, source_target_pairs={{0,8},{4,12},{8,16},{12,20},{16,24},{20,28},{1,9},{5,13},{9,17},{1... | collective-permute-start | bytes 786440 | tf_op jit(solution)/shard_map/ppermute | solution.py:44
  36.8 9.6 %collective-permute-start.10 = (f16[4,32,512]{2,1,0:T(8,128)(2,1)S(1)}, f16[4,32,512]{2,1,0:T(8,128)(2,1)S(1)}, u32[]{:S(2)}, u32[]{:S(2)}) collective-permute-start(f16[4,32,512]{2,1,0:T(8,128)(2,1)S(1)} %collective-permute-done.9), channel_id=1, source_target_pairs={{0,4},{4,0},{8,12},{12,8},{16,20},{20,16},{24,28},{28,24},{1,5},{5... | collective-permute-start | bytes 393224 | tf_op jit(solution)/shard_map/ppermute | solution.py:229
  38.9 7.6 %collective-permute-start.8 = (f16[4,32,512]{2,1,0:T(8,128)(2,1)S(1)}, f16[4,32,512]{2,1,0:T(8,128)(2,1)S(1)}, u32[]{:S(2)}, u32[]{:S(2)}) collective-permute-start(f16[4,32,512]{2,1,0:T(8,128)(2,1)S(1)} %collective-permute-done.7), channel_id=1, source_target_pairs={{0,1},{1,0},{2,3},{3,2},{4,5},{5,4},{6,7},{7,6},{8,9},{9,8},{10,11... | collective-permute-start | bytes 393224 | tf_op jit(solution)/shard_map/ppermute | solution.py:232
  52.4 7.5 %collective-permute-start.17 = (f16[264,512]{1,0:T(8,128)(2,1)S(1)}, f16[264,512]{1,0:T(8,128)(2,1)S(1)}, u32[]{:S(2)}, u32[]{:S(2)}) collective-permute-start(f16[264,512]{1,0:T(8,128)(2,1)S(1)} %convert_element_type.42), channel_id=1, source_target_pairs={{0,1},{1,0},{2,3},{3,2},{4,5},{5,4},{6,7},{7,6},{8,9},{9,8},{10,11... | collective-permute-start | bytes 811016 | tf_op jit(solution)/shard_map/ppermute | solution.py:478

commit v17 on v14

--- a/solution.py
+++ b/solution.py
@@ -167,7 +167,7 @@
         name="arrange",
     )(weight, green, got)
     received = [None] * (outer - 1)
-    for k in range(1, outer):
+    for k in range(outer - 1, 0, -1):
         route = [(z * 2 + x, partner(z, k, outer) * 2 + x) for z in range(outer) for x in range(2)]
         received[k - 1] = lax.ppermute(shares[k - 1], "energy", route)
 
@@ -214,21 +214,17 @@
 def gather_energy(chunk):
     outer = lax.axis_size("energy") // 2
     here = lax.axis_index("energy") // 2
-    wholes = [
-        lax.dynamic_update_index_in_dim(jnp.zeros((outer,) + part.shape, part.dtype), part, here, 0)
-        for part in chunk
-    ]
-    for k in range(1, outer):
+    freqs, share, width = chunk.shape
+    whole = jnp.zeros((freqs, outer, share, width), chunk.dtype)
+    whole = lax.dynamic_update_slice_in_dim(whole, chunk[:, None], here, 1)
+    for k in range(outer - 1, 0, -1):
         route = [(z * 2 + x, partner(z, k, outer) * 2 + x) for z in range(outer) for x in range(2)]
         got = lax.ppermute(chunk, "energy", route)
-        wholes = [
-            lax.dynamic_update_index_in_dim(whole, part, origin(here, k, outer), 0)
-            for whole, part in zip(wholes, got)
-        ]
-    return wholes
-
-
-def gather_square(parts):
+        whole = lax.dynamic_update_slice_in_dim(whole, got[:, None], origin(here, k, outer), 1)
+    return whole
+
+
+def gather_square(part):
     energies = lax.axis_size("energy")
 
     def along_x(part):
@@ -237,10 +233,10 @@
     def along_rep(part):
         return lax.ppermute(part, "rep", [(0, 1), (1, 0)])
 
-    beside = [along_x(part) for part in parts]
-    above = [along_rep(part) for part in parts]
+    beside = along_x(part)
+    above = along_rep(part)
     apart = [along_rep(beside[0]), along_x(above[1])]
-    return [*parts, *beside, *above, *apart]
+    return [*part, *beside, *above, *apart]
 
 
 def gathered(chunk):

time: 61 us -> 63.5 us (1.041)
  waiting for transfers between devices: 25.9 us -> 31.1 us
  starting transfers between devices: 22.6 us -> 19.9 us
    ppermute x3 -> x2, starting transfers between devices: 4.06 us -> 1.2 us  [along_x(): return lax.ppermute(part, 'energy', [(e, e ^ 1) for e in range(energies)])]
    ppermute x1, waiting for transfers between devices: 5.21 us -> 7.1 us  [body(): lax.ppermute(packed.astype(coded), 'rep', [(0, 1), (1, 0)])]
    ppermute x3, starting transfers between devices: 4.45 us -> 6.13 us  [gather_energy(): got = lax.ppermute(chunk, 'energy', route)]
    ppermute x3 -> x2, waiting for transfers between devices: 4.55 us -> 5.69 us  [along_x(): return lax.ppermute(part, 'energy', [(e, e ^ 1) for e in range(energies)])]
    ppermute x1, starting transfers between devices: 1.59 us -> 0.57 us  [body(): lax.ppermute(packed.astype(coded), 'rep', [(0, 1), (1, 0)])]
    ppermute x3, waiting for transfers between devices: 2.74 us -> 3.74 us  [shifted(): return lax.ppermute(block, axis, route)]
    ppermute x3 -> x2, waiting for transfers between devices: 0.75 us -> 1.41 us  [along_rep(): return lax.ppermute(part, 'rep', [(0, 1), (1, 0)])]
    ppermute x3 -> x2, starting transfers between devices: 3.55 us -> 3.1 us  [along_rep(): return lax.ppermute(part, 'rep', [(0, 1), (1, 0)])]
  transfers between devices with their start and end apart: 18 -> 16, of which waited for: 10 -> 9; matrix products, arithmetic and copies ran while one was open for 0% -> 0% of each run, Pallas kernels for 5% -> 4%
where the time goes in v17:
time: 63.5 us; the launch traced here: 63.3 us
  waiting for transfers between devices  31.1 us (49%)
  starting transfers between devices  19.9 us (31%)
  Pallas kernels  8.98 us (14%)
  between operations  2.91 us (5%)
    ppermute x1, waiting for transfers between devices, body(): lax.ppermute(packed.astype(coded), 'rep', [(0, 1), (1, 0)])  7.1 us
    ppermute x3, starting transfers between devices, gather_energy(): got = lax.ppermute(chunk, 'energy', route)  6.13 us
    ppermute x3, waiting for transfers between devices, gather_energy(): got = lax.ppermute(chunk, 'energy', route)  5.84 us
    ppermute x2, waiting for transfers between devices, along_x(): return lax.ppermute(part, 'energy', [(e, e ^ 1) for e in range(energies)])  5.69 us
    ppermute x1, waiting for transfers between devices, polar_share(): got = lax.ppermute(sent, 'energy', [(e, e ^ 1) for e in range(energies)])  4.88 us
    ppermute x3, starting transfers between devices, polar_share(): received[k - 1] = lax.ppermute(shares[k - 1], 'energy', route)  4.45 us
    ppermute x3, starting transfers between devices, shifted(): return lax.ppermute(block, axis, route)  3.86 us
    ppermute x3, waiting for transfers between devices, shifted(): return lax.ppermute(block, axis, route)  3.74 us
  transfers between devices with their start and end apart: 16, of which 9 were waited for; matrix products, arithmetic and copies ran while one was open for 0% of the time, Pallas kernels for 4%

profile of v17, /device:TPU:26, one launch (start us, length us, event | category | flops | bytes accessed | tf_op | source)
XLA Modules:
  0.0 63.3 jit_solution(6946725237869285774)
XLA Ops:
  0.6 0.0 copy-start.1
  0.6 0.0 copy-start
  1.4 0.9 %prepare.1 = bf16[136,512]{1,0:T(8,128)(2,1)S(1)} custom-call(f32[1]{0:T(128)S(6)} %copy.18.weight_ref.refs_3_, bf16[256,512]{1,0:T(8,128)(2,1)} %bitcast.52), custom_call_target="tpu_custom_call" | custom-call | tf_op jit(solution)/shard_map/prepare/pallas_call | solution.py:151
  2.3 0.6 collective-permute-start
  2.9 4.9 %collective-permute-done.got_ref.refs_9_ = bf16[136,512]{1,0:T(8,128)(2,1)S(1)} collective-permute-done((bf16[136,512]{1,0:T(8,128)(2,1)S(1)}, bf16[136,512]{1,0:T(8,128)(2,1)S(1)}, u32[]{:S(2)}, u32[]{:S(2)}) %collective-permute-start) | collective-permute-done | bytes 139296 | tf_op jit(solution)/shard_map/ppermute | solution.py:160
  7.8 0.0 copy-done.1
  7.8 0.5 collective-permute-start.1
  8.3 0.3 collective-permute-start.2
  8.7 3.6 %collective-permute-start.3 = (bf16[72,512]{1,0:T(8,128)(2,1)S(1)}, bf16[72,512]{1,0:T(8,128)(2,1)S(1)}, u32[]{:S(2)}, u32[]{:S(2)}) collective-permute-start(bf16[72,512]{1,0:T(8,128)(2,1)S(1)} %get-tuple-element.17), channel_id=1, source_target_pairs={{0,24},{4,28},{8,16},{12,20},{16,8},{20,12},{24,0},{28,4},{1,25},{... | collective-permute-start | bytes 221192 | tf_op jit(solution)/shard_map/ppermute | solution.py:172
  13.6 0.0 copy-start.2
  13.6 0.0 copy-start.3
  13.6 0.0 collective-permute-done.1.refs_0_
  13.6 2.4 %collective-permute-done.2.refs_1_ = bf16[72,512]{1,0:T(8,128)(2,1)S(1)} collective-permute-done((bf16[72,512]{1,0:T(8,128)(2,1)S(1)}, bf16[72,512]{1,0:T(8,128)(2,1)S(1)}, u32[]{:S(2)}, u32[]{:S(2)}) %collective-permute-start.2) | collective-permute-done | bytes 73760 | tf_op jit(solution)/shard_map/ppermute | solution.py:172
  16.1 0.0 collective-permute-done.3.refs_2_
  16.1 0.0 copy-done
  16.1 0.0 copy-done.2
  16.1 0.0 copy-done.3
  16.1 0.8 %polar.1 = f32[2,32,512]{2,1,0:T(8,128)S(1)} custom-call(bf16[72,512]{1,0:T(8,128)(2,1)S(1)} %collective-permute-done.1.refs_0_, bf16[72,512]{1,0:T(8,128)(2,1)S(1)} %collective-permute-done.2.refs_1_, bf16[72,512]{1,0:T(8,128)(2,1)S(1)} %collective-permute-done.3.refs_2_, f32[1]{0:T(128)S(6)} %copy.18.weight_ref.refs_3_, s32[2]{0:T(128)S(1)} %copy-done.2, ...), custom_call_target="tpu_custom_call" | custom-call | tf_op jit(solution)/shard_map/polar/pallas_call | solution.py:178
  17.0 2.5 %collective-permute-start.4 = (f16[2,32,512]{2,1,0:T(8,128)(2,1)S(1)}, f16[2,32,512]{2,1,0:T(8,128)(2,1)S(1)}, u32[]{:S(2)}, u32[]{:S(2)}) collective-permute-start(f16[2,32,512]{2,1,0:T(8,128)(2,1)S(1)} %get-tuple-element.31), channel_id=1, source_target_pairs={{0,24},{4,28},{8,16},{12,20},{16,8},{20,12},{24,0},{28,4},{1,25},{... | collective-permute-start | bytes 196616 | tf_op jit(solution)/shard_map/ppermute | solution.py:222
  19.5 1.3 %collective-permute-start.11 = (bf16[256,512]{1,0:T(8,128)(2,1)S(1)}, bf16[256,512]{1,0:T(8,128)(2,1)S(1)}, u32[]{:S(2)}, u32[]{:S(2)}) collective-permute-start(bf16[256,512]{1,0:T(8,128)(2,1)S(1)} %bitcast.55), channel_id=1, source_target_pairs={{0,8},{4,12},{8,16},{12,20},{16,24},{20,28},{1,9},{5,13},{9,17},{1... | collective-permute-start | bytes 786440 | tf_op jit(solution)/shard_map/ppermute | solution.py:44
  20.8 1.6 %collective-permute-start.5 = (f16[2,32,512]{2,1,0:T(8,128)(2,1)S(1)}, f16[2,32,512]{2,1,0:T(8,128)(2,1)S(1)}, u32[]{:S(2)}, u32[]{:S(2)}) collective-permute-start(f16[2,32,512]{2,1,0:T(8,128)(2,1)S(1)} %get-tuple-element.31), channel_id=1, source_target_pairs={{0,16},{4,20},{8,24},{12,28},{16,0},{20,4},{24,8},{28,12},{1,17},{... | collective-permute-start | bytes 196616 | tf_op jit(solution)/shard_map/ppermute | solution.py:222
  22.4 2.0 %collective-permute-start.6 = (f16[2,32,512]{2,1,0:T(8,128)(2,1)S(1)}, f16[2,32,512]{2,1,0:T(8,128)(2,1)S(1)}, u32[]{:S(2)}, u32[]{:S(2)}) collective-permute-start(f16[2,32,512]{2,1,0:T(8,128)(2,1)S(1)} %get-tuple-element.31), channel_id=1, source_target_pairs={{0,8},{4,12},{8,0},{12,4},{16,24},{20,28},{24,16},{28,20},{1,9},{5... | collective-permute-start | bytes 196616 | tf_op jit(solution)/shard_map/ppermute | solution.py:222
  24.4 0.0 collective-permute-done.4
  24.4 4.6 %collective-permute-done.5 = f16[2,32,512]{2,1,0:T(8,128)(2,1)S(1)} collective-permute-done((f16[2,32,512]{2,1,0:T(8,128)(2,1)S(1)}, f16[2,32,512]{2,1,0:T(8,128)(2,1)S(1)}, u32[]{:S(2)}, u32[]{:S(2)}) %collective-permute-start.5) | collective-permute-done | bytes 65568 | tf_op jit(solution)/shard_map/ppermute | solution.py:222
  29.1 1.2 %collective-permute-done.6 = f16[2,32,512]{2,1,0:T(8,128)(2,1)S(1)} collective-permute-done((f16[2,32,512]{2,1,0:T(8,128)(2,1)S(1)}, f16[2,32,512]{2,1,0:T(8,128)(2,1)S(1)}, u32[]{:S(2)}, u32[]{:S(2)}) %collective-permute-start.6) | collective-permute-done | bytes 65568 | tf_op jit(solution)/shard_map/ppermute | solution.py:222
  30.3 0.6 collective-permute-start.7
  30.9 1.5 %collective-permute-start.9 = (f16[2,4,32,512]{3,2,1,0:T(8,128)(2,1)S(1)}, f16[2,4,32,512]{3,2,1,0:T(8,128)(2,1)S(1)}, u32[]{:S(2)}, u32[]{:S(2)}) collective-permute-start(f16[2,4,32,512]{3,2,1,0:T(8,128)(2,1)S(1)} %bitcast_dynamic-update-slice_fusion.3), channel_id=1, source_target_pairs={{0,1},{1,0},{2,3},{3,2},{4,5},{5,4},{6,7},{7,6},{8,9},{9,8},{10,11... | collective-permute-start | bytes 786440 | tf_op jit(solution)/shard_map/ppermute | solution.py:234
  32.4 0.0 collective-permute-start.14
  32.4 0.0 collective-permute-done.11.two_ref.refs_10_
  32.4 0.6 chosen.1
  33.0 1.3 %collective-permute-start.13 = (bf16[256,512]{1,0:T(8,128)(2,1)S(1)}, bf16[256,512]{1,0:T(8,128)(2,1)S(1)}, u32[]{:S(2)}, u32[]{:S(2)}) collective-permute-start(bf16[256,512]{1,0:T(8,128)(2,1)S(1)} %chosen.1), channel_id=1, source_target_pairs={{0,4},{4,8},{8,12},{12,16},{16,20},{20,24},{24,28},{1,5},{5,9},{9,... | collective-permute-start | bytes 786440 | tf_op jit(solution)/shard_map/ppermute | solution.py:44
  34.3 1.3 %collective-permute-start.12 = (bf16[256,512]{1,0:T(8,128)(2,1)S(1)}, bf16[256,512]{1,0:T(8,128)(2,1)S(1)}, u32[]{:S(2)}, u32[]{:S(2)}) collective-permute-start(bf16[256,512]{1,0:T(8,128)(2,1)S(1)} %collective-permute-done.11.two_ref.refs_10_), channel_id=1, source_target_pairs={{0,8},{4,12},{8,16},{12,20},{16,24},{20,28},{1,9},{5,13},{9,17},{1... | collective-permute-start | bytes 786440 | tf_op jit(solution)/shard_map/ppermute | solution.py:44
  35.6 1.1 %collective-permute-done.7 = f16[2,4,32,512]{3,2,1,0:T(8,128)(2,1)S(1)} collective-permute-done((f16[2,4,32,512]{3,2,1,0:T(8,128)(2,1)S(1)}, f16[2,4,32,512]{3,2,1,0:T(8,128)(2,1)S(1)}, u32[]{:S(2)}, u32[]{:S(2)}) %collective-permute-start.7) | collective-permute-done | bytes 262176 | tf_op jit(solution)/shard_map/ppermute | solution.py:231
  36.7 0.1 fusion.1
  36.8 1.6 %collective-permute-start.8 = (f16[4,32,512]{2,1,0:T(8,128)(2,1)S(1)}, f16[4,32,512]{2,1,0:T(8,128)(2,1)S(1)}, u32[]{:S(2)}, u32[]{:S(2)}) collective-permute-start(f16[4,32,512]{2,1,0:T(8,128)(2,1)S(1)} %get-tuple-element.37), channel_id=1, source_target_pairs={{0,1},{1,0},{2,3},{3,2},{4,5},{5,4},{6,7},{7,6},{8,9},{9,8},{10,11... | collective-permute-start | bytes 393224 | tf_op jit(solution)/shard_map/ppermute | solution.py:234
  38.4 0.0 collective-permute-done.9
  38.4 0.1 fusion.5
  38.5 0.6 collective-permute-start.10
  39.1 0.1 fusion.2
  39.1 1.3 %early.1 = (f32[2,256,512]{2,1,0:T(8,128)S(1)}, bf16[2,512,512]{2,1,0:T(8,128)(2,1)S(1)}, bf16[2,512,512]{2,1,0:T(8,128)(2,1)S(1)}) custom-call(f32[4,32,512]{2,1,0:T(8,128)S(1)} %get-tuple-element.39.refs_0_, f32[4,32,512]{2,1,0:T(8,128)S(1)} %get-tuple-element.38.refs_1_, f32[4,32,512]{2,1,0:T(8,128)S(1)} %get-tuple-element.36.refs_2_, ...), custom_call_target="tpu_custom_call" | custom-call | tf_op jit(solution)/shard_map/early/pallas_call | solution.py:366
  40.4 1.4 %collective-permute-done.8 = f16[4,32,512]{2,1,0:T(8,128)(2,1)S(1)} collective-permute-done((f16[4,32,512]{2,1,0:T(8,128)(2,1)S(1)}, f16[4,32,512]{2,1,0:T(8,128)(2,1)S(1)}, u32[]{:S(2)}, u32[]{:S(2)}) %collective-permute-start.8) | collective-permute-done | bytes 131104 | tf_op jit(solution)/shard_map/ppermute | solution.py:234
  41.9 4.6 %collective-permute-done.10 = f16[4,32,512]{2,1,0:T(8,128)(2,1)S(1)} collective-permute-done((f16[4,32,512]{2,1,0:T(8,128)(2,1)S(1)}, f16[4,32,512]{2,1,0:T(8,128)(2,1)S(1)}, u32[]{:S(2)}, u32[]{:S(2)}) %collective-permute-start.10) | collective-permute-done | bytes 131104 | tf_op jit(solution)/shard_map/ppermute | solution.py:231
  46.5 0.0 collective-permute-done.14.refs_13_
  46.5 0.0 collective-permute-done.13.refs_12_
  46.5 3.7 %collective-permute-done.12.refs_11_ = bf16[256,512]{1,0:T(8,128)(2,1)S(1)} collective-permute-done((bf16[256,512]{1,0:T(8,128)(2,1)S(1)}, bf16[256,512]{1,0:T(8,128)(2,1)S(1)}, u32[]{:S(2)}, u32[]{:S(2)}) %collective-permute-start.12) | collective-permute-done | bytes 262176 | tf_op jit(solution)/shard_map/ppermute | solution.py:44
  50.2 3.2 %dyson.1 = (bf16[2,256,512]{2,1,0:T(8,128)(2,1)}, f32[264,512]{1,0:T(8,128)S(1)}, f32[256,512]{1,0:T(8,128)S(1)}, f32[8,512]{1,0:T(8,128)S(1)}) custom-call(f32[4,32,512]{2,1,0:T(8,128)S(1)} %convert_element_type.42.refs_0_, f32[4,32,512]{2,1,0:T(8,128)S(1)} %convert_element_type.43.refs_1_, f32[2,256,512]{2,1,0:T(8,128)S(1)} %get-tuple-element.18.refs_2_, ...), custom_call_target="tpu_custom_call" | custom-call | tf_op jit(solution)/shard_map/dyson/pallas_call | solution.py:382
  53.4 0.6 collective-permute-start.15
  54.0 0.4 begin.1
  54.4 7.1 %collective-permute-done.15 = f16[264,512]{1,0:T(8,128)(2,1)S(1)} collective-permute-done((f16[264,512]{1,0:T(8,128)(2,1)S(1)}, f16[264,512]{1,0:T(8,128)(2,1)S(1)}, u32[]{:S(2)}, u32[]{:S(2)}) %collective-permute-start.15) | collective-permute-done | bytes 270368 | tf_op jit(solution)/shard_map/ppermute | solution.py:471
  61.5 0.1 convert_element_type.55.theirs_ref
  61.6 1.7 %finish.1 = f32[256,512]{1,0:T(8,128)} custom-call(s32[1]{0:T(128)S(6)} %copy.20.refs_6_.steps_ref, f32[256,512]{1,0:T(8,128)S(1)} %get-tuple-element.21.step_ref, f32[256,512]{1,0:T(8,128)S(1)} %get-tuple-element.24.square_ref, bf16[256,512]{1,0:T(8,128)(2,1)S(1)} %get-tuple-element.25.high_ref, bf16[256,512]{1,0:T(8,128)(2,1)S(1)} %get-tuple-element.26.low_ref, ...), custom_call_target="tpu_custom_call" | custom-call | tf_op jit(solution)/shard_map/finish/pallas_call | solution.py:482
  (9 shorter events, 0.2 us)
Async XLA Ops:
  0.6 7.2 %copy-start.1 = (bf16[1,1,256,512]{3,2,1,0:T(8,128)(2,1)S(1)}, bf16[1,1,256,512]{3,2,1,0:T(8,128)(2,1)}, u32[]{:S(2)}) copy-start(bf16[1,1,256,512]{3,2,1,0:T(8,128)(2,1)} %param.8) | copy-start | bytes 786436
  0.6 15.4 %copy-start = (f32[1,256,512]{2,1,0:T(8,128)S(1)}, f32[1,256,512]{2,1,0:T(8,128)}, u32[]{:S(2)}) copy-start(f32[1,256,512]{2,1,0:T(8,128)} %param.11) | copy-start | bytes 1572868
  2.3 5.5 %collective-permute-start = (bf16[136,512]{1,0:T(8,128)(2,1)S(1)}, bf16[136,512]{1,0:T(8,128)(2,1)S(1)}, u32[]{:S(2)}, u32[]{:S(2)}) collective-permute-start(bf16[136,512]{1,0:T(8,128)(2,1)S(1)} %prepare.1), channel_id=1, source_target_pairs={{0,4},{4,0},{8,12},{12,8},{16,20},{20,16},{24,28},{28,24},{1,5},{5... | collective-permute-start | bytes 417800 | tf_op jit(solution)/shard_map/ppermute | solution.py:160
  7.8 5.8 %collective-permute-start.1 = (bf16[72,512]{1,0:T(8,128)(2,1)S(1)}, bf16[72,512]{1,0:T(8,128)(2,1)S(1)}, u32[]{:S(2)}, u32[]{:S(2)}) collective-permute-start(bf16[72,512]{1,0:T(8,128)(2,1)S(1)} %get-tuple-element.15), channel_id=1, source_target_pairs={{0,8},{4,12},{8,0},{12,4},{16,24},{20,28},{24,16},{28,20},{1,9},{5... | collective-permute-start | bytes 221192 | tf_op jit(solution)/shard_map/ppermute | solution.py:172
  8.3 7.7 %collective-permute-start.2 = (bf16[72,512]{1,0:T(8,128)(2,1)S(1)}, bf16[72,512]{1,0:T(8,128)(2,1)S(1)}, u32[]{:S(2)}, u32[]{:S(2)}) collective-permute-start(bf16[72,512]{1,0:T(8,128)(2,1)S(1)} %get-tuple-element.16), channel_id=1, source_target_pairs={{0,16},{4,20},{8,24},{12,28},{16,0},{20,4},{24,8},{28,12},{1,17},{... | collective-permute-start | bytes 221192 | tf_op jit(solution)/shard_map/ppermute | solution.py:172
  8.7 7.4 %collective-permute-start.3 = (bf16[72,512]{1,0:T(8,128)(2,1)S(1)}, bf16[72,512]{1,0:T(8,128)(2,1)S(1)}, u32[]{:S(2)}, u32[]{:S(2)}) collective-permute-start(bf16[72,512]{1,0:T(8,128)(2,1)S(1)} %get-tuple-element.17), channel_id=1, source_target_pairs={{0,24},{4,28},{8,16},{12,20},{16,8},{20,12},{24,0},{28,4},{1,25},{... | collective-permute-start | bytes 221192 | tf_op jit(solution)/shard_map/ppermute | solution.py:172
  13.6 2.5 %copy-start.2 = (s32[2]{0:T(128)S(1)}, s32[2]{0:T(128)}, u32[]{:S(2)}) copy-start(s32[2]{0:T(128)} %refs_5_.3) | copy-start | bytes 28
  13.6 2.5 %copy-start.3 = (s32[2]{0:T(128)S(1)}, s32[2]{0:T(128)}, u32[]{:S(2)}) copy-start(s32[2]{0:T(128)} %refs_6_.2) | copy-start | bytes 28
  17.0 7.4 %collective-permute-start.4 = (f16[2,32,512]{2,1,0:T(8,128)(2,1)S(1)}, f16[2,32,512]{2,1,0:T(8,128)(2,1)S(1)}, u32[]{:S(2)}, u32[]{:S(2)}) collective-permute-start(f16[2,32,512]{2,1,0:T(8,128)(2,1)S(1)} %get-tuple-element.31), channel_id=1, source_target_pairs={{0,24},{4,28},{8,16},{12,20},{16,8},{20,12},{24,0},{28,4},{1,25},{... | collective-permute-start | bytes 196616 | tf_op jit(solution)/shard_map/ppermute | solution.py:222
  19.5 13.0 %collective-permute-start.11 = (bf16[256,512]{1,0:T(8,128)(2,1)S(1)}, bf16[256,512]{1,0:T(8,128)(2,1)S(1)}, u32[]{:S(2)}, u32[]{:S(2)}) collective-permute-start(bf16[256,512]{1,0:T(8,128)(2,1)S(1)} %bitcast.55), channel_id=1, source_target_pairs={{0,8},{4,12},{8,16},{12,20},{16,24},{20,28},{1,9},{5,13},{9,17},{1... | collective-permute-start | bytes 786440 | tf_op jit(solution)/shard_map/ppermute | solution.py:44
  20.8 8.3 %collective-permute-start.5 = (f16[2,32,512]{2,1,0:T(8,128)(2,1)S(1)}, f16[2,32,512]{2,1,0:T(8,128)(2,1)S(1)}, u32[]{:S(2)}, u32[]{:S(2)}) collective-permute-start(f16[2,32,512]{2,1,0:T(8,128)(2,1)S(1)} %get-tuple-element.31), channel_id=1, source_target_pairs={{0,16},{4,20},{8,24},{12,28},{16,0},{20,4},{24,8},{28,12},{1,17},{... | collective-permute-start | bytes 196616 | tf_op jit(solution)/shard_map/ppermute | solution.py:222
  22.4 7.9 %collective-permute-start.6 = (f16[2,32,512]{2,1,0:T(8,128)(2,1)S(1)}, f16[2,32,512]{2,1,0:T(8,128)(2,1)S(1)}, u32[]{:S(2)}, u32[]{:S(2)}) collective-permute-start(f16[2,32,512]{2,1,0:T(8,128)(2,1)S(1)} %get-tuple-element.31), channel_id=1, source_target_pairs={{0,8},{4,12},{8,0},{12,4},{16,24},{20,28},{24,16},{28,20},{1,9},{5... | collective-permute-start | bytes 196616 | tf_op jit(solution)/shard_map/ppermute | solution.py:222
  30.3 6.4 %collective-permute-start.7 = (f16[2,4,32,512]{3,2,1,0:T(8,128)(2,1)S(1)}, f16[2,4,32,512]{3,2,1,0:T(8,128)(2,1)S(1)}, u32[]{:S(2)}, u32[]{:S(2)}) collective-permute-start(f16[2,4,32,512]{3,2,1,0:T(8,128)(2,1)S(1)} %bitcast_dynamic-update-slice_fusion.3), channel_id=1, source_target_pairs={{0,4},{4,0},{8,12},{12,8},{16,20},{20,16},{24,28},{28,24},{1,5},{5... | collective-permute-start | bytes 786440 | tf_op jit(solution)/shard_map/ppermute | solution.py:231
  30.9 7.5 %collective-permute-start.9 = (f16[2,4,32,512]{3,2,1,0:T(8,128)(2,1)S(1)}, f16[2,4,32,512]{3,2,1,0:T(8,128)(2,1)S(1)}, u32[]{:S(2)}, u32[]{:S(2)}) collective-permute-start(f16[2,4,32,512]{3,2,1,0:T(8,128)(2,1)S(1)} %bitcast_dynamic-update-slice_fusion.3), channel_id=1, source_target_pairs={{0,1},{1,0},{2,3},{3,2},{4,5},{5,4},{6,7},{7,6},{8,9},{9,8},{10,11... | collective-permute-start | bytes 786440 | tf_op jit(solution)/shard_map/ppermute | solution.py:234
  32.4 14.0 %collective-permute-start.14 = (bf16[256,512]{1,0:T(8,128)(2,1)S(1)}, bf16[256,512]{1,0:T(8,128)(2,1)S(1)}, u32[]{:S(2)}, u32[]{:S(2)}) collective-permute-start(bf16[256,512]{1,0:T(8,128)(2,1)S(1)} %bitcast.56), channel_id=1, source_target_pairs={{0,2},{2,0},{1,3},{3,1},{4,6},{6,4},{5,7},{7,5},{8,10},{10,8},{9,1... | collective-permute-start | bytes 786440 | tf_op jit(solution)/shard_map/ppermute | solution.py:462
  33.0 13.5 %collective-permute-start.13 = (bf16[256,512]{1,0:T(8,128)(2,1)S(1)}, bf16[256,512]{1,0:T(8,128)(2,1)S(1)}, u32[]{:S(2)}, u32[]{:S(2)}) collective-permute-start(bf16[256,512]{1,0:T(8,128)(2,1)S(1)} %chosen.1), channel_id=1, source_target_pairs={{0,4},{4,8},{8,12},{12,16},{16,20},{20,24},{24,28},{1,5},{5,9},{9,... | collective-permute-start | bytes 786440 | tf_op jit(solution)/shard_map/ppermute | solution.py:44
  34.3 15.9 %collective-permute-start.12 = (bf16[256,512]{1,0:T(8,128)(2,1)S(1)}, bf16[256,512]{1,0:T(8,128)(2,1)S(1)}, u32[]{:S(2)}, u32[]{:S(2)}) collective-permute-start(bf16[256,512]{1,0:T(8,128)(2,1)S(1)} %collective-permute-done.11.two_ref.refs_10_), channel_id=1, source_target_pairs={{0,8},{4,12},{8,16},{12,20},{16,24},{20,28},{1,9},{5,13},{9,17},{1... | collective-permute-start | bytes 786440 | tf_op jit(solution)/shard_map/ppermute | solution.py:44
  36.8 5.0 %collective-permute-start.8 = (f16[4,32,512]{2,1,0:T(8,128)(2,1)S(1)}, f16[4,32,512]{2,1,0:T(8,128)(2,1)S(1)}, u32[]{:S(2)}, u32[]{:S(2)}) collective-permute-start(f16[4,32,512]{2,1,0:T(8,128)(2,1)S(1)} %get-tuple-element.37), channel_id=1, source_target_pairs={{0,1},{1,0},{2,3},{3,2},{4,5},{5,4},{6,7},{7,6},{8,9},{9,8},{10,11... | collective-permute-start | bytes 393224 | tf_op jit(solution)/shard_map/ppermute | solution.py:234
  38.5 8.0 %collective-permute-start.10 = (f16[4,32,512]{2,1,0:T(8,128)(2,1)S(1)}, f16[4,32,512]{2,1,0:T(8,128)(2,1)S(1)}, u32[]{:S(2)}, u32[]{:S(2)}) collective-permute-start(f16[4,32,512]{2,1,0:T(8,128)(2,1)S(1)} %get-tuple-element.34), channel_id=1, source_target_pairs={{0,4},{4,0},{8,12},{12,8},{16,20},{20,16},{24,28},{28,24},{1,5},{5... | collective-permute-start | bytes 393224 | tf_op jit(solution)/shard_map/ppermute | solution.py:231
  53.4 8.1 %collective-permute-start.15 = (f16[264,512]{1,0:T(8,128)(2,1)S(1)}, f16[264,512]{1,0:T(8,128)(2,1)S(1)}, u32[]{:S(2)}, u32[]{:S(2)}) collective-permute-start(f16[264,512]{1,0:T(8,128)(2,1)S(1)} %convert_element_type.54), channel_id=1, source_target_pairs={{0,1},{1,0},{2,3},{3,2},{4,5},{5,4},{6,7},{7,6},{8,9},{9,8},{10,11... | collective-permute-start | bytes 811016 | tf_op jit(solution)/shard_map/ppermute | solution.py:471

commit v18 on v14

--- a/solution.py
+++ b/solution.py
@@ -167,7 +167,7 @@
         name="arrange",
     )(weight, green, got)
     received = [None] * (outer - 1)
-    for k in range(1, outer):
+    for k in range(outer - 1, 0, -1):
         route = [(z * 2 + x, partner(z, k, outer) * 2 + x) for z in range(outer) for x in range(2)]
         received[k - 1] = lax.ppermute(shares[k - 1], "energy", route)
 
@@ -218,7 +218,7 @@
         lax.dynamic_update_index_in_dim(jnp.zeros((outer,) + part.shape, part.dtype), part, here, 0)
         for part in chunk
     ]
-    for k in range(1, outer):
+    for k in range(outer - 1, 0, -1):
         route = [(z * 2 + x, partner(z, k, outer) * 2 + x) for z in range(outer) for x in range(2)]
         got = lax.ppermute(chunk, "energy", route)
         wholes = [
@@ -239,7 +239,7 @@
 
     beside = [along_x(part) for part in parts]
     above = [along_rep(part) for part in parts]
-    apart = [along_rep(beside[0]), along_x(above[1])]
+    apart = [along_rep(part) for part in beside]
     return [*parts, *beside, *above, *apart]
 
 

time: 61 us -> 61.1 us (level); the launches traced: 60.8 us -> 60 us
  starting transfers between devices: 22.6 us -> 21.1 us
    ppermute x3 -> x2, waiting for transfers between devices: 4.55 us -> 1.33 us  [along_x(): return lax.ppermute(part, 'energy', [(e, e ^ 1) for e in range(energies)])]
    ppermute x3 -> x4, waiting for transfers between devices: 0.75 us -> 3.67 us  [along_rep(): return lax.ppermute(part, 'rep', [(0, 1), (1, 0)])]
    ppermute x3 -> x2, starting transfers between devices: 4.06 us -> 2.03 us  [along_x(): return lax.ppermute(part, 'energy', [(e, e ^ 1) for e in range(energies)])]
    ppermute x3, waiting for transfers between devices: 2.74 us -> 4.41 us  [shifted(): return lax.ppermute(block, axis, route)]
    ppermute x3, waiting for transfers between devices: 5.69 us -> 4.98 us  [gather_energy(): got = lax.ppermute(chunk, 'energy', route)]
    ppermute x3 -> x4, starting transfers between devices: 3.55 us -> 4.18 us  [along_rep(): return lax.ppermute(part, 'rep', [(0, 1), (1, 0)])]
  transfers between devices with their start and end apart: 18 -> 18, of which waited for: 10 -> 11; matrix products, arithmetic and copies ran while one was open for 0% -> 0% of each run, Pallas kernels for 5% -> 5%
where the time goes in v18:
time: 61.1 us; the launch traced here: 60 us
  waiting for transfers between devices  26.5 us (43%)
  starting transfers between devices  21.1 us (35%)
  Pallas kernels  8.97 us (15%)
  between operations  2.97 us (5%)
    ppermute x1, waiting for transfers between devices, body(): lax.ppermute(packed.astype(coded), 'rep', [(0, 1), (1, 0)])  5.21 us
    ppermute x3, waiting for transfers between devices, gather_energy(): got = lax.ppermute(chunk, 'energy', route)  4.98 us
    ppermute x1, waiting for transfers between devices, polar_share(): got = lax.ppermute(sent, 'energy', [(e, e ^ 1) for e in range(energies)])  4.88 us
    ppermute x3, starting transfers between devices, polar_share(): received[k - 1] = lax.ppermute(shares[k - 1], 'energy', route)  4.45 us
    ppermute x3, starting transfers between devices, gather_energy(): got = lax.ppermute(chunk, 'energy', route)  4.45 us
    ppermute x3, waiting for transfers between devices, shifted(): return lax.ppermute(block, axis, route)  4.41 us
    ppermute x4, starting transfers between devices, along_rep(): return lax.ppermute(part, 'rep', [(0, 1), (1, 0)])  4.18 us
    ppermute x3, starting transfers between devices, shifted(): return lax.ppermute(block, axis, route)  3.84 us
  transfers between devices with their start and end apart: 18, of which 11 were waited for; matrix products, arithmetic and copies ran while one was open for 0% of the time, Pallas kernels for 5%

profile of v18, /device:TPU:26, one launch (start us, length us, event | category | flops | bytes accessed | tf_op | source)
XLA Modules:
  0.0 60.0 jit_solution(1748569890234891516)
XLA Ops:
  0.6 0.0 copy-start.1
  0.6 0.0 copy-start
  1.4 0.9 %prepare.1 = bf16[136,512]{1,0:T(8,128)(2,1)S(1)} custom-call(f32[1]{0:T(128)S(6)} %copy.19.weight_ref.refs_3_, bf16[256,512]{1,0:T(8,128)(2,1)} %bitcast.10), custom_call_target="tpu_custom_call" | custom-call | tf_op jit(solution)/shard_map/prepare/pallas_call | solution.py:151
  2.3 0.6 collective-permute-start
  2.9 4.9 %collective-permute-done.got_ref.refs_9_ = bf16[136,512]{1,0:T(8,128)(2,1)S(1)} collective-permute-done((bf16[136,512]{1,0:T(8,128)(2,1)S(1)}, bf16[136,512]{1,0:T(8,128)(2,1)S(1)}, u32[]{:S(2)}, u32[]{:S(2)}) %collective-permute-start) | collective-permute-done | bytes 139296 | tf_op jit(solution)/shard_map/ppermute | solution.py:160
  7.8 0.0 copy-done.1
  7.8 0.5 collective-permute-start.1
  8.3 0.3 collective-permute-start.2
  8.7 3.6 %collective-permute-start.3 = (bf16[72,512]{1,0:T(8,128)(2,1)S(1)}, bf16[72,512]{1,0:T(8,128)(2,1)S(1)}, u32[]{:S(2)}, u32[]{:S(2)}) collective-permute-start(bf16[72,512]{1,0:T(8,128)(2,1)S(1)} %get-tuple-element.17), channel_id=1, source_target_pairs={{0,24},{4,28},{8,16},{12,20},{16,8},{20,12},{24,0},{28,4},{1,25},{... | collective-permute-start | bytes 221192 | tf_op jit(solution)/shard_map/ppermute | solution.py:172
  12.3 1.3 %collective-permute-start.13 = (bf16[256,512]{1,0:T(8,128)(2,1)S(1)}, bf16[256,512]{1,0:T(8,128)(2,1)S(1)}, u32[]{:S(2)}, u32[]{:S(2)}) collective-permute-start(bf16[256,512]{1,0:T(8,128)(2,1)S(1)} %bitcast.12), channel_id=1, source_target_pairs={{0,8},{4,12},{8,16},{12,20},{16,24},{20,28},{1,9},{5,13},{9,17},{1... | collective-permute-start | bytes 786440 | tf_op jit(solution)/shard_map/ppermute | solution.py:44
  14.9 0.0 copy-start.2
  14.9 0.0 copy-start.3
  14.9 0.0 collective-permute-done.1.refs_0_
  14.9 1.5 %collective-permute-done.2.refs_1_ = bf16[72,512]{1,0:T(8,128)(2,1)S(1)} collective-permute-done((bf16[72,512]{1,0:T(8,128)(2,1)S(1)}, bf16[72,512]{1,0:T(8,128)(2,1)S(1)}, u32[]{:S(2)}, u32[]{:S(2)}) %collective-permute-start.2) | collective-permute-done | bytes 73760 | tf_op jit(solution)/shard_map/ppermute | solution.py:172
  16.4 0.6 collective-permute-done.3.refs_2_
  17.0 0.0 copy-done
  17.0 0.0 copy-done.2
  17.0 0.0 copy-done.3
  17.0 0.8 %polar.1 = f32[2,32,512]{2,1,0:T(8,128)S(1)} custom-call(bf16[72,512]{1,0:T(8,128)(2,1)S(1)} %collective-permute-done.1.refs_0_, bf16[72,512]{1,0:T(8,128)(2,1)S(1)} %collective-permute-done.2.refs_1_, bf16[72,512]{1,0:T(8,128)(2,1)S(1)} %collective-permute-done.3.refs_2_, f32[1]{0:T(128)S(6)} %copy.19.weight_ref.refs_3_, s32[2]{0:T(128)S(1)} %copy-done.2, ...), custom_call_target="tpu_custom_call" | custom-call | tf_op jit(solution)/shard_map/polar/pallas_call | solution.py:178
  17.8 1.9 %collective-permute-start.6 = (f16[2,32,512]{2,1,0:T(8,128)(2,1)S(1)}, f16[2,32,512]{2,1,0:T(8,128)(2,1)S(1)}, u32[]{:S(2)}, u32[]{:S(2)}) collective-permute-start(f16[2,32,512]{2,1,0:T(8,128)(2,1)S(1)} %convert_element_type.33), channel_id=1, source_target_pairs={{0,8},{4,12},{8,0},{12,4},{16,24},{20,28},{24,16},{28,20},{1,9},{5... | collective-permute-start | bytes 196616 | tf_op jit(solution)/shard_map/ppermute | solution.py:223
  19.8 0.2 collective-permute-start.5
  19.9 2.4 %collective-permute-start.4 = (f16[2,32,512]{2,1,0:T(8,128)(2,1)S(1)}, f16[2,32,512]{2,1,0:T(8,128)(2,1)S(1)}, u32[]{:S(2)}, u32[]{:S(2)}) collective-permute-start(f16[2,32,512]{2,1,0:T(8,128)(2,1)S(1)} %convert_element_type.33), channel_id=1, source_target_pairs={{0,24},{4,28},{8,16},{12,20},{16,8},{20,12},{24,0},{28,4},{1,25},{... | collective-permute-start | bytes 196616 | tf_op jit(solution)/shard_map/ppermute | solution.py:223
  22.4 3.7 %collective-permute-done.4 = f16[2,32,512]{2,1,0:T(8,128)(2,1)S(1)} collective-permute-done((f16[2,32,512]{2,1,0:T(8,128)(2,1)S(1)}, f16[2,32,512]{2,1,0:T(8,128)(2,1)S(1)}, u32[]{:S(2)}, u32[]{:S(2)}) %collective-permute-start.4) | collective-permute-done | bytes 65568 | tf_op jit(solution)/shard_map/ppermute | solution.py:223
  26.1 1.3 %collective-permute-done.5 = f16[2,32,512]{2,1,0:T(8,128)(2,1)S(1)} collective-permute-done((f16[2,32,512]{2,1,0:T(8,128)(2,1)S(1)}, f16[2,32,512]{2,1,0:T(8,128)(2,1)S(1)}, u32[]{:S(2)}, u32[]{:S(2)}) %collective-permute-start.5) | collective-permute-done | bytes 65568 | tf_op jit(solution)/shard_map/ppermute | solution.py:223
  27.4 0.0 collective-permute-done.6
  27.4 1.6 %collective-permute-start.12 = (f16[4,32,512]{2,1,0:T(8,128)(2,1)S(1)}, f16[4,32,512]{2,1,0:T(8,128)(2,1)S(1)}, u32[]{:S(2)}, u32[]{:S(2)}) collective-permute-start(f16[4,32,512]{2,1,0:T(8,128)(2,1)S(1)} %get-tuple-element.30), channel_id=1, source_target_pairs={{0,1},{1,0},{2,3},{3,2},{4,5},{5,4},{6,7},{7,6},{8,9},{9,8},{10,11... | collective-permute-start | bytes 393224 | tf_op jit(solution)/shard_map/ppermute | solution.py:238
  29.0 0.5 collective-permute-start.9
  29.6 0.0 collective-permute-start.16
  29.6 0.5 collective-permute-start.11
  30.1 0.0 collective-permute-done.13.two_ref.refs_10_
  30.1 1.5 %collective-permute-start.7 = (f16[4,32,512]{2,1,0:T(8,128)(2,1)S(1)}, f16[4,32,512]{2,1,0:T(8,128)(2,1)S(1)}, u32[]{:S(2)}, u32[]{:S(2)}) collective-permute-start(f16[4,32,512]{2,1,0:T(8,128)(2,1)S(1)} %get-tuple-element.31), channel_id=1, source_target_pairs={{0,4},{4,0},{8,12},{12,8},{16,20},{20,16},{24,28},{28,24},{1,5},{5... | collective-permute-start | bytes 393224 | tf_op jit(solution)/shard_map/ppermute | solution.py:235
  31.6 0.6 chosen.1
  32.1 0.3 collective-permute-done.12
  32.5 1.3 %collective-permute-start.15 = (bf16[256,512]{1,0:T(8,128)(2,1)S(1)}, bf16[256,512]{1,0:T(8,128)(2,1)S(1)}, u32[]{:S(2)}, u32[]{:S(2)}) collective-permute-start(bf16[256,512]{1,0:T(8,128)(2,1)S(1)} %chosen.1), channel_id=1, source_target_pairs={{0,4},{4,8},{8,12},{12,16},{16,20},{20,24},{24,28},{1,5},{5,9},{9,... | collective-permute-start | bytes 786440 | tf_op jit(solution)/shard_map/ppermute | solution.py:44
  33.8 1.3 %collective-permute-done.9 = f16[4,32,512]{2,1,0:T(8,128)(2,1)S(1)} collective-permute-done((f16[4,32,512]{2,1,0:T(8,128)(2,1)S(1)}, f16[4,32,512]{2,1,0:T(8,128)(2,1)S(1)}, u32[]{:S(2)}, u32[]{:S(2)}) %collective-permute-start.9) | collective-permute-done | bytes 131104 | tf_op jit(solution)/shard_map/ppermute | solution.py:235
  35.1 1.3 %collective-permute-start.14 = (bf16[256,512]{1,0:T(8,128)(2,1)S(1)}, bf16[256,512]{1,0:T(8,128)(2,1)S(1)}, u32[]{:S(2)}, u32[]{:S(2)}) collective-permute-start(bf16[256,512]{1,0:T(8,128)(2,1)S(1)} %collective-permute-done.13.two_ref.refs_10_), channel_id=1, source_target_pairs={{0,8},{4,12},{8,16},{12,20},{16,24},{20,28},{1,9},{5,13},{9,17},{1... | collective-permute-start | bytes 786440 | tf_op jit(solution)/shard_map/ppermute | solution.py:44
  36.4 0.0 collective-permute-done.11
  36.4 1.1 %collective-permute-start.10 = (f16[4,32,512]{2,1,0:T(8,128)(2,1)S(1)}, f16[4,32,512]{2,1,0:T(8,128)(2,1)S(1)}, u32[]{:S(2)}, u32[]{:S(2)}) collective-permute-start(f16[4,32,512]{2,1,0:T(8,128)(2,1)S(1)} %collective-permute-done.9), channel_id=1, source_target_pairs={{0,1},{1,0},{2,3},{3,2},{4,5},{5,4},{6,7},{7,6},{8,9},{9,8},{10,11... | collective-permute-start | bytes 393224 | tf_op jit(solution)/shard_map/ppermute | solution.py:238
  37.5 0.0 collective-permute-done.7
  37.5 1.0 %collective-permute-start.8 = (f16[4,32,512]{2,1,0:T(8,128)(2,1)S(1)}, f16[4,32,512]{2,1,0:T(8,128)(2,1)S(1)}, u32[]{:S(2)}, u32[]{:S(2)}) collective-permute-start(f16[4,32,512]{2,1,0:T(8,128)(2,1)S(1)} %collective-permute-done.7), channel_id=1, source_target_pairs={{0,1},{1,0},{2,3},{3,2},{4,5},{5,4},{6,7},{7,6},{8,9},{9,8},{10,11... | collective-permute-start | bytes 393224 | tf_op jit(solution)/shard_map/ppermute | solution.py:238
  38.7 1.3 %early.1 = (f32[2,256,512]{2,1,0:T(8,128)S(1)}, bf16[2,512,512]{2,1,0:T(8,128)(2,1)S(1)}, bf16[2,512,512]{2,1,0:T(8,128)(2,1)S(1)}) custom-call(f32[4,32,512]{2,1,0:T(8,128)S(1)} %convert_element_type.36.refs_0_, f32[4,32,512]{2,1,0:T(8,128)S(1)} %convert_element_type.37.refs_1_, f32[4,32,512]{2,1,0:T(8,128)S(1)} %convert_element_type.38.refs_2_, ...), custom_call_target="tpu_custom_call" | custom-call | tf_op jit(solution)/shard_map/early/pallas_call | solution.py:370
  40.0 2.0 %collective-permute-done.10 = f16[4,32,512]{2,1,0:T(8,128)(2,1)S(1)} collective-permute-done((f16[4,32,512]{2,1,0:T(8,128)(2,1)S(1)}, f16[4,32,512]{2,1,0:T(8,128)(2,1)S(1)}, u32[]{:S(2)}, u32[]{:S(2)}) %collective-permute-start.10) | collective-permute-done | bytes 131104 | tf_op jit(solution)/shard_map/ppermute | solution.py:238
  42.0 1.4 %collective-permute-done.8 = f16[4,32,512]{2,1,0:T(8,128)(2,1)S(1)} collective-permute-done((f16[4,32,512]{2,1,0:T(8,128)(2,1)S(1)}, f16[4,32,512]{2,1,0:T(8,128)(2,1)S(1)}, u32[]{:S(2)}, u32[]{:S(2)}) %collective-permute-start.8) | collective-permute-done | bytes 131104 | tf_op jit(solution)/shard_map/ppermute | solution.py:238
  43.4 0.0 collective-permute-done.16.refs_13_
  43.4 0.0 collective-permute-done.15.refs_12_
  43.4 4.4 %collective-permute-done.14.refs_11_ = bf16[256,512]{1,0:T(8,128)(2,1)S(1)} collective-permute-done((bf16[256,512]{1,0:T(8,128)(2,1)S(1)}, bf16[256,512]{1,0:T(8,128)(2,1)S(1)}, u32[]{:S(2)}, u32[]{:S(2)}) %collective-permute-start.14) | collective-permute-done | bytes 262176 | tf_op jit(solution)/shard_map/ppermute | solution.py:44
  47.8 3.2 %dyson.1 = (bf16[2,256,512]{2,1,0:T(8,128)(2,1)}, f32[264,512]{1,0:T(8,128)S(1)}, f32[256,512]{1,0:T(8,128)S(1)}, f32[8,512]{1,0:T(8,128)S(1)}) custom-call(f32[4,32,512]{2,1,0:T(8,128)S(1)} %convert_element_type.34.refs_0_, f32[4,32,512]{2,1,0:T(8,128)S(1)} %convert_element_type.35.refs_1_, f32[2,256,512]{2,1,0:T(8,128)S(1)} %get-tuple-element.18.refs_2_, ...), custom_call_target="tpu_custom_call" | custom-call | tf_op jit(solution)/shard_map/dyson/pallas_call | solution.py:386
  51.0 1.6 %collective-permute-start.17 = (f16[264,512]{1,0:T(8,128)(2,1)S(1)}, f16[264,512]{1,0:T(8,128)(2,1)S(1)}, u32[]{:S(2)}, u32[]{:S(2)}) collective-permute-start(f16[264,512]{1,0:T(8,128)(2,1)S(1)} %convert_element_type.42), channel_id=1, source_target_pairs={{0,1},{1,0},{2,3},{3,2},{4,5},{5,4},{6,7},{7,6},{8,9},{9,8},{10,11... | collective-permute-start | bytes 811016 | tf_op jit(solution)/shard_map/ppermute | solution.py:475
  52.6 0.4 begin.1
  53.0 5.2 %collective-permute-done.17 = f16[264,512]{1,0:T(8,128)(2,1)S(1)} collective-permute-done((f16[264,512]{1,0:T(8,128)(2,1)S(1)}, f16[264,512]{1,0:T(8,128)(2,1)S(1)}, u32[]{:S(2)}, u32[]{:S(2)}) %collective-permute-start.17) | collective-permute-done | bytes 270368 | tf_op jit(solution)/shard_map/ppermute | solution.py:475
  58.2 0.1 convert_element_type.43.theirs_ref
  58.3 1.7 %finish.1 = f32[256,512]{1,0:T(8,128)} custom-call(s32[1]{0:T(128)S(6)} %copy.21.refs_6_.steps_ref, f32[256,512]{1,0:T(8,128)S(1)} %get-tuple-element.21.step_ref, f32[256,512]{1,0:T(8,128)S(1)} %get-tuple-element.24.square_ref, bf16[256,512]{1,0:T(8,128)(2,1)S(1)} %get-tuple-element.25.high_ref, bf16[256,512]{1,0:T(8,128)(2,1)S(1)} %get-tuple-element.26.low_ref, ...), custom_call_target="tpu_custom_call" | custom-call | tf_op jit(solution)/shard_map/finish/pallas_call | solution.py:486
  (18 shorter events, 0.4 us)
Async XLA Ops:
  0.6 7.2 %copy-start.1 = (bf16[1,1,256,512]{3,2,1,0:T(8,128)(2,1)S(1)}, bf16[1,1,256,512]{3,2,1,0:T(8,128)(2,1)}, u32[]{:S(2)}) copy-start(bf16[1,1,256,512]{3,2,1,0:T(8,128)(2,1)} %param.8) | copy-start | bytes 786436
  0.6 16.3 %copy-start = (f32[1,256,512]{2,1,0:T(8,128)S(1)}, f32[1,256,512]{2,1,0:T(8,128)}, u32[]{:S(2)}) copy-start(f32[1,256,512]{2,1,0:T(8,128)} %param.11) | copy-start | bytes 1572868
  2.3 5.5 %collective-permute-start = (bf16[136,512]{1,0:T(8,128)(2,1)S(1)}, bf16[136,512]{1,0:T(8,128)(2,1)S(1)}, u32[]{:S(2)}, u32[]{:S(2)}) collective-permute-start(bf16[136,512]{1,0:T(8,128)(2,1)S(1)} %prepare.1), channel_id=1, source_target_pairs={{0,4},{4,0},{8,12},{12,8},{16,20},{20,16},{24,28},{28,24},{1,5},{5... | collective-permute-start | bytes 417800 | tf_op jit(solution)/shard_map/ppermute | solution.py:160
  7.8 7.1 %collective-permute-start.1 = (bf16[72,512]{1,0:T(8,128)(2,1)S(1)}, bf16[72,512]{1,0:T(8,128)(2,1)S(1)}, u32[]{:S(2)}, u32[]{:S(2)}) collective-permute-start(bf16[72,512]{1,0:T(8,128)(2,1)S(1)} %get-tuple-element.15), channel_id=1, source_target_pairs={{0,8},{4,12},{8,0},{12,4},{16,24},{20,28},{24,16},{28,20},{1,9},{5... | collective-permute-start | bytes 221192 | tf_op jit(solution)/shard_map/ppermute | solution.py:172
  8.3 8.1 %collective-permute-start.2 = (bf16[72,512]{1,0:T(8,128)(2,1)S(1)}, bf16[72,512]{1,0:T(8,128)(2,1)S(1)}, u32[]{:S(2)}, u32[]{:S(2)}) collective-permute-start(bf16[72,512]{1,0:T(8,128)(2,1)S(1)} %get-tuple-element.16), channel_id=1, source_target_pairs={{0,16},{4,20},{8,24},{12,28},{16,0},{20,4},{24,8},{28,12},{1,17},{... | collective-permute-start | bytes 221192 | tf_op jit(solution)/shard_map/ppermute | solution.py:172
  8.7 8.3 %collective-permute-start.3 = (bf16[72,512]{1,0:T(8,128)(2,1)S(1)}, bf16[72,512]{1,0:T(8,128)(2,1)S(1)}, u32[]{:S(2)}, u32[]{:S(2)}) collective-permute-start(bf16[72,512]{1,0:T(8,128)(2,1)S(1)} %get-tuple-element.17), channel_id=1, source_target_pairs={{0,24},{4,28},{8,16},{12,20},{16,8},{20,12},{24,0},{28,4},{1,25},{... | collective-permute-start | bytes 221192 | tf_op jit(solution)/shard_map/ppermute | solution.py:172
  12.3 17.8 %collective-permute-start.13 = (bf16[256,512]{1,0:T(8,128)(2,1)S(1)}, bf16[256,512]{1,0:T(8,128)(2,1)S(1)}, u32[]{:S(2)}, u32[]{:S(2)}) collective-permute-start(bf16[256,512]{1,0:T(8,128)(2,1)S(1)} %bitcast.12), channel_id=1, source_target_pairs={{0,8},{4,12},{8,16},{12,20},{16,24},{20,28},{1,9},{5,13},{9,17},{1... | collective-permute-start | bytes 786440 | tf_op jit(solution)/shard_map/ppermute | solution.py:44
  14.9 2.1 %copy-start.2 = (s32[2]{0:T(128)S(1)}, s32[2]{0:T(128)}, u32[]{:S(2)}) copy-start(s32[2]{0:T(128)} %refs_5_.3) | copy-start | bytes 28
  14.9 2.1 %copy-start.3 = (s32[2]{0:T(128)S(1)}, s32[2]{0:T(128)}, u32[]{:S(2)}) copy-start(s32[2]{0:T(128)} %refs_6_.2) | copy-start | bytes 28
  17.8 9.6 %collective-permute-start.6 = (f16[2,32,512]{2,1,0:T(8,128)(2,1)S(1)}, f16[2,32,512]{2,1,0:T(8,128)(2,1)S(1)}, u32[]{:S(2)}, u32[]{:S(2)}) collective-permute-start(f16[2,32,512]{2,1,0:T(8,128)(2,1)S(1)} %convert_element_type.33), channel_id=1, source_target_pairs={{0,8},{4,12},{8,0},{12,4},{16,24},{20,28},{24,16},{28,20},{1,9},{5... | collective-permute-start | bytes 196616 | tf_op jit(solution)/shard_map/ppermute | solution.py:223
  19.8 7.6 %collective-permute-start.5 = (f16[2,32,512]{2,1,0:T(8,128)(2,1)S(1)}, f16[2,32,512]{2,1,0:T(8,128)(2,1)S(1)}, u32[]{:S(2)}, u32[]{:S(2)}) collective-permute-start(f16[2,32,512]{2,1,0:T(8,128)(2,1)S(1)} %convert_element_type.33), channel_id=1, source_target_pairs={{0,16},{4,20},{8,24},{12,28},{16,0},{20,4},{24,8},{28,12},{1,17},{... | collective-permute-start | bytes 196616 | tf_op jit(solution)/shard_map/ppermute | solution.py:223
  19.9 6.2 %collective-permute-start.4 = (f16[2,32,512]{2,1,0:T(8,128)(2,1)S(1)}, f16[2,32,512]{2,1,0:T(8,128)(2,1)S(1)}, u32[]{:S(2)}, u32[]{:S(2)}) collective-permute-start(f16[2,32,512]{2,1,0:T(8,128)(2,1)S(1)} %convert_element_type.33), channel_id=1, source_target_pairs={{0,24},{4,28},{8,16},{12,20},{16,8},{20,12},{24,0},{28,4},{1,25},{... | collective-permute-start | bytes 196616 | tf_op jit(solution)/shard_map/ppermute | solution.py:223
  27.4 5.0 %collective-permute-start.12 = (f16[4,32,512]{2,1,0:T(8,128)(2,1)S(1)}, f16[4,32,512]{2,1,0:T(8,128)(2,1)S(1)}, u32[]{:S(2)}, u32[]{:S(2)}) collective-permute-start(f16[4,32,512]{2,1,0:T(8,128)(2,1)S(1)} %get-tuple-element.30), channel_id=1, source_target_pairs={{0,1},{1,0},{2,3},{3,2},{4,5},{5,4},{6,7},{7,6},{8,9},{9,8},{10,11... | collective-permute-start | bytes 393224 | tf_op jit(solution)/shard_map/ppermute | solution.py:238
  29.0 6.1 %collective-permute-start.9 = (f16[4,32,512]{2,1,0:T(8,128)(2,1)S(1)}, f16[4,32,512]{2,1,0:T(8,128)(2,1)S(1)}, u32[]{:S(2)}, u32[]{:S(2)}) collective-permute-start(f16[4,32,512]{2,1,0:T(8,128)(2,1)S(1)} %get-tuple-element.30), channel_id=1, source_target_pairs={{0,4},{4,0},{8,12},{12,8},{16,20},{20,16},{24,28},{28,24},{1,5},{5... | collective-permute-start | bytes 393224 | tf_op jit(solution)/shard_map/ppermute | solution.py:235
  29.6 13.8 %collective-permute-start.16 = (bf16[256,512]{1,0:T(8,128)(2,1)S(1)}, bf16[256,512]{1,0:T(8,128)(2,1)S(1)}, u32[]{:S(2)}, u32[]{:S(2)}) collective-permute-start(bf16[256,512]{1,0:T(8,128)(2,1)S(1)} %bitcast.14), channel_id=1, source_target_pairs={{0,2},{2,0},{1,3},{3,1},{4,6},{6,4},{5,7},{7,5},{8,10},{10,8},{9,1... | collective-permute-start | bytes 786440 | tf_op jit(solution)/shard_map/ppermute | solution.py:466
  29.6 6.8 %collective-permute-start.11 = (f16[4,32,512]{2,1,0:T(8,128)(2,1)S(1)}, f16[4,32,512]{2,1,0:T(8,128)(2,1)S(1)}, u32[]{:S(2)}, u32[]{:S(2)}) collective-permute-start(f16[4,32,512]{2,1,0:T(8,128)(2,1)S(1)} %get-tuple-element.31), channel_id=1, source_target_pairs={{0,1},{1,0},{2,3},{3,2},{4,5},{5,4},{6,7},{7,6},{8,9},{9,8},{10,11... | collective-permute-start | bytes 393224 | tf_op jit(solution)/shard_map/ppermute | solution.py:238
  30.1 7.4 %collective-permute-start.7 = (f16[4,32,512]{2,1,0:T(8,128)(2,1)S(1)}, f16[4,32,512]{2,1,0:T(8,128)(2,1)S(1)}, u32[]{:S(2)}, u32[]{:S(2)}) collective-permute-start(f16[4,32,512]{2,1,0:T(8,128)(2,1)S(1)} %get-tuple-element.31), channel_id=1, source_target_pairs={{0,4},{4,0},{8,12},{12,8},{16,20},{20,16},{24,28},{28,24},{1,5},{5... | collective-permute-start | bytes 393224 | tf_op jit(solution)/shard_map/ppermute | solution.py:235
  32.5 10.9 %collective-permute-start.15 = (bf16[256,512]{1,0:T(8,128)(2,1)S(1)}, bf16[256,512]{1,0:T(8,128)(2,1)S(1)}, u32[]{:S(2)}, u32[]{:S(2)}) collective-permute-start(bf16[256,512]{1,0:T(8,128)(2,1)S(1)} %chosen.1), channel_id=1, source_target_pairs={{0,4},{4,8},{8,12},{12,16},{16,20},{20,24},{24,28},{1,5},{5,9},{9,... | collective-permute-start | bytes 786440 | tf_op jit(solution)/shard_map/ppermute | solution.py:44
  35.1 12.7 %collective-permute-start.14 = (bf16[256,512]{1,0:T(8,128)(2,1)S(1)}, bf16[256,512]{1,0:T(8,128)(2,1)S(1)}, u32[]{:S(2)}, u32[]{:S(2)}) collective-permute-start(bf16[256,512]{1,0:T(8,128)(2,1)S(1)} %collective-permute-done.13.two_ref.refs_10_), channel_id=1, source_target_pairs={{0,8},{4,12},{8,16},{12,20},{16,24},{20,28},{1,9},{5,13},{9,17},{1... | collective-permute-start | bytes 786440 | tf_op jit(solution)/shard_map/ppermute | solution.py:44
  36.4 5.5 %collective-permute-start.10 = (f16[4,32,512]{2,1,0:T(8,128)(2,1)S(1)}, f16[4,32,512]{2,1,0:T(8,128)(2,1)S(1)}, u32[]{:S(2)}, u32[]{:S(2)}) collective-permute-start(f16[4,32,512]{2,1,0:T(8,128)(2,1)S(1)} %collective-permute-done.9), channel_id=1, source_target_pairs={{0,1},{1,0},{2,3},{3,2},{4,5},{5,4},{6,7},{7,6},{8,9},{9,8},{10,11... | collective-permute-start | bytes 393224 | tf_op jit(solution)/shard_map/ppermute | solution.py:238
  37.5 5.8 %collective-permute-start.8 = (f16[4,32,512]{2,1,0:T(8,128)(2,1)S(1)}, f16[4,32,512]{2,1,0:T(8,128)(2,1)S(1)}, u32[]{:S(2)}, u32[]{:S(2)}) collective-permute-start(f16[4,32,512]{2,1,0:T(8,128)(2,1)S(1)} %collective-permute-done.7), channel_id=1, source_target_pairs={{0,1},{1,0},{2,3},{3,2},{4,5},{5,4},{6,7},{7,6},{8,9},{9,8},{10,11... | collective-permute-start | bytes 393224 | tf_op jit(solution)/shard_map/ppermute | solution.py:238
  51.0 7.2 %collective-permute-start.17 = (f16[264,512]{1,0:T(8,128)(2,1)S(1)}, f16[264,512]{1,0:T(8,128)(2,1)S(1)}, u32[]{:S(2)}, u32[]{:S(2)}) collective-permute-start(f16[264,512]{1,0:T(8,128)(2,1)S(1)} %convert_element_type.42), channel_id=1, source_target_pairs={{0,1},{1,0},{2,3},{3,2},{4,5},{5,4},{6,7},{7,6},{8,9},{9,8},{10,11... | collective-permute-start | bytes 811016 | tf_op jit(solution)/shard_map/ppermute | solution.py:475
